TPU v7x, 32 devices: a whole 2x2x4 slice. The times are simulated.
32 devices in a mesh: parts: 2 (over y), line: 4 (over x, core), cross: 4 (over z).
Axes of the slice: x: 2, y: 2, z: 4, core: 2. Of those that a mesh axis runs over, the one named last changes fastest.
Arguments:
- ham_tiles: float32 [128, 64, 768], P(('parts', 'line', 'cross')), parts along dimension 0, may hold values from -0.21875 to 0.21875
- ham_cols: int32 [128, 12], P(('parts', 'line', 'cross')), parts along dimension 0, may hold values from 0 to 15, as said below
- ham_count: int32 [128], P(('parts', 'line', 'cross')), parts along dimension 0, may hold values from 3 to 12, as said below
- dens_tiles: float32 [128, 64, 512], P(('parts', 'line', 'cross')), parts along dimension 0, may hold values from -6 to 6
- dens_cols: int32 [128, 8], P(('parts', 'line', 'cross')), parts along dimension 0, may hold values from 0 to 15, as said below
- dens_count: int32 [128], P(('parts', 'line', 'cross')), parts along dimension 0, may hold values from 2 to 8, as said below
- over_tiles: float32 [128, 64, 768], P(('parts', 'line', 'cross')), parts along dimension 0, may hold values from -0.21875 to 0.21875
Outputs:
- product_rows: float32 [128, 64, 1024], P(('parts', 'line', 'cross')), parts along dimension 0
- window: float32 [128, 64, 3072], P(('parts', 'line', 'cross')), parts along dimension 0
There are 2 independent parts, one for each index of `parts`. A program takes and returns all parts, laid end to end along the dimension named above; each array names one. Nothing has to cross between parts.
Inputs may be any that keep to these rules, and one draw needn't show every extreme that they name: `ham_cols`: within a block row the column indices are distinct. Slots at or beyond the row's count are not part of the matrix. `dens_cols`: within a block row the column indices are distinct. Slots at or beyond the row's count are not part of the matrix. `ham_count`: the first block row of every region, and the block rows of one device in the middle of every region, use all 12 slots. `dens_count`: the first block row of every region, and the block rows of one device in the middle of every region, use all 8 slots.
All inputs are finite; a program needn't handle non-finite values.
Results may differ from a plain program's by a relative error of at most 0.0003.
Values sent between devices are 32-bit elements; how exact they have to be, the bound alone decides.
No kernel may reach another device: no remote copies, remote signals or barrier semaphores. Data moves between devices by JAX's collectives and lax.ppermute only.
A program may use at most 128 MiB of HBM per device.

v0:
```python
import jax
import jax.numpy as jnp
from jax import lax
from jax.sharding import PartitionSpec as P

R_DEV = 4


exact_prec = lax.Precision.HIGHEST


def from_behind(shard, axis, by):
    count = lax.axis_size(axis)
    return lax.ppermute(shard, axis, [(i, (i + by) % count) for i in range(count)])


def densify(tiles_in, columns, counts, width_cols):
    rows_count = tiles_in.shape[0]
    tile_size = tiles_in.shape[1]
    list_len = columns.shape[1]
    in_list = jnp.arange(list_len, dtype=jnp.int32)[None, :] < counts[:, None]
    matches = columns[:, :, None] == jnp.arange(width_cols, dtype=jnp.int32)[None, None, :]
    onehot = jnp.where(matches & in_list[:, :, None], 1.0, 0.0).astype(jnp.float32)
    shaped = tiles_in.reshape(rows_count, tile_size, list_len, tile_size)
    dense_rows = jnp.einsum("nkb,nxky->nxby", onehot, shaped, precision=exact_prec)
    return dense_rows.reshape(rows_count, tile_size, width_cols * tile_size)


def shards(ham_tiles, ham_cols, ham_count, dens_tiles, dens_cols, dens_count, over_tiles):
    region_rows = R_DEV * lax.axis_size("cross")
    own_rows = ham_tiles.shape[0]
    tile_size = ham_tiles.shape[1]
    ham_dense = densify(ham_tiles, ham_cols, ham_count, region_rows).reshape(
        own_rows * tile_size, region_rows * tile_size
    )
    piece_tiles = lax.all_gather(dens_tiles, "cross", axis=0, tiled=True)
    piece_cols = lax.all_gather(dens_cols, "cross", axis=0, tiled=True)
    piece_count = lax.all_gather(dens_count, "cross", axis=0, tiled=True)
    piece_rows = piece_tiles.shape[0]
    piece_dense = densify(piece_tiles, piece_cols, piece_count, region_rows).reshape(
        piece_rows * tile_size, region_rows * tile_size
    )
    product = jnp.dot(
        ham_dense, piece_dense, precision=exact_prec, preferred_element_type=jnp.float32
    )
    product_rows = product.reshape(own_rows, tile_size, region_rows * tile_size)
    weights = over_tiles.reshape(own_rows, tile_size, 3, own_rows, tile_size)
    terms = jnp.einsum("kxsjy,kyn->sjxn", weights, product_rows, precision=exact_prec)
    from_prev = from_behind(terms[2], "line", 1)
    from_next = from_behind(terms[0], "line", -1)
    own_term = terms[1]
    window = jnp.concatenate([from_prev, own_term, from_next], axis=-1)
    return (product_rows, window)


def solution(mesh):
    placed = (
        P(("parts", "line", "cross"), None, None),
        P(("parts", "line", "cross"), None),
        P(("parts", "line", "cross")),
        P(("parts", "line", "cross"), None, None),
        P(("parts", "line", "cross"), None),
        P(("parts", "line", "cross")),
        P(("parts", "line", "cross"), None, None),
    )
    return jax.shard_map(
        shards,
        mesh=mesh,
        in_specs=placed,
        out_specs=(
            P(("parts", "line", "cross"), None, None),
            P(("parts", "line", "cross"), None, None),
        ),
        check_vma=False,
    )
```

profile of v0, /device:TPU:0, one launch (start us, length us, event | category | flops | bytes accessed | tf_op | source)
XLA Modules:
  0.0 124.3 jit_solution(11365427121358235478)
XLA Ops:
  7.2 0.0 copy-start.3
  7.2 0.0 copy-start.1
  7.2 0.0 all-gather.3.cloned.1.call-start
  7.2 0.7 all-gather.3.cloned.1.call-update
  7.9 2.8 %reshape.60 = f32[4,64,12,64]{3,2,1,0:T(8,128)} reshape(f32[4,64,768]{2,1,0:T(8,128)} %param.7) | data formatting | bytes 1572864 | tf_op jit(solution)/shard_map/reshape | solution.py:24
  10.7 0.0 copy-done.3
  10.7 0.1 iota_compare_fusion.3
  10.8 0.0 copy-done.1
  10.8 3.5 %convolution_bitcast_fusion.2 = f32[4,64,16,64]{3,2,1,0:T(8,128)S(1)} fusion(f32[4,64,12,64]{3,2,1,0:T(8,128)} %reshape.60, s32[4,12]{1,0:T(4,128)S(1)} %copy-done.1, pred[4,12]{1,0:T(4,128)(4,1)S(1)} %iota_compare_fusion.3), kind=kOutput, calls=%fused_computation.3 | convolution fusion | flops 37751040 | bytes 1835248 | tf_op jit(solution)/shard_map/nkb,nxky->nxby/dot_general | solution.py:25
  14.2 0.0 copy-start.5
  14.2 0.0 copy-start.4
  14.2 0.0 copy-start.2
  14.2 0.6 dot_general.15
  14.8 1.9 %reshape.62 = f32[4,64,3,4,64]{4,3,2,1,0:T(4,128)S(1)} reshape(f32[4,64,768]{2,1,0:T(8,128)} %param.13) | data formatting | bytes 1572864 | tf_op jit(solution)/shard_map/reshape | solution.py:47
  16.7 0.0 copy-done.5
  16.7 0.6 dynamic-slice
  18.0 0.0 copy-done.4
  18.0 0.2 dynamic-update-slice
  18.2 10.7 %all-reduce = s32[16]{0:T(128)S(1)} all-reduce(s32[16]{0:T(128)S(1)} %dynamic-update-slice), channel_id=1, replica_groups=mesh['parts'=2,'line'=4,'cross'=4] {'cross'}, use_global_device_ids=true, to_apply=%add | all-reduce | flops 16 | bytes 128
  29.0 0.0 copy-done.2
  29.0 12.3 %all-gather = s32[4,4,8]{2,1,0:T(4,128)S(1)} all-gather(s32[1,4,8]{2,1,0:T(4,128)S(1)} %bitcast.42), channel_id=1, replica_groups=mesh['parts'=2,'line'=4,'cross'=4] {'cross'}, dimensions={0}, use_global_device_ids=true | all-gather | bytes 640 | tf_op jit(solution)/shard_map/all_gather | solution.py:37
  41.3 0.1 iota_compare_fusion.2
  41.3 17.4 %all-gather.3.cloned.1.call-done = f32[16,64,512]{2,1,0:T(8,128)} async-done(((f32[4,64,512]{2,1,0:T(8,128)}), f32[16,64,512]{2,1,0:T(8,128)}) %all-gather.3.cloned.1.call-update) | async-done | bytes 2097168 | tf_op jit(solution)/shard_map/all_gather | solution.py:36
  58.7 4.4 %reshape.61 = f32[16,64,8,64]{3,2,1,0:T(8,128)} reshape(f32[16,64,512]{2,1,0:T(8,128)} %all-gather.3.cloned.1.call-done) | data formatting | bytes 4194304 | tf_op jit(solution)/shard_map/reshape | solution.py:24
  63.1 11.3 %convolution_bitcast_fusion = f32[16,64,16,64]{3,2,1,0:T(8,128)} fusion(f32[16,64,8,64]{3,2,1,0:T(8,128)} %reshape.61, s32[16,8]{1,0:T(8,128)S(1)} %bitcast.41, pred[16,8]{1,0:T(8,128)(4,1)S(1)} %iota_compare_fusion.2), kind=kOutput, calls=%fused_computation | convolution fusion | flops 100669440 | bytes 6292096 | tf_op jit(solution)/shard_map/nkb,nxky->nxby/dot_general | solution.py:25
  74.4 7.6 %reshape.72 = f32[1024,1024,1]{1,0,2:T(8,128)} reshape(f32[16,64,16,64]{3,2,1,0:T(8,128)} %convolution_bitcast_fusion) | data formatting | bytes 8388608 | tf_op jit(solution)/shard_map/reshape;reshape | solution.py:40
  82.0 5.7 %fusion.22 = f32[4,64,1024]{2,1,0:T(8,128)S(1)} fusion(f32[4,64,1024]{2,1,0:T(8,128)S(1)} %dot_general.15, f32[1024,1024,1]{1,0,2:T(8,128)} %reshape.72), kind=kOutput, calls=%fused_computation.31 | convolution fusion | flops 3221225472 | bytes 6291456 | tf_op jit(solution)/shard_map/dot_general | solution.py:43
  87.7 0.0 copy-start
  87.7 2.9 %convolution_bitcast_fusion.1 = f32[3,4,64,1024]{3,2,1,0:T(8,128)S(1)} fusion(f32[4,64,3,4,64]{4,3,2,1,0:T(4,128)S(1)} %reshape.62, f32[4,64,1024]{2,1,0:T(8,128)S(1)} %fusion.22), kind=kOutput, calls=%fused_computation.2 | convolution fusion | flops 2415919104 | bytes 4980736 | tf_op jit(solution)/shard_map/kxsjy,kyn->sjxn/dot_general | solution.py:48
  90.6 0.0 copy-done
  90.6 0.3 slice_bitcast_fusion.2
  90.9 0.1 collective-permute-start
  91.0 1.7 %collective-permute-start.1 = (f32[4,64,1024]{2,1,0:T(8,128)S(1)}, f32[4,64,1024]{2,1,0:T(8,128)S(1)}, u32[]{:S(2)}, u32[]{:S(2)}) collective-permute-start(f32[4,64,1024]{2,1,0:T(8,128)S(1)} %get-tuple-element.3), channel_id=1, source_target_pairs={{0,12},{4,0},{8,4},{12,8},{1,13},{5,1},{9,5},{13,9},{2,14},{6,2},{... | collective-permute-start | bytes 3145736 | tf_op jit(solution)/shard_map/ppermute | solution.py:14
  92.7 21.9 %collective-permute-done = f32[4,64,1024]{2,1,0:T(8,128)S(1)} collective-permute-done((f32[4,64,1024]{2,1,0:T(8,128)S(1)}, f32[4,64,1024]{2,1,0:T(8,128)S(1)}, u32[]{:S(2)}, u32[]{:S(2)}) %collective-permute-start) | collective-permute-done | bytes 1048608 | tf_op jit(solution)/shard_map/ppermute | solution.py:14
  114.6 0.8 collective-permute-done.1
  115.4 2.0 %pad_maximum_fusion = f32[4,64,3072]{2,1,0:T(8,128)} fusion(f32[4,64,1024]{2,1,0:T(8,128)S(1)} %collective-permute-done.1, f32[4,64,1024]{2,1,0:T(8,128)S(1)} %get-tuple-element.4, f32[4,64,1024]{2,1,0:T(8,128)S(1)} %collective-permute-done), kind=kLoop, calls=%fused_computation.1 | loop fusion | flops 1572864 | bytes 6291456 | tf_op jit(solution)/shard_map/concatenate | solution.py:52
  (1 shorter events, 0.0 us)
Async XLA Ops:
  7.2 3.5 %copy-start.3 = (s32[4]{0:T(128)S(1)}, s32[4]{0:T(128)}, u32[]{:S(2)}) copy-start(s32[4]{0:T(128)} %param.9) | copy-start | bytes 52
  7.2 3.6 %copy-start.1 = (s32[4,12]{1,0:T(4,128)S(1)}, s32[4,12]{1,0:T(4,128)}, u32[]{:S(2)}) copy-start(s32[4,12]{1,0:T(4,128)} %param.8) | copy-start | bytes 580
  7.2 51.5 %all-gather.3.cloned.1.call-start = ((), (), s32[]{:S(2)}) async-start(), calls=%async_computation | async-start | bytes 2621440 | tf_op jit(solution)/shard_map/all_gather | solution.py:36
  14.2 2.5 %copy-start.5 = (u32[32]{0:T(128)S(1)}, u32[32]{0:T(128)}, u32[]{:S(2)}) copy-start(u32[32]{0:T(128)} %constant.13) | copy-start | bytes 388
  14.2 3.8 %copy-start.4 = (s32[4]{0:T(128)S(1)}, s32[4]{0:T(128)}, u32[]{:S(2)}) copy-start(s32[4]{0:T(128)} %param.12) | copy-start | bytes 52
  14.2 14.8 %copy-start.2 = (s32[4,8]{1,0:T(4,128)S(1)}, s32[4,8]{1,0:T(4,128)}, u32[]{:S(2)}) copy-start(s32[4,8]{1,0:T(4,128)} %param.11) | copy-start | bytes 388
  87.7 2.9 %copy-start = (f32[4,64,1024]{2,1,0:T(8,128)}, f32[4,64,1024]{2,1,0:T(8,128)S(1)}, u32[]{:S(2)}) copy-start(f32[4,64,1024]{2,1,0:T(8,128)S(1)} %fusion.22) | copy-start | bytes 3145732
  90.9 23.7 %collective-permute-start = (f32[4,64,1024]{2,1,0:T(8,128)S(1)}, f32[4,64,1024]{2,1,0:T(8,128)S(1)}, u32[]{:S(2)}, u32[]{:S(2)}) collective-permute-start(f32[4,64,1024]{2,1,0:T(8,128)S(1)} %get-tuple-element.2), channel_id=1, source_target_pairs={{0,4},{4,8},{8,12},{12,0},{1,5},{5,9},{9,13},{13,1},{2,6},{6,10},{... | collective-permute-start | bytes 3145736 | tf_op jit(solution)/shard_map/ppermute | solution.py:14
  91.0 24.4 %collective-permute-start.1 = (f32[4,64,1024]{2,1,0:T(8,128)S(1)}, f32[4,64,1024]{2,1,0:T(8,128)S(1)}, u32[]{:S(2)}, u32[]{:S(2)}) collective-permute-start(f32[4,64,1024]{2,1,0:T(8,128)S(1)} %get-tuple-element.3), channel_id=1, source_target_pairs={{0,12},{4,0},{8,4},{12,8},{1,13},{5,1},{9,5},{13,9},{2,14},{6,2},{... | collective-permute-start | bytes 3145736 | tf_op jit(solution)/shard_map/ppermute | solution.py:14
Sparse Core Ops, SparseCore 0:
  9.6 49.0 all-gather.2
where the time goes:
time: 125 us; the launch traced here: 124 us
  waiting for transfers between devices  40.7 us (33%)
  matrix products  23.3 us (19%)
  blocking collectives  23 us (18%)
  local copies, waits for them, and re-layouts  18.4 us (15%)
  between operations  14.8 us (12%)
  other arithmetic  2.15 us (2%)
  starting transfers between devices  1.83 us (1%)
    ppermute x2, waiting for transfers between devices, from_behind(): lax.ppermute(shard, axis, [(i, (i + by) % count) for i in range(count)])  22.7 us
    all_gather x1, waiting for transfers between devices, shards(): piece_tiles = lax.all_gather(dens_tiles, 'cross', axis=0, tiled=True)  17.4 us
    dot_general x2, matrix products, densify(): jnp.einsum('nkb,nxky->nxby', onehot, shaped, precision=exact_prec)  14.7 us
    all_gather x1, blocking collectives, shards(): piece_cols = lax.all_gather(dens_cols, 'cross', axis=0, tiled=True)  12.3 us
    unnamed x1, blocking collectives  10.7 us
    another operation x1, local copies, waits for them, and re-layouts, shards(): densify(piece_tiles, piece_cols, piece_count, region_rows)  7.62 us
    reshape x2, local copies, waits for them, and re-layouts, densify(): shaped = tiles_in.reshape(rows_count, tile_size, list_len, tile_size)  7.16 us
    dot_general x1, matrix products, shards(): jnp.dot(ham_dense, piece_dense, precision=exact_prec, preferred_element_t...  5.7 us
  transfers between devices with their start and end apart: 3, of which 3 were waited for; matrix products, arithmetic and copies ran while one was open for 8% of the time, Pallas kernels for 0%

commit v1 on v0

v1 whole, which is shorter than its diff:
```python
import functools

import jax
import jax.numpy as jnp
from jax import lax
from jax.experimental import pallas as pl
from jax.experimental.pallas import tpu as pltpu
from jax.sharding import PartitionSpec as P

LANES = 128
F32 = jnp.float32
BF16 = jnp.bfloat16
VMEM = pltpu.VMEM
SMEM = pltpu.SMEM


def rotate(x, axis, by):
    count = lax.axis_size(axis)
    return lax.ppermute(x, axis, [(i, (i + by) % count) for i in range(count)])


def slot_table(columns, counts, width):
    slots = jnp.arange(columns.shape[1], dtype=jnp.int32)
    wanted = jnp.arange(width, dtype=jnp.int32)
    hit = (columns[:, None, :] == wanted[None, :, None]) & (
        slots[None, None, :] < counts[:, None, None]
    )
    return jnp.max(jnp.where(hit, slots + 1, 0), axis=2)


def split(v):
    hi = v.astype(BF16)
    return hi, (v - hi.astype(F32)).astype(BF16)


def low_lanes(rows):
    return lax.broadcasted_iota(jnp.int32, (rows, LANES), 1) < LANES // 2


def block_at(row_ref, code, upper):
    slot = jnp.maximum(code - 1, 0)
    v = row_ref[:, pl.ds(pl.multiple_of((slot >> 1) * LANES, LANES), LANES)]
    v = jnp.where((slot & 1) != upper, pltpu.roll(v, LANES // 2, 1), v)
    return jnp.where(code > 0, v, jnp.zeros_like(v))


def pair_at(row_ref, table, r, pair):
    v0 = block_at(row_ref, table[r, 2 * pair], 0)
    v1 = block_at(row_ref, table[r, 2 * pair + 1], 1)
    return jnp.where(low_lanes(v0.shape[0]), v0, v1)


def densify_half(chunk_ref, first, table, b):
    tile = chunk_ref.shape[1]
    for r in range(2):
        for pair in range(table.shape[1] // 2):
            hi, lo = split(pair_at(chunk_ref.at[first + r], table, first + r, pair))
            lanes = slice(pair * LANES, (pair + 1) * LANES)
            b[r * tile : (r + 1) * tile, lanes] = hi
            b[(2 + r) * tile : (3 + r) * tile, lanes] = lo


def times_half(a, b, lanes):
    depth = b.shape[0]
    return jnp.dot(a[:, :depth], b[:, lanes], preferred_element_type=F32) + jnp.dot(
        a[:, depth:], b[: depth // 2, lanes], preferred_element_type=F32
    )


def lane_blocks(width, step=256):
    return [slice(i, i + step) for i in range(0, width, step)]


def shard_of(step):
    count = lax.axis_size("cross")
    return lax.rem(lax.axis_index("cross") + count - step, count)


def first_kernel(ham_table, dens_table, ham, dens, a, acc, b):
    rows, tile, _ = ham.shape
    for q in range(rows):
        for pair in range(ham_table.shape[1] // 2):
            hi, lo = split(pair_at(ham.at[q], ham_table, q, pair))
            a[pair, q * tile : (q + 1) * tile, 0:LANES] = hi
            a[pair, q * tile : (q + 1) * tile, LANES : 2 * LANES] = hi
            a[pair, q * tile : (q + 1) * tile, 2 * LANES : 3 * LANES] = lo
    for half in range(rows // 2):
        densify_half(dens, 2 * half, dens_table, b)
        pair = shard_of(0) * (rows // 2) + half
        for lanes in lane_blocks(acc.shape[1]):
            part = times_half(a[pair], b, lanes)
            acc[:, lanes] = part if half == 0 else acc[:, lanes] + part


def add_kernel(step, halves, count, dens_table, a, acc_in, *rest):
    chunks, (acc, b) = rest[:count], rest[count:]
    per_shard = dens_table.shape[0] // 2
    for i, half in enumerate(halves):
        for r in range(2):
            pass
        table = dens_table.at[pl.ds(2 * half, 2)]
        densify_half(chunks[i], 0, table, b)
        pair = shard_of(step) * per_shard + half
        for lanes in lane_blocks(acc.shape[1]):
            before = acc_in if i == 0 else acc
            acc[:, lanes] = before[:, lanes] + times_half(a[pair], b, lanes)


def last_kernel(step, half, side, dens_table, a, acc_in, chunk, out, b):
    per_shard = dens_table.shape[0] // 2
    width = out.shape[1]
    table = dens_table.at[pl.ds(2 * half, 2)]
    tile = chunk.shape[1]
    first = side * width // LANES
    for r in range(2):
        for pair in range(width // LANES):
            hi, lo = split(pair_at(chunk.at[r], table, r, first + pair))
            lanes = slice(pair * LANES, (pair + 1) * LANES)
            b[r * tile : (r + 1) * tile, lanes] = hi
            b[(2 + r) * tile : (3 + r) * tile, lanes] = lo
    pair = shard_of(step) * per_shard + half
    for lanes in lane_blocks(width):
        source = slice(side * width + lanes.start, side * width + lanes.stop)
        out[:, lanes] = acc_in[:, source] + times_half(a[pair], b, lanes)


def margin_kernel(over, before, after, hi_out, lo_out):
    rows, tile, _ = over.shape
    wide = rows * tile
    for s, (ref, start) in enumerate(((before, 0), (over, wide), (after, 0))):
        for j in range(rows):
            for pair in range(rows // 2):
                at = start + j * tile
                lanes = slice(at // LANES * LANES, at // LANES * LANES + LANES)
                v0, v1 = ref[2 * pair, :, lanes], ref[2 * pair + 1, :, lanes]
                if at % LANES == 0:
                    v1 = pltpu.roll(v1, LANES // 2, 1)
                else:
                    v0 = pltpu.roll(v0, LANES // 2, 1)
                hi, lo = split(jnp.where(low_lanes(tile), v0, v1))
                to = slice(pair * LANES, (pair + 1) * LANES)
                hi_out[s, j * tile : (j + 1) * tile, to] = hi
                lo_out[s, j * tile : (j + 1) * tile, to] = lo


def weighted(m_hi, m_lo, s, p, store):
    for lanes in lane_blocks(p.shape[1]):
        hi, lo = split(p[:, lanes])
        store(
            lanes,
            jnp.dot(m_hi[s], hi, preferred_element_type=F32)
            + jnp.dot(m_hi[s], lo, preferred_element_type=F32)
            + jnp.dot(m_lo[s], hi, preferred_element_type=F32),
        )


def own_kernel(m_hi, m_lo, *rest):
    sides = len(rest) // 2 - 1
    parts = rest[:sides]
    product, window, term, sems = rest[sides:]
    rows, tile, width = product.shape
    step = width // sides
    copies = []
    for i, part in enumerate(parts):
        for q in range(rows):
            copies.append(
                pltpu.make_async_copy(
                    part.at[pl.ds(q * tile, tile)],
                    product.at[q, :, pl.ds(i * step, step)],
                    sems.at[0, i * rows + q],
                )
            )
            copies[-1].start()
    for i, part in enumerate(parts):

        def store(lanes, v, i=i):
            term[:, i * step + lanes.start : i * step + lanes.stop] = v

        weighted(m_hi, m_lo, 1, part, store)
    for q in range(rows):
        copies.append(
            pltpu.make_async_copy(
                term.at[pl.ds(q * tile, tile)],
                window.at[q, :, pl.ds(width, width)],
                sems.at[1, q],
            )
        )
        copies[-1].start()
    for copy in copies:
        copy.wait()


def arrived_kernel(side, m_hi, m_lo, before, after, window_in, window, term, sems):
    rows, tile, triple = window.shape
    width = triple // 3
    step = before.shape[1]
    copies = []
    for slot, (s, p) in enumerate(((0, before), (2, after))):

        def store(lanes, v, slot=slot):
            term[slot, :, lanes] = v

        weighted(m_hi, m_lo, s, p, store)
        for q in range(rows):
            copies.append(
                pltpu.make_async_copy(
                    term.at[slot, pl.ds(q * tile, tile)],
                    window.at[q, :, pl.ds(s * width + side * step, step)],
                    sems.at[slot, q],
                )
            )
            copies[-1].start()
    for copy in copies:
        copy.wait()


def call(kernel, name, out_shape, in_spaces, out_spaces, scratch, flops, moved, aliases=None):
    return pl.pallas_call(
        kernel,
        name=name,
        out_shape=out_shape,
        in_specs=[pl.BlockSpec(memory_space=s) for s in in_spaces],
        out_specs=jax.tree.map(lambda s: pl.BlockSpec(memory_space=s), out_spaces),
        scratch_shapes=scratch,
        input_output_aliases=aliases or {},
        cost_estimate=pl.CostEstimate(flops=flops, bytes_accessed=moved, transcendentals=0),
        compiler_params=pltpu.CompilerParams(vmem_limit_bytes=24 << 20),
    )


def shards(ham_tiles, ham_cols, ham_count, dens_tiles, dens_cols, dens_count, over_tiles):
    count = lax.axis_size("cross")
    rows, tile, _ = ham_tiles.shape
    blocks = rows * count
    width = blocks * tile
    tall = rows * tile
    per_shard = rows // 2
    sds = jax.ShapeDtypeStruct

    halves = [dens_tiles[2 * h : 2 * h + 2] for h in range(per_shard)]
    dens_table = slot_table(dens_cols, dens_count, blocks)
    ham_table = slot_table(ham_cols, ham_count, blocks)
    arrivals = []
    for step in range(1, count):
        halves = [rotate(h, "cross", 1) for h in halves]
        arrivals.append((halves, rotate(dens_table, "cross", step)))
    wide = rows * tile
    over_before = rotate(over_tiles[:, :, 2 * wide :], "line", 1)
    over_after = rotate(over_tiles[:, :, :wide], "line", -1)

    b_scratch = [VMEM((4 * tile, width), BF16)]
    a, acc = call(
        first_kernel,
        "first",
        (sds((blocks // 2, tall, 3 * LANES), BF16), sds((tall, width), F32)),
        (SMEM, SMEM, VMEM, VMEM),
        (VMEM, VMEM),
        b_scratch,
        2 * 3 * tall * tall * width,
        4 << 20,
    )(ham_table, dens_table, ham_tiles, dens_tiles)
    for step in range(1, count):
        chunks, table = arrivals[step - 1]
        last = step == count - 1
        todo = list(range(per_shard - 1 if last else per_shard))
        acc = call(
            functools.partial(add_kernel, step, todo, len(todo)),
            "add%d" % step,
            sds((tall, width), F32),
            (SMEM,) + (VMEM,) * (2 + len(todo)),
            VMEM,
            b_scratch,
            2 * 3 * tall * tall * width,
            4 << 20,
        )(table, a, acc, *[chunks[h] for h in todo])
    sides = 2
    part = width // sides
    parts = [
        call(
            functools.partial(last_kernel, count - 1, per_shard - 1, side),
            "last%d" % side,
            sds((tall, part), F32),
            (SMEM, VMEM, VMEM, VMEM),
            VMEM,
            [VMEM((4 * tile, part), BF16)],
            2 * 3 * tall * 2 * tile * part,
            2 << 20,
        )(table, a, acc, chunks[-1])
        for side in range(sides)
    ]
    before = [rotate(p, "line", 1) for p in parts]
    after = [rotate(p, "line", -1) for p in parts]

    m_hi, m_lo = call(
        margin_kernel,
        "margin",
        (sds((3, tall, tall), BF16),) * 2,
        (VMEM,) * 3,
        (VMEM, VMEM),
        [],
        1 << 20,
        2 << 20,
    )(over_tiles, over_before, over_after)
    product, window = call(
        own_kernel,
        "own",
        (sds((rows, tile, width), F32), sds((rows, tile, 3 * width), F32)),
        (VMEM,) * (2 + sides),
        (pl.ANY, pl.ANY),
        [VMEM((tall, width), F32), pltpu.SemaphoreType.DMA((2, sides * rows))],
        2 * 3 * tall * tall * width,
        4 << 20,
    )(m_hi, m_lo, *parts)
    for side in range(sides):
        window = call(
            functools.partial(arrived_kernel, side),
            "arrived%d" % side,
            sds((rows, tile, 3 * width), F32),
            (VMEM,) * 4 + (pl.ANY,),
            pl.ANY,
            [VMEM((2, tall, part), F32), pltpu.SemaphoreType.DMA((2, rows))],
            2 * 3 * tall * tall * part * 2,
            4 << 20,
            {4: 0},
        )(m_hi, m_lo, before[side], after[side], window)
    return (product, window)


def solution(mesh):
    whole = P(("parts", "line", "cross"))
    return jax.shard_map(
        shards,
        mesh=mesh,
        in_specs=(whole,) * 7,
        out_specs=(whole, whole),
        check_vma=False,
    )
```

time: 125 us -> 75.4 us (0.60)
  matrix products: 23.3 us -> 0 us
  blocking collectives: 23 us -> 0 us
  between operations: 14.8 us -> 0.82 us
  Pallas kernels: 0 us -> 13.9 us
  local copies, waits for them, and re-layouts: 18.4 us -> 5.08 us
  starting transfers between devices: 1.83 us -> 12.4 us
    dot_general x4 -> x0, matrix products: 23.3 us -> none  [the longest x2 14.7 us: densify(): jnp.einsum('nkb,nxky->nxby', onehot, shaped, precision=exact_prec)]
    ppermute x2 -> x15, waiting for transfers between devices: 22.7 us -> 40.3 us  [rotate(): return lax.ppermute(x, axis, [(i, (i + by) % count) for i in range(count)])]
    all_gather x1 -> x0, waiting for transfers between devices: 17.4 us -> none  [shards(): piece_tiles = lax.all_gather(dens_tiles, 'cross', axis=0, tiled=True)]
    pallas_call x0 -> x10, Pallas kernels: none -> 13.9 us  [the longest x3 4.52 us: shards(): call(functools.partial(add_kernel, step, todo, len(todo)), 'add%d' % step...]
    all_gather x1 -> x0, blocking collectives: 12.3 us -> none  [shards(): piece_cols = lax.all_gather(dens_cols, 'cross', axis=0, tiled=True)]
    unnamed x1 -> x0, blocking collectives: 10.7 us -> none
    ppermute x2 -> x15, starting transfers between devices: 1.79 us -> 12.4 us  [rotate(): return lax.ppermute(x, axis, [(i, (i + by) % count) for i in range(count)])]
    reshape x3 -> x0, local copies, waits for them, and re-layouts: 9.06 us -> none  [the longest x2 7.16 us: densify(): shaped = tiles_in.reshape(rows_count, tile_size, list_len, tile_size)]
  transfers between devices with their start and end apart: 3 -> 15, of which waited for: 3 -> 6; matrix products, arithmetic and copies ran while one was open for 8% -> 5% of each run, Pallas kernels for 0% -> 17%
where the time goes in v1:
time: 75.4 us; the launch traced here: 74.8 us
  waiting for transfers between devices  40.3 us (53%)
  Pallas kernels  13.9 us (18%)
  starting transfers between devices  12.4 us (16%)
  local copies, waits for them, and re-layouts  5.08 us (7%)
  other arithmetic  2.28 us (3%)
  between operations  0.82 us (1%)
    ppermute x15, waiting for transfers between devices, rotate(): return lax.ppermute(x, axis, [(i, (i + by) % count) for i in range(count)])  40.3 us
    ppermute x15, starting transfers between devices, rotate(): return lax.ppermute(x, axis, [(i, (i + by) % count) for i in range(count)])  12.4 us
    pallas_call x3, Pallas kernels, shards(): call(functools.partial(add_kernel, step, todo, len(todo)), 'add%d' % step...  4.52 us
    unnamed x7, local copies, waits for them, and re-layouts  2.95 us
    pallas_call x2, Pallas kernels, shards(): call(functools.partial(arrived_kernel, side), 'arrived%d' % side, sds((ro...  2.92 us
    pallas_call x1, Pallas kernels, shards(): call(first_kernel, 'first', (sds((blocks // 2, tall, 3 * LANES), BF16), s...  2.3 us
    pallas_call x2, Pallas kernels, shards(): call(functools.partial(last_kernel, count - 1, per_shard - 1, side), 'las...  2.17 us
    pallas_call x1, Pallas kernels, shards(): call(own_kernel, 'own', (sds((rows, tile, width), F32), sds((rows, tile,...  1.71 us
  transfers between devices with their start and end apart: 15, of which 6 were waited for; matrix products, arithmetic and copies ran while one was open for 5% of the time, Pallas kernels for 17%

profile of v1, /device:TPU:0, one launch (start us, length us, event | category | flops | bytes accessed | tf_op | source)
XLA Modules:
  0.0 74.8 jit_solution(16642351234957686966)
XLA Ops:
  0.6 1.1 %fusion.3 = (f32[2,64,512]{2,1,0:T(8,128)S(1)}, f32[2,64,512]{2,1,0:T(8,128)S(1)}) fusion(f32[4,64,512]{2,1,0:T(8,128)} %dens.1), kind=kLoop, calls=%fused_computation.11 | loop fusion | bytes 1048576 | tf_op jit(solution)/shard_map/slice | solution.py:240
  1.7 3.1 %collective-permute-start.5 = (f32[2,64,512]{2,1,0:T(8,128)S(1)}, f32[2,64,512]{2,1,0:T(8,128)S(1)}, u32[]{:S(2)}, u32[]{:S(2)}) collective-permute-start(f32[2,64,512]{2,1,0:T(8,128)S(1)} %get-tuple-element.17), channel_id=1, source_target_pairs={{0,1},{1,2},{2,3},{3,0},{4,5},{5,6},{6,7},{7,4},{8,9},{9,10},{10,1... | collective-permute-start | bytes 786440 | tf_op jit(solution)/shard_map/ppermute | solution.py:19
  4.8 1.6 %collective-permute-start.6 = (f32[2,64,512]{2,1,0:T(8,128)S(1)}, f32[2,64,512]{2,1,0:T(8,128)S(1)}, u32[]{:S(2)}, u32[]{:S(2)}) collective-permute-start(f32[2,64,512]{2,1,0:T(8,128)S(1)} %get-tuple-element.16), channel_id=1, source_target_pairs={{0,1},{1,2},{2,3},{3,0},{4,5},{5,6},{6,7},{7,4},{8,9},{9,10},{10,1... | collective-permute-start | bytes 786440 | tf_op jit(solution)/shard_map/ppermute | solution.py:19
  6.4 0.7 iota_compare_fusion.3
  7.1 0.8 %select_reduce_fusion.1.dens_table = s32[4,16]{1,0:T(4,128)S(1)} fusion(s32[8]{0:T(128)S(1)} %iota_add_fusion.1, s32[4,8]{1,0:T(4,128)} %param.11, pred[4,8]{1,0:T(4,128)(4,1)S(1)} %iota_compare_fusion.3), kind=kLoop, calls=%fused_computation.3 | loop fusion | flops 1984 | bytes 448 | tf_op jit(solution)/shard_map/reduce_max | solution.py:28
  7.9 1.6 %collective-permute-start.4 = (s32[4,16]{1,0:T(4,128)S(1)}, s32[4,16]{1,0:T(4,128)S(1)}, u32[]{:S(2)}, u32[]{:S(2)}) collective-permute-start(s32[4,16]{1,0:T(4,128)S(1)} %select_reduce_fusion.1.dens_table), channel_id=1, source_target_pairs={{0,1},{1,2},{2,3},{3,0},{4,5},{5,6},{6,7},{7,4},{8,9},{9,10},{10,1... | collective-permute-start | bytes 776 | tf_op jit(solution)/shard_map/ppermute | solution.py:19
  9.5 1.2 %collective-permute-start.3 = (s32[4,16]{1,0:T(4,128)S(1)}, s32[4,16]{1,0:T(4,128)S(1)}, u32[]{:S(2)}, u32[]{:S(2)}) collective-permute-start(s32[4,16]{1,0:T(4,128)S(1)} %select_reduce_fusion.1.dens_table), channel_id=1, source_target_pairs={{0,2},{1,3},{2,0},{3,1},{4,6},{5,7},{6,4},{7,5},{8,10},{9,11},{10,... | collective-permute-start | bytes 776 | tf_op jit(solution)/shard_map/ppermute | solution.py:19
  10.7 1.2 %collective-permute-start.2 = (s32[4,16]{1,0:T(4,128)S(1)}, s32[4,16]{1,0:T(4,128)S(1)}, u32[]{:S(2)}, u32[]{:S(2)}) collective-permute-start(s32[4,16]{1,0:T(4,128)S(1)} %select_reduce_fusion.1.dens_table), channel_id=1, source_target_pairs={{0,3},{1,0},{2,1},{3,2},{4,7},{5,4},{6,5},{7,6},{8,11},{9,8},{10,9... | collective-permute-start | bytes 776 | tf_op jit(solution)/shard_map/ppermute | solution.py:19
  11.9 2.1 %collective-permute-done.5.rest_0_ = f32[2,64,512]{2,1,0:T(8,128)S(1)} collective-permute-done((f32[2,64,512]{2,1,0:T(8,128)S(1)}, f32[2,64,512]{2,1,0:T(8,128)S(1)}, u32[]{:S(2)}, u32[]{:S(2)}) %collective-permute-start.5) | collective-permute-done | bytes 262176 | tf_op jit(solution)/shard_map/ppermute | solution.py:19
  14.0 0.0 collective-permute-start.7
  14.0 1.1 %fusion.2 = (f32[4,64,256]{2,1,0:T(8,128)S(1)}, f32[4,64,256]{2,1,0:T(8,128)S(1)}) fusion(f32[4,64,768]{2,1,0:T(8,128)} %over.1), kind=kLoop, calls=%fused_computation.10 | loop fusion | bytes 1048576 | tf_op jit(solution)/shard_map/slice | solution.py:249
  15.1 4.6 %collective-permute-done.6.rest_1_ = f32[2,64,512]{2,1,0:T(8,128)S(1)} collective-permute-done((f32[2,64,512]{2,1,0:T(8,128)S(1)}, f32[2,64,512]{2,1,0:T(8,128)S(1)}, u32[]{:S(2)}, u32[]{:S(2)}) %collective-permute-start.6) | collective-permute-done | bytes 262176 | tf_op jit(solution)/shard_map/ppermute | solution.py:19
  19.6 0.0 collective-permute-start.8
  19.6 0.7 iota_compare_fusion.2
  20.3 5.1 %collective-permute-done.7.rest_0_ = f32[2,64,512]{2,1,0:T(8,128)S(1)} collective-permute-done((f32[2,64,512]{2,1,0:T(8,128)S(1)}, f32[2,64,512]{2,1,0:T(8,128)S(1)}, u32[]{:S(2)}, u32[]{:S(2)}) %collective-permute-start.7) | collective-permute-done | bytes 262176 | tf_op jit(solution)/shard_map/ppermute | solution.py:19
  25.4 0.8 %copy.11 = s32[4,12]{0,1:T(8,128)S(1)} copy(s32[4,12]{1,0:T(4,128)} %param.8) | data formatting | bytes 384 | tf_op args[1]
  26.1 4.8 %collective-permute-done.8.rest_1_ = f32[2,64,512]{2,1,0:T(8,128)S(1)} collective-permute-done((f32[2,64,512]{2,1,0:T(8,128)S(1)}, f32[2,64,512]{2,1,0:T(8,128)S(1)}, u32[]{:S(2)}, u32[]{:S(2)}) %collective-permute-start.8) | collective-permute-done | bytes 262176 | tf_op jit(solution)/shard_map/ppermute | solution.py:19
  31.0 0.0 collective-permute-start.10
  31.0 0.1 select_reduce_fusion.ham_table
  31.1 0.0 copy-start.1
  31.1 1.0 %copy-done.1 = f32[4,64,512]{2,1,0:T(8,128)S(1)} copy-done((f32[4,64,512]{2,1,0:T(8,128)S(1)}, f32[4,64,512]{2,1,0:T(8,128)}, u32[]{:S(2)}) %copy-start.1) | copy-done | bytes 524312
  32.1 1.1 %copy-done.2 = f32[4,64,768]{2,1,0:T(8,128)S(1)} copy-done((f32[4,64,768]{2,1,0:T(8,128)S(1)}, f32[4,64,768]{2,1,0:T(8,128)}, u32[]{:S(2)}) %copy-start.2) | copy-done | bytes 786456
  33.3 2.3 %first.1 = (bf16[8,256,384]{2,1,0:T(8,128)(2,1)S(1)}, f32[256,1024]{1,0:T(8,128)S(1)}) custom-call(s32[4,16]{1,0:T(4,128)S(1)} %select_reduce_fusion.ham_table, s32[4,16]{1,0:T(4,128)S(1)} %select_reduce_fusion.1.dens_table, f32[4,64,768]{2,1,0:T(8,128)S(1)} %copy-done.2, f32[4,64,512]{2,1,0:T(8,128)S(1)} %copy-done.1), custom_call_target="tpu_custom_call" | custom-call | flops 402653184 | bytes 4194304 | tf_op jit(solution)/shard_map/first/pallas_call | solution.py:252
  35.6 0.0 collective-permute-done.4.dens_table
  35.6 0.1 collective-permute-start
  35.6 1.6 %add1.1.acc_in = f32[256,1024]{1,0:T(8,128)S(1)} custom-call(s32[4,16]{1,0:T(4,128)S(1)} %collective-permute-done.4.dens_table, bf16[8,256,384]{2,1,0:T(8,128)(2,1)S(1)} %get-tuple-element.10.a, f32[256,1024]{1,0:T(8,128)S(1)} %get-tuple-element.11.acc_in, f32[2,64,512]{2,1,0:T(8,128)S(1)} %collective-permute-done.5.rest_0_, ...), custom_call_target="tpu_custom_call" | custom-call | flops 402653184 | bytes 4194304 | tf_op jit(solution)/shard_map/add1/pallas_call | solution.py:266
  37.3 0.0 collective-permute-done.3.dens_table
  37.3 1.6 %add2.1.acc_in = f32[256,1024]{1,0:T(8,128)S(1)} custom-call(s32[4,16]{1,0:T(4,128)S(1)} %collective-permute-done.3.dens_table, bf16[8,256,384]{2,1,0:T(8,128)(2,1)S(1)} %get-tuple-element.10.a, f32[256,1024]{1,0:T(8,128)S(1)} %add1.1.acc_in, f32[2,64,512]{2,1,0:T(8,128)S(1)} %collective-permute-done.7.rest_0_, f32[2,64,512]{2,1,0:T(8,128)S(1)} %collective-permute-done.8.rest_1_), custom_call_target="tpu_custom_call" | custom-call | flops 402653184 | bytes 4194304 | tf_op jit(solution)/shard_map/add2/pallas_call | solution.py:266
  38.9 0.0 collective-permute-done.2.dens_table
  38.9 0.0 collective-permute-done.9.rest_0_
  39.0 1.3 %add3.1.acc_in = f32[256,1024]{1,0:T(8,128)S(1)} custom-call(s32[4,16]{1,0:T(4,128)S(1)} %collective-permute-done.2.dens_table, bf16[8,256,384]{2,1,0:T(8,128)(2,1)S(1)} %get-tuple-element.10.a, f32[256,1024]{1,0:T(8,128)S(1)} %add2.1.acc_in, f32[2,64,512]{2,1,0:T(8,128)S(1)} %collective-permute-done.9.rest_0_), custom_call_target="tpu_custom_call" | custom-call | flops 402653184 | bytes 4194304 | tf_op jit(solution)/shard_map/add3/pallas_call | solution.py:266
  40.2 0.0 copy-start
  40.2 1.1 %collective-permute-done.10.chunk = f32[2,64,512]{2,1,0:T(8,128)S(1)} collective-permute-done((f32[2,64,512]{2,1,0:T(8,128)S(1)}, f32[2,64,512]{2,1,0:T(8,128)S(1)}, u32[]{:S(2)}, u32[]{:S(2)}) %collective-permute-start.10) | collective-permute-done | bytes 262176 | tf_op jit(solution)/shard_map/ppermute | solution.py:19
  41.4 1.1 %last0.1.rest_0_ = f32[256,512]{1,0:T(8,128)S(1)} custom-call(s32[4,16]{1,0:T(4,128)S(1)} %collective-permute-done.2.dens_table, bf16[8,256,384]{2,1,0:T(8,128)(2,1)S(1)} %get-tuple-element.10.a, f32[256,1024]{1,0:T(8,128)S(1)} %add3.1.acc_in, f32[2,64,512]{2,1,0:T(8,128)S(1)} %collective-permute-done.10.chunk), custom_call_target="tpu_custom_call" | custom-call | flops 100663296 | bytes 2097152 | tf_op jit(solution)/shard_map/last0/pallas_call | solution.py:279
  42.5 0.8 %collective-permute-start.13 = (f32[256,512]{1,0:T(8,128)S(1)}, f32[256,512]{1,0:T(8,128)S(1)}, u32[]{:S(2)}, u32[]{:S(2)}) collective-permute-start(f32[256,512]{1,0:T(8,128)S(1)} %last0.1.rest_0_), channel_id=1, source_target_pairs={{0,4},{4,8},{8,12},{12,0},{1,5},{5,9},{9,13},{13,1},{2,6},{6,10},{... | collective-permute-start | bytes 1572872 | tf_op jit(solution)/shard_map/ppermute | solution.py:19
  43.2 1.0 %collective-permute-start.14 = (f32[256,512]{1,0:T(8,128)S(1)}, f32[256,512]{1,0:T(8,128)S(1)}, u32[]{:S(2)}, u32[]{:S(2)}) collective-permute-start(f32[256,512]{1,0:T(8,128)S(1)} %last0.1.rest_0_), channel_id=1, source_target_pairs={{0,12},{4,0},{8,4},{12,8},{1,13},{5,1},{9,5},{13,9},{2,14},{6,2},{... | collective-permute-start | bytes 1572872 | tf_op jit(solution)/shard_map/ppermute | solution.py:19
  44.3 1.1 %last1.1.rest_1_ = f32[256,512]{1,0:T(8,128)S(1)} custom-call(s32[4,16]{1,0:T(4,128)S(1)} %collective-permute-done.2.dens_table, bf16[8,256,384]{2,1,0:T(8,128)(2,1)S(1)} %get-tuple-element.10.a, f32[256,1024]{1,0:T(8,128)S(1)} %add3.1.acc_in, f32[2,64,512]{2,1,0:T(8,128)S(1)} %collective-permute-done.10.chunk), custom_call_target="tpu_custom_call" | custom-call | flops 100663296 | bytes 2097152 | tf_op jit(solution)/shard_map/last1/pallas_call | solution.py:279
  45.4 0.1 collective-permute-start.11
  45.4 1.7 %collective-permute-start.12 = (f32[256,512]{1,0:T(8,128)S(1)}, f32[256,512]{1,0:T(8,128)S(1)}, u32[]{:S(2)}, u32[]{:S(2)}) collective-permute-start(f32[256,512]{1,0:T(8,128)S(1)} %last1.1.rest_1_), channel_id=1, source_target_pairs={{0,12},{4,0},{8,4},{12,8},{1,13},{5,1},{9,5},{13,9},{2,14},{6,2},{... | collective-permute-start | bytes 1572872 | tf_op jit(solution)/shard_map/ppermute | solution.py:19
  47.2 0.0 collective-permute-start.1
  47.2 22.6 %collective-permute-done.1.after = f32[4,64,256]{2,1,0:T(8,128)S(1)} collective-permute-done((f32[4,64,256]{2,1,0:T(8,128)S(1)}, f32[4,64,256]{2,1,0:T(8,128)S(1)}, u32[]{:S(2)}, u32[]{:S(2)}) %collective-permute-start.1) | collective-permute-done | bytes 262176 | tf_op jit(solution)/shard_map/ppermute | solution.py:19
  69.8 0.3 margin.1
  70.1 1.7 %own.1 = (f32[4,64,1024]{2,1,0:T(8,128)}, f32[4,64,3072]{2,1,0:T(8,128)}) custom-call(bf16[3,256,256]{2,1,0:T(8,128)(2,1)S(1)} %get-tuple-element.8.m_hi, bf16[3,256,256]{2,1,0:T(8,128)(2,1)S(1)} %get-tuple-element.9.m_lo, f32[256,512]{1,0:T(8,128)S(1)} %last0.1.rest_0_, f32[256,512]{1,0:T(8,128)S(1)} %last1.1.rest_1_), custom_call_target="tpu_custom_call" | custom-call | flops 402653184 | bytes 4194304 | tf_op jit(solution)/shard_map/own/pallas_call | solution.py:304
  71.8 0.0 collective-permute-done.14.after
  71.8 1.5 %arrived0.1.window_in = f32[4,64,3072]{2,1,0:T(8,128)} custom-call(bf16[3,256,256]{2,1,0:T(8,128)(2,1)S(1)} %get-tuple-element.8.m_hi, bf16[3,256,256]{2,1,0:T(8,128)(2,1)S(1)} %get-tuple-element.9.m_lo, f32[256,512]{1,0:T(8,128)S(1)} %collective-permute-done.13.before, ...), custom_call_target="tpu_custom_call", output_to_operand_aliasing={{}: (4, {})} | custom-call | flops 402653184 | bytes 4194304 | tf_op jit(solution)/shard_map/arrived0/pallas_call | solution.py:315
  73.3 0.0 collective-permute-done.11.before
  73.3 0.0 collective-permute-done.12.after
  73.3 1.5 %arrived1.1 = f32[4,64,3072]{2,1,0:T(8,128)} custom-call(bf16[3,256,256]{2,1,0:T(8,128)(2,1)S(1)} %get-tuple-element.8.m_hi, bf16[3,256,256]{2,1,0:T(8,128)(2,1)S(1)} %get-tuple-element.9.m_lo, f32[256,512]{1,0:T(8,128)S(1)} %collective-permute-done.11.before, f32[256,512]{1,0:T(8,128)S(1)} %collective-permute-done.12.after, ...), custom_call_target="tpu_custom_call", output_to_operand_aliasing={{}: (4, {})} | custom-call | flops 402653184 | bytes 4194304 | tf_op jit(solution)/shard_map/arrived1/pallas_call | solution.py:315
  (7 shorter events, 0.0 us)
Async XLA Ops:
  1.7 12.3 %collective-permute-start.5 = (f32[2,64,512]{2,1,0:T(8,128)S(1)}, f32[2,64,512]{2,1,0:T(8,128)S(1)}, u32[]{:S(2)}, u32[]{:S(2)}) collective-permute-start(f32[2,64,512]{2,1,0:T(8,128)S(1)} %get-tuple-element.17), channel_id=1, source_target_pairs={{0,1},{1,2},{2,3},{3,0},{4,5},{5,6},{6,7},{7,4},{8,9},{9,10},{10,1... | collective-permute-start | bytes 786440 | tf_op jit(solution)/shard_map/ppermute | solution.py:19
  4.8 14.8 %collective-permute-start.6 = (f32[2,64,512]{2,1,0:T(8,128)S(1)}, f32[2,64,512]{2,1,0:T(8,128)S(1)}, u32[]{:S(2)}, u32[]{:S(2)}) collective-permute-start(f32[2,64,512]{2,1,0:T(8,128)S(1)} %get-tuple-element.16), channel_id=1, source_target_pairs={{0,1},{1,2},{2,3},{3,0},{4,5},{5,6},{6,7},{7,4},{8,9},{9,10},{10,1... | collective-permute-start | bytes 786440 | tf_op jit(solution)/shard_map/ppermute | solution.py:19
  7.9 27.7 %collective-permute-start.4 = (s32[4,16]{1,0:T(4,128)S(1)}, s32[4,16]{1,0:T(4,128)S(1)}, u32[]{:S(2)}, u32[]{:S(2)}) collective-permute-start(s32[4,16]{1,0:T(4,128)S(1)} %select_reduce_fusion.1.dens_table), channel_id=1, source_target_pairs={{0,1},{1,2},{2,3},{3,0},{4,5},{5,6},{6,7},{7,4},{8,9},{9,10},{10,1... | collective-permute-start | bytes 776 | tf_op jit(solution)/shard_map/ppermute | solution.py:19
  9.5 27.8 %collective-permute-start.3 = (s32[4,16]{1,0:T(4,128)S(1)}, s32[4,16]{1,0:T(4,128)S(1)}, u32[]{:S(2)}, u32[]{:S(2)}) collective-permute-start(s32[4,16]{1,0:T(4,128)S(1)} %select_reduce_fusion.1.dens_table), channel_id=1, source_target_pairs={{0,2},{1,3},{2,0},{3,1},{4,6},{5,7},{6,4},{7,5},{8,10},{9,11},{10,... | collective-permute-start | bytes 776 | tf_op jit(solution)/shard_map/ppermute | solution.py:19
  10.7 28.2 %collective-permute-start.2 = (s32[4,16]{1,0:T(4,128)S(1)}, s32[4,16]{1,0:T(4,128)S(1)}, u32[]{:S(2)}, u32[]{:S(2)}) collective-permute-start(s32[4,16]{1,0:T(4,128)S(1)} %select_reduce_fusion.1.dens_table), channel_id=1, source_target_pairs={{0,3},{1,0},{2,1},{3,2},{4,7},{5,4},{6,5},{7,6},{8,11},{9,8},{10,9... | collective-permute-start | bytes 776 | tf_op jit(solution)/shard_map/ppermute | solution.py:19
  14.0 11.4 %collective-permute-start.7 = (f32[2,64,512]{2,1,0:T(8,128)S(1)}, f32[2,64,512]{2,1,0:T(8,128)S(1)}, u32[]{:S(2)}, u32[]{:S(2)}) collective-permute-start(f32[2,64,512]{2,1,0:T(8,128)S(1)} %collective-permute-done.5.rest_0_), channel_id=1, source_target_pairs={{0,1},{1,2},{2,3},{3,0},{4,5},{5,6},{6,7},{7,4},{8,9},{9,10},{10,1... | collective-permute-start | bytes 786440 | tf_op jit(solution)/shard_map/ppermute | solution.py:19
  19.6 11.3 %collective-permute-start.8 = (f32[2,64,512]{2,1,0:T(8,128)S(1)}, f32[2,64,512]{2,1,0:T(8,128)S(1)}, u32[]{:S(2)}, u32[]{:S(2)}) collective-permute-start(f32[2,64,512]{2,1,0:T(8,128)S(1)} %collective-permute-done.6.rest_1_), channel_id=1, source_target_pairs={{0,1},{1,2},{2,3},{3,0},{4,5},{5,6},{6,7},{7,4},{8,9},{9,10},{10,1... | collective-permute-start | bytes 786440 | tf_op jit(solution)/shard_map/ppermute | solution.py:19
  25.3 13.6 %collective-permute-start.9 = (f32[2,64,512]{2,1,0:T(8,128)S(1)}, f32[2,64,512]{2,1,0:T(8,128)S(1)}, u32[]{:S(2)}, u32[]{:S(2)}) collective-permute-start(f32[2,64,512]{2,1,0:T(8,128)S(1)} %collective-permute-done.7.rest_0_), channel_id=1, source_target_pairs={{0,1},{1,2},{2,3},{3,0},{4,5},{5,6},{6,7},{7,4},{8,9},{9,10},{10,1... | collective-permute-start | bytes 786440 | tf_op jit(solution)/shard_map/ppermute | solution.py:19
  31.0 10.4 %collective-permute-start.10 = (f32[2,64,512]{2,1,0:T(8,128)S(1)}, f32[2,64,512]{2,1,0:T(8,128)S(1)}, u32[]{:S(2)}, u32[]{:S(2)}) collective-permute-start(f32[2,64,512]{2,1,0:T(8,128)S(1)} %collective-permute-done.8.rest_1_), channel_id=1, source_target_pairs={{0,1},{1,2},{2,3},{3,0},{4,5},{5,6},{6,7},{7,4},{8,9},{9,10},{10,1... | collective-permute-start | bytes 786440 | tf_op jit(solution)/shard_map/ppermute | solution.py:19
  31.1 1.0 %copy-start.1 = (f32[4,64,512]{2,1,0:T(8,128)S(1)}, f32[4,64,512]{2,1,0:T(8,128)}, u32[]{:S(2)}) copy-start(f32[4,64,512]{2,1,0:T(8,128)} %dens.1) | copy-start | bytes 1572868
  32.1 1.1 %copy-start.2 = (f32[4,64,768]{2,1,0:T(8,128)S(1)}, f32[4,64,768]{2,1,0:T(8,128)}, u32[]{:S(2)}) copy-start(f32[4,64,768]{2,1,0:T(8,128)} %ham.1) | copy-start | bytes 2359300
  35.6 11.6 %collective-permute-start = (f32[4,64,256]{2,1,0:T(8,128)S(1)}, f32[4,64,256]{2,1,0:T(8,128)S(1)}, u32[]{:S(2)}, u32[]{:S(2)}) collective-permute-start(f32[4,64,256]{2,1,0:T(8,128)S(1)} %get-tuple-element.15), channel_id=1, source_target_pairs={{0,4},{4,8},{8,12},{12,0},{1,5},{5,9},{9,13},{13,1},{2,6},{6,10},{... | collective-permute-start | bytes 786440 | tf_op jit(solution)/shard_map/ppermute | solution.py:19
  40.2 29.6 %copy-start = (f32[4,64,768]{2,1,0:T(8,128)S(1)}, f32[4,64,768]{2,1,0:T(8,128)}, u32[]{:S(2)}) copy-start(f32[4,64,768]{2,1,0:T(8,128)} %over.1) | copy-start | bytes 2359300
  42.5 29.3 %collective-permute-start.13 = (f32[256,512]{1,0:T(8,128)S(1)}, f32[256,512]{1,0:T(8,128)S(1)}, u32[]{:S(2)}, u32[]{:S(2)}) collective-permute-start(f32[256,512]{1,0:T(8,128)S(1)} %last0.1.rest_0_), channel_id=1, source_target_pairs={{0,4},{4,8},{8,12},{12,0},{1,5},{5,9},{9,13},{13,1},{2,6},{6,10},{... | collective-permute-start | bytes 1572872 | tf_op jit(solution)/shard_map/ppermute | solution.py:19
  43.2 28.6 %collective-permute-start.14 = (f32[256,512]{1,0:T(8,128)S(1)}, f32[256,512]{1,0:T(8,128)S(1)}, u32[]{:S(2)}, u32[]{:S(2)}) collective-permute-start(f32[256,512]{1,0:T(8,128)S(1)} %last0.1.rest_0_), channel_id=1, source_target_pairs={{0,12},{4,0},{8,4},{12,8},{1,13},{5,1},{9,5},{13,9},{2,14},{6,2},{... | collective-permute-start | bytes 1572872 | tf_op jit(solution)/shard_map/ppermute | solution.py:19
  45.4 27.9 %collective-permute-start.11 = (f32[256,512]{1,0:T(8,128)S(1)}, f32[256,512]{1,0:T(8,128)S(1)}, u32[]{:S(2)}, u32[]{:S(2)}) collective-permute-start(f32[256,512]{1,0:T(8,128)S(1)} %last1.1.rest_1_), channel_id=1, source_target_pairs={{0,4},{4,8},{8,12},{12,0},{1,5},{5,9},{9,13},{13,1},{2,6},{6,10},{... | collective-permute-start | bytes 1572872 | tf_op jit(solution)/shard_map/ppermute | solution.py:19
  45.4 27.9 %collective-permute-start.12 = (f32[256,512]{1,0:T(8,128)S(1)}, f32[256,512]{1,0:T(8,128)S(1)}, u32[]{:S(2)}, u32[]{:S(2)}) collective-permute-start(f32[256,512]{1,0:T(8,128)S(1)} %last1.1.rest_1_), channel_id=1, source_target_pairs={{0,12},{4,0},{8,4},{12,8},{1,13},{5,1},{9,5},{13,9},{2,14},{6,2},{... | collective-permute-start | bytes 1572872 | tf_op jit(solution)/shard_map/ppermute | solution.py:19
  47.2 22.6 %collective-permute-start.1 = (f32[4,64,256]{2,1,0:T(8,128)S(1)}, f32[4,64,256]{2,1,0:T(8,128)S(1)}, u32[]{:S(2)}, u32[]{:S(2)}) collective-permute-start(f32[4,64,256]{2,1,0:T(8,128)S(1)} %get-tuple-element.14), channel_id=1, source_target_pairs={{0,12},{4,0},{8,4},{12,8},{1,13},{5,1},{9,5},{13,9},{2,14},{6,2},{... | collective-permute-start | bytes 786440 | tf_op jit(solution)/shard_map/ppermute | solution.py:19

commit v2 on v1

--- a/solution.py
+++ b/solution.py
@@ -17,6 +17,26 @@
 def rotate(x, axis, by):
     count = lax.axis_size(axis)
     return lax.ppermute(x, axis, [(i, (i + by) % count) for i in range(count)])
+
+
+def ring_order(count):
+    return list(range(0, count, 2))[:1] + list(range(1, count, 2)) + list(range(0, count, 2))[:0:-1]
+
+
+def pass_on(x, by):
+    order = ring_order(lax.axis_size("cross"))
+    return lax.ppermute(
+        x, "cross", [(d, order[(i + by) % len(order)]) for i, d in enumerate(order)]
+    )
+
+
+def shard_of(step):
+    order = ring_order(lax.axis_size("cross"))
+    me = lax.axis_index("cross")
+    owner = jnp.int32(0)
+    for i, d in enumerate(order):
+        owner = jnp.where(me == d, order[i - step], owner)
+    return owner
 
 
 def slot_table(columns, counts, width):
@@ -69,11 +89,6 @@
 
 def lane_blocks(width, step=256):
     return [slice(i, i + step) for i in range(0, width, step)]
-
-
-def shard_of(step):
-    count = lax.axis_size("cross")
-    return lax.rem(lax.axis_index("cross") + count - step, count)
 
 
 def first_kernel(ham_table, dens_table, ham, dens, a, acc, b):
@@ -96,8 +111,6 @@
     chunks, (acc, b) = rest[:count], rest[count:]
     per_shard = dens_table.shape[0] // 2
     for i, half in enumerate(halves):
-        for r in range(2):
-            pass
         table = dens_table.at[pl.ds(2 * half, 2)]
         densify_half(chunks[i], 0, table, b)
         pair = shard_of(step) * per_shard + half
@@ -106,22 +119,26 @@
             acc[:, lanes] = before[:, lanes] + times_half(a[pair], b, lanes)
 
 
-def last_kernel(step, half, side, dens_table, a, acc_in, chunk, out, b):
+def last_kernel(step, half, first, widths, dens_table, a, acc_in, chunk, *rest):
+    outs, b = rest[:-1], rest[-1]
     per_shard = dens_table.shape[0] // 2
-    width = out.shape[1]
+    width = sum(widths)
     table = dens_table.at[pl.ds(2 * half, 2)]
     tile = chunk.shape[1]
-    first = side * width // LANES
     for r in range(2):
         for pair in range(width // LANES):
-            hi, lo = split(pair_at(chunk.at[r], table, r, first + pair))
+            hi, lo = split(pair_at(chunk.at[r], table, r, first // LANES + pair))
             lanes = slice(pair * LANES, (pair + 1) * LANES)
             b[r * tile : (r + 1) * tile, lanes] = hi
             b[(2 + r) * tile : (3 + r) * tile, lanes] = lo
     pair = shard_of(step) * per_shard + half
-    for lanes in lane_blocks(width):
-        source = slice(side * width + lanes.start, side * width + lanes.stop)
-        out[:, lanes] = acc_in[:, source] + times_half(a[pair], b, lanes)
+    at = 0
+    for out, piece in zip(outs, widths):
+        for lanes in lane_blocks(piece):
+            here = slice(at + lanes.start, at + lanes.stop)
+            source = slice(first + here.start, first + here.stop)
+            out[:, lanes] = acc_in[:, source] + times_half(a[pair], b, here)
+        at += piece
 
 
 def margin_kernel(over, before, after, hi_out, lo_out):
@@ -154,35 +171,38 @@
         )
 
 
-def own_kernel(m_hi, m_lo, *rest):
-    sides = len(rest) // 2 - 1
-    parts = rest[:sides]
-    product, window, term, sems = rest[sides:]
+def own_kernel(pieces, m_hi, m_lo, *rest):
+    parts = rest[: len(pieces)]
+    product, window, term, sems = rest[len(pieces) :]
     rows, tile, width = product.shape
-    step = width // sides
     copies = []
+    at = 0
     for i, part in enumerate(parts):
+        step = part.shape[1]
         for q in range(rows):
             copies.append(
                 pltpu.make_async_copy(
                     part.at[pl.ds(q * tile, tile)],
-                    product.at[q, :, pl.ds(i * step, step)],
-                    sems.at[0, i * rows + q],
+                    product.at[q, :, pl.ds(at, step)],
+                    sems.at[i, q],
                 )
             )
             copies[-1].start()
-    for i, part in enumerate(parts):
-
-        def store(lanes, v, i=i):
-            term[:, i * step + lanes.start : i * step + lanes.stop] = v
+        at += step
+    at = 0
+    for part in parts:
+
+        def store(lanes, v, at=at):
+            term[:, at + lanes.start : at + lanes.stop] = v
 
         weighted(m_hi, m_lo, 1, part, store)
+        at += part.shape[1]
     for q in range(rows):
         copies.append(
             pltpu.make_async_copy(
                 term.at[pl.ds(q * tile, tile)],
                 window.at[q, :, pl.ds(width, width)],
-                sems.at[1, q],
+                sems.at[len(parts), q],
             )
         )
         copies[-1].start()
@@ -190,26 +210,25 @@
         copy.wait()
 
 
-def arrived_kernel(side, m_hi, m_lo, before, after, window_in, window, term, sems):
+def arrived_kernel(at, m_hi, m_lo, before, after, window_in, window, term, sems):
     rows, tile, triple = window.shape
     width = triple // 3
-    step = before.shape[1]
     copies = []
     for slot, (s, p) in enumerate(((0, before), (2, after))):
 
-        def store(lanes, v, slot=slot):
+        def store(lanes, v, slot=slot, s=s):
             term[slot, :, lanes] = v
+            for q in range(rows):
+                copies.append(
+                    pltpu.make_async_copy(
+                        term.at[slot, pl.ds(q * tile, tile), lanes],
+                        window.at[q, :, pl.ds(s * width + at + lanes.start, lanes.stop - lanes.start)],
+                        sems.at[len(copies)],
+                    )
+                )
+                copies[-1].start()
 
         weighted(m_hi, m_lo, s, p, store)
-        for q in range(rows):
-            copies.append(
-                pltpu.make_async_copy(
-                    term.at[slot, pl.ds(q * tile, tile)],
-                    window.at[q, :, pl.ds(s * width + side * step, step)],
-                    sems.at[slot, q],
-                )
-            )
-            copies[-1].start()
     for copy in copies:
         copy.wait()
 
@@ -238,15 +257,11 @@
     sds = jax.ShapeDtypeStruct
 
     halves = [dens_tiles[2 * h : 2 * h + 2] for h in range(per_shard)]
+    halves, dens_cols, dens_count = lax.optimization_barrier((halves, dens_cols, dens_count))
     dens_table = slot_table(dens_cols, dens_count, blocks)
     ham_table = slot_table(ham_cols, ham_count, blocks)
-    arrivals = []
-    for step in range(1, count):
-        halves = [rotate(h, "cross", 1) for h in halves]
-        arrivals.append((halves, rotate(dens_table, "cross", step)))
-    wide = rows * tile
-    over_before = rotate(over_tiles[:, :, 2 * wide :], "line", 1)
-    over_after = rotate(over_tiles[:, :, :wide], "line", -1)
+    over_before = rotate(over_tiles[:, :, 2 * tall :], "line", 1)
+    over_after = rotate(over_tiles[:, :, :tall], "line", -1)
 
     b_scratch = [VMEM((4 * tile, width), BF16)]
     a, acc = call(
@@ -259,38 +274,6 @@
         2 * 3 * tall * tall * width,
         4 << 20,
     )(ham_table, dens_table, ham_tiles, dens_tiles)
-    for step in range(1, count):
-        chunks, table = arrivals[step - 1]
-        last = step == count - 1
-        todo = list(range(per_shard - 1 if last else per_shard))
-        acc = call(
-            functools.partial(add_kernel, step, todo, len(todo)),
-            "add%d" % step,
-            sds((tall, width), F32),
-            (SMEM,) + (VMEM,) * (2 + len(todo)),
-            VMEM,
-            b_scratch,
-            2 * 3 * tall * tall * width,
-            4 << 20,
-        )(table, a, acc, *[chunks[h] for h in todo])
-    sides = 2
-    part = width // sides
-    parts = [
-        call(
-            functools.partial(last_kernel, count - 1, per_shard - 1, side),
-            "last%d" % side,
-            sds((tall, part), F32),
-            (SMEM, VMEM, VMEM, VMEM),
-            VMEM,
-            [VMEM((4 * tile, part), BF16)],
-            2 * 3 * tall * 2 * tile * part,
-            2 << 20,
-        )(table, a, acc, chunks[-1])
-        for side in range(sides)
-    ]
-    before = [rotate(p, "line", 1) for p in parts]
-    after = [rotate(p, "line", -1) for p in parts]
-
     m_hi, m_lo = call(
         margin_kernel,
         "margin",
@@ -301,28 +284,70 @@
         1 << 20,
         2 << 20,
     )(over_tiles, over_before, over_after)
+    done = acc
+    for step in range(1, count):
+        if step > 1:
+            halves[-1], done, m_hi, m_lo = lax.optimization_barrier(
+                (halves[-1], done, m_hi, m_lo) if step == 3 else (halves[-1], done)
+            ) + (() if step == 3 else (m_hi, m_lo))
+        chunks = halves = [pass_on(h, 1) for h in halves]
+        table = pass_on(dens_table, step)
+        last = step == count - 1
+        todo = list(range(per_shard - 1 if last else per_shard))
+        done, acc = acc, call(
+            functools.partial(add_kernel, step, todo, len(todo)),
+            "add%d" % step,
+            sds((tall, width), F32),
+            (SMEM,) + (VMEM,) * (2 + len(todo)),
+            VMEM,
+            b_scratch,
+            2 * 3 * tall * tall * width,
+            4 << 20,
+        )(table, a, acc, *[chunks[h] for h in todo])
+        halves = list(halves)
+    pieces = (width // 2, width // 4, width // 4)
+    parts = []
+    for i, piece in enumerate(pieces):
+        parts += call(
+            functools.partial(
+                last_kernel, count - 1, per_shard - 1, sum(pieces[:i]), (piece,)
+            ),
+            "last%d" % i,
+            [sds((tall, piece), F32)],
+            (SMEM, VMEM, VMEM, VMEM),
+            [VMEM],
+            [VMEM((4 * tile, piece), BF16)],
+            1024,
+            1024,
+        )(table, a, acc, chunks[-1])
+        if i + 1 < len(pieces):
+            parts[-1], acc = lax.optimization_barrier((parts[-1], acc))
+    before = [rotate(p, "line", 1) for p in parts]
+    after = [rotate(p, "line", -1) for p in parts]
     product, window = call(
-        own_kernel,
+        functools.partial(own_kernel, pieces),
         "own",
         (sds((rows, tile, width), F32), sds((rows, tile, 3 * width), F32)),
-        (VMEM,) * (2 + sides),
+        (VMEM,) * (2 + len(pieces)),
         (pl.ANY, pl.ANY),
-        [VMEM((tall, width), F32), pltpu.SemaphoreType.DMA((2, sides * rows))],
-        2 * 3 * tall * tall * width,
-        4 << 20,
+        [VMEM((tall, width), F32), pltpu.SemaphoreType.DMA((len(pieces) + 1, rows))],
+        1024,
+        1024,
     )(m_hi, m_lo, *parts)
-    for side in range(sides):
+    at = 0
+    for i, piece in enumerate(pieces):
         window = call(
-            functools.partial(arrived_kernel, side),
-            "arrived%d" % side,
+            functools.partial(arrived_kernel, at),
+            "arrived%d" % i,
             sds((rows, tile, 3 * width), F32),
             (VMEM,) * 4 + (pl.ANY,),
             pl.ANY,
-            [VMEM((2, tall, part), F32), pltpu.SemaphoreType.DMA((2, rows))],
-            2 * 3 * tall * tall * part * 2,
-            4 << 20,
+            [VMEM((2, tall, piece), F32), pltpu.SemaphoreType.DMA((2 * rows * piece // 256,))],
+            1024,
+            1024,
             {4: 0},
-        )(m_hi, m_lo, before[side], after[side], window)
+        )(m_hi, m_lo, before[i], after[i], window)
+        at += piece
     return (product, window)
 
 

time: 75.4 us -> 74.3 us (0.985)
  waiting for transfers between devices: 40.3 us -> 28.6 us
  starting transfers between devices: 12.4 us -> 21.1 us
  Pallas kernels: 13.9 us -> 15.8 us
    ppermute x15 -> x8, waiting for transfers between devices: 40.3 us -> 14.5 us  [rotate(): return lax.ppermute(x, axis, [(i, (i + by) % count) for i in range(count)])]
    ppermute x0 -> x9, starting transfers between devices: none -> 15.6 us  [pass_on(): lax.ppermute(x, 'cross', [(d, order[(i + by) % len(order)]) for i, d in e...]
    ppermute x0 -> x9, waiting for transfers between devices: none -> 14.1 us  [pass_on(): lax.ppermute(x, 'cross', [(d, order[(i + by) % len(order)]) for i, d in e...]
    ppermute x15 -> x8, starting transfers between devices: 12.4 us -> 5.43 us  [rotate(): return lax.ppermute(x, axis, [(i, (i + by) % count) for i in range(count)])]
    pallas_call x5 -> x7, Pallas kernels: 6.8 us -> 8.66 us  [the longest x3 4.01 us: shards(): call(functools.partial(arrived_kernel, at), 'arrived%d' % i, sds((rows, t...]
  transfers between devices with their start and end apart: 15 -> 17, of which waited for: 6 -> 9; matrix products, arithmetic and copies ran while one was open for 5% -> 6% of each run, Pallas kernels for 17% -> 18%
where the time goes in v2:
time: 74.3 us; the launch traced here: 73.6 us
  waiting for transfers between devices  28.6 us (38%)
  starting transfers between devices  21.1 us (28%)
  Pallas kernels  15.8 us (21%)
  local copies, waits for them, and re-layouts  5.16 us (7%)
  other arithmetic  2.28 us (3%)
  between operations  0.83 us (1%)
    ppermute x9, starting transfers between devices, pass_on(): lax.ppermute(x, 'cross', [(d, order[(i + by) % len(order)]) for i, d in e...  15.6 us
    ppermute x8, waiting for transfers between devices, rotate(): return lax.ppermute(x, axis, [(i, (i + by) % count) for i in range(count)])  14.5 us
    ppermute x9, waiting for transfers between devices, pass_on(): lax.ppermute(x, 'cross', [(d, order[(i + by) % len(order)]) for i, d in e...  14.1 us
    ppermute x8, starting transfers between devices, rotate(): return lax.ppermute(x, axis, [(i, (i + by) % count) for i in range(count)])  5.43 us
    pallas_call x3, Pallas kernels, shards(): call(functools.partial(add_kernel, step, todo, len(todo)), 'add%d' % step...  4.51 us
    pallas_call x3, Pallas kernels, shards(): call(functools.partial(arrived_kernel, at), 'arrived%d' % i, sds((rows, t...  4.01 us
    unnamed x7, local copies, waits for them, and re-layouts  2.95 us
    pallas_call x3, Pallas kernels, shards(): call(functools.partial(last_kernel, count - 1, per_shard - 1, sum(pieces[...  2.95 us
  transfers between devices with their start and end apart: 17, of which 9 were waited for; matrix products, arithmetic and copies ran while one was open for 6% of the time, Pallas kernels for 18%

profile of v2, /device:TPU:0, one launch (start us, length us, event | category | flops | bytes accessed | tf_op | source)
XLA Modules:
  0.0 73.6 jit_solution(7675544643641229995)
XLA Ops:
  0.6 0.0 copy-start
  0.6 1.1 %fusion.3 = (f32[2,64,512]{2,1,0:T(8,128)S(1)}, f32[2,64,512]{2,1,0:T(8,128)S(1)}) fusion(f32[4,64,512]{2,1,0:T(8,128)} %dens.1), kind=kLoop, calls=%fused_computation.11 | loop fusion | bytes 1048576 | tf_op jit(solution)/shard_map/slice | solution.py:259
  1.8 3.1 %collective-permute-start = (f32[2,64,512]{2,1,0:T(8,128)S(1)}, f32[2,64,512]{2,1,0:T(8,128)S(1)}, u32[]{:S(2)}, u32[]{:S(2)}) collective-permute-start(f32[2,64,512]{2,1,0:T(8,128)S(1)} %get-tuple-element.20), channel_id=1, source_target_pairs={{0,1},{1,3},{3,2},{2,0},{4,5},{5,7},{7,6},{6,4},{8,9},{9,11},{11,1... | collective-permute-start | bytes 786440 | tf_op jit(solution)/shard_map/ppermute | solution.py:28
  4.9 2.6 %collective-permute-start.3 = (f32[2,64,512]{2,1,0:T(8,128)S(1)}, f32[2,64,512]{2,1,0:T(8,128)S(1)}, u32[]{:S(2)}, u32[]{:S(2)}) collective-permute-start(f32[2,64,512]{2,1,0:T(8,128)S(1)} %get-tuple-element.26), channel_id=1, source_target_pairs={{0,1},{1,3},{3,2},{2,0},{4,5},{5,7},{7,6},{6,4},{8,9},{9,11},{11,1... | collective-permute-start | bytes 786440 | tf_op jit(solution)/shard_map/ppermute | solution.py:28
  7.4 1.1 %fusion.2 = (f32[4,64,256]{2,1,0:T(8,128)S(1)}, f32[4,64,256]{2,1,0:T(8,128)S(1)}) fusion(f32[4,64,768]{2,1,0:T(8,128)} %over.1), kind=kLoop, calls=%fused_computation.10 | loop fusion | bytes 1048576 | tf_op jit(solution)/shard_map/slice | solution.py:264
  8.5 0.1 collective-permute-start.4
  8.6 1.7 %collective-permute-start.5 = (f32[4,64,256]{2,1,0:T(8,128)S(1)}, f32[4,64,256]{2,1,0:T(8,128)S(1)}, u32[]{:S(2)}, u32[]{:S(2)}) collective-permute-start(f32[4,64,256]{2,1,0:T(8,128)S(1)} %get-tuple-element.38), channel_id=1, source_target_pairs={{0,12},{4,0},{8,4},{12,8},{1,13},{5,1},{9,5},{13,9},{2,14},{6,2},{... | collective-permute-start | bytes 786440 | tf_op jit(solution)/shard_map/ppermute | solution.py:19
  10.3 0.7 iota_compare_fusion.3
  11.0 0.7 iota_compare_fusion.2
  11.7 0.8 %select_reduce_fusion.1.dens_table = s32[4,16]{1,0:T(4,128)S(1)} fusion(s32[8]{0:T(128)S(1)} %iota_add_fusion, s32[4,8]{1,0:T(4,128)} %param.11, pred[4,8]{1,0:T(4,128)(4,1)S(1)} %iota_compare_fusion.3), kind=kLoop, calls=%fused_computation.3 | loop fusion | flops 1984 | bytes 448 | tf_op jit(solution)/shard_map/reduce_max | solution.py:48
  12.5 0.8 %copy.12 = s32[4,12]{0,1:T(8,128)S(1)} copy(s32[4,12]{1,0:T(4,128)} %param.8) | data formatting | bytes 384 | tf_op args[1]
  13.3 0.1 select_reduce_fusion.ham_table
  13.4 4.4 %collective-permute-done.3.rest_0_ = f32[2,64,512]{2,1,0:T(8,128)S(1)} collective-permute-done((f32[2,64,512]{2,1,0:T(8,128)S(1)}, f32[2,64,512]{2,1,0:T(8,128)S(1)}, u32[]{:S(2)}, u32[]{:S(2)}) %collective-permute-start.3) | collective-permute-done | bytes 262176 | tf_op jit(solution)/shard_map/ppermute | solution.py:28
  17.8 0.8 %collective-permute-start.8 = (f32[2,64,512]{2,1,0:T(8,128)S(1)}, f32[2,64,512]{2,1,0:T(8,128)S(1)}, u32[]{:S(2)}, u32[]{:S(2)}) collective-permute-start(f32[2,64,512]{2,1,0:T(8,128)S(1)} %collective-permute-done.3.rest_0_), channel_id=1, source_target_pairs={{0,1},{1,3},{3,2},{2,0},{4,5},{5,7},{7,6},{6,4},{8,9},{9,11},{11,1... | collective-permute-start | bytes 786440 | tf_op jit(solution)/shard_map/ppermute | solution.py:28
  18.6 1.0 %copy-done.1 = f32[4,64,512]{2,1,0:T(8,128)S(1)} copy-done((f32[4,64,512]{2,1,0:T(8,128)S(1)}, f32[4,64,512]{2,1,0:T(8,128)}, u32[]{:S(2)}) %copy-start.1) | copy-done | bytes 524312
  19.7 1.1 %copy-done.2 = f32[4,64,768]{2,1,0:T(8,128)S(1)} copy-done((f32[4,64,768]{2,1,0:T(8,128)S(1)}, f32[4,64,768]{2,1,0:T(8,128)}, u32[]{:S(2)}) %copy-start.2) | copy-done | bytes 786456
  20.8 2.3 %first.1 = (bf16[8,256,384]{2,1,0:T(8,128)(2,1)S(1)}, f32[256,1024]{1,0:T(8,128)S(1)}) custom-call(s32[4,16]{1,0:T(4,128)S(1)} %select_reduce_fusion.ham_table, s32[4,16]{1,0:T(4,128)S(1)} %select_reduce_fusion.1.dens_table, f32[4,64,768]{2,1,0:T(8,128)S(1)} %copy-done.2, f32[4,64,512]{2,1,0:T(8,128)S(1)} %copy-done.1), custom_call_target="tpu_custom_call" | custom-call | flops 402653184 | bytes 4194304 | tf_op jit(solution)/shard_map/first/pallas_call | solution.py:267
  23.1 3.4 %collective-permute-start.1 = (f32[2,64,512]{2,1,0:T(8,128)S(1)}, f32[2,64,512]{2,1,0:T(8,128)S(1)}, u32[]{:S(2)}, u32[]{:S(2)}) collective-permute-start(f32[2,64,512]{2,1,0:T(8,128)S(1)} %collective-permute-done.rest_1_), channel_id=1, source_target_pairs={{0,1},{1,3},{3,2},{2,0},{4,5},{5,7},{7,6},{6,4},{8,9},{9,11},{11,1... | collective-permute-start | bytes 786440 | tf_op jit(solution)/shard_map/ppermute | solution.py:28
  26.6 0.1 collective-permute-start.2
  26.6 0.0 collective-permute-done.4.before
  26.6 0.3 margin.1
  26.9 0.1 collective-permute-done.8.rest_0_
  27.0 0.7 %collective-permute-start.9 = (f32[2,64,512]{2,1,0:T(8,128)S(1)}, f32[2,64,512]{2,1,0:T(8,128)S(1)}, u32[]{:S(2)}, u32[]{:S(2)}) collective-permute-start(f32[2,64,512]{2,1,0:T(8,128)S(1)} %collective-permute-done.8.rest_0_), channel_id=1, source_target_pairs={{0,1},{1,3},{3,2},{2,0},{4,5},{5,7},{7,6},{6,4},{8,9},{9,11},{11,1... | collective-permute-start | bytes 786440 | tf_op jit(solution)/shard_map/ppermute | solution.py:28
  27.7 5.7 %collective-permute-done.2.dens_table = s32[4,16]{1,0:T(4,128)S(1)} collective-permute-done((s32[4,16]{1,0:T(4,128)S(1)}, s32[4,16]{1,0:T(4,128)S(1)}, u32[]{:S(2)}, u32[]{:S(2)}) %collective-permute-start.2) | collective-permute-done | bytes 288 | tf_op jit(solution)/shard_map/ppermute | solution.py:28
  33.4 1.6 %add1.1.acc_in = f32[256,1024]{1,0:T(8,128)S(1)} custom-call(s32[4,16]{1,0:T(4,128)S(1)} %collective-permute-done.2.dens_table, bf16[8,256,384]{2,1,0:T(8,128)(2,1)S(1)} %get-tuple-element.25.a, f32[256,1024]{1,0:T(8,128)S(1)} %get-tuple-element.23.acc_in, f32[2,64,512]{2,1,0:T(8,128)S(1)} %collective-permute-done.3.rest_0_, ...), custom_call_target="tpu_custom_call" | custom-call | flops 402653184 | bytes 4194304 | tf_op jit(solution)/shard_map/add1/pallas_call | solution.py:297
  35.0 2.5 %collective-permute-start.10 = (f32[2,64,512]{2,1,0:T(8,128)S(1)}, f32[2,64,512]{2,1,0:T(8,128)S(1)}, u32[]{:S(2)}, u32[]{:S(2)}) collective-permute-start(f32[2,64,512]{2,1,0:T(8,128)S(1)} %collective-permute-done.1.rest_1_), channel_id=1, source_target_pairs={{0,1},{1,3},{3,2},{2,0},{4,5},{5,7},{7,6},{6,4},{8,9},{9,11},{11,1... | collective-permute-start | bytes 786440 | tf_op jit(solution)/shard_map/ppermute | solution.py:28
  37.6 0.4 collective-permute-start.7
  38.0 1.9 %collective-permute-start.6 = (s32[4,16]{1,0:T(4,128)S(1)}, s32[4,16]{1,0:T(4,128)S(1)}, u32[]{:S(2)}, u32[]{:S(2)}) collective-permute-start(s32[4,16]{1,0:T(4,128)S(1)} %select_reduce_fusion.1.dens_table), channel_id=1, source_target_pairs={{0,2},{1,0},{3,1},{2,3},{4,6},{5,4},{7,5},{6,7},{8,10},{9,8},{11,9... | collective-permute-start | bytes 776 | tf_op jit(solution)/shard_map/ppermute | solution.py:28
  39.9 3.9 %collective-permute-done.7.dens_table = s32[4,16]{1,0:T(4,128)S(1)} collective-permute-done((s32[4,16]{1,0:T(4,128)S(1)}, s32[4,16]{1,0:T(4,128)S(1)}, u32[]{:S(2)}, u32[]{:S(2)}) %collective-permute-start.7) | collective-permute-done | bytes 288 | tf_op jit(solution)/shard_map/ppermute | solution.py:28
  43.8 1.6 %add2.1.acc_in = f32[256,1024]{1,0:T(8,128)S(1)} custom-call(s32[4,16]{1,0:T(4,128)S(1)} %collective-permute-done.7.dens_table, bf16[8,256,384]{2,1,0:T(8,128)(2,1)S(1)} %get-tuple-element.25.a, f32[256,1024]{1,0:T(8,128)S(1)} %add1.1.acc_in, f32[2,64,512]{2,1,0:T(8,128)S(1)} %collective-permute-done.8.rest_0_, f32[2,64,512]{2,1,0:T(8,128)S(1)} %collective-permute-done.1.rest_1_), custom_call_target="tpu_custom_call" | custom-call | flops 402653184 | bytes 4194304 | tf_op jit(solution)/shard_map/add2/pallas_call | solution.py:297
  45.5 1.3 %add3.1.acc_in = f32[256,1024]{1,0:T(8,128)S(1)} custom-call(s32[4,16]{1,0:T(4,128)S(1)} %collective-permute-done.6.dens_table, bf16[8,256,384]{2,1,0:T(8,128)(2,1)S(1)} %get-tuple-element.25.a, f32[256,1024]{1,0:T(8,128)S(1)} %add2.1.acc_in, f32[2,64,512]{2,1,0:T(8,128)S(1)} %collective-permute-done.9.rest_0_), custom_call_target="tpu_custom_call" | custom-call | flops 402653184 | bytes 4194304 | tf_op jit(solution)/shard_map/add3/pallas_call | solution.py:297
  46.8 1.1 %last0.1.rest_0_ = f32[256,512]{1,0:T(8,128)S(1)} custom-call(s32[4,16]{1,0:T(4,128)S(1)} %collective-permute-done.6.dens_table, bf16[8,256,384]{2,1,0:T(8,128)(2,1)S(1)} %get-tuple-element.25.a, f32[256,1024]{1,0:T(8,128)S(1)} %add3.1.acc_in, f32[2,64,512]{2,1,0:T(8,128)S(1)} %collective-permute-done.10.chunk), custom_call_target="tpu_custom_call" | custom-call | flops 1024 | bytes 1024 | tf_op jit(solution)/shard_map/last0/pallas_call | solution.py:311
  47.9 0.1 collective-permute-start.15
  47.9 1.7 %collective-permute-start.16 = (f32[256,512]{1,0:T(8,128)S(1)}, f32[256,512]{1,0:T(8,128)S(1)}, u32[]{:S(2)}, u32[]{:S(2)}) collective-permute-start(f32[256,512]{1,0:T(8,128)S(1)} %last0.1.rest_0_), channel_id=1, source_target_pairs={{0,12},{4,0},{8,4},{12,8},{1,13},{5,1},{9,5},{13,9},{2,14},{6,2},{... | collective-permute-start | bytes 1572872 | tf_op jit(solution)/shard_map/ppermute | solution.py:19
  49.7 0.9 %last1.1.rest_1_ = f32[256,256]{1,0:T(8,128)S(1)} custom-call(s32[4,16]{1,0:T(4,128)S(1)} %collective-permute-done.6.dens_table, bf16[8,256,384]{2,1,0:T(8,128)(2,1)S(1)} %get-tuple-element.25.a, f32[256,1024]{1,0:T(8,128)S(1)} %add3.1.acc_in, f32[2,64,512]{2,1,0:T(8,128)S(1)} %collective-permute-done.10.chunk), custom_call_target="tpu_custom_call" | custom-call | flops 1024 | bytes 1024 | tf_op jit(solution)/shard_map/last1/pallas_call | solution.py:311
  50.6 0.1 collective-permute-start.13
  50.7 1.7 %collective-permute-start.14 = (f32[256,256]{1,0:T(8,128)S(1)}, f32[256,256]{1,0:T(8,128)S(1)}, u32[]{:S(2)}, u32[]{:S(2)}) collective-permute-start(f32[256,256]{1,0:T(8,128)S(1)} %last1.1.rest_1_), channel_id=1, source_target_pairs={{0,12},{4,0},{8,4},{12,8},{1,13},{5,1},{9,5},{13,9},{2,14},{6,2},{... | collective-permute-start | bytes 786440 | tf_op jit(solution)/shard_map/ppermute | solution.py:19
  52.4 0.9 %last2.1.rest_2_ = f32[256,256]{1,0:T(8,128)S(1)} custom-call(s32[4,16]{1,0:T(4,128)S(1)} %collective-permute-done.6.dens_table, bf16[8,256,384]{2,1,0:T(8,128)(2,1)S(1)} %get-tuple-element.25.a, f32[256,1024]{1,0:T(8,128)S(1)} %add3.1.acc_in, f32[2,64,512]{2,1,0:T(8,128)S(1)} %collective-permute-done.10.chunk), custom_call_target="tpu_custom_call" | custom-call | flops 1024 | bytes 1024 | tf_op jit(solution)/shard_map/last2/pallas_call | solution.py:311
  53.4 0.1 collective-permute-start.11
  53.4 6.9 %collective-permute-done.15.before = f32[256,512]{1,0:T(8,128)S(1)} collective-permute-done((f32[256,512]{1,0:T(8,128)S(1)}, f32[256,512]{1,0:T(8,128)S(1)}, u32[]{:S(2)}, u32[]{:S(2)}) %collective-permute-start.15) | collective-permute-done | bytes 524320 | tf_op jit(solution)/shard_map/ppermute | solution.py:19
  60.3 1.7 %own.1 = (f32[4,64,1024]{2,1,0:T(8,128)}, f32[4,64,3072]{2,1,0:T(8,128)}) custom-call(bf16[3,256,256]{2,1,0:T(8,128)(2,1)S(1)} %get-tuple-element.29.m_hi, bf16[3,256,256]{2,1,0:T(8,128)(2,1)S(1)} %get-tuple-element.30.m_lo, f32[256,512]{1,0:T(8,128)S(1)} %last0.1.rest_0_, f32[256,256]{1,0:T(8,128)S(1)} %last1.1.rest_1_, f32[256,256]{1,0:T(8,128)S(1)} %last2.1.rest_2_), custom_call_target="tpu_custom_call" | custom-call | flops 1024 | bytes 1024 | tf_op jit(solution)/shard_map/own/pallas_call | solution.py:327
  62.0 1.5 %arrived0.1.window_in = f32[4,64,3072]{2,1,0:T(8,128)} custom-call(bf16[3,256,256]{2,1,0:T(8,128)(2,1)S(1)} %get-tuple-element.29.m_hi, bf16[3,256,256]{2,1,0:T(8,128)(2,1)S(1)} %get-tuple-element.30.m_lo, f32[256,512]{1,0:T(8,128)S(1)} %collective-permute-done.15.before, ...), custom_call_target="tpu_custom_call", output_to_operand_aliasing={{}: (4, {})} | custom-call | flops 1024 | bytes 1024 | tf_op jit(solution)/shard_map/arrived0/pallas_call | solution.py:339
  63.6 2.4 %collective-permute-done.13.before = f32[256,256]{1,0:T(8,128)S(1)} collective-permute-done((f32[256,256]{1,0:T(8,128)S(1)}, f32[256,256]{1,0:T(8,128)S(1)}, u32[]{:S(2)}, u32[]{:S(2)}) %collective-permute-start.13) | collective-permute-done | bytes 262176 | tf_op jit(solution)/shard_map/ppermute | solution.py:19
  65.9 1.7 %collective-permute-done.14.after = f32[256,256]{1,0:T(8,128)S(1)} collective-permute-done((f32[256,256]{1,0:T(8,128)S(1)}, f32[256,256]{1,0:T(8,128)S(1)}, u32[]{:S(2)}, u32[]{:S(2)}) %collective-permute-start.14) | collective-permute-done | bytes 262176 | tf_op jit(solution)/shard_map/ppermute | solution.py:19
  67.6 1.2 %arrived1.1.window_in = f32[4,64,3072]{2,1,0:T(8,128)} custom-call(bf16[3,256,256]{2,1,0:T(8,128)(2,1)S(1)} %get-tuple-element.29.m_hi, bf16[3,256,256]{2,1,0:T(8,128)(2,1)S(1)} %get-tuple-element.30.m_lo, f32[256,256]{1,0:T(8,128)S(1)} %collective-permute-done.13.before, ...), custom_call_target="tpu_custom_call", output_to_operand_aliasing={{}: (4, {})} | custom-call | flops 1024 | bytes 1024 | tf_op jit(solution)/shard_map/arrived1/pallas_call | solution.py:339
  68.8 2.7 %collective-permute-done.11.before = f32[256,256]{1,0:T(8,128)S(1)} collective-permute-done((f32[256,256]{1,0:T(8,128)S(1)}, f32[256,256]{1,0:T(8,128)S(1)}, u32[]{:S(2)}, u32[]{:S(2)}) %collective-permute-start.11) | collective-permute-done | bytes 262176 | tf_op jit(solution)/shard_map/ppermute | solution.py:19
  71.5 0.9 %collective-permute-done.12.after = f32[256,256]{1,0:T(8,128)S(1)} collective-permute-done((f32[256,256]{1,0:T(8,128)S(1)}, f32[256,256]{1,0:T(8,128)S(1)}, u32[]{:S(2)}, u32[]{:S(2)}) %collective-permute-start.12) | collective-permute-done | bytes 262176 | tf_op jit(solution)/shard_map/ppermute | solution.py:19
  72.4 1.2 %arrived2.1 = f32[4,64,3072]{2,1,0:T(8,128)} custom-call(bf16[3,256,256]{2,1,0:T(8,128)(2,1)S(1)} %get-tuple-element.29.m_hi, bf16[3,256,256]{2,1,0:T(8,128)(2,1)S(1)} %get-tuple-element.30.m_lo, f32[256,256]{1,0:T(8,128)S(1)} %collective-permute-done.11.before, f32[256,256]{1,0:T(8,128)S(1)} %collective-permute-done.12.after, ...), custom_call_target="tpu_custom_call", output_to_operand_aliasing={{}: (4, {})} | custom-call | flops 1024 | bytes 1024 | tf_op jit(solution)/shard_map/arrived2/pallas_call | solution.py:339
  (13 shorter events, 0.0 us)
Async XLA Ops:
  0.6 26.0 %copy-start = (f32[4,64,768]{2,1,0:T(8,128)S(1)}, f32[4,64,768]{2,1,0:T(8,128)}, u32[]{:S(2)}) copy-start(f32[4,64,768]{2,1,0:T(8,128)} %over.1) | copy-start | bytes 2359300
  1.8 21.3 %collective-permute-start = (f32[2,64,512]{2,1,0:T(8,128)S(1)}, f32[2,64,512]{2,1,0:T(8,128)S(1)}, u32[]{:S(2)}, u32[]{:S(2)}) collective-permute-start(f32[2,64,512]{2,1,0:T(8,128)S(1)} %get-tuple-element.20), channel_id=1, source_target_pairs={{0,1},{1,3},{3,2},{2,0},{4,5},{5,7},{7,6},{6,4},{8,9},{9,11},{11,1... | collective-permute-start | bytes 786440 | tf_op jit(solution)/shard_map/ppermute | solution.py:28
  4.9 12.9 %collective-permute-start.3 = (f32[2,64,512]{2,1,0:T(8,128)S(1)}, f32[2,64,512]{2,1,0:T(8,128)S(1)}, u32[]{:S(2)}, u32[]{:S(2)}) collective-permute-start(f32[2,64,512]{2,1,0:T(8,128)S(1)} %get-tuple-element.26), channel_id=1, source_target_pairs={{0,1},{1,3},{3,2},{2,0},{4,5},{5,7},{7,6},{6,4},{8,9},{9,11},{11,1... | collective-permute-start | bytes 786440 | tf_op jit(solution)/shard_map/ppermute | solution.py:28
  8.5 18.1 %collective-permute-start.4 = (f32[4,64,256]{2,1,0:T(8,128)S(1)}, f32[4,64,256]{2,1,0:T(8,128)S(1)}, u32[]{:S(2)}, u32[]{:S(2)}) collective-permute-start(f32[4,64,256]{2,1,0:T(8,128)S(1)} %get-tuple-element.39), channel_id=1, source_target_pairs={{0,4},{4,8},{8,12},{12,0},{1,5},{5,9},{9,13},{13,1},{2,6},{6,10},{... | collective-permute-start | bytes 786440 | tf_op jit(solution)/shard_map/ppermute | solution.py:19
  8.6 18.0 %collective-permute-start.5 = (f32[4,64,256]{2,1,0:T(8,128)S(1)}, f32[4,64,256]{2,1,0:T(8,128)S(1)}, u32[]{:S(2)}, u32[]{:S(2)}) collective-permute-start(f32[4,64,256]{2,1,0:T(8,128)S(1)} %get-tuple-element.38), channel_id=1, source_target_pairs={{0,12},{4,0},{8,4},{12,8},{1,13},{5,1},{9,5},{13,9},{2,14},{6,2},{... | collective-permute-start | bytes 786440 | tf_op jit(solution)/shard_map/ppermute | solution.py:19
  17.8 9.2 %collective-permute-start.8 = (f32[2,64,512]{2,1,0:T(8,128)S(1)}, f32[2,64,512]{2,1,0:T(8,128)S(1)}, u32[]{:S(2)}, u32[]{:S(2)}) collective-permute-start(f32[2,64,512]{2,1,0:T(8,128)S(1)} %collective-permute-done.3.rest_0_), channel_id=1, source_target_pairs={{0,1},{1,3},{3,2},{2,0},{4,5},{5,7},{7,6},{6,4},{8,9},{9,11},{11,1... | collective-permute-start | bytes 786440 | tf_op jit(solution)/shard_map/ppermute | solution.py:28
  18.6 1.0 %copy-start.1 = (f32[4,64,512]{2,1,0:T(8,128)S(1)}, f32[4,64,512]{2,1,0:T(8,128)}, u32[]{:S(2)}) copy-start(f32[4,64,512]{2,1,0:T(8,128)} %dens.1) | copy-start | bytes 1572868
  19.7 1.1 %copy-start.2 = (f32[4,64,768]{2,1,0:T(8,128)S(1)}, f32[4,64,768]{2,1,0:T(8,128)}, u32[]{:S(2)}) copy-start(f32[4,64,768]{2,1,0:T(8,128)} %ham.1) | copy-start | bytes 2359300
  23.1 11.9 %collective-permute-start.1 = (f32[2,64,512]{2,1,0:T(8,128)S(1)}, f32[2,64,512]{2,1,0:T(8,128)S(1)}, u32[]{:S(2)}, u32[]{:S(2)}) collective-permute-start(f32[2,64,512]{2,1,0:T(8,128)S(1)} %collective-permute-done.rest_1_), channel_id=1, source_target_pairs={{0,1},{1,3},{3,2},{2,0},{4,5},{5,7},{7,6},{6,4},{8,9},{9,11},{11,1... | collective-permute-start | bytes 786440 | tf_op jit(solution)/shard_map/ppermute | solution.py:28
  26.6 6.8 %collective-permute-start.2 = (s32[4,16]{1,0:T(4,128)S(1)}, s32[4,16]{1,0:T(4,128)S(1)}, u32[]{:S(2)}, u32[]{:S(2)}) collective-permute-start(s32[4,16]{1,0:T(4,128)S(1)} %select_reduce_fusion.1.dens_table), channel_id=1, source_target_pairs={{0,1},{1,3},{3,2},{2,0},{4,5},{5,7},{7,6},{6,4},{8,9},{9,11},{11,1... | collective-permute-start | bytes 776 | tf_op jit(solution)/shard_map/ppermute | solution.py:28
  27.0 18.5 %collective-permute-start.9 = (f32[2,64,512]{2,1,0:T(8,128)S(1)}, f32[2,64,512]{2,1,0:T(8,128)S(1)}, u32[]{:S(2)}, u32[]{:S(2)}) collective-permute-start(f32[2,64,512]{2,1,0:T(8,128)S(1)} %collective-permute-done.8.rest_0_), channel_id=1, source_target_pairs={{0,1},{1,3},{3,2},{2,0},{4,5},{5,7},{7,6},{6,4},{8,9},{9,11},{11,1... | collective-permute-start | bytes 786440 | tf_op jit(solution)/shard_map/ppermute | solution.py:28
  35.0 11.8 %collective-permute-start.10 = (f32[2,64,512]{2,1,0:T(8,128)S(1)}, f32[2,64,512]{2,1,0:T(8,128)S(1)}, u32[]{:S(2)}, u32[]{:S(2)}) collective-permute-start(f32[2,64,512]{2,1,0:T(8,128)S(1)} %collective-permute-done.1.rest_1_), channel_id=1, source_target_pairs={{0,1},{1,3},{3,2},{2,0},{4,5},{5,7},{7,6},{6,4},{8,9},{9,11},{11,1... | collective-permute-start | bytes 786440 | tf_op jit(solution)/shard_map/ppermute | solution.py:28
  37.6 6.3 %collective-permute-start.7 = (s32[4,16]{1,0:T(4,128)S(1)}, s32[4,16]{1,0:T(4,128)S(1)}, u32[]{:S(2)}, u32[]{:S(2)}) collective-permute-start(s32[4,16]{1,0:T(4,128)S(1)} %select_reduce_fusion.1.dens_table), channel_id=1, source_target_pairs={{0,3},{1,2},{3,0},{2,1},{4,7},{5,6},{7,4},{6,5},{8,11},{9,10},{11,... | collective-permute-start | bytes 776 | tf_op jit(solution)/shard_map/ppermute | solution.py:28
  38.0 7.5 %collective-permute-start.6 = (s32[4,16]{1,0:T(4,128)S(1)}, s32[4,16]{1,0:T(4,128)S(1)}, u32[]{:S(2)}, u32[]{:S(2)}) collective-permute-start(s32[4,16]{1,0:T(4,128)S(1)} %select_reduce_fusion.1.dens_table), channel_id=1, source_target_pairs={{0,2},{1,0},{3,1},{2,3},{4,6},{5,4},{7,5},{6,7},{8,10},{9,8},{11,9... | collective-permute-start | bytes 776 | tf_op jit(solution)/shard_map/ppermute | solution.py:28
  47.9 12.4 %collective-permute-start.15 = (f32[256,512]{1,0:T(8,128)S(1)}, f32[256,512]{1,0:T(8,128)S(1)}, u32[]{:S(2)}, u32[]{:S(2)}) collective-permute-start(f32[256,512]{1,0:T(8,128)S(1)} %last0.1.rest_0_), channel_id=1, source_target_pairs={{0,4},{4,8},{8,12},{12,0},{1,5},{5,9},{9,13},{13,1},{2,6},{6,10},{... | collective-permute-start | bytes 1572872 | tf_op jit(solution)/shard_map/ppermute | solution.py:19
  47.9 14.1 %collective-permute-start.16 = (f32[256,512]{1,0:T(8,128)S(1)}, f32[256,512]{1,0:T(8,128)S(1)}, u32[]{:S(2)}, u32[]{:S(2)}) collective-permute-start(f32[256,512]{1,0:T(8,128)S(1)} %last0.1.rest_0_), channel_id=1, source_target_pairs={{0,12},{4,0},{8,4},{12,8},{1,13},{5,1},{9,5},{13,9},{2,14},{6,2},{... | collective-permute-start | bytes 1572872 | tf_op jit(solution)/shard_map/ppermute | solution.py:19
  50.6 15.3 %collective-permute-start.13 = (f32[256,256]{1,0:T(8,128)S(1)}, f32[256,256]{1,0:T(8,128)S(1)}, u32[]{:S(2)}, u32[]{:S(2)}) collective-permute-start(f32[256,256]{1,0:T(8,128)S(1)} %last1.1.rest_1_), channel_id=1, source_target_pairs={{0,4},{4,8},{8,12},{12,0},{1,5},{5,9},{9,13},{13,1},{2,6},{6,10},{... | collective-permute-start | bytes 786440 | tf_op jit(solution)/shard_map/ppermute | solution.py:19
  50.7 16.9 %collective-permute-start.14 = (f32[256,256]{1,0:T(8,128)S(1)}, f32[256,256]{1,0:T(8,128)S(1)}, u32[]{:S(2)}, u32[]{:S(2)}) collective-permute-start(f32[256,256]{1,0:T(8,128)S(1)} %last1.1.rest_1_), channel_id=1, source_target_pairs={{0,12},{4,0},{8,4},{12,8},{1,13},{5,1},{9,5},{13,9},{2,14},{6,2},{... | collective-permute-start | bytes 786440 | tf_op jit(solution)/shard_map/ppermute | solution.py:19
  53.4 18.2 %collective-permute-start.11 = (f32[256,256]{1,0:T(8,128)S(1)}, f32[256,256]{1,0:T(8,128)S(1)}, u32[]{:S(2)}, u32[]{:S(2)}) collective-permute-start(f32[256,256]{1,0:T(8,128)S(1)} %last2.1.rest_2_), channel_id=1, source_target_pairs={{0,4},{4,8},{8,12},{12,0},{1,5},{5,9},{9,13},{13,1},{2,6},{6,10},{... | collective-permute-start | bytes 786440 | tf_op jit(solution)/shard_map/ppermute | solution.py:19
  60.3 12.1 %collective-permute-start.12 = (f32[256,256]{1,0:T(8,128)S(1)}, f32[256,256]{1,0:T(8,128)S(1)}, u32[]{:S(2)}, u32[]{:S(2)}) collective-permute-start(f32[256,256]{1,0:T(8,128)S(1)} %last2.1.rest_2_), channel_id=1, source_target_pairs={{0,12},{4,0},{8,4},{12,8},{1,13},{5,1},{9,5},{13,9},{2,14},{6,2},{... | collective-permute-start | bytes 786440 | tf_op jit(solution)/shard_map/ppermute | solution.py:19

commit v3 on v2

--- a/solution.py
+++ b/solution.py
@@ -39,13 +39,27 @@
     return owner
 
 
-def slot_table(columns, counts, width):
-    slots = jnp.arange(columns.shape[1], dtype=jnp.int32)
-    wanted = jnp.arange(width, dtype=jnp.int32)
-    hit = (columns[:, None, :] == wanted[None, :, None]) & (
-        slots[None, None, :] < counts[:, None, None]
-    )
-    return jnp.max(jnp.where(hit, slots + 1, 0), axis=2)
+def fill_table(table, columns, counts):
+    rows, width = table.shape
+    for r in range(rows):
+        for c in range(width):
+            table[r, c] = 0
+        for slot in range(columns.shape[1]):
+
+            @pl.when(slot < counts[r])
+            def _(r=r, slot=slot):
+                table[r, columns[r, slot]] = slot + 1
+
+
+def prep_kernel(columns, counts, dens, *rest):
+    halves, table, sems = rest[:-2], rest[-2], rest[-1]
+    copies = []
+    for h, half in enumerate(halves):
+        copies.append(pltpu.make_async_copy(dens.at[pl.ds(2 * h, 2)], half, sems.at[h]))
+        copies[-1].start()
+    fill_table(table, columns, counts)
+    for copy in copies:
+        copy.wait()
 
 
 def split(v):
@@ -70,11 +84,11 @@
     return jnp.where(low_lanes(v0.shape[0]), v0, v1)
 
 
-def densify_half(chunk_ref, first, table, b):
-    tile = chunk_ref.shape[1]
+def densify_half(chunk, table, half, b, first=0):
+    tile = chunk.shape[1]
     for r in range(2):
-        for pair in range(table.shape[1] // 2):
-            hi, lo = split(pair_at(chunk_ref.at[first + r], table, first + r, pair))
+        for pair in range(b.shape[1] // LANES):
+            hi, lo = split(pair_at(chunk.at[r], table, 2 * half + r, first + pair))
             lanes = slice(pair * LANES, (pair + 1) * LANES)
             b[r * tile : (r + 1) * tile, lanes] = hi
             b[(2 + r) * tile : (3 + r) * tile, lanes] = lo
@@ -91,54 +105,48 @@
     return [slice(i, i + step) for i in range(0, width, step)]
 
 
-def first_kernel(ham_table, dens_table, ham, dens, a, acc, b):
+def first_kernel(ham_cols, ham_count, dens_table, ham, *rest):
+    (a, acc, ham_table, ham_here, b, sems), halves = rest[-6:], rest[:-6]
     rows, tile, _ = ham.shape
+    copies = [
+        pltpu.make_async_copy(ham.at[q], ham_here.at[q], sems.at[q]) for q in range(rows)
+    ]
+    for copy in copies:
+        copy.start()
+    fill_table(ham_table, ham_cols, ham_count)
     for q in range(rows):
+        copies[q].wait()
         for pair in range(ham_table.shape[1] // 2):
-            hi, lo = split(pair_at(ham.at[q], ham_table, q, pair))
+            hi, lo = split(pair_at(ham_here.at[q], ham_table, q, pair))
             a[pair, q * tile : (q + 1) * tile, 0:LANES] = hi
             a[pair, q * tile : (q + 1) * tile, LANES : 2 * LANES] = hi
             a[pair, q * tile : (q + 1) * tile, 2 * LANES : 3 * LANES] = lo
-    for half in range(rows // 2):
-        densify_half(dens, 2 * half, dens_table, b)
-        pair = shard_of(0) * (rows // 2) + half
+    for h, half in enumerate(halves):
+        densify_half(half, dens_table, h, b)
+        pair = shard_of(0) * (rows // 2) + h
         for lanes in lane_blocks(acc.shape[1]):
             part = times_half(a[pair], b, lanes)
-            acc[:, lanes] = part if half == 0 else acc[:, lanes] + part
-
-
-def add_kernel(step, halves, count, dens_table, a, acc_in, *rest):
-    chunks, (acc, b) = rest[:count], rest[count:]
+            acc[:, lanes] = part if h == 0 else acc[:, lanes] + part
+
+
+def add_kernel(step, halves, dens_table, a, acc_in, *rest):
+    chunks, (acc, b) = rest[:-2], rest[-2:]
     per_shard = dens_table.shape[0] // 2
     for i, half in enumerate(halves):
-        table = dens_table.at[pl.ds(2 * half, 2)]
-        densify_half(chunks[i], 0, table, b)
+        densify_half(chunks[i], dens_table, half, b)
         pair = shard_of(step) * per_shard + half
         for lanes in lane_blocks(acc.shape[1]):
             before = acc_in if i == 0 else acc
             acc[:, lanes] = before[:, lanes] + times_half(a[pair], b, lanes)
 
 
-def last_kernel(step, half, first, widths, dens_table, a, acc_in, chunk, *rest):
-    outs, b = rest[:-1], rest[-1]
+def last_kernel(step, half, first, dens_table, a, acc_in, chunk, out, b):
     per_shard = dens_table.shape[0] // 2
-    width = sum(widths)
-    table = dens_table.at[pl.ds(2 * half, 2)]
-    tile = chunk.shape[1]
-    for r in range(2):
-        for pair in range(width // LANES):
-            hi, lo = split(pair_at(chunk.at[r], table, r, first // LANES + pair))
-            lanes = slice(pair * LANES, (pair + 1) * LANES)
-            b[r * tile : (r + 1) * tile, lanes] = hi
-            b[(2 + r) * tile : (3 + r) * tile, lanes] = lo
+    densify_half(chunk, dens_table, half, b, first // LANES)
     pair = shard_of(step) * per_shard + half
-    at = 0
-    for out, piece in zip(outs, widths):
-        for lanes in lane_blocks(piece):
-            here = slice(at + lanes.start, at + lanes.stop)
-            source = slice(first + here.start, first + here.stop)
-            out[:, lanes] = acc_in[:, source] + times_half(a[pair], b, here)
-        at += piece
+    for lanes in lane_blocks(out.shape[1]):
+        source = slice(first + lanes.start, first + lanes.stop)
+        out[:, lanes] = acc_in[:, source] + times_half(a[pair], b, lanes)
 
 
 def margin_kernel(over, before, after, hi_out, lo_out):
@@ -256,70 +264,86 @@
     per_shard = rows // 2
     sds = jax.ShapeDtypeStruct
 
-    halves = [dens_tiles[2 * h : 2 * h + 2] for h in range(per_shard)]
-    halves, dens_cols, dens_count = lax.optimization_barrier((halves, dens_cols, dens_count))
-    dens_table = slot_table(dens_cols, dens_count, blocks)
-    ham_table = slot_table(ham_cols, ham_count, blocks)
-    over_before = rotate(over_tiles[:, :, 2 * tall :], "line", 1)
-    over_after = rotate(over_tiles[:, :, :tall], "line", -1)
-
+    ham_tiles, dens_tiles = (
+        pltpu.with_memory_space_constraint(x, pltpu.HBM) for x in (ham_tiles, dens_tiles)
+    )
+    *halves, table = call(
+        prep_kernel,
+        "prep",
+        [sds((2, tile, dens_tiles.shape[2]), F32)] * per_shard + [sds((rows, blocks), jnp.int32)],
+        (SMEM, SMEM, pltpu.HBM),
+        [VMEM] * per_shard + [SMEM],
+        [pltpu.SemaphoreType.DMA((per_shard,))],
+        1024,
+        1024,
+    )(dens_cols, dens_count, dens_tiles)
+    tables = [pass_on(table, step) for step in range(1, count)]
     b_scratch = [VMEM((4 * tile, width), BF16)]
     a, acc = call(
         first_kernel,
         "first",
         (sds((blocks // 2, tall, 3 * LANES), BF16), sds((tall, width), F32)),
-        (SMEM, SMEM, VMEM, VMEM),
+        (SMEM, SMEM, SMEM, pltpu.HBM) + (VMEM,) * per_shard,
         (VMEM, VMEM),
-        b_scratch,
-        2 * 3 * tall * tall * width,
-        4 << 20,
-    )(ham_table, dens_table, ham_tiles, dens_tiles)
-    m_hi, m_lo = call(
-        margin_kernel,
-        "margin",
-        (sds((3, tall, tall), BF16),) * 2,
-        (VMEM,) * 3,
-        (VMEM, VMEM),
-        [],
+        [pltpu.SMEM((rows, blocks), jnp.int32), VMEM(ham_tiles.shape, F32)]
+        + b_scratch
+        + [pltpu.SemaphoreType.DMA((rows,))],
         1 << 20,
-        2 << 20,
-    )(over_tiles, over_before, over_after)
-    done = acc
+        1 << 20,
+    )(ham_cols, ham_count, table, ham_tiles, *halves)
+    halves = [pass_on(h, 1) for h in halves]
     for step in range(1, count):
-        if step > 1:
-            halves[-1], done, m_hi, m_lo = lax.optimization_barrier(
-                (halves[-1], done, m_hi, m_lo) if step == 3 else (halves[-1], done)
-            ) + (() if step == 3 else (m_hi, m_lo))
-        chunks = halves = [pass_on(h, 1) for h in halves]
-        table = pass_on(dens_table, step)
+        if step == 1:
+            halves[0], a, acc, over_tiles = lax.optimization_barrier(
+                (halves[0], a, acc, over_tiles)
+            )
+            halves[-1], *tables = lax.optimization_barrier((halves[-1], *tables))
+            over_before = rotate(over_tiles[:, :, 2 * tall :], "line", 1)
+            over_after = rotate(over_tiles[:, :, :tall], "line", -1)
+            m_hi, m_lo = call(
+                margin_kernel,
+                "margin",
+                (sds((3, tall, tall), BF16),) * 2,
+                (VMEM,) * 3,
+                (VMEM, VMEM),
+                [],
+                1 << 20,
+                2 << 20,
+            )(over_tiles, over_before, over_after)
+        else:
+            halves[0], acc = lax.optimization_barrier((halves[0], acc))
+        if step == 2:
+            halves[-1], m_hi, m_lo = lax.optimization_barrier((halves[-1], m_hi, m_lo))
         last = step == count - 1
+        arrived = list(halves)
+        if not last:
+            halves = [pass_on(h, 1) for h in halves]
         todo = list(range(per_shard - 1 if last else per_shard))
-        done, acc = acc, call(
-            functools.partial(add_kernel, step, todo, len(todo)),
+        acc = call(
+            functools.partial(add_kernel, step, todo),
             "add%d" % step,
             sds((tall, width), F32),
             (SMEM,) + (VMEM,) * (2 + len(todo)),
             VMEM,
             b_scratch,
-            2 * 3 * tall * tall * width,
-            4 << 20,
-        )(table, a, acc, *[chunks[h] for h in todo])
-        halves = list(halves)
-    pieces = (width // 2, width // 4, width // 4)
+            1 << 20,
+            1 << 20,
+        )(tables[step - 1], a, acc, *[arrived[h] for h in todo])
+    pieces = (width // 2, width // 2)
     parts = []
     for i, piece in enumerate(pieces):
-        parts += call(
-            functools.partial(
-                last_kernel, count - 1, per_shard - 1, sum(pieces[:i]), (piece,)
-            ),
-            "last%d" % i,
-            [sds((tall, piece), F32)],
-            (SMEM, VMEM, VMEM, VMEM),
-            [VMEM],
-            [VMEM((4 * tile, piece), BF16)],
-            1024,
-            1024,
-        )(table, a, acc, chunks[-1])
+        parts.append(
+            call(
+                functools.partial(last_kernel, count - 1, per_shard - 1, sum(pieces[:i])),
+                "last%d" % i,
+                sds((tall, piece), F32),
+                (SMEM, VMEM, VMEM, VMEM),
+                VMEM,
+                [VMEM((4 * tile, piece), BF16)],
+                1024,
+                1024,
+            )(tables[-1], a, acc, halves[-1])
+        )
         if i + 1 < len(pieces):
             parts[-1], acc = lax.optimization_barrier((parts[-1], acc))
     before = [rotate(p, "line", 1) for p in parts]

time: 74.3 us -> 71.2 us (0.958)
  other arithmetic: 2.28 us -> 0 us
  starting transfers between devices: 21.1 us -> 19.2 us
  Pallas kernels: 15.8 us -> 17.4 us
  local copies, waits for them, and re-layouts: 5.16 us -> 3.73 us
  waiting for transfers between devices: 28.6 us -> 29.6 us
    pallas_call x3 -> x4, Pallas kernels: 4.51 us -> 6.75 us  [the longest x3 4.51 us: shards(): call(functools.partial(add_kernel, step, todo), 'add%d' % step, sds((tall...]
    ppermute x8 -> x6, waiting for transfers between devices: 14.5 us -> 16.6 us  [rotate(): return lax.ppermute(x, axis, [(i, (i + by) % count) for i in range(count)])]
    ppermute x8 -> x6, starting transfers between devices: 5.43 us -> 3.58 us  [rotate(): return lax.ppermute(x, axis, [(i, (i + by) % count) for i in range(count)])]
    lt x2 -> x0, other arithmetic: 1.39 us -> none  [slot_table(): slots[None, None, :] < counts[:, None, None]]
    pallas_call x1, Pallas kernels: 2.3 us -> 3.47 us  [shards(): call(first_kernel, 'first', (sds((blocks // 2, tall, 3 * LANES), BF16), s...]
    slice x1 -> x0, local copies, waits for them, and re-layouts: 1.14 us -> none  [shards(): halves = [dens_tiles[2 * h:2 * h + 2] for h in range(per_shard)]]
    ppermute x9, waiting for transfers between devices: 14.1 us -> 12.9 us  [pass_on(): lax.ppermute(x, 'cross', [(d, order[(i + by) % len(order)]) for i, d in e...]
    pallas_call x3 -> x2, Pallas kernels: 4.01 us -> 3.05 us  [shards(): call(functools.partial(arrived_kernel, at), 'arrived%d' % i, sds((rows, t...]
  transfers between devices with their start and end apart: 17 -> 15, of which waited for: 9 -> 10; matrix products, arithmetic and copies ran while one was open for 6% -> 2% of each run, Pallas kernels for 18% -> 18%
where the time goes in v3:
time: 71.2 us; the launch traced here: 70.6 us
  waiting for transfers between devices  29.6 us (42%)
  starting transfers between devices  19.2 us (27%)
  Pallas kernels  17.4 us (24%)
  local copies, waits for them, and re-layouts  3.73 us (5%)
  between operations  0.77 us (1%)
    ppermute x6, waiting for transfers between devices, rotate(): return lax.ppermute(x, axis, [(i, (i + by) % count) for i in range(count)])  16.6 us
    ppermute x9, starting transfers between devices, pass_on(): lax.ppermute(x, 'cross', [(d, order[(i + by) % len(order)]) for i, d in e...  15.6 us
    ppermute x9, waiting for transfers between devices, pass_on(): lax.ppermute(x, 'cross', [(d, order[(i + by) % len(order)]) for i, d in e...  12.9 us
    pallas_call x3, Pallas kernels, shards(): call(functools.partial(add_kernel, step, todo), 'add%d' % step, sds((tall...  4.51 us
    ppermute x6, starting transfers between devices, rotate(): return lax.ppermute(x, axis, [(i, (i + by) % count) for i in range(count)])  3.58 us
    pallas_call x1, Pallas kernels, shards(): call(first_kernel, 'first', (sds((blocks // 2, tall, 3 * LANES), BF16), s...  3.47 us
    pallas_call x2, Pallas kernels, shards(): call(functools.partial(arrived_kernel, at), 'arrived%d' % i, sds((rows, t...  3.05 us
    unnamed x10, local copies, waits for them, and re-layouts  2.67 us
  transfers between devices with their start and end apart: 15, of which 10 were waited for; matrix products, arithmetic and copies ran while one was open for 2% of the time, Pallas kernels for 18%

profile of v3, /device:TPU:0, one launch (start us, length us, event | category | flops | bytes accessed | tf_op | source)
XLA Modules:
  0.0 70.6 jit_solution(1224217467796621581)
XLA Ops:
  0.6 0.0 copy-start.1
  0.6 0.7 copy-done.1
  1.3 0.7 copy-done.3
  2.0 2.2 %prep.1 = (f32[2,64,512]{2,1,0:T(8,128)S(1)}, f32[2,64,512]{2,1,0:T(8,128)S(1)}, s32[4,16]{1,0:T(4,128)S(1)}) custom-call(s32[4,8]{1,0:T(4,128)S(1)} %copy-done.1, s32[4]{0:T(128)S(1)} %copy-done.3, f32[4,64,512]{2,1,0:T(8,128)} %dens.1), custom_call_target="tpu_custom_call" | custom-call | flops 1024 | bytes 1024 | tf_op jit(solution)/shard_map/prep/pallas_call | solution.py:270
  4.2 3.1 %collective-permute-start.5 = (f32[2,64,512]{2,1,0:T(8,128)S(1)}, f32[2,64,512]{2,1,0:T(8,128)S(1)}, u32[]{:S(2)}, u32[]{:S(2)}) collective-permute-start(f32[2,64,512]{2,1,0:T(8,128)S(1)} %get-tuple-element.31.rest_0_), channel_id=1, source_target_pairs={{0,1},{1,3},{3,2},{2,0},{4,5},{5,7},{7,6},{6,4},{8,9},{9,11},{11,1... | collective-permute-start | bytes 786440 | tf_op jit(solution)/shard_map/ppermute | solution.py:28
  7.3 2.6 %collective-permute-start = (f32[2,64,512]{2,1,0:T(8,128)S(1)}, f32[2,64,512]{2,1,0:T(8,128)S(1)}, u32[]{:S(2)}, u32[]{:S(2)}) collective-permute-start(f32[2,64,512]{2,1,0:T(8,128)S(1)} %get-tuple-element.28.rest_1_), channel_id=1, source_target_pairs={{0,1},{1,3},{3,2},{2,0},{4,5},{5,7},{7,6},{6,4},{8,9},{9,11},{11,1... | collective-permute-start | bytes 786440 | tf_op jit(solution)/shard_map/ppermute | solution.py:28
  9.9 0.4 collective-permute-start.1
  10.3 1.3 %collective-permute-start.2 = (s32[4,16]{1,0:T(4,128)S(1)}, s32[4,16]{1,0:T(4,128)S(1)}, u32[]{:S(2)}, u32[]{:S(2)}) collective-permute-start(s32[4,16]{1,0:T(4,128)S(1)} %get-tuple-element.29.dens_table), channel_id=1, source_target_pairs={{0,3},{1,2},{3,0},{2,1},{4,7},{5,6},{7,4},{6,5},{8,11},{9,10},{11,... | collective-permute-start | bytes 776 | tf_op jit(solution)/shard_map/ppermute | solution.py:28
  11.7 1.1 %collective-permute-start.3 = (s32[4,16]{1,0:T(4,128)S(1)}, s32[4,16]{1,0:T(4,128)S(1)}, u32[]{:S(2)}, u32[]{:S(2)}) collective-permute-start(s32[4,16]{1,0:T(4,128)S(1)} %get-tuple-element.29.dens_table), channel_id=1, source_target_pairs={{0,2},{1,0},{3,1},{2,3},{4,6},{5,4},{7,5},{6,7},{8,10},{9,8},{11,9... | collective-permute-start | bytes 776 | tf_op jit(solution)/shard_map/ppermute | solution.py:28
  12.8 0.7 copy-done.2
  13.5 0.7 copy-done.4
  14.1 3.5 %first.1 = (bf16[8,256,384]{2,1,0:T(8,128)(2,1)S(1)}, f32[256,1024]{1,0:T(8,128)S(1)}) custom-call(s32[4,12]{1,0:T(4,128)S(1)} %copy-done.2, s32[4]{0:T(128)S(1)} %copy-done.4, s32[4,16]{1,0:T(4,128)S(1)} %get-tuple-element.29.dens_table, f32[4,64,768]{2,1,0:T(8,128)} %ham.1, f32[2,64,512]{2,1,0:T(8,128)S(1)} %get-tuple-element.31.rest_0_, ...), custom_call_target="tpu_custom_call" | custom-call | flops 1048576 | bytes 1048576 | tf_op jit(solution)/shard_map/first/pallas_call | solution.py:282
  17.6 0.0 collective-permute-done.5.rest_0_
  17.6 0.9 %collective-permute-start.8 = (f32[2,64,512]{2,1,0:T(8,128)S(1)}, f32[2,64,512]{2,1,0:T(8,128)S(1)}, u32[]{:S(2)}, u32[]{:S(2)}) collective-permute-start(f32[2,64,512]{2,1,0:T(8,128)S(1)} %collective-permute-done.5.rest_0_), channel_id=1, source_target_pairs={{0,1},{1,3},{3,2},{2,0},{4,5},{5,7},{7,6},{6,4},{8,9},{9,11},{11,1... | collective-permute-start | bytes 786440 | tf_op jit(solution)/shard_map/ppermute | solution.py:28
  18.6 1.1 %fusion = (f32[4,64,256]{2,1,0:T(8,128)S(1)}, f32[4,64,256]{2,1,0:T(8,128)S(1)}) fusion(f32[4,64,768]{2,1,0:T(8,128)} %over), kind=kLoop, calls=%fused_computation | loop fusion | bytes 1048576 | tf_op jit(solution)/shard_map/slice | solution.py:302
  19.6 1.0 %collective-permute-done.1.dens_table = s32[4,16]{1,0:T(4,128)S(1)} collective-permute-done((s32[4,16]{1,0:T(4,128)S(1)}, s32[4,16]{1,0:T(4,128)S(1)}, u32[]{:S(2)}, u32[]{:S(2)}) %collective-permute-start.1) | collective-permute-done | bytes 288 | tf_op jit(solution)/shard_map/ppermute | solution.py:28
  20.7 0.0 collective-permute-start.6
  20.7 2.0 %collective-permute-done.2.dens_table = s32[4,16]{1,0:T(4,128)S(1)} collective-permute-done((s32[4,16]{1,0:T(4,128)S(1)}, s32[4,16]{1,0:T(4,128)S(1)}, u32[]{:S(2)}, u32[]{:S(2)}) %collective-permute-start.2) | collective-permute-done | bytes 288 | tf_op jit(solution)/shard_map/ppermute | solution.py:28
  22.6 0.0 collective-permute-start.7
  22.6 0.0 collective-permute-done.3.dens_table
  22.6 0.0 collective-permute-done.rest_1_
  22.6 1.4 %collective-permute-start.4 = (f32[2,64,512]{2,1,0:T(8,128)S(1)}, f32[2,64,512]{2,1,0:T(8,128)S(1)}, u32[]{:S(2)}, u32[]{:S(2)}) collective-permute-start(f32[2,64,512]{2,1,0:T(8,128)S(1)} %collective-permute-done.rest_1_), channel_id=1, source_target_pairs={{0,1},{1,3},{3,2},{2,0},{4,5},{5,7},{7,6},{6,4},{8,9},{9,11},{11,1... | collective-permute-start | bytes 786440 | tf_op jit(solution)/shard_map/ppermute | solution.py:28
  24.1 1.6 %add1.1.acc_in = f32[256,1024]{1,0:T(8,128)S(1)} custom-call(s32[4,16]{1,0:T(4,128)S(1)} %collective-permute-done.1.dens_table, bf16[8,256,384]{2,1,0:T(8,128)(2,1)S(1)} %get-tuple-element.40.a, f32[256,1024]{1,0:T(8,128)S(1)} %get-tuple-element.43.acc_in, f32[2,64,512]{2,1,0:T(8,128)S(1)} %collective-permute-done.5.rest_0_, ...), custom_call_target="tpu_custom_call" | custom-call | flops 1048576 | bytes 1048576 | tf_op jit(solution)/shard_map/add1/pallas_call | solution.py:322
  25.7 0.3 collective-permute-done.8.rest_0_
  26.0 3.2 %collective-permute-start.9 = (f32[2,64,512]{2,1,0:T(8,128)S(1)}, f32[2,64,512]{2,1,0:T(8,128)S(1)}, u32[]{:S(2)}, u32[]{:S(2)}) collective-permute-start(f32[2,64,512]{2,1,0:T(8,128)S(1)} %collective-permute-done.8.rest_0_), channel_id=1, source_target_pairs={{0,1},{1,3},{3,2},{2,0},{4,5},{5,7},{7,6},{6,4},{8,9},{9,11},{11,1... | collective-permute-start | bytes 786440 | tf_op jit(solution)/shard_map/ppermute | solution.py:28
  29.2 0.0 collective-permute-done.6.before
  29.2 0.0 collective-permute-done.7.after
  29.2 0.0 copy-done
  29.2 0.3 margin.1
  29.5 3.2 %collective-permute-done.4.rest_1_ = f32[2,64,512]{2,1,0:T(8,128)S(1)} collective-permute-done((f32[2,64,512]{2,1,0:T(8,128)S(1)}, f32[2,64,512]{2,1,0:T(8,128)S(1)}, u32[]{:S(2)}, u32[]{:S(2)}) %collective-permute-start.4) | collective-permute-done | bytes 262176 | tf_op jit(solution)/shard_map/ppermute | solution.py:28
  32.7 1.5 %collective-permute-start.10 = (f32[2,64,512]{2,1,0:T(8,128)S(1)}, f32[2,64,512]{2,1,0:T(8,128)S(1)}, u32[]{:S(2)}, u32[]{:S(2)}) collective-permute-start(f32[2,64,512]{2,1,0:T(8,128)S(1)} %collective-permute-done.4.rest_1_), channel_id=1, source_target_pairs={{0,1},{1,3},{3,2},{2,0},{4,5},{5,7},{7,6},{6,4},{8,9},{9,11},{11,1... | collective-permute-start | bytes 786440 | tf_op jit(solution)/shard_map/ppermute | solution.py:28
  34.2 1.6 %add2.1.acc_in = f32[256,1024]{1,0:T(8,128)S(1)} custom-call(s32[4,16]{1,0:T(4,128)S(1)} %collective-permute-done.2.dens_table, bf16[8,256,384]{2,1,0:T(8,128)(2,1)S(1)} %get-tuple-element.40.a, f32[256,1024]{1,0:T(8,128)S(1)} %add1.1.acc_in, f32[2,64,512]{2,1,0:T(8,128)S(1)} %collective-permute-done.8.rest_0_, f32[2,64,512]{2,1,0:T(8,128)S(1)} %collective-permute-done.4.rest_1_), custom_call_target="tpu_custom_call" | custom-call | flops 1048576 | bytes 1048576 | tf_op jit(solution)/shard_map/add2/pallas_call | solution.py:322
  35.8 2.5 %collective-permute-done.9.rest_0_ = f32[2,64,512]{2,1,0:T(8,128)S(1)} collective-permute-done((f32[2,64,512]{2,1,0:T(8,128)S(1)}, f32[2,64,512]{2,1,0:T(8,128)S(1)}, u32[]{:S(2)}, u32[]{:S(2)}) %collective-permute-start.9) | collective-permute-done | bytes 262176 | tf_op jit(solution)/shard_map/ppermute | solution.py:28
  38.3 1.3 %add3.1.acc_in = f32[256,1024]{1,0:T(8,128)S(1)} custom-call(s32[4,16]{1,0:T(4,128)S(1)} %collective-permute-done.3.dens_table, bf16[8,256,384]{2,1,0:T(8,128)(2,1)S(1)} %get-tuple-element.40.a, f32[256,1024]{1,0:T(8,128)S(1)} %add2.1.acc_in, f32[2,64,512]{2,1,0:T(8,128)S(1)} %collective-permute-done.9.rest_0_), custom_call_target="tpu_custom_call" | custom-call | flops 1048576 | bytes 1048576 | tf_op jit(solution)/shard_map/add3/pallas_call | solution.py:322
  39.6 3.9 %collective-permute-done.10.chunk = f32[2,64,512]{2,1,0:T(8,128)S(1)} collective-permute-done((f32[2,64,512]{2,1,0:T(8,128)S(1)}, f32[2,64,512]{2,1,0:T(8,128)S(1)}, u32[]{:S(2)}, u32[]{:S(2)}) %collective-permute-start.10) | collective-permute-done | bytes 262176 | tf_op jit(solution)/shard_map/ppermute | solution.py:28
  43.5 1.1 %last0.1.rest_0_ = f32[256,512]{1,0:T(8,128)S(1)} custom-call(s32[4,16]{1,0:T(4,128)S(1)} %collective-permute-done.3.dens_table, bf16[8,256,384]{2,1,0:T(8,128)(2,1)S(1)} %get-tuple-element.40.a, f32[256,1024]{1,0:T(8,128)S(1)} %add3.1.acc_in, f32[2,64,512]{2,1,0:T(8,128)S(1)} %collective-permute-done.10.chunk), custom_call_target="tpu_custom_call" | custom-call | flops 1024 | bytes 1024 | tf_op jit(solution)/shard_map/last0/pallas_call | solution.py:336
  44.6 0.1 collective-permute-start.13
  44.7 1.7 %collective-permute-start.14 = (f32[256,512]{1,0:T(8,128)S(1)}, f32[256,512]{1,0:T(8,128)S(1)}, u32[]{:S(2)}, u32[]{:S(2)}) collective-permute-start(f32[256,512]{1,0:T(8,128)S(1)} %last0.1.rest_0_), channel_id=1, source_target_pairs={{0,12},{4,0},{8,4},{12,8},{1,13},{5,1},{9,5},{13,9},{2,14},{6,2},{... | collective-permute-start | bytes 1572872 | tf_op jit(solution)/shard_map/ppermute | solution.py:19
  46.4 1.1 %last1.1.rest_1_ = f32[256,512]{1,0:T(8,128)S(1)} custom-call(s32[4,16]{1,0:T(4,128)S(1)} %collective-permute-done.3.dens_table, bf16[8,256,384]{2,1,0:T(8,128)(2,1)S(1)} %get-tuple-element.40.a, f32[256,1024]{1,0:T(8,128)S(1)} %add3.1.acc_in, f32[2,64,512]{2,1,0:T(8,128)S(1)} %collective-permute-done.10.chunk), custom_call_target="tpu_custom_call" | custom-call | flops 1024 | bytes 1024 | tf_op jit(solution)/shard_map/last1/pallas_call | solution.py:336
  47.5 0.1 collective-permute-start.11
  47.6 1.7 %collective-permute-start.12 = (f32[256,512]{1,0:T(8,128)S(1)}, f32[256,512]{1,0:T(8,128)S(1)}, u32[]{:S(2)}, u32[]{:S(2)}) collective-permute-start(f32[256,512]{1,0:T(8,128)S(1)} %last1.1.rest_1_), channel_id=1, source_target_pairs={{0,12},{4,0},{8,4},{12,8},{1,13},{5,1},{9,5},{13,9},{2,14},{6,2},{... | collective-permute-start | bytes 1572872 | tf_op jit(solution)/shard_map/ppermute | solution.py:19
  49.3 1.7 %own.1 = (f32[4,64,1024]{2,1,0:T(8,128)}, f32[4,64,3072]{2,1,0:T(8,128)}) custom-call(bf16[3,256,256]{2,1,0:T(8,128)(2,1)S(1)} %get-tuple-element.37.m_hi, bf16[3,256,256]{2,1,0:T(8,128)(2,1)S(1)} %get-tuple-element.38.m_lo, f32[256,512]{1,0:T(8,128)S(1)} %last0.1.rest_0_, f32[256,512]{1,0:T(8,128)S(1)} %last1.1.rest_1_), custom_call_target="tpu_custom_call" | custom-call | flops 1024 | bytes 1024 | tf_op jit(solution)/shard_map/own/pallas_call | solution.py:351
  51.0 6.0 %collective-permute-done.13.before = f32[256,512]{1,0:T(8,128)S(1)} collective-permute-done((f32[256,512]{1,0:T(8,128)S(1)}, f32[256,512]{1,0:T(8,128)S(1)}, u32[]{:S(2)}, u32[]{:S(2)}) %collective-permute-start.13) | collective-permute-done | bytes 524320 | tf_op jit(solution)/shard_map/ppermute | solution.py:19
  57.0 1.7 %collective-permute-done.14.after = f32[256,512]{1,0:T(8,128)S(1)} collective-permute-done((f32[256,512]{1,0:T(8,128)S(1)}, f32[256,512]{1,0:T(8,128)S(1)}, u32[]{:S(2)}, u32[]{:S(2)}) %collective-permute-start.14) | collective-permute-done | bytes 524320 | tf_op jit(solution)/shard_map/ppermute | solution.py:19
  58.7 1.5 %arrived0.1.window_in = f32[4,64,3072]{2,1,0:T(8,128)} custom-call(bf16[3,256,256]{2,1,0:T(8,128)(2,1)S(1)} %get-tuple-element.37.m_hi, bf16[3,256,256]{2,1,0:T(8,128)(2,1)S(1)} %get-tuple-element.38.m_lo, f32[256,512]{1,0:T(8,128)S(1)} %collective-permute-done.13.before, ...), custom_call_target="tpu_custom_call", output_to_operand_aliasing={{}: (4, {})} | custom-call | flops 1024 | bytes 1024 | tf_op jit(solution)/shard_map/arrived0/pallas_call | solution.py:363
  60.2 8.0 %collective-permute-done.11.before = f32[256,512]{1,0:T(8,128)S(1)} collective-permute-done((f32[256,512]{1,0:T(8,128)S(1)}, f32[256,512]{1,0:T(8,128)S(1)}, u32[]{:S(2)}, u32[]{:S(2)}) %collective-permute-start.11) | collective-permute-done | bytes 524320 | tf_op jit(solution)/shard_map/ppermute | solution.py:19
  68.2 0.9 %collective-permute-done.12.after = f32[256,512]{1,0:T(8,128)S(1)} collective-permute-done((f32[256,512]{1,0:T(8,128)S(1)}, f32[256,512]{1,0:T(8,128)S(1)}, u32[]{:S(2)}, u32[]{:S(2)}) %collective-permute-start.12) | collective-permute-done | bytes 524320 | tf_op jit(solution)/shard_map/ppermute | solution.py:19
  69.1 1.5 %arrived1.1 = f32[4,64,3072]{2,1,0:T(8,128)} custom-call(bf16[3,256,256]{2,1,0:T(8,128)(2,1)S(1)} %get-tuple-element.37.m_hi, bf16[3,256,256]{2,1,0:T(8,128)(2,1)S(1)} %get-tuple-element.38.m_lo, f32[256,512]{1,0:T(8,128)S(1)} %collective-permute-done.11.before, f32[256,512]{1,0:T(8,128)S(1)} %collective-permute-done.12.after, ...), custom_call_target="tpu_custom_call", output_to_operand_aliasing={{}: (4, {})} | custom-call | flops 1024 | bytes 1024 | tf_op jit(solution)/shard_map/arrived1/pallas_call | solution.py:363
  (4 shorter events, 0.0 us)
Async XLA Ops:
  0.6 0.7 copy-start.1
  1.3 0.7 copy-start.3
  4.2 13.4 %collective-permute-start.5 = (f32[2,64,512]{2,1,0:T(8,128)S(1)}, f32[2,64,512]{2,1,0:T(8,128)S(1)}, u32[]{:S(2)}, u32[]{:S(2)}) collective-permute-start(f32[2,64,512]{2,1,0:T(8,128)S(1)} %get-tuple-element.31.rest_0_), channel_id=1, source_target_pairs={{0,1},{1,3},{3,2},{2,0},{4,5},{5,7},{7,6},{6,4},{8,9},{9,11},{11,1... | collective-permute-start | bytes 786440 | tf_op jit(solution)/shard_map/ppermute | solution.py:28
  7.3 15.4 %collective-permute-start = (f32[2,64,512]{2,1,0:T(8,128)S(1)}, f32[2,64,512]{2,1,0:T(8,128)S(1)}, u32[]{:S(2)}, u32[]{:S(2)}) collective-permute-start(f32[2,64,512]{2,1,0:T(8,128)S(1)} %get-tuple-element.28.rest_1_), channel_id=1, source_target_pairs={{0,1},{1,3},{3,2},{2,0},{4,5},{5,7},{7,6},{6,4},{8,9},{9,11},{11,1... | collective-permute-start | bytes 786440 | tf_op jit(solution)/shard_map/ppermute | solution.py:28
  9.9 19.3 %copy-start = (f32[4,64,768]{2,1,0:T(8,128)S(1)}, f32[4,64,768]{2,1,0:T(8,128)}, u32[]{:S(2)}) copy-start(f32[4,64,768]{2,1,0:T(8,128)} %over) | copy-start | bytes 2359300
  9.9 10.8 %collective-permute-start.1 = (s32[4,16]{1,0:T(4,128)S(1)}, s32[4,16]{1,0:T(4,128)S(1)}, u32[]{:S(2)}, u32[]{:S(2)}) collective-permute-start(s32[4,16]{1,0:T(4,128)S(1)} %get-tuple-element.29.dens_table), channel_id=1, source_target_pairs={{0,1},{1,3},{3,2},{2,0},{4,5},{5,7},{7,6},{6,4},{8,9},{9,11},{11,1... | collective-permute-start | bytes 776 | tf_op jit(solution)/shard_map/ppermute | solution.py:28
  10.3 12.3 %collective-permute-start.2 = (s32[4,16]{1,0:T(4,128)S(1)}, s32[4,16]{1,0:T(4,128)S(1)}, u32[]{:S(2)}, u32[]{:S(2)}) collective-permute-start(s32[4,16]{1,0:T(4,128)S(1)} %get-tuple-element.29.dens_table), channel_id=1, source_target_pairs={{0,3},{1,2},{3,0},{2,1},{4,7},{5,6},{7,4},{6,5},{8,11},{9,10},{11,... | collective-permute-start | bytes 776 | tf_op jit(solution)/shard_map/ppermute | solution.py:28
  11.7 11.0 %collective-permute-start.3 = (s32[4,16]{1,0:T(4,128)S(1)}, s32[4,16]{1,0:T(4,128)S(1)}, u32[]{:S(2)}, u32[]{:S(2)}) collective-permute-start(s32[4,16]{1,0:T(4,128)S(1)} %get-tuple-element.29.dens_table), channel_id=1, source_target_pairs={{0,2},{1,0},{3,1},{2,3},{4,6},{5,4},{7,5},{6,7},{8,10},{9,8},{11,9... | collective-permute-start | bytes 776 | tf_op jit(solution)/shard_map/ppermute | solution.py:28
  12.8 0.7 copy-start.2
  13.5 0.7 copy-start.4
  17.6 8.4 %collective-permute-start.8 = (f32[2,64,512]{2,1,0:T(8,128)S(1)}, f32[2,64,512]{2,1,0:T(8,128)S(1)}, u32[]{:S(2)}, u32[]{:S(2)}) collective-permute-start(f32[2,64,512]{2,1,0:T(8,128)S(1)} %collective-permute-done.5.rest_0_), channel_id=1, source_target_pairs={{0,1},{1,3},{3,2},{2,0},{4,5},{5,7},{7,6},{6,4},{8,9},{9,11},{11,1... | collective-permute-start | bytes 786440 | tf_op jit(solution)/shard_map/ppermute | solution.py:28
  20.7 8.5 %collective-permute-start.6 = (f32[4,64,256]{2,1,0:T(8,128)S(1)}, f32[4,64,256]{2,1,0:T(8,128)S(1)}, u32[]{:S(2)}, u32[]{:S(2)}) collective-permute-start(f32[4,64,256]{2,1,0:T(8,128)S(1)} %get-tuple-element.55), channel_id=1, source_target_pairs={{0,4},{4,8},{8,12},{12,0},{1,5},{5,9},{9,13},{13,1},{2,6},{6,10},{... | collective-permute-start | bytes 786440 | tf_op jit(solution)/shard_map/ppermute | solution.py:19
  22.6 6.5 %collective-permute-start.7 = (f32[4,64,256]{2,1,0:T(8,128)S(1)}, f32[4,64,256]{2,1,0:T(8,128)S(1)}, u32[]{:S(2)}, u32[]{:S(2)}) collective-permute-start(f32[4,64,256]{2,1,0:T(8,128)S(1)} %get-tuple-element.54), channel_id=1, source_target_pairs={{0,12},{4,0},{8,4},{12,8},{1,13},{5,1},{9,5},{13,9},{2,14},{6,2},{... | collective-permute-start | bytes 786440 | tf_op jit(solution)/shard_map/ppermute | solution.py:19
  22.6 10.1 %collective-permute-start.4 = (f32[2,64,512]{2,1,0:T(8,128)S(1)}, f32[2,64,512]{2,1,0:T(8,128)S(1)}, u32[]{:S(2)}, u32[]{:S(2)}) collective-permute-start(f32[2,64,512]{2,1,0:T(8,128)S(1)} %collective-permute-done.rest_1_), channel_id=1, source_target_pairs={{0,1},{1,3},{3,2},{2,0},{4,5},{5,7},{7,6},{6,4},{8,9},{9,11},{11,1... | collective-permute-start | bytes 786440 | tf_op jit(solution)/shard_map/ppermute | solution.py:28
  26.0 12.3 %collective-permute-start.9 = (f32[2,64,512]{2,1,0:T(8,128)S(1)}, f32[2,64,512]{2,1,0:T(8,128)S(1)}, u32[]{:S(2)}, u32[]{:S(2)}) collective-permute-start(f32[2,64,512]{2,1,0:T(8,128)S(1)} %collective-permute-done.8.rest_0_), channel_id=1, source_target_pairs={{0,1},{1,3},{3,2},{2,0},{4,5},{5,7},{7,6},{6,4},{8,9},{9,11},{11,1... | collective-permute-start | bytes 786440 | tf_op jit(solution)/shard_map/ppermute | solution.py:28
  32.7 10.8 %collective-permute-start.10 = (f32[2,64,512]{2,1,0:T(8,128)S(1)}, f32[2,64,512]{2,1,0:T(8,128)S(1)}, u32[]{:S(2)}, u32[]{:S(2)}) collective-permute-start(f32[2,64,512]{2,1,0:T(8,128)S(1)} %collective-permute-done.4.rest_1_), channel_id=1, source_target_pairs={{0,1},{1,3},{3,2},{2,0},{4,5},{5,7},{7,6},{6,4},{8,9},{9,11},{11,1... | collective-permute-start | bytes 786440 | tf_op jit(solution)/shard_map/ppermute | solution.py:28
  44.6 12.4 %collective-permute-start.13 = (f32[256,512]{1,0:T(8,128)S(1)}, f32[256,512]{1,0:T(8,128)S(1)}, u32[]{:S(2)}, u32[]{:S(2)}) collective-permute-start(f32[256,512]{1,0:T(8,128)S(1)} %last0.1.rest_0_), channel_id=1, source_target_pairs={{0,4},{4,8},{8,12},{12,0},{1,5},{5,9},{9,13},{13,1},{2,6},{6,10},{... | collective-permute-start | bytes 1572872 | tf_op jit(solution)/shard_map/ppermute | solution.py:19
  44.7 14.0 %collective-permute-start.14 = (f32[256,512]{1,0:T(8,128)S(1)}, f32[256,512]{1,0:T(8,128)S(1)}, u32[]{:S(2)}, u32[]{:S(2)}) collective-permute-start(f32[256,512]{1,0:T(8,128)S(1)} %last0.1.rest_0_), channel_id=1, source_target_pairs={{0,12},{4,0},{8,4},{12,8},{1,13},{5,1},{9,5},{13,9},{2,14},{6,2},{... | collective-permute-start | bytes 1572872 | tf_op jit(solution)/shard_map/ppermute | solution.py:19
  47.5 20.8 %collective-permute-start.11 = (f32[256,512]{1,0:T(8,128)S(1)}, f32[256,512]{1,0:T(8,128)S(1)}, u32[]{:S(2)}, u32[]{:S(2)}) collective-permute-start(f32[256,512]{1,0:T(8,128)S(1)} %last1.1.rest_1_), channel_id=1, source_target_pairs={{0,4},{4,8},{8,12},{12,0},{1,5},{5,9},{9,13},{13,1},{2,6},{6,10},{... | collective-permute-start | bytes 1572872 | tf_op jit(solution)/shard_map/ppermute | solution.py:19
  47.6 21.6 %collective-permute-start.12 = (f32[256,512]{1,0:T(8,128)S(1)}, f32[256,512]{1,0:T(8,128)S(1)}, u32[]{:S(2)}, u32[]{:S(2)}) collective-permute-start(f32[256,512]{1,0:T(8,128)S(1)} %last1.1.rest_1_), channel_id=1, source_target_pairs={{0,12},{4,0},{8,4},{12,8},{1,13},{5,1},{9,5},{13,9},{2,14},{6,2},{... | collective-permute-start | bytes 1572872 | tf_op jit(solution)/shard_map/ppermute | solution.py:19

commit v4 on v3

v4 whole, which is shorter than its diff:
```python
import functools

import jax
import jax.numpy as jnp
from jax import lax
from jax.experimental import pallas as pl
from jax.experimental.pallas import tpu as pltpu
from jax.sharding import PartitionSpec as P

LANES = 128
F32 = jnp.float32
BF16 = jnp.bfloat16
VMEM = pltpu.VMEM
SMEM = pltpu.SMEM


AXES = ("parts", "line", "cross")


def permute(x, target):
    parts, line, cross = (lax.axis_size(axis) for axis in AXES)
    flat = lambda p, g, c: (p % parts * line + g % line) * cross + c
    places = [(p, g, c) for p in range(parts) for g in range(line) for c in range(cross)]
    return lax.ppermute(x, AXES, [(flat(*place), flat(*target(*place))) for place in places])


def rotate(x, by):
    return permute(x, lambda p, g, c: (p, g + by, c))


def ring_order(count):
    return list(range(0, count, 2))[:1] + list(range(1, count, 2)) + list(range(0, count, 2))[:0:-1]


def pass_on(x, by, parity=None):
    order = ring_order(lax.axis_size("cross"))
    after = {d: order[(i + by) % len(order)] for i, d in enumerate(order)}
    return permute(
        x,
        lambda p, g, c: (p, g, after[c]) if parity in (None, g % 2) else (p + 1, g, c),
    )


def parity_here():
    return lax.rem(lax.axis_index("line"), 2)


def shard_of(step):
    order = ring_order(lax.axis_size("cross"))
    me = lax.axis_index("cross")
    owner = jnp.int32(0)
    for i, d in enumerate(order):
        owner = jnp.where(me == d, order[i - step], owner)
    return owner


def fill_table(table, columns, counts):
    rows, width = table.shape
    for r in range(rows):
        for c in range(width):
            table[r, c] = 0
        for slot in range(columns.shape[1]):

            @pl.when(slot < counts[r])
            def _(r=r, slot=slot):
                table[r, columns[r, slot]] = slot + 1


def table_kernel(columns, counts, table):
    fill_table(table, columns, counts)


def split(v):
    hi = v.astype(BF16)
    return hi, (v - hi.astype(F32)).astype(BF16)


def low_lanes(rows):
    return lax.broadcasted_iota(jnp.int32, (rows, LANES), 1) < LANES // 2


def block_at(row_ref, code, upper):
    slot = jnp.maximum(code - 1, 0)
    v = row_ref[:, pl.ds(pl.multiple_of((slot >> 1) * LANES, LANES), LANES)]
    v = jnp.where((slot & 1) != upper, pltpu.roll(v, LANES // 2, 1), v)
    return jnp.where(code > 0, v, jnp.zeros_like(v))


def pair_at(row_ref, table, r, pair):
    v0 = block_at(row_ref, table[r, 2 * pair], 0)
    v1 = block_at(row_ref, table[r, 2 * pair + 1], 1)
    return jnp.where(low_lanes(v0.shape[0]), v0, v1)


def densify_half(chunk, table, half, b, first=0):
    tile = chunk.shape[1]
    for r in range(2):
        for pair in range(b.shape[1] // LANES):
            hi, lo = split(pair_at(chunk.at[r], table, 2 * half + r, first + pair))
            lanes = slice(pair * LANES, (pair + 1) * LANES)
            b[r * tile : (r + 1) * tile, lanes] = hi
            b[(2 + r) * tile : (3 + r) * tile, lanes] = lo


def times_half(a, b, lanes):
    depth = b.shape[0]
    return jnp.dot(a[:, :depth], b[:, lanes], preferred_element_type=F32) + jnp.dot(
        a[:, depth:], b[: depth // 2, lanes], preferred_element_type=F32
    )


def lane_blocks(width, step=256):
    return [slice(i, i + step) for i in range(0, width, step)]


def first_kernel(
    ham_cols, ham_count, dens_table, ham, dens, a, acc, ham_table, ham_here, b, sems
):
    rows, tile, _ = ham.shape
    copies = [
        pltpu.make_async_copy(ham.at[q], ham_here.at[q], sems.at[q]) for q in range(rows)
    ]
    for copy in copies:
        copy.start()
    fill_table(ham_table, ham_cols, ham_count)
    for q in range(rows):
        copies[q].wait()
        for pair in range(ham_table.shape[1] // 2):
            hi, lo = split(pair_at(ham_here.at[q], ham_table, q, pair))
            a[pair, q * tile : (q + 1) * tile, 0:LANES] = hi
            a[pair, q * tile : (q + 1) * tile, LANES : 2 * LANES] = hi
            a[pair, q * tile : (q + 1) * tile, 2 * LANES : 3 * LANES] = lo
    for h in range(rows // 2):
        densify_half(dens.at[pl.ds(2 * h, 2)], dens_table, h, b)
        pair = shard_of(0) * (rows // 2) + h
        for lanes in lane_blocks(acc.shape[1]):
            part = times_half(a[pair], b, lanes)
            acc[:, lanes] = part if h == 0 else acc[:, lanes] + part


def add_shard(step, first, dens_table, a, acc_in, shard, out, b):
    per_shard = dens_table.shape[0] // 2
    for half in range(per_shard):
        densify_half(shard.at[pl.ds(2 * half, 2)], dens_table, half, b, first // LANES)
        pair = shard_of(step) * per_shard + half
        for lanes in lane_blocks(out.shape[1]):
            if half == 0:
                before = acc_in[:, first + lanes.start : first + lanes.stop]
            else:
                before = out[:, lanes]
            out[:, lanes] = before + times_half(a[pair], b, lanes)


def add_kernel(step, dens_table, a, acc_in, even, odd, acc, b):
    for parity, shard in enumerate((even, odd)):

        @pl.when(parity_here() == parity)
        def _(shard=shard):
            add_shard(step, 0, dens_table, a, acc_in, shard, acc, b)


def even_kernel(step, dens_table, a, acc_in, shard, out, b):
    @pl.when(parity_here() == 0)
    def _():
        add_shard(step, 0, dens_table, a, acc_in, shard, out, b)


def odd_kernel(step, dens_table, a, acc_in, shard, even, *rest):
    outs, b = rest[:-1], rest[-1]
    piece = outs[0].shape[1]
    for i, out in enumerate(outs):

        @pl.when(parity_here() == 1)
        def _(i=i, out=out):
            add_shard(step, i * piece, dens_table, a, acc_in, shard, out, b)

        @pl.when(parity_here() == 0)
        def _(i=i, out=out):
            out[...] = even[:, i * piece : (i + 1) * piece]


def margin_kernel(over, before, after, hi_out, lo_out):
    rows, tile, _ = over.shape
    wide = rows * tile
    for s, (ref, start) in enumerate(((before, 0), (over, wide), (after, 0))):
        for j in range(rows):
            for pair in range(rows // 2):
                at = start + j * tile
                lanes = slice(at // LANES * LANES, at // LANES * LANES + LANES)
                v0, v1 = ref[2 * pair, :, lanes], ref[2 * pair + 1, :, lanes]
                if at % LANES == 0:
                    v1 = pltpu.roll(v1, LANES // 2, 1)
                else:
                    v0 = pltpu.roll(v0, LANES // 2, 1)
                hi, lo = split(jnp.where(low_lanes(tile), v0, v1))
                to = slice(pair * LANES, (pair + 1) * LANES)
                hi_out[s, j * tile : (j + 1) * tile, to] = hi
                lo_out[s, j * tile : (j + 1) * tile, to] = lo


def weighted(m_hi, m_lo, s, p, store):
    for lanes in lane_blocks(p.shape[1]):
        hi, lo = split(p[:, lanes])
        store(
            lanes,
            jnp.dot(m_hi[s], hi, preferred_element_type=F32)
            + jnp.dot(m_hi[s], lo, preferred_element_type=F32)
            + jnp.dot(m_lo[s], hi, preferred_element_type=F32),
        )


def own_kernel(m_hi, m_lo, *rest):
    parts, (product, window, term, sems) = rest[:-4], rest[-4:]
    rows, tile, width = product.shape
    step = width // len(parts)
    copies = []
    for i, part in enumerate(parts):
        for q in range(rows):
            copies.append(
                pltpu.make_async_copy(
                    part.at[pl.ds(q * tile, tile)],
                    product.at[q, :, pl.ds(i * step, step)],
                    sems.at[i, q],
                )
            )
            copies[-1].start()
    for i, part in enumerate(parts):

        def store(lanes, v, at=i * step):
            term[:, at + lanes.start : at + lanes.stop] = v

        weighted(m_hi, m_lo, 1, part, store)
    for q in range(rows):
        copies.append(
            pltpu.make_async_copy(
                term.at[pl.ds(q * tile, tile)],
                window.at[q, :, pl.ds(width, width)],
                sems.at[len(parts), q],
            )
        )
        copies[-1].start()
    for copy in copies:
        copy.wait()


def arrived_kernel(s, at, parity, m_hi, m_lo, p, window_in, window, term, sems):
    rows, tile, triple = window.shape
    start = s * triple // 3 + at

    def arrived():
        copies = []

        def store(lanes, v):
            term[:, lanes] = v
            for q in range(rows):
                to = pl.ds(start + lanes.start, lanes.stop - lanes.start)
                copies.append(
                    pltpu.make_async_copy(
                        term.at[pl.ds(q * tile, tile), lanes],
                        window.at[q, :, to],
                        sems.at[len(copies)],
                    )
                )
                copies[-1].start()

        weighted(m_hi, m_lo, s, p, store)
        for copy in copies:
            copy.wait()

    if parity is None:
        arrived()
    else:
        pl.when(parity_here() == parity)(arrived)


def call(kernel, name, out_shape, in_spaces, out_spaces, scratch, flops, moved, aliases=None):
    return pl.pallas_call(
        kernel,
        name=name,
        out_shape=out_shape,
        in_specs=[pl.BlockSpec(memory_space=s) for s in in_spaces],
        out_specs=jax.tree.map(lambda s: pl.BlockSpec(memory_space=s), out_spaces),
        scratch_shapes=scratch,
        input_output_aliases=aliases or {},
        cost_estimate=pl.CostEstimate(flops=flops, bytes_accessed=moved, transcendentals=0),
        compiler_params=pltpu.CompilerParams(vmem_limit_bytes=24 << 20),
    )


def shards(ham_tiles, ham_cols, ham_count, dens_tiles, dens_cols, dens_count, over_tiles):
    count = lax.axis_size("cross")
    rows, tile, _ = ham_tiles.shape
    blocks = rows * count
    width = blocks * tile
    tall = rows * tile
    per_shard = rows // 2
    sds = jax.ShapeDtypeStruct

    even = pass_on(dens_tiles, 1, 0)
    table = call(
        table_kernel,
        "table",
        sds((rows, blocks), jnp.int32),
        (SMEM, SMEM),
        SMEM,
        [],
        1024,
        1024,
    )(dens_cols, dens_count)
    tables = [pass_on(table, step) for step in range(1, count)]
    dens_late, table = lax.optimization_barrier((dens_tiles, table))
    odd = pass_on(dens_late, 1, 1)
    b_scratch = [VMEM((4 * tile, width), BF16)]
    for step in range(1, count):
        now = (even, odd)
        if step == 1:
            ham_tiles, even = lax.optimization_barrier((ham_tiles, even))
            a, acc = call(
                first_kernel,
                "first",
                (sds((blocks // 2, tall, 3 * LANES), BF16), sds((tall, width), F32)),
                (SMEM, SMEM, SMEM, pl.ANY, VMEM),
                (VMEM, VMEM),
                [pltpu.SMEM((rows, blocks), jnp.int32), VMEM(ham_tiles.shape, F32)]
                + b_scratch
                + [pltpu.SemaphoreType.DMA((rows,))],
                1 << 20,
                1 << 20,
            )(
                ham_cols,
                ham_count,
                table,
                pltpu.with_memory_space_constraint(ham_tiles, pltpu.HBM),
                dens_tiles,
            )
            odd, acc, over_tiles, *tables = lax.optimization_barrier(
                (odd, acc, over_tiles, *tables)
            )
            over_before = rotate(over_tiles[:, :, 2 * tall :], 1)
            over_after = rotate(over_tiles[:, :, :tall], -1)
            m_hi, m_lo = call(
                margin_kernel,
                "margin",
                (sds((3, tall, tall), BF16),) * 2,
                (VMEM,) * 3,
                (VMEM, VMEM),
                [],
                1 << 20,
                1 << 20,
            )(over_tiles, over_before, over_after)
        else:
            even, acc = lax.optimization_barrier((even, acc))
        if step == 2:
            odd, m_hi, m_lo = lax.optimization_barrier((odd, m_hi, m_lo))
        now = (even, odd)
        if step == count - 1:
            break
        even, odd = pass_on(even, 1, 0), pass_on(odd, 1, 1)
        acc = call(
            functools.partial(add_kernel, step),
            "add%d" % step,
            sds((tall, width), F32),
            (SMEM,) + (VMEM,) * 4,
            VMEM,
            b_scratch,
            1 << 20,
            1 << 20,
        )(tables[step - 1], a, acc, *now)

    sides = 2
    piece = width // sides
    even_part = call(
        functools.partial(even_kernel, count - 1),
        "even",
        sds((tall, width), F32),
        (SMEM, VMEM, VMEM, VMEM),
        VMEM,
        b_scratch,
        1024,
        1024,
    )(tables[-1], a, acc, even)
    parts = call(
        functools.partial(odd_kernel, count - 1),
        "odd",
        [sds((tall, piece), F32)] * sides,
        (SMEM, VMEM, VMEM, VMEM, VMEM),
        [VMEM] * sides,
        [VMEM((4 * tile, piece), BF16)],
        1024,
        1024,
    )(tables[-1], a, acc, odd, even_part)
    mate = lambda p, g, c: (p, g + 1 - g % 2 * 2, c)
    after = permute(even_part, lambda p, g, c: mate(p, g, c) if g % 2 else (p, g - 1, c))
    mates = [permute(part, mate) for part in parts]
    befores = [rotate(part, 1) for part in parts]
    product, window = call(
        own_kernel,
        "own",
        (sds((rows, tile, width), F32), sds((rows, tile, 3 * width), F32)),
        (VMEM,) * (2 + sides),
        (pl.ANY, pl.ANY),
        [VMEM((tall, width), F32), pltpu.SemaphoreType.DMA((sides + 1, rows))],
        1024,
        1024,
    )(m_hi, m_lo, *parts)
    steps = [(2, 0, 1, after)]
    steps += [(2, i * piece, 0, p) for i, p in enumerate(mates)]
    steps += [(0, i * piece, None, p) for i, p in enumerate(befores)]
    for i, (side, at, parity, p) in enumerate(steps):
        window = call(
            functools.partial(arrived_kernel, side, at, parity),
            "arrived%d" % i,
            sds((rows, tile, 3 * width), F32),
            (VMEM,) * 3 + (pl.ANY,),
            pl.ANY,
            [VMEM(p.shape, F32), pltpu.SemaphoreType.DMA((rows * p.shape[1] // 256,))],
            1024,
            1024,
            {3: 0},
        )(m_hi, m_lo, p, window)
    return (product, window)


def solution(mesh):
    whole = P(AXES)
    return jax.shard_map(
        shards,
        mesh=mesh,
        in_specs=(whole,) * 7,
        out_specs=(whole, whole),
        check_vma=False,
    )
```

time: 71.2 us -> 74.3 us (1.044)
  starting transfers between devices: 19.2 us -> 25.2 us
  waiting for transfers between devices: 29.6 us -> 26.9 us
    ppermute x15 -> x16, starting transfers between devices: 19.2 us -> 25.2 us  [permute(): lax.ppermute(x, AXES, [(flat(*place), flat(*target(*place))) for place in...]
    ppermute x15 -> x16, waiting for transfers between devices: 29.6 us -> 26.9 us  [permute(): lax.ppermute(x, AXES, [(flat(*place), flat(*target(*place))) for place in...]
    unnamed x10 -> x12, local copies, waits for them, and re-layouts: 2.67 us -> 3.72 us
    slice x1, local copies, waits for them, and re-layouts: 1.07 us -> 0.04 us  [shards(): over_after = rotate(over_tiles[:, :, :tall], -1)]
    pallas_call x9 -> x11, Pallas kernels: 13.6 us -> 13.7 us  [the longest x5 5.15 us: shards(): call(functools.partial(arrived_kernel, side, at, parity), 'arrived%d' % i...]
  transfers between devices with their start and end apart: 15 -> 16, of which waited for: 10 -> 6; matrix products, arithmetic and copies ran while one was open for 2% -> 0% of each run, Pallas kernels for 18% -> 22%
where the time goes in v4:
time: 74.3 us; the launch traced here: 74.1 us
  waiting for transfers between devices  26.9 us (36%)
  starting transfers between devices  25.2 us (34%)
  Pallas kernels  17.5 us (24%)
  local copies, waits for them, and re-layouts  3.75 us (5%)
  between operations  0.84 us (1%)
    ppermute x16, waiting for transfers between devices, permute(): lax.ppermute(x, AXES, [(flat(*place), flat(*target(*place))) for place in...  26.9 us
    ppermute x16, starting transfers between devices, permute(): lax.ppermute(x, AXES, [(flat(*place), flat(*target(*place))) for place in...  25.2 us
    pallas_call x5, Pallas kernels, shards(): call(functools.partial(arrived_kernel, side, at, parity), 'arrived%d' % i...  5.15 us
    unnamed x12, local copies, waits for them, and re-layouts  3.72 us
    pallas_call x1, Pallas kernels, shards(): call(first_kernel, 'first', (sds((blocks // 2, tall, 3 * LANES), BF16), s...  3.47 us
    pallas_call x2, Pallas kernels, shards(): call(functools.partial(add_kernel, step), 'add%d' % step, sds((tall, widt...  3.3 us
    pallas_call x1, Pallas kernels, shards(): call(own_kernel, 'own', (sds((rows, tile, width), F32), sds((rows, tile,...  1.67 us
    pallas_call x1, Pallas kernels, shards(): call(functools.partial(even_kernel, count - 1), 'even', sds((tall, width)...  1.65 us
  transfers between devices with their start and end apart: 16, of which 6 were waited for; matrix products, arithmetic and copies ran while one was open for 0% of the time, Pallas kernels for 22%

profile of v4, /device:TPU:0, one launch (start us, length us, event | category | flops | bytes accessed | tf_op | source)
XLA Modules:
  0.0 74.1 jit_solution(12271064895221798981)
XLA Ops:
  0.6 3.1 %collective-permute-start.1 = (f32[4,64,512]{2,1,0:T(8,128)}, f32[4,64,512]{2,1,0:T(8,128)S(1)}, u32[]{:S(2)}, u32[]{:S(2)}) collective-permute-start(f32[4,64,512]{2,1,0:T(8,128)} %dens.1), channel_id=1, source_target_pairs={{0,1},{1,3},{2,0},{3,2},{4,20},{5,21},{6,22},{7,23},{8,9},{9,11},{... | collective-permute-start | bytes 1572872 | tf_op jit(solution)/shard_map/ppermute | solution.py:24
  3.7 0.7 copy-done.3
  4.4 0.7 copy-done.5
  5.1 1.3 %table.1.dens_table = s32[4,16]{1,0:T(4,128)S(1)} custom-call(s32[4,8]{1,0:T(4,128)S(1)} %copy-done.3, s32[4]{0:T(128)S(1)} %copy-done.5), custom_call_target="tpu_custom_call" | custom-call | flops 1024 | bytes 1024 | tf_op jit(solution)/shard_map/table/pallas_call | solution.py:300
  6.3 1.6 %collective-permute-start = (f32[4,64,512]{2,1,0:T(8,128)}, f32[4,64,512]{2,1,0:T(8,128)S(1)}, u32[]{:S(2)}, u32[]{:S(2)}) collective-permute-start(f32[4,64,512]{2,1,0:T(8,128)} %dens.1), channel_id=1, source_target_pairs={{0,16},{1,17},{2,18},{3,19},{4,5},{5,7},{6,4},{7,6},{8,24},{9,25},... | collective-permute-start | bytes 1572872 | tf_op jit(solution)/shard_map/ppermute | solution.py:24
  7.9 6.6 %collective-permute-done.1.even = f32[4,64,512]{2,1,0:T(8,128)S(1)} collective-permute-done((f32[4,64,512]{2,1,0:T(8,128)}, f32[4,64,512]{2,1,0:T(8,128)S(1)}, u32[]{:S(2)}, u32[]{:S(2)}) %collective-permute-start.1) | collective-permute-done | bytes 524320 | tf_op jit(solution)/shard_map/ppermute | solution.py:24
  14.6 1.5 %collective-permute-start.8 = (f32[4,64,512]{2,1,0:T(8,128)S(1)}, f32[4,64,512]{2,1,0:T(8,128)S(1)}, u32[]{:S(2)}, u32[]{:S(2)}) collective-permute-start(f32[4,64,512]{2,1,0:T(8,128)S(1)} %collective-permute-done.1.even), channel_id=1, source_target_pairs={{0,1},{1,3},{2,0},{3,2},{4,20},{5,21},{6,22},{7,23},{8,9},{9,11},{... | collective-permute-start | bytes 1572872 | tf_op jit(solution)/shard_map/ppermute | solution.py:24
  16.1 3.3 %collective-permute-start.2 = (s32[4,16]{1,0:T(4,128)S(1)}, s32[4,16]{1,0:T(4,128)S(1)}, u32[]{:S(2)}, u32[]{:S(2)}) collective-permute-start(s32[4,16]{1,0:T(4,128)S(1)} %table.1.dens_table), channel_id=1, source_target_pairs={{0,1},{1,3},{2,0},{3,2},{4,5},{5,7},{6,4},{7,6},{8,9},{9,11},{10,8... | collective-permute-start | bytes 776 | tf_op jit(solution)/shard_map/ppermute | solution.py:24
  19.4 0.0 collective-permute-start.3
  19.4 1.5 %collective-permute-start.4 = (s32[4,16]{1,0:T(4,128)S(1)}, s32[4,16]{1,0:T(4,128)S(1)}, u32[]{:S(2)}, u32[]{:S(2)}) collective-permute-start(s32[4,16]{1,0:T(4,128)S(1)} %table.1.dens_table), channel_id=1, source_target_pairs={{0,2},{1,0},{2,3},{3,1},{4,6},{5,4},{6,7},{7,5},{8,10},{9,8},{10,1... | collective-permute-start | bytes 776 | tf_op jit(solution)/shard_map/ppermute | solution.py:24
  20.9 1.0 %copy-done.1 = f32[4,64,512]{2,1,0:T(8,128)S(1)} copy-done((f32[4,64,512]{2,1,0:T(8,128)S(1)}, f32[4,64,512]{2,1,0:T(8,128)}, u32[]{:S(2)}) %copy-start.1) | copy-done | bytes 524312
  21.9 0.7 copy-done.2
  22.6 0.7 copy-done.4
  23.2 3.5 %first.1 = (bf16[8,256,384]{2,1,0:T(8,128)(2,1)S(1)}, f32[256,1024]{1,0:T(8,128)S(1)}) custom-call(s32[4,12]{1,0:T(4,128)S(1)} %copy-done.2, s32[4]{0:T(128)S(1)} %copy-done.4, s32[4,16]{1,0:T(4,128)S(1)} %table.1.dens_table, f32[4,64,768]{2,1,0:T(8,128)} %ham, f32[4,64,512]{2,1,0:T(8,128)S(1)} %copy-done.1), custom_call_target="tpu_custom_call" | custom-call | flops 1048576 | bytes 1048576 | tf_op jit(solution)/shard_map/first/pallas_call | solution.py:318
  26.7 0.0 collective-permute-done.2.dens_table
  26.7 0.0 collective-permute-done.3.dens_table
  26.7 0.0 collective-permute-done.4.dens_table
  26.8 0.0 collective-permute-done.odd
  26.8 3.7 %collective-permute-start.5 = (f32[4,64,512]{2,1,0:T(8,128)S(1)}, f32[4,64,512]{2,1,0:T(8,128)S(1)}, u32[]{:S(2)}, u32[]{:S(2)}) collective-permute-start(f32[4,64,512]{2,1,0:T(8,128)S(1)} %collective-permute-done.odd), channel_id=1, source_target_pairs={{0,16},{1,17},{2,18},{3,19},{4,5},{5,7},{6,4},{7,6},{8,24},{9,25},... | collective-permute-start | bytes 1572872 | tf_op jit(solution)/shard_map/ppermute | solution.py:24
  30.5 1.6 %add1.1.acc_in = f32[256,1024]{1,0:T(8,128)S(1)} custom-call(s32[4,16]{1,0:T(4,128)S(1)} %collective-permute-done.2.dens_table, bf16[8,256,384]{2,1,0:T(8,128)(2,1)S(1)} %get-tuple-element.38.a, f32[256,1024]{1,0:T(8,128)S(1)} %get-tuple-element.41.acc_in, f32[4,64,512]{2,1,0:T(8,128)S(1)} %collective-permute-done.1.even, ...), custom_call_target="tpu_custom_call" | custom-call | flops 1048576 | bytes 1048576 | tf_op jit(solution)/shard_map/add1/pallas_call | solution.py:359
  32.1 0.0 collective-permute-done.8.even
  32.1 0.8 %collective-permute-start.9 = (f32[4,64,512]{2,1,0:T(8,128)S(1)}, f32[4,64,512]{2,1,0:T(8,128)S(1)}, u32[]{:S(2)}, u32[]{:S(2)}) collective-permute-start(f32[4,64,512]{2,1,0:T(8,128)S(1)} %collective-permute-done.8.even), channel_id=1, source_target_pairs={{0,1},{1,3},{2,0},{3,2},{4,20},{5,21},{6,22},{7,23},{8,9},{9,11},{... | collective-permute-start | bytes 1572872 | tf_op jit(solution)/shard_map/ppermute | solution.py:24
  32.9 0.1 collective-permute-start.6
  33.0 1.7 %collective-permute-start.7 = (f32[4,64,256]{2,1,0:T(8,128)S(1)}, f32[4,64,256]{2,1,0:T(8,128)S(1)}, u32[]{:S(2)}, u32[]{:S(2)}) collective-permute-start(f32[4,64,256]{2,1,0:T(8,128)S(1)} %get-tuple-element.52), channel_id=1, source_target_pairs={{0,12},{1,13},{2,14},{3,15},{4,0},{5,1},{6,2},{7,3},{8,4},{9,5},{1... | collective-permute-start | bytes 786440 | tf_op jit(solution)/shard_map/ppermute | solution.py:24
  34.7 5.0 %collective-permute-done.6.before = f32[4,64,256]{2,1,0:T(8,128)S(1)} collective-permute-done((f32[4,64,256]{2,1,0:T(8,128)S(1)}, f32[4,64,256]{2,1,0:T(8,128)S(1)}, u32[]{:S(2)}, u32[]{:S(2)}) %collective-permute-start.6) | collective-permute-done | bytes 262176 | tf_op jit(solution)/shard_map/ppermute | solution.py:24
  39.8 0.9 %collective-permute-done.7.after = f32[4,64,256]{2,1,0:T(8,128)S(1)} collective-permute-done((f32[4,64,256]{2,1,0:T(8,128)S(1)}, f32[4,64,256]{2,1,0:T(8,128)S(1)}, u32[]{:S(2)}, u32[]{:S(2)}) %collective-permute-start.7) | collective-permute-done | bytes 262176 | tf_op jit(solution)/shard_map/ppermute | solution.py:24
  40.6 0.3 margin.1
  40.9 0.0 collective-permute-done.5.odd
  40.9 0.1 collective-permute-start.10
  41.0 1.7 %add2.1.acc_in = f32[256,1024]{1,0:T(8,128)S(1)} custom-call(s32[4,16]{1,0:T(4,128)S(1)} %collective-permute-done.3.dens_table, bf16[8,256,384]{2,1,0:T(8,128)(2,1)S(1)} %get-tuple-element.38.a, f32[256,1024]{1,0:T(8,128)S(1)} %add1.1.acc_in, f32[4,64,512]{2,1,0:T(8,128)S(1)} %collective-permute-done.8.even, f32[4,64,512]{2,1,0:T(8,128)S(1)} %collective-permute-done.5.odd), custom_call_target="tpu_custom_call" | custom-call | flops 1048576 | bytes 1048576 | tf_op jit(solution)/shard_map/add2/pallas_call | solution.py:359
  42.7 1.7 %even.1 = f32[256,1024]{1,0:T(8,128)S(1)} custom-call(s32[4,16]{1,0:T(4,128)S(1)} %collective-permute-done.4.dens_table, bf16[8,256,384]{2,1,0:T(8,128)(2,1)S(1)} %get-tuple-element.38.a, f32[256,1024]{1,0:T(8,128)S(1)} %add2.1.acc_in, f32[4,64,512]{2,1,0:T(8,128)S(1)} %collective-permute-done.9.shard), custom_call_target="tpu_custom_call" | custom-call | flops 1024 | bytes 1024 | tf_op jit(solution)/shard_map/even/pallas_call | solution.py:372
  44.3 4.0 %collective-permute-start.15 = (f32[256,1024]{1,0:T(8,128)S(1)}, f32[256,1024]{1,0:T(8,128)S(1)}, u32[]{:S(2)}, u32[]{:S(2)}) collective-permute-start(f32[256,1024]{1,0:T(8,128)S(1)} %even.1), channel_id=1, source_target_pairs={{0,12},{1,13},{2,14},{3,15},{4,0},{5,1},{6,2},{7,3},{8,4},{9,5},{1... | collective-permute-start | bytes 3145736 | tf_op jit(solution)/shard_map/ppermute | solution.py:24
  48.3 1.9 %collective-permute-done.10.shard = f32[4,64,512]{2,1,0:T(8,128)S(1)} collective-permute-done((f32[4,64,512]{2,1,0:T(8,128)S(1)}, f32[4,64,512]{2,1,0:T(8,128)S(1)}, u32[]{:S(2)}, u32[]{:S(2)}) %collective-permute-start.10) | collective-permute-done | bytes 524320 | tf_op jit(solution)/shard_map/ppermute | solution.py:24
  50.1 0.7 odd.1
  50.8 2.2 %collective-permute-start.14 = (f32[256,512]{1,0:T(8,128)S(1)}, f32[256,512]{1,0:T(8,128)S(1)}, u32[]{:S(2)}, u32[]{:S(2)}) collective-permute-start(f32[256,512]{1,0:T(8,128)S(1)} %get-tuple-element.48.rest_0_), channel_id=1, source_target_pairs={{0,4},{1,5},{2,6},{3,7},{4,0},{5,1},{6,2},{7,3},{8,12},{9,13},{10,... | collective-permute-start | bytes 1572872 | tf_op jit(solution)/shard_map/ppermute | solution.py:24
  53.0 0.1 collective-permute-start.13
  53.1 0.4 collective-permute-start.12
  53.6 1.2 %collective-permute-start.11 = (f32[256,512]{1,0:T(8,128)S(1)}, f32[256,512]{1,0:T(8,128)S(1)}, u32[]{:S(2)}, u32[]{:S(2)}) collective-permute-start(f32[256,512]{1,0:T(8,128)S(1)} %get-tuple-element.49.rest_1_), channel_id=1, source_target_pairs={{0,4},{1,5},{2,6},{3,7},{4,8},{5,9},{6,10},{7,11},{8,12},{9,13},{1... | collective-permute-start | bytes 1572872 | tf_op jit(solution)/shard_map/ppermute | solution.py:24
  54.7 1.7 %own.1 = (f32[4,64,1024]{2,1,0:T(8,128)}, f32[4,64,3072]{2,1,0:T(8,128)}) custom-call(bf16[3,256,256]{2,1,0:T(8,128)(2,1)S(1)} %get-tuple-element.35.m_hi, bf16[3,256,256]{2,1,0:T(8,128)(2,1)S(1)} %get-tuple-element.36.m_lo, f32[256,512]{1,0:T(8,128)S(1)} %get-tuple-element.48.rest_0_, f32[256,512]{1,0:T(8,128)S(1)} %get-tuple-element.49.rest_1_), custom_call_target="tpu_custom_call" | custom-call | flops 1024 | bytes 1024 | tf_op jit(solution)/shard_map/own/pallas_call | solution.py:396
  56.4 9.6 %collective-permute-done.15.p = f32[256,1024]{1,0:T(8,128)S(1)} collective-permute-done((f32[256,1024]{1,0:T(8,128)S(1)}, f32[256,1024]{1,0:T(8,128)S(1)}, u32[]{:S(2)}, u32[]{:S(2)}) %collective-permute-start.15) | collective-permute-done | bytes 1048608 | tf_op jit(solution)/shard_map/ppermute | solution.py:24
  66.0 0.1 arrived0.1.window_in
  66.1 0.0 collective-permute-done.14.p
  66.2 1.3 %arrived1.1.window_in = f32[4,64,3072]{2,1,0:T(8,128)} custom-call(bf16[3,256,256]{2,1,0:T(8,128)(2,1)S(1)} %get-tuple-element.35.m_hi, bf16[3,256,256]{2,1,0:T(8,128)(2,1)S(1)} %get-tuple-element.36.m_lo, f32[256,512]{1,0:T(8,128)S(1)} %collective-permute-done.14.p, f32[4,64,3072]{2,1,0:T(8,128)} %arrived0.1.window_in), custom_call_target="tpu_custom_call", output_to_operand_aliasing={{}: (3, {})} | custom-call | flops 1024 | bytes 1024 | tf_op jit(solution)/shard_map/arrived1/pallas_call | solution.py:410
  67.4 0.0 collective-permute-done.13.p
  67.4 1.3 %arrived2.1.window_in = f32[4,64,3072]{2,1,0:T(8,128)} custom-call(bf16[3,256,256]{2,1,0:T(8,128)(2,1)S(1)} %get-tuple-element.35.m_hi, bf16[3,256,256]{2,1,0:T(8,128)(2,1)S(1)} %get-tuple-element.36.m_lo, f32[256,512]{1,0:T(8,128)S(1)} %collective-permute-done.13.p, f32[4,64,3072]{2,1,0:T(8,128)} %arrived1.1.window_in), custom_call_target="tpu_custom_call", output_to_operand_aliasing={{}: (3, {})} | custom-call | flops 1024 | bytes 1024 | tf_op jit(solution)/shard_map/arrived2/pallas_call | solution.py:410
  68.7 1.2 %arrived3.1.window_in = f32[4,64,3072]{2,1,0:T(8,128)} custom-call(bf16[3,256,256]{2,1,0:T(8,128)(2,1)S(1)} %get-tuple-element.35.m_hi, bf16[3,256,256]{2,1,0:T(8,128)(2,1)S(1)} %get-tuple-element.36.m_lo, f32[256,512]{1,0:T(8,128)S(1)} %collective-permute-done.12.p, f32[4,64,3072]{2,1,0:T(8,128)} %arrived2.1.window_in), custom_call_target="tpu_custom_call", output_to_operand_aliasing={{}: (3, {})} | custom-call | flops 1024 | bytes 1024 | tf_op jit(solution)/shard_map/arrived3/pallas_call | solution.py:410
  70.0 2.9 %collective-permute-done.11.p = f32[256,512]{1,0:T(8,128)S(1)} collective-permute-done((f32[256,512]{1,0:T(8,128)S(1)}, f32[256,512]{1,0:T(8,128)S(1)}, u32[]{:S(2)}, u32[]{:S(2)}) %collective-permute-start.11) | collective-permute-done | bytes 524320 | tf_op jit(solution)/shard_map/ppermute | solution.py:24
  72.8 1.2 %arrived4.1 = f32[4,64,3072]{2,1,0:T(8,128)} custom-call(bf16[3,256,256]{2,1,0:T(8,128)(2,1)S(1)} %get-tuple-element.35.m_hi, bf16[3,256,256]{2,1,0:T(8,128)(2,1)S(1)} %get-tuple-element.36.m_lo, f32[256,512]{1,0:T(8,128)S(1)} %collective-permute-done.11.p, f32[4,64,3072]{2,1,0:T(8,128)} %arrived3.1.window_in), custom_call_target="tpu_custom_call", output_to_operand_aliasing={{}: (3, {})} | custom-call | flops 1024 | bytes 1024 | tf_op jit(solution)/shard_map/arrived4/pallas_call | solution.py:410
  (10 shorter events, 0.1 us)
Async XLA Ops:
  0.6 32.3 %copy-start = (f32[4,64,768]{2,1,0:T(8,128)S(1)}, f32[4,64,768]{2,1,0:T(8,128)}, u32[]{:S(2)}) copy-start(f32[4,64,768]{2,1,0:T(8,128)} %over) | copy-start | bytes 2359300
  0.6 13.9 %collective-permute-start.1 = (f32[4,64,512]{2,1,0:T(8,128)}, f32[4,64,512]{2,1,0:T(8,128)S(1)}, u32[]{:S(2)}, u32[]{:S(2)}) collective-permute-start(f32[4,64,512]{2,1,0:T(8,128)} %dens.1), channel_id=1, source_target_pairs={{0,1},{1,3},{2,0},{3,2},{4,20},{5,21},{6,22},{7,23},{8,9},{9,11},{... | collective-permute-start | bytes 1572872 | tf_op jit(solution)/shard_map/ppermute | solution.py:24
  3.7 0.7 copy-start.3
  4.4 0.7 copy-start.5
  6.3 20.4 %collective-permute-start = (f32[4,64,512]{2,1,0:T(8,128)}, f32[4,64,512]{2,1,0:T(8,128)S(1)}, u32[]{:S(2)}, u32[]{:S(2)}) collective-permute-start(f32[4,64,512]{2,1,0:T(8,128)} %dens.1), channel_id=1, source_target_pairs={{0,16},{1,17},{2,18},{3,19},{4,5},{5,7},{6,4},{7,6},{8,24},{9,25},... | collective-permute-start | bytes 1572872 | tf_op jit(solution)/shard_map/ppermute | solution.py:24
  14.6 17.6 %collective-permute-start.8 = (f32[4,64,512]{2,1,0:T(8,128)S(1)}, f32[4,64,512]{2,1,0:T(8,128)S(1)}, u32[]{:S(2)}, u32[]{:S(2)}) collective-permute-start(f32[4,64,512]{2,1,0:T(8,128)S(1)} %collective-permute-done.1.even), channel_id=1, source_target_pairs={{0,1},{1,3},{2,0},{3,2},{4,20},{5,21},{6,22},{7,23},{8,9},{9,11},{... | collective-permute-start | bytes 1572872 | tf_op jit(solution)/shard_map/ppermute | solution.py:24
  16.1 10.6 %collective-permute-start.2 = (s32[4,16]{1,0:T(4,128)S(1)}, s32[4,16]{1,0:T(4,128)S(1)}, u32[]{:S(2)}, u32[]{:S(2)}) collective-permute-start(s32[4,16]{1,0:T(4,128)S(1)} %table.1.dens_table), channel_id=1, source_target_pairs={{0,1},{1,3},{2,0},{3,2},{4,5},{5,7},{6,4},{7,6},{8,9},{9,11},{10,8... | collective-permute-start | bytes 776 | tf_op jit(solution)/shard_map/ppermute | solution.py:24
  19.4 7.4 %collective-permute-start.3 = (s32[4,16]{1,0:T(4,128)S(1)}, s32[4,16]{1,0:T(4,128)S(1)}, u32[]{:S(2)}, u32[]{:S(2)}) collective-permute-start(s32[4,16]{1,0:T(4,128)S(1)} %table.1.dens_table), channel_id=1, source_target_pairs={{0,3},{1,2},{2,1},{3,0},{4,7},{5,6},{6,5},{7,4},{8,11},{9,10},{10,... | collective-permute-start | bytes 776 | tf_op jit(solution)/shard_map/ppermute | solution.py:24
  19.4 7.4 %collective-permute-start.4 = (s32[4,16]{1,0:T(4,128)S(1)}, s32[4,16]{1,0:T(4,128)S(1)}, u32[]{:S(2)}, u32[]{:S(2)}) collective-permute-start(s32[4,16]{1,0:T(4,128)S(1)} %table.1.dens_table), channel_id=1, source_target_pairs={{0,2},{1,0},{2,3},{3,1},{4,6},{5,4},{6,7},{7,5},{8,10},{9,8},{10,1... | collective-permute-start | bytes 776 | tf_op jit(solution)/shard_map/ppermute | solution.py:24
  20.9 1.0 %copy-start.1 = (f32[4,64,512]{2,1,0:T(8,128)S(1)}, f32[4,64,512]{2,1,0:T(8,128)}, u32[]{:S(2)}) copy-start(f32[4,64,512]{2,1,0:T(8,128)} %dens.1) | copy-start | bytes 1572868
  21.9 0.7 copy-start.2
  22.6 0.7 copy-start.4
  26.8 14.1 %collective-permute-start.5 = (f32[4,64,512]{2,1,0:T(8,128)S(1)}, f32[4,64,512]{2,1,0:T(8,128)S(1)}, u32[]{:S(2)}, u32[]{:S(2)}) collective-permute-start(f32[4,64,512]{2,1,0:T(8,128)S(1)} %collective-permute-done.odd), channel_id=1, source_target_pairs={{0,16},{1,17},{2,18},{3,19},{4,5},{5,7},{6,4},{7,6},{8,24},{9,25},... | collective-permute-start | bytes 1572872 | tf_op jit(solution)/shard_map/ppermute | solution.py:24
  32.1 10.5 %collective-permute-start.9 = (f32[4,64,512]{2,1,0:T(8,128)S(1)}, f32[4,64,512]{2,1,0:T(8,128)S(1)}, u32[]{:S(2)}, u32[]{:S(2)}) collective-permute-start(f32[4,64,512]{2,1,0:T(8,128)S(1)} %collective-permute-done.8.even), channel_id=1, source_target_pairs={{0,1},{1,3},{2,0},{3,2},{4,20},{5,21},{6,22},{7,23},{8,9},{9,11},{... | collective-permute-start | bytes 1572872 | tf_op jit(solution)/shard_map/ppermute | solution.py:24
  32.9 6.8 %collective-permute-start.6 = (f32[4,64,256]{2,1,0:T(8,128)S(1)}, f32[4,64,256]{2,1,0:T(8,128)S(1)}, u32[]{:S(2)}, u32[]{:S(2)}) collective-permute-start(f32[4,64,256]{2,1,0:T(8,128)S(1)} %get-tuple-element.53), channel_id=1, source_target_pairs={{0,4},{1,5},{2,6},{3,7},{4,8},{5,9},{6,10},{7,11},{8,12},{9,13},{1... | collective-permute-start | bytes 786440 | tf_op jit(solution)/shard_map/ppermute | solution.py:24
  33.0 7.6 %collective-permute-start.7 = (f32[4,64,256]{2,1,0:T(8,128)S(1)}, f32[4,64,256]{2,1,0:T(8,128)S(1)}, u32[]{:S(2)}, u32[]{:S(2)}) collective-permute-start(f32[4,64,256]{2,1,0:T(8,128)S(1)} %get-tuple-element.52), channel_id=1, source_target_pairs={{0,12},{1,13},{2,14},{3,15},{4,0},{5,1},{6,2},{7,3},{8,4},{9,5},{1... | collective-permute-start | bytes 786440 | tf_op jit(solution)/shard_map/ppermute | solution.py:24
  40.9 9.2 %collective-permute-start.10 = (f32[4,64,512]{2,1,0:T(8,128)S(1)}, f32[4,64,512]{2,1,0:T(8,128)S(1)}, u32[]{:S(2)}, u32[]{:S(2)}) collective-permute-start(f32[4,64,512]{2,1,0:T(8,128)S(1)} %collective-permute-done.5.odd), channel_id=1, source_target_pairs={{0,16},{1,17},{2,18},{3,19},{4,5},{5,7},{6,4},{7,6},{8,24},{9,25},... | collective-permute-start | bytes 1572872 | tf_op jit(solution)/shard_map/ppermute | solution.py:24
  44.3 21.7 %collective-permute-start.15 = (f32[256,1024]{1,0:T(8,128)S(1)}, f32[256,1024]{1,0:T(8,128)S(1)}, u32[]{:S(2)}, u32[]{:S(2)}) collective-permute-start(f32[256,1024]{1,0:T(8,128)S(1)} %even.1), channel_id=1, source_target_pairs={{0,12},{1,13},{2,14},{3,15},{4,0},{5,1},{6,2},{7,3},{8,4},{9,5},{1... | collective-permute-start | bytes 3145736 | tf_op jit(solution)/shard_map/ppermute | solution.py:24
  50.8 15.3 %collective-permute-start.14 = (f32[256,512]{1,0:T(8,128)S(1)}, f32[256,512]{1,0:T(8,128)S(1)}, u32[]{:S(2)}, u32[]{:S(2)}) collective-permute-start(f32[256,512]{1,0:T(8,128)S(1)} %get-tuple-element.48.rest_0_), channel_id=1, source_target_pairs={{0,4},{1,5},{2,6},{3,7},{4,0},{5,1},{6,2},{7,3},{8,12},{9,13},{10,... | collective-permute-start | bytes 1572872 | tf_op jit(solution)/shard_map/ppermute | solution.py:24
  53.0 14.4 %collective-permute-start.13 = (f32[256,512]{1,0:T(8,128)S(1)}, f32[256,512]{1,0:T(8,128)S(1)}, u32[]{:S(2)}, u32[]{:S(2)}) collective-permute-start(f32[256,512]{1,0:T(8,128)S(1)} %get-tuple-element.49.rest_1_), channel_id=1, source_target_pairs={{0,4},{1,5},{2,6},{3,7},{4,0},{5,1},{6,2},{7,3},{8,12},{9,13},{10,... | collective-permute-start | bytes 1572872 | tf_op jit(solution)/shard_map/ppermute | solution.py:24
  53.1 15.6 %collective-permute-start.12 = (f32[256,512]{1,0:T(8,128)S(1)}, f32[256,512]{1,0:T(8,128)S(1)}, u32[]{:S(2)}, u32[]{:S(2)}) collective-permute-start(f32[256,512]{1,0:T(8,128)S(1)} %get-tuple-element.48.rest_0_), channel_id=1, source_target_pairs={{0,4},{1,5},{2,6},{3,7},{4,8},{5,9},{6,10},{7,11},{8,12},{9,13},{1... | collective-permute-start | bytes 1572872 | tf_op jit(solution)/shard_map/ppermute | solution.py:24
  53.6 19.3 %collective-permute-start.11 = (f32[256,512]{1,0:T(8,128)S(1)}, f32[256,512]{1,0:T(8,128)S(1)}, u32[]{:S(2)}, u32[]{:S(2)}) collective-permute-start(f32[256,512]{1,0:T(8,128)S(1)} %get-tuple-element.49.rest_1_), channel_id=1, source_target_pairs={{0,4},{1,5},{2,6},{3,7},{4,8},{5,9},{6,10},{7,11},{8,12},{9,13},{1... | collective-permute-start | bytes 1572872 | tf_op jit(solution)/shard_map/ppermute | solution.py:24

commit v5 on v4

v5 whole, which is shorter than its diff:
```python
import functools

import jax
import jax.numpy as jnp
from jax import lax
from jax.experimental import pallas as pl
from jax.experimental.pallas import tpu as pltpu
from jax.sharding import PartitionSpec as P

LANES = 128
F32 = jnp.float32
BF16 = jnp.bfloat16
VMEM = pltpu.VMEM
SMEM = pltpu.SMEM


AXES = ("parts", "line", "cross")


def permute(x, target):
    parts, line, cross = (lax.axis_size(axis) for axis in AXES)
    flat = lambda p, g, c: (p % parts * line + g % line) * cross + c
    places = [(p, g, c) for p in range(parts) for g in range(line) for c in range(cross)]
    return lax.ppermute(x, AXES, [(flat(*place), flat(*target(*place))) for place in places])


def rotate(x, by):
    return permute(x, lambda p, g, c: (p, g + by, c))


def ring_order(count):
    return list(range(0, count, 2))[:1] + list(range(1, count, 2)) + list(range(0, count, 2))[:0:-1]


def pass_on(x, by, parity=None):
    order = ring_order(lax.axis_size("cross"))
    after = {d: order[(i + by) % len(order)] for i, d in enumerate(order)}
    return permute(
        x,
        lambda p, g, c: (p, g, after[c]) if parity in (None, g % 2) else (p + 1, g, c),
    )


def parity_here():
    return lax.rem(lax.axis_index("line"), 2)


def shard_of(step):
    order = ring_order(lax.axis_size("cross"))
    me = lax.axis_index("cross")
    owner = jnp.int32(0)
    for i, d in enumerate(order):
        owner = jnp.where(me == d, order[i - step], owner)
    return owner


def fill_table(table, columns, counts):
    rows, width = table.shape
    for r in range(rows):
        for c in range(width):
            table[r, c] = 0
        for slot in range(columns.shape[1]):

            @pl.when(slot < counts[r])
            def _(r=r, slot=slot):
                table[r, columns[r, slot]] = slot + 1


def table_kernel(columns, counts, table):
    fill_table(table, columns, counts)


def split(v):
    hi = v.astype(BF16)
    return hi, (v - hi.astype(F32)).astype(BF16)


def low_lanes(rows):
    return lax.broadcasted_iota(jnp.int32, (rows, LANES), 1) < LANES // 2


def block_at(row_ref, code, upper):
    slot = jnp.maximum(code - 1, 0)
    v = row_ref[:, pl.ds(pl.multiple_of((slot >> 1) * LANES, LANES), LANES)]
    v = jnp.where((slot & 1) != upper, pltpu.roll(v, LANES // 2, 1), v)
    return jnp.where(code > 0, v, jnp.zeros_like(v))


def pair_at(row_ref, table, r, pair):
    v0 = block_at(row_ref, table[r, 2 * pair], 0)
    v1 = block_at(row_ref, table[r, 2 * pair + 1], 1)
    return jnp.where(low_lanes(v0.shape[0]), v0, v1)


def densify_half(chunk, table, half, b, first=0):
    tile = chunk.shape[1]
    for r in range(2):
        for pair in range(b.shape[1] // LANES):
            hi, lo = split(pair_at(chunk.at[r], table, 2 * half + r, first + pair))
            lanes = slice(pair * LANES, (pair + 1) * LANES)
            b[r * tile : (r + 1) * tile, lanes] = hi
            b[(2 + r) * tile : (3 + r) * tile, lanes] = lo


def times_half(a, b, lanes):
    depth = b.shape[0]
    return jnp.dot(a[:, :depth], b[:, lanes], preferred_element_type=F32) + jnp.dot(
        a[:, depth:], b[: depth // 2, lanes], preferred_element_type=F32
    )


def lane_blocks(width, step=256):
    return [slice(i, i + step) for i in range(0, width, step)]


def ham_kernel(ham_cols, ham_count, ham, a, ham_table, ham_here, sems):
    rows, tile, _ = ham.shape
    copies = [
        pltpu.make_async_copy(ham.at[q], ham_here.at[q], sems.at[q]) for q in range(rows)
    ]
    for copy in copies:
        copy.start()
    fill_table(ham_table, ham_cols, ham_count)
    for q in range(rows):
        copies[q].wait()
        for pair in range(ham_table.shape[1] // 2):
            hi, lo = split(pair_at(ham_here.at[q], ham_table, q, pair))
            a[pair, q * tile : (q + 1) * tile, 0:LANES] = hi
            a[pair, q * tile : (q + 1) * tile, LANES : 2 * LANES] = hi
            a[pair, q * tile : (q + 1) * tile, 2 * LANES : 3 * LANES] = lo


def add_shard(step, first, dens_table, a, acc_in, shard, out, b):
    per_shard = dens_table.shape[0] // 2
    for half in range(per_shard):
        densify_half(shard.at[pl.ds(2 * half, 2)], dens_table, half, b, first // LANES)
        pair = shard_of(step) * per_shard + half
        for lanes in lane_blocks(out.shape[1]):
            part = times_half(a[pair], b, lanes)
            if half > 0:
                part += out[:, lanes]
            elif acc_in is not None:
                part += acc_in[:, first + lanes.start : first + lanes.stop]
            out[:, lanes] = part


def own_shard_kernel(dens_table, a, dens, acc, b):
    add_shard(0, 0, dens_table, a, None, dens, acc, b)


def add_kernel(step, dens_table, a, acc_in, even, odd, acc, b):
    for parity, shard in enumerate((even, odd)):

        @pl.when(parity_here() == parity)
        def _(shard=shard):
            add_shard(step, 0, dens_table, a, acc_in, shard, acc, b)


def margin_kernel(over, hi_out, lo_out):
    rows, tile, _ = over.shape
    for s in range(3):
        for j in range(rows):
            for pair in range(rows // 2):
                at = (s * rows + j) * tile
                lanes = slice(at // LANES * LANES, at // LANES * LANES + LANES)
                v0, v1 = over[2 * pair, :, lanes], over[2 * pair + 1, :, lanes]
                if at % LANES == 0:
                    v1 = pltpu.roll(v1, LANES // 2, 1)
                else:
                    v0 = pltpu.roll(v0, LANES // 2, 1)
                hi, lo = split(jnp.where(low_lanes(tile), v0, v1))
                to = slice(pair * LANES, (pair + 1) * LANES)
                hi_out[s, j * tile : (j + 1) * tile, to] = hi
                lo_out[s, j * tile : (j + 1) * tile, to] = lo


def store_at(out):
    def weigh(m_hi, m_lo, s, p):
        for lanes in lane_blocks(p.shape[1]):
            hi, lo = split(p[:, lanes])
            out[:, lanes] = (
                jnp.dot(m_hi[s], hi, preferred_element_type=F32)
                + jnp.dot(m_hi[s], lo, preferred_element_type=F32)
                + jnp.dot(m_lo[s], hi, preferred_element_type=F32)
            )

    return weigh


def even_kernel(step, dens_table, a, acc_in, shard, m_hi, m_lo, p, prev_term, b):
    @pl.when(parity_here() == 0)
    def _():
        add_shard(step, 0, dens_table, a, acc_in, shard, p, b)
        store_at(prev_term)(m_hi, m_lo, 0, p)


def odd_kernel(step, dens_table, a, acc_in, shard, m_hi, m_lo, even_p, p, prev_term, *rest):
    next_terms, b = rest[:-1], rest[-1]

    @pl.when(parity_here() == 1)
    def _():
        add_shard(step, 0, dens_table, a, acc_in, shard, p, b)

    @pl.when(parity_here() == 0)
    def _():
        p[...] = even_p[...]

    piece = next_terms[0].shape[1]
    for i, out in enumerate(next_terms):
        store_at(out)(m_hi, m_lo, 2, p.at[:, pl.ds(i * piece, piece)])

    @pl.when(parity_here() == 1)
    def _():
        store_at(prev_term)(m_hi, m_lo, 0, p)


def own_kernel(m_hi, m_lo, p, product, window, term, sems):
    rows, tile, width = product.shape

    def start(ref, out, at, kind):
        for q in range(rows):
            copies.append(
                pltpu.make_async_copy(
                    ref.at[pl.ds(q * tile, tile)], out.at[q, :, pl.ds(at, width)], sems.at[kind, q]
                )
            )
            copies[-1].start()

    copies = []
    start(p, product, 0, 0)
    store_at(term)(m_hi, m_lo, 1, p)
    start(term, window, width, 1)
    for copy in copies:
        copy.wait()


def arrived_kernel(at, parity, term, window_in, window, sems):
    rows, tile, _ = window.shape

    def move():
        copies = [
            pltpu.make_async_copy(
                term.at[pl.ds(q * tile, tile)],
                window.at[q, :, pl.ds(at, term.shape[1])],
                sems.at[q],
            )
            for q in range(rows)
        ]
        for copy in copies:
            copy.start()
        for copy in copies:
            copy.wait()

    if parity is None:
        move()
    else:
        pl.when(parity_here() == parity)(move)


def call(kernel, name, out_shape, in_spaces, out_spaces, scratch, flops, moved, aliases=None):
    return pl.pallas_call(
        kernel,
        name=name,
        out_shape=out_shape,
        in_specs=[pl.BlockSpec(memory_space=s) for s in in_spaces],
        out_specs=jax.tree.map(lambda s: pl.BlockSpec(memory_space=s), out_spaces),
        scratch_shapes=scratch,
        input_output_aliases=aliases or {},
        cost_estimate=pl.CostEstimate(flops=flops, bytes_accessed=moved, transcendentals=0),
        compiler_params=pltpu.CompilerParams(vmem_limit_bytes=24 << 20),
    )


def shards(ham_tiles, ham_cols, ham_count, dens_tiles, dens_cols, dens_count, over_tiles):
    count = lax.axis_size("cross")
    rows, tile, _ = ham_tiles.shape
    blocks = rows * count
    width = blocks * tile
    tall = rows * tile
    per_shard = rows // 2
    sds = jax.ShapeDtypeStruct

    ham_cols, ham_count, dens_cols, dens_count, ham_tiles = (
        pltpu.with_memory_space_constraint(x, pltpu.HBM)
        for x in (ham_cols, ham_count, dens_cols, dens_count, ham_tiles)
    )
    even = pass_on(dens_tiles, 1, 0)
    m_hi, m_lo = call(
        margin_kernel,
        "margin",
        (sds((3, tall, tall), BF16),) * 2,
        (VMEM,),
        (VMEM, VMEM),
        [],
        1 << 20,
        1 << 20,
    )(over_tiles)
    table = call(
        table_kernel,
        "table",
        sds((rows, blocks), jnp.int32),
        (SMEM, SMEM),
        SMEM,
        [],
        1024,
        1024,
    )(dens_cols, dens_count)
    dens_late, table = lax.optimization_barrier((dens_tiles, table))
    odd = pass_on(dens_late, 1, 1)
    tables = [pass_on(table, 1)]
    b_scratch = [VMEM((4 * tile, width), BF16)]
    evens, odds = [even], [odd]
    acc = None
    for step in range(1, count):
        even, odd = evens[-1], odds[-1]
        if step == 1:
            even, ham_tiles, table = lax.optimization_barrier((even, ham_tiles, table))
            tables += [pass_on(table, ahead) for ahead in range(2, count)]
            a = call(
                ham_kernel,
                "ham",
                sds((blocks // 2, tall, 3 * LANES), BF16),
                (SMEM, SMEM, pltpu.HBM),
                VMEM,
                [
                    pltpu.SMEM((rows, blocks), jnp.int32),
                    VMEM(ham_tiles.shape, F32),
                    pltpu.SemaphoreType.DMA((rows,)),
                ],
                1 << 20,
                1 << 20,
            )(ham_cols, ham_count, ham_tiles)
            odd, a, dens_own = lax.optimization_barrier((odd, a, dens_tiles))
            acc = call(
                own_shard_kernel,
                "own_shard",
                sds((tall, width), F32),
                (SMEM, VMEM, VMEM),
                VMEM,
                b_scratch,
                1 << 20,
                1 << 20,
            )(table, a, dens_own)
        else:
            even, acc, *tables = lax.optimization_barrier((even, acc, *tables))
            acc = call(
                functools.partial(add_kernel, step - 1),
                "add%d" % (step - 1),
                sds((tall, width), F32),
                (SMEM,) + (VMEM,) * 4,
                VMEM,
                b_scratch,
                1 << 20,
                1 << 20,
            )(tables[step - 2], a, acc, evens[-2], odds[-2])
            if step < count - 1:
                odd, acc = lax.optimization_barrier((odd, acc))
            if step == 2:
                odd, m_hi, m_lo = lax.optimization_barrier((odd, m_hi, m_lo))
        evens[-1], odds[-1] = even, odd
        if step < count - 1:
            evens.append(pass_on(even, 1, 0))
            odds.append(pass_on(odd, 1, 1))

    sides = 2
    piece = width // sides
    whole = sds((tall, width), F32)
    even_p, even_term = call(
        functools.partial(even_kernel, count - 1),
        "even",
        (whole, whole),
        (SMEM,) + (VMEM,) * 5,
        (VMEM, VMEM),
        b_scratch,
        1024,
        1024,
    )(tables[-1], a, acc, evens[-1], m_hi, m_lo)
    p, odd_term, *next_terms = call(
        functools.partial(odd_kernel, count - 1),
        "odd",
        [whole, whole] + [sds((tall, piece), F32)] * sides,
        (SMEM,) + (VMEM,) * 6,
        [VMEM] * (2 + sides),
        b_scratch,
        1024,
        1024,
    )(tables[-1], a, acc, odds[-1], m_hi, m_lo, even_p)
    mate = lambda p, g, c: (p, g + 1 - g % 2 * 2, c)
    over_x = permute(even_term, lambda p, g, c: mate(p, g, c) if g % 2 else (p, g - 1, c))
    between = permute(odd_term, mate)
    befores = [rotate(term, 1) for term in next_terms]
    product, window = call(
        own_kernel,
        "own",
        (sds((rows, tile, width), F32), sds((rows, tile, 3 * width), F32)),
        (VMEM,) * 3,
        (pl.ANY, pl.ANY),
        [VMEM((tall, width), F32), pltpu.SemaphoreType.DMA((2, rows))],
        1024,
        1024,
    )(m_hi, m_lo, p)
    steps = [(2 * width, 1, over_x), (2 * width, 0, between)]
    steps += [(i * piece, None, term) for i, term in enumerate(befores)]
    for i, (at, parity, term) in enumerate(steps):
        window = call(
            functools.partial(arrived_kernel, at, parity),
            "arrived%d" % i,
            sds((rows, tile, 3 * width), F32),
            (VMEM, pl.ANY),
            pl.ANY,
            [pltpu.SemaphoreType.DMA((rows,))],
            1024,
            1024,
            {1: 0},
        )(term, window)
    return (product, window)


def solution(mesh):
    whole = P(AXES)
    return jax.shard_map(
        shards,
        mesh=mesh,
        in_specs=(whole,) * 7,
        out_specs=(whole, whole),
        check_vma=False,
    )
```

time: 74.3 us -> 77.8 us (1.047)
  the two profiles are of different devices: /device:TPU:0 before, /device:TPU:4 now
where the time goes in v5:
time: 77.8 us; the launch traced here: 77.6 us
  waiting for transfers between devices  45.6 us (59%)
  Pallas kernels  16.8 us (22%)
  starting transfers between devices  13.2 us (17%)
  local copies, waits for them, and re-layouts  1.05 us (1%)
  between operations  0.8 us (1%)
    ppermute x13, waiting for transfers between devices, permute(): lax.ppermute(x, AXES, [(flat(*place), flat(*target(*place))) for place in...  45.6 us
    ppermute x13, starting transfers between devices, permute(): lax.ppermute(x, AXES, [(flat(*place), flat(*target(*place))) for place in...  13.2 us
    pallas_call x2, Pallas kernels, shards(): call(functools.partial(add_kernel, step - 1), 'add%d' % (step - 1), sds((...  3.3 us
    pallas_call x4, Pallas kernels, shards(): call(functools.partial(arrived_kernel, at, parity), 'arrived%d' % i, sds(...  2.69 us
    pallas_call x1, Pallas kernels, shards(): call(ham_kernel, 'ham', sds((blocks // 2, tall, 3 * LANES), BF16), (SMEM,...  2.51 us
    pallas_call x1, Pallas kernels, shards(): call(functools.partial(even_kernel, count - 1), 'even', (whole, whole), (...  2.06 us
    pallas_call x1, Pallas kernels, shards(): call(own_kernel, 'own', (sds((rows, tile, width), F32), sds((rows, tile,...  1.71 us
    pallas_call x1, Pallas kernels, shards(): call(own_shard_kernel, 'own_shard', sds((tall, width), F32), (SMEM, VMEM,...  1.62 us
  transfers between devices with their start and end apart: 13, of which 6 were waited for; matrix products, arithmetic and copies ran while one was open for 0% of the time, Pallas kernels for 21%

profile of v5, /device:TPU:4, one launch (start us, length us, event | category | flops | bytes accessed | tf_op | source)
XLA Modules:
  0.0 77.6 jit_solution(11891963707639681848)
XLA Ops:
  0.6 0.0 copy-start
  0.6 1.6 %collective-permute-start.1 = (f32[4,64,512]{2,1,0:T(8,128)}, f32[4,64,512]{2,1,0:T(8,128)S(1)}, u32[]{:S(2)}, u32[]{:S(2)}) collective-permute-start(f32[4,64,512]{2,1,0:T(8,128)} %dens), channel_id=1, source_target_pairs={{0,1},{1,3},{2,0},{3,2},{4,20},{5,21},{6,22},{7,23},{8,9},{9,11},{... | collective-permute-start | bytes 1572872 | tf_op jit(solution)/shard_map/ppermute | solution.py:24
  2.3 1.4 %table.1.dens_table = s32[4,16]{1,0:T(4,128)S(1)} custom-call(s32[4,8]{1,0:T(4,128)} %columns.1, s32[4]{0:T(128)} %counts.1), custom_call_target="tpu_custom_call" | custom-call | flops 1024 | bytes 1024 | tf_op jit(solution)/shard_map/table/pallas_call | solution.py:298
  3.7 0.6 collective-permute-start
  4.2 11.9 %collective-permute-done.1.even = f32[4,64,512]{2,1,0:T(8,128)S(1)} collective-permute-done((f32[4,64,512]{2,1,0:T(8,128)}, f32[4,64,512]{2,1,0:T(8,128)S(1)}, u32[]{:S(2)}, u32[]{:S(2)}) %collective-permute-start.1) | collective-permute-done | bytes 524320 | tf_op jit(solution)/shard_map/ppermute | solution.py:24
  16.2 0.8 %collective-permute-start.3 = (f32[4,64,512]{2,1,0:T(8,128)S(1)}, f32[4,64,512]{2,1,0:T(8,128)S(1)}, u32[]{:S(2)}, u32[]{:S(2)}) collective-permute-start(f32[4,64,512]{2,1,0:T(8,128)S(1)} %collective-permute-done.1.even), channel_id=1, source_target_pairs={{0,1},{1,3},{2,0},{3,2},{4,20},{5,21},{6,22},{7,23},{8,9},{9,11},{... | collective-permute-start | bytes 1572872 | tf_op jit(solution)/shard_map/ppermute | solution.py:24
  17.0 2.5 %ham.1.a = bf16[8,256,384]{2,1,0:T(8,128)(2,1)S(1)} custom-call(s32[4,12]{1,0:T(4,128)} %ham_cols.1, s32[4]{0:T(128)} %ham_count.1, f32[4,64,768]{2,1,0:T(8,128)} %ham.2), custom_call_target="tpu_custom_call" | custom-call | flops 1048576 | bytes 1048576 | tf_op jit(solution)/shard_map/ham/pallas_call | solution.py:319
  19.5 0.0 collective-permute-done.odd
  19.5 0.1 collective-permute-start.2
  19.6 3.3 %collective-permute-start.4 = (s32[4,16]{1,0:T(4,128)S(1)}, s32[4,16]{1,0:T(4,128)S(1)}, u32[]{:S(2)}, u32[]{:S(2)}) collective-permute-start(s32[4,16]{1,0:T(4,128)S(1)} %table.1.dens_table), channel_id=1, source_target_pairs={{0,1},{1,3},{2,0},{3,2},{4,5},{5,7},{6,4},{7,6},{8,9},{9,11},{10,8... | collective-permute-start | bytes 776 | tf_op jit(solution)/shard_map/ppermute | solution.py:24
  22.9 0.0 collective-permute-start.6
  22.9 2.4 %collective-permute-start.5 = (s32[4,16]{1,0:T(4,128)S(1)}, s32[4,16]{1,0:T(4,128)S(1)}, u32[]{:S(2)}, u32[]{:S(2)}) collective-permute-start(s32[4,16]{1,0:T(4,128)S(1)} %table.1.dens_table), channel_id=1, source_target_pairs={{0,3},{1,2},{2,1},{3,0},{4,7},{5,6},{6,5},{7,4},{8,11},{9,10},{10,... | collective-permute-start | bytes 776 | tf_op jit(solution)/shard_map/ppermute | solution.py:24
  25.3 0.0 copy-start.1
  25.4 1.0 %copy-done.1 = f32[4,64,512]{2,1,0:T(8,128)S(1)} copy-done((f32[4,64,512]{2,1,0:T(8,128)S(1)}, f32[4,64,512]{2,1,0:T(8,128)}, u32[]{:S(2)}) %copy-start.1) | copy-done | bytes 524312
  26.4 1.6 %own_shard.1.acc_in = f32[256,1024]{1,0:T(8,128)S(1)} custom-call(s32[4,16]{1,0:T(4,128)S(1)} %table.1.dens_table, bf16[8,256,384]{2,1,0:T(8,128)(2,1)S(1)} %ham.1.a, f32[4,64,512]{2,1,0:T(8,128)S(1)} %copy-done.1), custom_call_target="tpu_custom_call" | custom-call | flops 1048576 | bytes 1048576 | tf_op jit(solution)/shard_map/own_shard/pallas_call | solution.py:334
  28.0 3.2 %collective-permute-done.4.dens_table = s32[4,16]{1,0:T(4,128)S(1)} collective-permute-done((s32[4,16]{1,0:T(4,128)S(1)}, s32[4,16]{1,0:T(4,128)S(1)}, u32[]{:S(2)}, u32[]{:S(2)}) %collective-permute-start.4) | collective-permute-done | bytes 288 | tf_op jit(solution)/shard_map/ppermute | solution.py:24
  31.2 0.0 collective-permute-done.6.dens_table
  31.2 1.0 %collective-permute-done.5.dens_table = s32[4,16]{1,0:T(4,128)S(1)} collective-permute-done((s32[4,16]{1,0:T(4,128)S(1)}, s32[4,16]{1,0:T(4,128)S(1)}, u32[]{:S(2)}, u32[]{:S(2)}) %collective-permute-start.5) | collective-permute-done | bytes 288 | tf_op jit(solution)/shard_map/ppermute | solution.py:24
  32.2 0.0 collective-permute-done.3.even
  32.2 0.5 collective-permute-start.7
  32.8 0.0 copy-done
  32.8 0.3 margin.1
  33.1 1.7 %add1.1.acc_in = f32[256,1024]{1,0:T(8,128)S(1)} custom-call(s32[4,16]{1,0:T(4,128)S(1)} %collective-permute-done.4.dens_table, bf16[8,256,384]{2,1,0:T(8,128)(2,1)S(1)} %ham.1.a, f32[256,1024]{1,0:T(8,128)S(1)} %own_shard.1.acc_in, f32[4,64,512]{2,1,0:T(8,128)S(1)} %collective-permute-done.1.even, f32[4,64,512]{2,1,0:T(8,128)S(1)} %collective-permute-done.odd), custom_call_target="tpu_custom_call" | custom-call | flops 1048576 | bytes 1048576 | tf_op jit(solution)/shard_map/add1/pallas_call | solution.py:346
  34.7 0.0 collective-permute-done.2.odd
  34.7 0.1 collective-permute-start.8
  34.8 12.6 %collective-permute-done.7.shard = f32[4,64,512]{2,1,0:T(8,128)S(1)} collective-permute-done((f32[4,64,512]{2,1,0:T(8,128)S(1)}, f32[4,64,512]{2,1,0:T(8,128)S(1)}, u32[]{:S(2)}, u32[]{:S(2)}) %collective-permute-start.7) | collective-permute-done | bytes 524320 | tf_op jit(solution)/shard_map/ppermute | solution.py:24
  47.5 1.6 %add2.1.acc_in = f32[256,1024]{1,0:T(8,128)S(1)} custom-call(s32[4,16]{1,0:T(4,128)S(1)} %collective-permute-done.5.dens_table, bf16[8,256,384]{2,1,0:T(8,128)(2,1)S(1)} %ham.1.a, f32[256,1024]{1,0:T(8,128)S(1)} %add1.1.acc_in, f32[4,64,512]{2,1,0:T(8,128)S(1)} %collective-permute-done.3.even, f32[4,64,512]{2,1,0:T(8,128)S(1)} %collective-permute-done.2.odd), custom_call_target="tpu_custom_call" | custom-call | flops 1048576 | bytes 1048576 | tf_op jit(solution)/shard_map/add2/pallas_call | solution.py:346
  49.1 2.1 %even.1 = (f32[256,1024]{1,0:T(8,128)S(1)}, f32[256,1024]{1,0:T(8,128)S(1)}) custom-call(s32[4,16]{1,0:T(4,128)S(1)} %collective-permute-done.6.dens_table, bf16[8,256,384]{2,1,0:T(8,128)(2,1)S(1)} %ham.1.a, f32[256,1024]{1,0:T(8,128)S(1)} %add2.1.acc_in, f32[4,64,512]{2,1,0:T(8,128)S(1)} %collective-permute-done.7.shard, ...), custom_call_target="tpu_custom_call" | custom-call | flops 1024 | bytes 1024 | tf_op jit(solution)/shard_map/even/pallas_call | solution.py:368
  51.2 0.1 collective-permute-start.12
  51.2 0.0 collective-permute-done.8.shard
  51.3 1.3 %odd.1 = (f32[256,1024]{1,0:T(8,128)S(1)}, f32[256,1024]{1,0:T(8,128)S(1)}, f32[256,512]{1,0:T(8,128)S(1)}, f32[256,512]{1,0:T(8,128)S(1)}) custom-call(s32[4,16]{1,0:T(4,128)S(1)} %collective-permute-done.6.dens_table, bf16[8,256,384]{2,1,0:T(8,128)(2,1)S(1)} %ham.1.a, f32[256,1024]{1,0:T(8,128)S(1)} %add2.1.acc_in, ...), custom_call_target="tpu_custom_call" | custom-call | flops 1024 | bytes 1024 | tf_op jit(solution)/shard_map/odd/pallas_call | solution.py:378
  52.5 2.1 %collective-permute-start.11 = (f32[256,1024]{1,0:T(8,128)S(1)}, f32[256,1024]{1,0:T(8,128)S(1)}, u32[]{:S(2)}, u32[]{:S(2)}) collective-permute-start(f32[256,1024]{1,0:T(8,128)S(1)} %get-tuple-element.63), channel_id=1, source_target_pairs={{0,4},{1,5},{2,6},{3,7},{4,0},{5,1},{6,2},{7,3},{8,12},{9,13},{10,... | collective-permute-start | bytes 3145736 | tf_op jit(solution)/shard_map/ppermute | solution.py:24
  54.7 0.1 collective-permute-start.10
  54.7 1.5 %collective-permute-start.9 = (f32[256,512]{1,0:T(8,128)S(1)}, f32[256,512]{1,0:T(8,128)S(1)}, u32[]{:S(2)}, u32[]{:S(2)}) collective-permute-start(f32[256,512]{1,0:T(8,128)S(1)} %get-tuple-element.61), channel_id=1, source_target_pairs={{0,4},{1,5},{2,6},{3,7},{4,8},{5,9},{6,10},{7,11},{8,12},{9,13},{1... | collective-permute-start | bytes 1572872 | tf_op jit(solution)/shard_map/ppermute | solution.py:24
  56.3 1.7 %own.1 = (f32[4,64,1024]{2,1,0:T(8,128)}, f32[4,64,3072]{2,1,0:T(8,128)}) custom-call(bf16[3,256,256]{2,1,0:T(8,128)(2,1)S(1)} %get-tuple-element.47.m_hi, bf16[3,256,256]{2,1,0:T(8,128)(2,1)S(1)} %get-tuple-element.48.m_lo, f32[256,1024]{1,0:T(8,128)S(1)} %get-tuple-element.59.p), custom_call_target="tpu_custom_call" | custom-call | flops 1024 | bytes 1024 | tf_op jit(solution)/shard_map/own/pallas_call | solution.py:392
  58.0 12.4 %collective-permute-done.12.term = f32[256,1024]{1,0:T(8,128)S(1)} collective-permute-done((f32[256,1024]{1,0:T(8,128)S(1)}, f32[256,1024]{1,0:T(8,128)S(1)}, u32[]{:S(2)}, u32[]{:S(2)}) %collective-permute-start.12) | collective-permute-done | bytes 1048608 | tf_op jit(solution)/shard_map/ppermute | solution.py:24
  70.4 0.0 collective-permute-done.11.term
  70.4 1.0 %arrived1.1.window_in = f32[4,64,3072]{2,1,0:T(8,128)} custom-call(f32[256,1024]{1,0:T(8,128)S(1)} %collective-permute-done.11.term, f32[4,64,3072]{2,1,0:T(8,128)} %arrived0.1.window_in), custom_call_target="tpu_custom_call", output_to_operand_aliasing={{}: (1, {})} | custom-call | flops 1024 | bytes 1024 | tf_op jit(solution)/shard_map/arrived1/pallas_call | solution.py:405
  71.4 0.0 collective-permute-done.10.term
  71.5 0.8 %arrived2.1.window_in = f32[4,64,3072]{2,1,0:T(8,128)} custom-call(f32[256,512]{1,0:T(8,128)S(1)} %collective-permute-done.10.term, f32[4,64,3072]{2,1,0:T(8,128)} %arrived1.1.window_in), custom_call_target="tpu_custom_call", output_to_operand_aliasing={{}: (1, {})} | custom-call | flops 1024 | bytes 1024 | tf_op jit(solution)/shard_map/arrived2/pallas_call | solution.py:405
  72.3 4.5 %collective-permute-done.9.term = f32[256,512]{1,0:T(8,128)S(1)} collective-permute-done((f32[256,512]{1,0:T(8,128)S(1)}, f32[256,512]{1,0:T(8,128)S(1)}, u32[]{:S(2)}, u32[]{:S(2)}) %collective-permute-start.9) | collective-permute-done | bytes 524320 | tf_op jit(solution)/shard_map/ppermute | solution.py:24
  76.7 0.8 %arrived3.1 = f32[4,64,3072]{2,1,0:T(8,128)} custom-call(f32[256,512]{1,0:T(8,128)S(1)} %collective-permute-done.9.term, f32[4,64,3072]{2,1,0:T(8,128)} %arrived2.1.window_in), custom_call_target="tpu_custom_call", output_to_operand_aliasing={{}: (1, {})} | custom-call | flops 1024 | bytes 1024 | tf_op jit(solution)/shard_map/arrived3/pallas_call | solution.py:405
  (1 shorter events, 0.0 us)
Async XLA Ops:
  0.6 32.2 %copy-start = (f32[4,64,768]{2,1,0:T(8,128)S(1)}, f32[4,64,768]{2,1,0:T(8,128)}, u32[]{:S(2)}) copy-start(f32[4,64,768]{2,1,0:T(8,128)} %over.1) | copy-start | bytes 2359300
  0.6 15.5 %collective-permute-start.1 = (f32[4,64,512]{2,1,0:T(8,128)}, f32[4,64,512]{2,1,0:T(8,128)S(1)}, u32[]{:S(2)}, u32[]{:S(2)}) collective-permute-start(f32[4,64,512]{2,1,0:T(8,128)} %dens), channel_id=1, source_target_pairs={{0,1},{1,3},{2,0},{3,2},{4,20},{5,21},{6,22},{7,23},{8,9},{9,11},{... | collective-permute-start | bytes 1572872 | tf_op jit(solution)/shard_map/ppermute | solution.py:24
  3.7 15.8 %collective-permute-start = (f32[4,64,512]{2,1,0:T(8,128)}, f32[4,64,512]{2,1,0:T(8,128)S(1)}, u32[]{:S(2)}, u32[]{:S(2)}) collective-permute-start(f32[4,64,512]{2,1,0:T(8,128)} %dens), channel_id=1, source_target_pairs={{0,16},{1,17},{2,18},{3,19},{4,5},{5,7},{6,4},{7,6},{8,24},{9,25},... | collective-permute-start | bytes 1572872 | tf_op jit(solution)/shard_map/ppermute | solution.py:24
  16.2 16.1 %collective-permute-start.3 = (f32[4,64,512]{2,1,0:T(8,128)S(1)}, f32[4,64,512]{2,1,0:T(8,128)S(1)}, u32[]{:S(2)}, u32[]{:S(2)}) collective-permute-start(f32[4,64,512]{2,1,0:T(8,128)S(1)} %collective-permute-done.1.even), channel_id=1, source_target_pairs={{0,1},{1,3},{2,0},{3,2},{4,20},{5,21},{6,22},{7,23},{8,9},{9,11},{... | collective-permute-start | bytes 1572872 | tf_op jit(solution)/shard_map/ppermute | solution.py:24
  19.5 15.2 %collective-permute-start.2 = (f32[4,64,512]{2,1,0:T(8,128)S(1)}, f32[4,64,512]{2,1,0:T(8,128)S(1)}, u32[]{:S(2)}, u32[]{:S(2)}) collective-permute-start(f32[4,64,512]{2,1,0:T(8,128)S(1)} %collective-permute-done.odd), channel_id=1, source_target_pairs={{0,16},{1,17},{2,18},{3,19},{4,5},{5,7},{6,4},{7,6},{8,24},{9,25},... | collective-permute-start | bytes 1572872 | tf_op jit(solution)/shard_map/ppermute | solution.py:24
  19.6 11.6 %collective-permute-start.4 = (s32[4,16]{1,0:T(4,128)S(1)}, s32[4,16]{1,0:T(4,128)S(1)}, u32[]{:S(2)}, u32[]{:S(2)}) collective-permute-start(s32[4,16]{1,0:T(4,128)S(1)} %table.1.dens_table), channel_id=1, source_target_pairs={{0,1},{1,3},{2,0},{3,2},{4,5},{5,7},{6,4},{7,6},{8,9},{9,11},{10,8... | collective-permute-start | bytes 776 | tf_op jit(solution)/shard_map/ppermute | solution.py:24
  22.9 8.3 %collective-permute-start.6 = (s32[4,16]{1,0:T(4,128)S(1)}, s32[4,16]{1,0:T(4,128)S(1)}, u32[]{:S(2)}, u32[]{:S(2)}) collective-permute-start(s32[4,16]{1,0:T(4,128)S(1)} %table.1.dens_table), channel_id=1, source_target_pairs={{0,2},{1,0},{2,3},{3,1},{4,6},{5,4},{6,7},{7,5},{8,10},{9,8},{10,1... | collective-permute-start | bytes 776 | tf_op jit(solution)/shard_map/ppermute | solution.py:24
  22.9 9.3 %collective-permute-start.5 = (s32[4,16]{1,0:T(4,128)S(1)}, s32[4,16]{1,0:T(4,128)S(1)}, u32[]{:S(2)}, u32[]{:S(2)}) collective-permute-start(s32[4,16]{1,0:T(4,128)S(1)} %table.1.dens_table), channel_id=1, source_target_pairs={{0,3},{1,2},{2,1},{3,0},{4,7},{5,6},{6,5},{7,4},{8,11},{9,10},{10,... | collective-permute-start | bytes 776 | tf_op jit(solution)/shard_map/ppermute | solution.py:24
  25.3 1.0 %copy-start.1 = (f32[4,64,512]{2,1,0:T(8,128)S(1)}, f32[4,64,512]{2,1,0:T(8,128)}, u32[]{:S(2)}) copy-start(f32[4,64,512]{2,1,0:T(8,128)} %dens) | copy-start | bytes 1572868
  32.2 15.2 %collective-permute-start.7 = (f32[4,64,512]{2,1,0:T(8,128)S(1)}, f32[4,64,512]{2,1,0:T(8,128)S(1)}, u32[]{:S(2)}, u32[]{:S(2)}) collective-permute-start(f32[4,64,512]{2,1,0:T(8,128)S(1)} %collective-permute-done.3.even), channel_id=1, source_target_pairs={{0,1},{1,3},{2,0},{3,2},{4,20},{5,21},{6,22},{7,23},{8,9},{9,11},{... | collective-permute-start | bytes 1572872 | tf_op jit(solution)/shard_map/ppermute | solution.py:24
  34.7 16.5 %collective-permute-start.8 = (f32[4,64,512]{2,1,0:T(8,128)S(1)}, f32[4,64,512]{2,1,0:T(8,128)S(1)}, u32[]{:S(2)}, u32[]{:S(2)}) collective-permute-start(f32[4,64,512]{2,1,0:T(8,128)S(1)} %collective-permute-done.2.odd), channel_id=1, source_target_pairs={{0,16},{1,17},{2,18},{3,19},{4,5},{5,7},{6,4},{7,6},{8,24},{9,25},... | collective-permute-start | bytes 1572872 | tf_op jit(solution)/shard_map/ppermute | solution.py:24
  51.2 19.2 %collective-permute-start.12 = (f32[256,1024]{1,0:T(8,128)S(1)}, f32[256,1024]{1,0:T(8,128)S(1)}, u32[]{:S(2)}, u32[]{:S(2)}) collective-permute-start(f32[256,1024]{1,0:T(8,128)S(1)} %get-tuple-element.64), channel_id=1, source_target_pairs={{0,12},{1,13},{2,14},{3,15},{4,0},{5,1},{6,2},{7,3},{8,4},{9,5},{1... | collective-permute-start | bytes 3145736 | tf_op jit(solution)/shard_map/ppermute | solution.py:24
  52.5 17.9 %collective-permute-start.11 = (f32[256,1024]{1,0:T(8,128)S(1)}, f32[256,1024]{1,0:T(8,128)S(1)}, u32[]{:S(2)}, u32[]{:S(2)}) collective-permute-start(f32[256,1024]{1,0:T(8,128)S(1)} %get-tuple-element.63), channel_id=1, source_target_pairs={{0,4},{1,5},{2,6},{3,7},{4,0},{5,1},{6,2},{7,3},{8,12},{9,13},{10,... | collective-permute-start | bytes 3145736 | tf_op jit(solution)/shard_map/ppermute | solution.py:24
  54.7 16.8 %collective-permute-start.10 = (f32[256,512]{1,0:T(8,128)S(1)}, f32[256,512]{1,0:T(8,128)S(1)}, u32[]{:S(2)}, u32[]{:S(2)}) collective-permute-start(f32[256,512]{1,0:T(8,128)S(1)} %get-tuple-element.62), channel_id=1, source_target_pairs={{0,4},{1,5},{2,6},{3,7},{4,8},{5,9},{6,10},{7,11},{8,12},{9,13},{1... | collective-permute-start | bytes 1572872 | tf_op jit(solution)/shard_map/ppermute | solution.py:24
  54.7 22.0 %collective-permute-start.9 = (f32[256,512]{1,0:T(8,128)S(1)}, f32[256,512]{1,0:T(8,128)S(1)}, u32[]{:S(2)}, u32[]{:S(2)}) collective-permute-start(f32[256,512]{1,0:T(8,128)S(1)} %get-tuple-element.61), channel_id=1, source_target_pairs={{0,4},{1,5},{2,6},{3,7},{4,8},{5,9},{6,10},{7,11},{8,12},{9,13},{1... | collective-permute-start | bytes 1572872 | tf_op jit(solution)/shard_map/ppermute | solution.py:24

commit v6 on v5

--- a/solution.py
+++ b/solution.py
@@ -292,8 +292,8 @@
         (VMEM,),
         (VMEM, VMEM),
         [],
-        1 << 20,
-        1 << 20,
+        1024,
+        1024,
     )(over_tiles)
     table = call(
         table_kernel,
@@ -305,7 +305,21 @@
         1024,
         1024,
     )(dens_cols, dens_count)
-    dens_late, table = lax.optimization_barrier((dens_tiles, table))
+    a = call(
+        ham_kernel,
+        "ham",
+        sds((blocks // 2, tall, 3 * LANES), BF16),
+        (SMEM, SMEM, pltpu.HBM),
+        VMEM,
+        [
+            pltpu.SMEM((rows, blocks), jnp.int32),
+            VMEM(ham_tiles.shape, F32),
+            pltpu.SemaphoreType.DMA((rows,)),
+        ],
+        1024,
+        1024,
+    )(ham_cols, ham_count, ham_tiles)
+    dens_late, table, a = lax.optimization_barrier((dens_tiles, table, a))
     odd = pass_on(dens_late, 1, 1)
     tables = [pass_on(table, 1)]
     b_scratch = [VMEM((4 * tile, width), BF16)]
@@ -314,23 +328,9 @@
     for step in range(1, count):
         even, odd = evens[-1], odds[-1]
         if step == 1:
-            even, ham_tiles, table = lax.optimization_barrier((even, ham_tiles, table))
+            even, table = lax.optimization_barrier((even, table))
             tables += [pass_on(table, ahead) for ahead in range(2, count)]
-            a = call(
-                ham_kernel,
-                "ham",
-                sds((blocks // 2, tall, 3 * LANES), BF16),
-                (SMEM, SMEM, pltpu.HBM),
-                VMEM,
-                [
-                    pltpu.SMEM((rows, blocks), jnp.int32),
-                    VMEM(ham_tiles.shape, F32),
-                    pltpu.SemaphoreType.DMA((rows,)),
-                ],
-                1 << 20,
-                1 << 20,
-            )(ham_cols, ham_count, ham_tiles)
-            odd, a, dens_own = lax.optimization_barrier((odd, a, dens_tiles))
+            odd, dens_own = lax.optimization_barrier((odd, dens_tiles))
             acc = call(
                 own_shard_kernel,
                 "own_shard",
@@ -338,11 +338,12 @@
                 (SMEM, VMEM, VMEM),
                 VMEM,
                 b_scratch,
-                1 << 20,
-                1 << 20,
+                1024,
+                1024,
             )(table, a, dens_own)
         else:
-            even, acc, *tables = lax.optimization_barrier((even, acc, *tables))
+            if step < count - 1:
+                even, acc, *tables = lax.optimization_barrier((even, acc, *tables))
             acc = call(
                 functools.partial(add_kernel, step - 1),
                 "add%d" % (step - 1),
@@ -350,8 +351,8 @@
                 (SMEM,) + (VMEM,) * 4,
                 VMEM,
                 b_scratch,
-                1 << 20,
-                1 << 20,
+                1024,
+                1024,
             )(tables[step - 2], a, acc, evens[-2], odds[-2])
             if step < count - 1:
                 odd, acc = lax.optimization_barrier((odd, acc))

time: 77.8 us -> 77.6 us (level)
  the two profiles are of different devices: /device:TPU:4 before, /device:TPU:0 now
where the time goes in v6:
time: 77.6 us; the launch traced here: 77.4 us
  waiting for transfers between devices  40.4 us (52%)
  starting transfers between devices  18.1 us (23%)
  Pallas kernels  16.9 us (22%)
  local copies, waits for them, and re-layouts  1.14 us (1%)
  between operations  0.8 us (1%)
    ppermute x13, waiting for transfers between devices, permute(): lax.ppermute(x, AXES, [(flat(*place), flat(*target(*place))) for place in...  40.4 us
    ppermute x13, starting transfers between devices, permute(): lax.ppermute(x, AXES, [(flat(*place), flat(*target(*place))) for place in...  18.1 us
    pallas_call x2, Pallas kernels, shards(): call(functools.partial(add_kernel, step - 1), 'add%d' % (step - 1), sds((...  3.31 us
    pallas_call x4, Pallas kernels, shards(): call(functools.partial(arrived_kernel, at, parity), 'arrived%d' % i, sds(...  2.69 us
    pallas_call x1, Pallas kernels, shards(): call(ham_kernel, 'ham', sds((blocks // 2, tall, 3 * LANES), BF16), (SMEM,...  2.51 us
    pallas_call x1, Pallas kernels, shards(): call(functools.partial(even_kernel, count - 1), 'even', (whole, whole), (...  2.06 us
    pallas_call x1, Pallas kernels, shards(): call(own_kernel, 'own', (sds((rows, tile, width), F32), sds((rows, tile,...  1.71 us
    pallas_call x1, Pallas kernels, shards(): call(own_shard_kernel, 'own_shard', sds((tall, width), F32), (SMEM, VMEM,...  1.64 us
  transfers between devices with their start and end apart: 13, of which 6 were waited for; matrix products, arithmetic and copies ran while one was open for 0% of the time, Pallas kernels for 21%

profile of v6, /device:TPU:0, one launch (start us, length us, event | category | flops | bytes accessed | tf_op | source)
XLA Modules:
  0.0 77.4 jit_solution(10850552771734862557)
XLA Ops:
  0.6 0.0 copy-start.1
  0.6 3.1 %collective-permute-start.2 = (f32[4,64,512]{2,1,0:T(8,128)}, f32[4,64,512]{2,1,0:T(8,128)S(1)}, u32[]{:S(2)}, u32[]{:S(2)}) collective-permute-start(f32[4,64,512]{2,1,0:T(8,128)} %dens), channel_id=1, source_target_pairs={{0,1},{1,3},{2,0},{3,2},{4,20},{5,21},{6,22},{7,23},{8,9},{9,11},{... | collective-permute-start | bytes 1572872 | tf_op jit(solution)/shard_map/ppermute | solution.py:24
  3.7 1.4 %table.1.dens_table = s32[4,16]{1,0:T(4,128)S(1)} custom-call(s32[4,8]{1,0:T(4,128)} %columns.1, s32[4]{0:T(128)} %counts.1), custom_call_target="tpu_custom_call" | custom-call | flops 1024 | bytes 1024 | tf_op jit(solution)/shard_map/table/pallas_call | solution.py:298
  5.1 2.5 %ham.2.a = bf16[8,256,384]{2,1,0:T(8,128)(2,1)S(1)} custom-call(s32[4,12]{1,0:T(4,128)} %ham_cols.1, s32[4]{0:T(128)} %ham_count.1, f32[4,64,768]{2,1,0:T(8,128)} %ham.3), custom_call_target="tpu_custom_call" | custom-call | flops 1024 | bytes 1024 | tf_op jit(solution)/shard_map/ham/pallas_call | solution.py:308
  7.6 1.6 %collective-permute-start = (f32[4,64,512]{2,1,0:T(8,128)}, f32[4,64,512]{2,1,0:T(8,128)S(1)}, u32[]{:S(2)}, u32[]{:S(2)}) collective-permute-start(f32[4,64,512]{2,1,0:T(8,128)} %dens), channel_id=1, source_target_pairs={{0,16},{1,17},{2,18},{3,19},{4,5},{5,7},{6,4},{7,6},{8,24},{9,25},... | collective-permute-start | bytes 1572872 | tf_op jit(solution)/shard_map/ppermute | solution.py:24
  9.2 4.0 %collective-permute-done.2.even = f32[4,64,512]{2,1,0:T(8,128)S(1)} collective-permute-done((f32[4,64,512]{2,1,0:T(8,128)}, f32[4,64,512]{2,1,0:T(8,128)S(1)}, u32[]{:S(2)}, u32[]{:S(2)}) %collective-permute-start.2) | collective-permute-done | bytes 524320 | tf_op jit(solution)/shard_map/ppermute | solution.py:24
  13.3 1.5 %collective-permute-start.3 = (f32[4,64,512]{2,1,0:T(8,128)S(1)}, f32[4,64,512]{2,1,0:T(8,128)S(1)}, u32[]{:S(2)}, u32[]{:S(2)}) collective-permute-start(f32[4,64,512]{2,1,0:T(8,128)S(1)} %collective-permute-done.2.even), channel_id=1, source_target_pairs={{0,1},{1,3},{2,0},{3,2},{4,20},{5,21},{6,22},{7,23},{8,9},{9,11},{... | collective-permute-start | bytes 1572872 | tf_op jit(solution)/shard_map/ppermute | solution.py:24
  14.8 6.4 %collective-permute-done.odd = f32[4,64,512]{2,1,0:T(8,128)S(1)} collective-permute-done((f32[4,64,512]{2,1,0:T(8,128)}, f32[4,64,512]{2,1,0:T(8,128)S(1)}, u32[]{:S(2)}, u32[]{:S(2)}) %collective-permute-start) | collective-permute-done | bytes 524320 | tf_op jit(solution)/shard_map/ppermute | solution.py:24
  21.2 1.3 %collective-permute-start.1 = (f32[4,64,512]{2,1,0:T(8,128)S(1)}, f32[4,64,512]{2,1,0:T(8,128)S(1)}, u32[]{:S(2)}, u32[]{:S(2)}) collective-permute-start(f32[4,64,512]{2,1,0:T(8,128)S(1)} %collective-permute-done.odd), channel_id=1, source_target_pairs={{0,16},{1,17},{2,18},{3,19},{4,5},{5,7},{6,4},{7,6},{8,24},{9,25},... | collective-permute-start | bytes 1572872 | tf_op jit(solution)/shard_map/ppermute | solution.py:24
  22.5 3.7 %collective-permute-start.4 = (s32[4,16]{1,0:T(4,128)S(1)}, s32[4,16]{1,0:T(4,128)S(1)}, u32[]{:S(2)}, u32[]{:S(2)}) collective-permute-start(s32[4,16]{1,0:T(4,128)S(1)} %table.1.dens_table), channel_id=1, source_target_pairs={{0,1},{1,3},{2,0},{3,2},{4,5},{5,7},{6,4},{7,6},{8,9},{9,11},{10,8... | collective-permute-start | bytes 776 | tf_op jit(solution)/shard_map/ppermute | solution.py:24
  26.2 0.0 copy-start
  26.2 1.1 %copy-done = f32[4,64,768]{2,1,0:T(8,128)S(1)} copy-done((f32[4,64,768]{2,1,0:T(8,128)S(1)}, f32[4,64,768]{2,1,0:T(8,128)}, u32[]{:S(2)}) %copy-start) | copy-done | bytes 786456
  27.4 0.3 margin.1
  27.6 0.1 collective-permute-start.6
  27.7 2.4 %collective-permute-start.5 = (s32[4,16]{1,0:T(4,128)S(1)}, s32[4,16]{1,0:T(4,128)S(1)}, u32[]{:S(2)}, u32[]{:S(2)}) collective-permute-start(s32[4,16]{1,0:T(4,128)S(1)} %table.1.dens_table), channel_id=1, source_target_pairs={{0,3},{1,2},{2,1},{3,0},{4,7},{5,6},{6,5},{7,4},{8,11},{9,10},{10,... | collective-permute-start | bytes 776 | tf_op jit(solution)/shard_map/ppermute | solution.py:24
  30.1 0.0 copy-done.1
  30.1 1.6 %own_shard.1.acc_in = f32[256,1024]{1,0:T(8,128)S(1)} custom-call(s32[4,16]{1,0:T(4,128)S(1)} %table.1.dens_table, bf16[8,256,384]{2,1,0:T(8,128)(2,1)S(1)} %ham.2.a, f32[4,64,512]{2,1,0:T(8,128)S(1)} %copy-done.1), custom_call_target="tpu_custom_call" | custom-call | flops 1024 | bytes 1024 | tf_op jit(solution)/shard_map/own_shard/pallas_call | solution.py:334
  31.7 0.0 collective-permute-done.4.dens_table
  31.7 0.0 collective-permute-done.6.dens_table
  31.7 1.4 %collective-permute-done.5.dens_table = s32[4,16]{1,0:T(4,128)S(1)} collective-permute-done((s32[4,16]{1,0:T(4,128)S(1)}, s32[4,16]{1,0:T(4,128)S(1)}, u32[]{:S(2)}, u32[]{:S(2)}) %collective-permute-start.5) | collective-permute-done | bytes 288 | tf_op jit(solution)/shard_map/ppermute | solution.py:24
  33.2 0.0 collective-permute-done.3.even
  33.2 1.7 %add1.1.acc_in = f32[256,1024]{1,0:T(8,128)S(1)} custom-call(s32[4,16]{1,0:T(4,128)S(1)} %collective-permute-done.4.dens_table, bf16[8,256,384]{2,1,0:T(8,128)(2,1)S(1)} %ham.2.a, f32[256,1024]{1,0:T(8,128)S(1)} %own_shard.1.acc_in, f32[4,64,512]{2,1,0:T(8,128)S(1)} %collective-permute-done.2.even, f32[4,64,512]{2,1,0:T(8,128)S(1)} %collective-permute-done.odd), custom_call_target="tpu_custom_call" | custom-call | flops 1024 | bytes 1024 | tf_op jit(solution)/shard_map/add1/pallas_call | solution.py:347
  34.8 0.0 collective-permute-done.1.odd
  34.8 0.2 collective-permute-start.8
  35.0 0.5 collective-permute-start.7
  35.5 1.7 %add2.1.acc_in = f32[256,1024]{1,0:T(8,128)S(1)} custom-call(s32[4,16]{1,0:T(4,128)S(1)} %collective-permute-done.5.dens_table, bf16[8,256,384]{2,1,0:T(8,128)(2,1)S(1)} %ham.2.a, f32[256,1024]{1,0:T(8,128)S(1)} %add1.1.acc_in, f32[4,64,512]{2,1,0:T(8,128)S(1)} %collective-permute-done.3.even, f32[4,64,512]{2,1,0:T(8,128)S(1)} %collective-permute-done.1.odd), custom_call_target="tpu_custom_call" | custom-call | flops 1024 | bytes 1024 | tf_op jit(solution)/shard_map/add2/pallas_call | solution.py:347
  37.2 11.7 %collective-permute-done.8.shard = f32[4,64,512]{2,1,0:T(8,128)S(1)} collective-permute-done((f32[4,64,512]{2,1,0:T(8,128)S(1)}, f32[4,64,512]{2,1,0:T(8,128)S(1)}, u32[]{:S(2)}, u32[]{:S(2)}) %collective-permute-start.8) | collective-permute-done | bytes 524320 | tf_op jit(solution)/shard_map/ppermute | solution.py:24
  48.9 2.1 %even.1 = (f32[256,1024]{1,0:T(8,128)S(1)}, f32[256,1024]{1,0:T(8,128)S(1)}) custom-call(s32[4,16]{1,0:T(4,128)S(1)} %collective-permute-done.6.dens_table, bf16[8,256,384]{2,1,0:T(8,128)(2,1)S(1)} %ham.2.a, f32[256,1024]{1,0:T(8,128)S(1)} %add2.1.acc_in, f32[4,64,512]{2,1,0:T(8,128)S(1)} %collective-permute-done.8.shard, ...), custom_call_target="tpu_custom_call" | custom-call | flops 1024 | bytes 1024 | tf_op jit(solution)/shard_map/even/pallas_call | solution.py:369
  51.0 0.1 collective-permute-start.12
  51.0 0.0 collective-permute-done.7.shard
  51.1 1.3 %odd.1 = (f32[256,1024]{1,0:T(8,128)S(1)}, f32[256,1024]{1,0:T(8,128)S(1)}, f32[256,512]{1,0:T(8,128)S(1)}, f32[256,512]{1,0:T(8,128)S(1)}) custom-call(s32[4,16]{1,0:T(4,128)S(1)} %collective-permute-done.6.dens_table, bf16[8,256,384]{2,1,0:T(8,128)(2,1)S(1)} %ham.2.a, f32[256,1024]{1,0:T(8,128)S(1)} %add2.1.acc_in, ...), custom_call_target="tpu_custom_call" | custom-call | flops 1024 | bytes 1024 | tf_op jit(solution)/shard_map/odd/pallas_call | solution.py:379
  52.3 2.1 %collective-permute-start.11 = (f32[256,1024]{1,0:T(8,128)S(1)}, f32[256,1024]{1,0:T(8,128)S(1)}, u32[]{:S(2)}, u32[]{:S(2)}) collective-permute-start(f32[256,1024]{1,0:T(8,128)S(1)} %get-tuple-element.53), channel_id=1, source_target_pairs={{0,4},{1,5},{2,6},{3,7},{4,0},{5,1},{6,2},{7,3},{8,12},{9,13},{10,... | collective-permute-start | bytes 3145736 | tf_op jit(solution)/shard_map/ppermute | solution.py:24
  54.5 0.1 collective-permute-start.10
  54.5 1.5 %collective-permute-start.9 = (f32[256,512]{1,0:T(8,128)S(1)}, f32[256,512]{1,0:T(8,128)S(1)}, u32[]{:S(2)}, u32[]{:S(2)}) collective-permute-start(f32[256,512]{1,0:T(8,128)S(1)} %get-tuple-element.51), channel_id=1, source_target_pairs={{0,4},{1,5},{2,6},{3,7},{4,8},{5,9},{6,10},{7,11},{8,12},{9,13},{1... | collective-permute-start | bytes 1572872 | tf_op jit(solution)/shard_map/ppermute | solution.py:24
  56.1 1.7 %own.1 = (f32[4,64,1024]{2,1,0:T(8,128)}, f32[4,64,3072]{2,1,0:T(8,128)}) custom-call(bf16[3,256,256]{2,1,0:T(8,128)(2,1)S(1)} %get-tuple-element.41.m_hi, bf16[3,256,256]{2,1,0:T(8,128)(2,1)S(1)} %get-tuple-element.42.m_lo, f32[256,1024]{1,0:T(8,128)S(1)} %get-tuple-element.49.p), custom_call_target="tpu_custom_call" | custom-call | flops 1024 | bytes 1024 | tf_op jit(solution)/shard_map/own/pallas_call | solution.py:393
  57.8 12.4 %collective-permute-done.12.term = f32[256,1024]{1,0:T(8,128)S(1)} collective-permute-done((f32[256,1024]{1,0:T(8,128)S(1)}, f32[256,1024]{1,0:T(8,128)S(1)}, u32[]{:S(2)}, u32[]{:S(2)}) %collective-permute-start.12) | collective-permute-done | bytes 1048608 | tf_op jit(solution)/shard_map/ppermute | solution.py:24
  70.2 0.0 collective-permute-done.11.term
  70.2 1.0 %arrived1.1.window_in = f32[4,64,3072]{2,1,0:T(8,128)} custom-call(f32[256,1024]{1,0:T(8,128)S(1)} %collective-permute-done.11.term, f32[4,64,3072]{2,1,0:T(8,128)} %arrived0.1.window_in), custom_call_target="tpu_custom_call", output_to_operand_aliasing={{}: (1, {})} | custom-call | flops 1024 | bytes 1024 | tf_op jit(solution)/shard_map/arrived1/pallas_call | solution.py:406
  71.2 0.0 collective-permute-done.10.term
  71.3 0.8 %arrived2.1.window_in = f32[4,64,3072]{2,1,0:T(8,128)} custom-call(f32[256,512]{1,0:T(8,128)S(1)} %collective-permute-done.10.term, f32[4,64,3072]{2,1,0:T(8,128)} %arrived1.1.window_in), custom_call_target="tpu_custom_call", output_to_operand_aliasing={{}: (1, {})} | custom-call | flops 1024 | bytes 1024 | tf_op jit(solution)/shard_map/arrived2/pallas_call | solution.py:406
  72.1 4.5 %collective-permute-done.9.term = f32[256,512]{1,0:T(8,128)S(1)} collective-permute-done((f32[256,512]{1,0:T(8,128)S(1)}, f32[256,512]{1,0:T(8,128)S(1)}, u32[]{:S(2)}, u32[]{:S(2)}) %collective-permute-start.9) | collective-permute-done | bytes 524320 | tf_op jit(solution)/shard_map/ppermute | solution.py:24
  76.5 0.8 %arrived3.1 = f32[4,64,3072]{2,1,0:T(8,128)} custom-call(f32[256,512]{1,0:T(8,128)S(1)} %collective-permute-done.9.term, f32[4,64,3072]{2,1,0:T(8,128)} %arrived2.1.window_in), custom_call_target="tpu_custom_call", output_to_operand_aliasing={{}: (1, {})} | custom-call | flops 1024 | bytes 1024 | tf_op jit(solution)/shard_map/arrived3/pallas_call | solution.py:406
  (1 shorter events, 0.0 us)
Async XLA Ops:
  0.6 29.4 %copy-start.1 = (f32[4,64,512]{2,1,0:T(8,128)S(1)}, f32[4,64,512]{2,1,0:T(8,128)}, u32[]{:S(2)}) copy-start(f32[4,64,512]{2,1,0:T(8,128)} %dens) | copy-start | bytes 1572868
  0.6 12.6 %collective-permute-start.2 = (f32[4,64,512]{2,1,0:T(8,128)}, f32[4,64,512]{2,1,0:T(8,128)S(1)}, u32[]{:S(2)}, u32[]{:S(2)}) collective-permute-start(f32[4,64,512]{2,1,0:T(8,128)} %dens), channel_id=1, source_target_pairs={{0,1},{1,3},{2,0},{3,2},{4,20},{5,21},{6,22},{7,23},{8,9},{9,11},{... | collective-permute-start | bytes 1572872 | tf_op jit(solution)/shard_map/ppermute | solution.py:24
  7.6 13.6 %collective-permute-start = (f32[4,64,512]{2,1,0:T(8,128)}, f32[4,64,512]{2,1,0:T(8,128)S(1)}, u32[]{:S(2)}, u32[]{:S(2)}) collective-permute-start(f32[4,64,512]{2,1,0:T(8,128)} %dens), channel_id=1, source_target_pairs={{0,16},{1,17},{2,18},{3,19},{4,5},{5,7},{6,4},{7,6},{8,24},{9,25},... | collective-permute-start | bytes 1572872 | tf_op jit(solution)/shard_map/ppermute | solution.py:24
  13.3 19.9 %collective-permute-start.3 = (f32[4,64,512]{2,1,0:T(8,128)S(1)}, f32[4,64,512]{2,1,0:T(8,128)S(1)}, u32[]{:S(2)}, u32[]{:S(2)}) collective-permute-start(f32[4,64,512]{2,1,0:T(8,128)S(1)} %collective-permute-done.2.even), channel_id=1, source_target_pairs={{0,1},{1,3},{2,0},{3,2},{4,20},{5,21},{6,22},{7,23},{8,9},{9,11},{... | collective-permute-start | bytes 1572872 | tf_op jit(solution)/shard_map/ppermute | solution.py:24
  21.2 13.6 %collective-permute-start.1 = (f32[4,64,512]{2,1,0:T(8,128)S(1)}, f32[4,64,512]{2,1,0:T(8,128)S(1)}, u32[]{:S(2)}, u32[]{:S(2)}) collective-permute-start(f32[4,64,512]{2,1,0:T(8,128)S(1)} %collective-permute-done.odd), channel_id=1, source_target_pairs={{0,16},{1,17},{2,18},{3,19},{4,5},{5,7},{6,4},{7,6},{8,24},{9,25},... | collective-permute-start | bytes 1572872 | tf_op jit(solution)/shard_map/ppermute | solution.py:24
  22.5 9.2 %collective-permute-start.4 = (s32[4,16]{1,0:T(4,128)S(1)}, s32[4,16]{1,0:T(4,128)S(1)}, u32[]{:S(2)}, u32[]{:S(2)}) collective-permute-start(s32[4,16]{1,0:T(4,128)S(1)} %table.1.dens_table), channel_id=1, source_target_pairs={{0,1},{1,3},{2,0},{3,2},{4,5},{5,7},{6,4},{7,6},{8,9},{9,11},{10,8... | collective-permute-start | bytes 776 | tf_op jit(solution)/shard_map/ppermute | solution.py:24
  26.2 1.1 %copy-start = (f32[4,64,768]{2,1,0:T(8,128)S(1)}, f32[4,64,768]{2,1,0:T(8,128)}, u32[]{:S(2)}) copy-start(f32[4,64,768]{2,1,0:T(8,128)} %over.1) | copy-start | bytes 2359300
  27.6 4.1 %collective-permute-start.6 = (s32[4,16]{1,0:T(4,128)S(1)}, s32[4,16]{1,0:T(4,128)S(1)}, u32[]{:S(2)}, u32[]{:S(2)}) collective-permute-start(s32[4,16]{1,0:T(4,128)S(1)} %table.1.dens_table), channel_id=1, source_target_pairs={{0,2},{1,0},{2,3},{3,1},{4,6},{5,4},{6,7},{7,5},{8,10},{9,8},{10,1... | collective-permute-start | bytes 776 | tf_op jit(solution)/shard_map/ppermute | solution.py:24
  27.7 5.4 %collective-permute-start.5 = (s32[4,16]{1,0:T(4,128)S(1)}, s32[4,16]{1,0:T(4,128)S(1)}, u32[]{:S(2)}, u32[]{:S(2)}) collective-permute-start(s32[4,16]{1,0:T(4,128)S(1)} %table.1.dens_table), channel_id=1, source_target_pairs={{0,3},{1,2},{2,1},{3,0},{4,7},{5,6},{6,5},{7,4},{8,11},{9,10},{10,... | collective-permute-start | bytes 776 | tf_op jit(solution)/shard_map/ppermute | solution.py:24
  34.8 14.1 %collective-permute-start.8 = (f32[4,64,512]{2,1,0:T(8,128)S(1)}, f32[4,64,512]{2,1,0:T(8,128)S(1)}, u32[]{:S(2)}, u32[]{:S(2)}) collective-permute-start(f32[4,64,512]{2,1,0:T(8,128)S(1)} %collective-permute-done.3.even), channel_id=1, source_target_pairs={{0,1},{1,3},{2,0},{3,2},{4,20},{5,21},{6,22},{7,23},{8,9},{9,11},{... | collective-permute-start | bytes 1572872 | tf_op jit(solution)/shard_map/ppermute | solution.py:24
  35.0 16.0 %collective-permute-start.7 = (f32[4,64,512]{2,1,0:T(8,128)S(1)}, f32[4,64,512]{2,1,0:T(8,128)S(1)}, u32[]{:S(2)}, u32[]{:S(2)}) collective-permute-start(f32[4,64,512]{2,1,0:T(8,128)S(1)} %collective-permute-done.1.odd), channel_id=1, source_target_pairs={{0,16},{1,17},{2,18},{3,19},{4,5},{5,7},{6,4},{7,6},{8,24},{9,25},... | collective-permute-start | bytes 1572872 | tf_op jit(solution)/shard_map/ppermute | solution.py:24
  51.0 19.2 %collective-permute-start.12 = (f32[256,1024]{1,0:T(8,128)S(1)}, f32[256,1024]{1,0:T(8,128)S(1)}, u32[]{:S(2)}, u32[]{:S(2)}) collective-permute-start(f32[256,1024]{1,0:T(8,128)S(1)} %get-tuple-element.54), channel_id=1, source_target_pairs={{0,12},{1,13},{2,14},{3,15},{4,0},{5,1},{6,2},{7,3},{8,4},{9,5},{1... | collective-permute-start | bytes 3145736 | tf_op jit(solution)/shard_map/ppermute | solution.py:24
  52.3 17.9 %collective-permute-start.11 = (f32[256,1024]{1,0:T(8,128)S(1)}, f32[256,1024]{1,0:T(8,128)S(1)}, u32[]{:S(2)}, u32[]{:S(2)}) collective-permute-start(f32[256,1024]{1,0:T(8,128)S(1)} %get-tuple-element.53), channel_id=1, source_target_pairs={{0,4},{1,5},{2,6},{3,7},{4,0},{5,1},{6,2},{7,3},{8,12},{9,13},{10,... | collective-permute-start | bytes 3145736 | tf_op jit(solution)/shard_map/ppermute | solution.py:24
  54.5 16.8 %collective-permute-start.10 = (f32[256,512]{1,0:T(8,128)S(1)}, f32[256,512]{1,0:T(8,128)S(1)}, u32[]{:S(2)}, u32[]{:S(2)}) collective-permute-start(f32[256,512]{1,0:T(8,128)S(1)} %get-tuple-element.52), channel_id=1, source_target_pairs={{0,4},{1,5},{2,6},{3,7},{4,8},{5,9},{6,10},{7,11},{8,12},{9,13},{1... | collective-permute-start | bytes 1572872 | tf_op jit(solution)/shard_map/ppermute | solution.py:24
  54.5 22.0 %collective-permute-start.9 = (f32[256,512]{1,0:T(8,128)S(1)}, f32[256,512]{1,0:T(8,128)S(1)}, u32[]{:S(2)}, u32[]{:S(2)}) collective-permute-start(f32[256,512]{1,0:T(8,128)S(1)} %get-tuple-element.51), channel_id=1, source_target_pairs={{0,4},{1,5},{2,6},{3,7},{4,8},{5,9},{6,10},{7,11},{8,12},{9,13},{1... | collective-permute-start | bytes 1572872 | tf_op jit(solution)/shard_map/ppermute | solution.py:24

commit v7 on v6

v7 whole, which is shorter than its diff:
```python
import functools

import jax
import jax.numpy as jnp
from jax import lax
from jax.experimental import pallas as pl
from jax.experimental.pallas import tpu as pltpu
from jax.sharding import PartitionSpec as P

LANES = 128
F32 = jnp.float32
BF16 = jnp.bfloat16
VMEM = pltpu.VMEM
SMEM = pltpu.SMEM


AXES = ("parts", "line", "cross")


def permute(x, target):
    parts, line, cross = (lax.axis_size(axis) for axis in AXES)
    flat = lambda p, g, c: (p % parts * line + g % line) * cross + c
    places = [(p, g, c) for p in range(parts) for g in range(line) for c in range(cross)]
    return lax.ppermute(x, AXES, [(flat(*place), flat(*target(*place))) for place in places])


def rotate(x, by):
    return permute(x, lambda p, g, c: (p, g + by, c))


def ring_order(count):
    return list(range(0, count, 2))[:1] + list(range(1, count, 2)) + list(range(0, count, 2))[:0:-1]


def pass_on(x, by):
    order = ring_order(lax.axis_size("cross"))
    after = {d: order[(i + by) % len(order)] for i, d in enumerate(order)}
    return permute(x, lambda p, g, c: (p, g, after[c]))


def shard_of(step):
    order = ring_order(lax.axis_size("cross"))
    me = lax.axis_index("cross")
    owner = jnp.int32(0)
    for i, d in enumerate(order):
        owner = jnp.where(me == d, order[i - step], owner)
    return owner


def fill_table(table, columns, counts):
    rows, width = table.shape
    for r in range(rows):
        for c in range(width):
            table[r, c] = 0
        for slot in range(columns.shape[1]):

            @pl.when(slot < counts[r])
            def _(r=r, slot=slot):
                table[r, columns[r, slot]] = slot + 1


def table_kernel(columns, counts, table):
    fill_table(table, columns, counts)


def split(v):
    hi = v.astype(BF16)
    return hi, (v - hi.astype(F32)).astype(BF16)


def low_lanes(rows):
    return lax.broadcasted_iota(jnp.int32, (rows, LANES), 1) < LANES // 2


def block_at(row_ref, code, upper):
    slot = jnp.maximum(code - 1, 0)
    v = row_ref[:, pl.ds(pl.multiple_of((slot >> 1) * LANES, LANES), LANES)]
    v = jnp.where((slot & 1) != upper, pltpu.roll(v, LANES // 2, 1), v)
    return jnp.where(code > 0, v, jnp.zeros_like(v))


def pair_at(row_ref, table, r, pair):
    v0 = block_at(row_ref, table[r, 2 * pair], 0)
    v1 = block_at(row_ref, table[r, 2 * pair + 1], 1)
    return jnp.where(low_lanes(v0.shape[0]), v0, v1)


def densify_half(chunk, table, half, b, first=0):
    tile = chunk.shape[1]
    for r in range(2):
        for pair in range(b.shape[1] // LANES):
            hi, lo = split(pair_at(chunk.at[r], table, 2 * half + r, first + pair))
            lanes = slice(pair * LANES, (pair + 1) * LANES)
            b[r * tile : (r + 1) * tile, lanes] = hi
            b[(2 + r) * tile : (3 + r) * tile, lanes] = lo


def times_half(a, b, lanes):
    depth = b.shape[0]
    return jnp.dot(a[:, :depth], b[:, lanes], preferred_element_type=F32) + jnp.dot(
        a[:, depth:], b[: depth // 2, lanes], preferred_element_type=F32
    )


def lane_blocks(width, step=256):
    return [slice(i, i + step) for i in range(0, width, step)]


def ham_kernel(ham_cols, ham_count, ham, a, ham_table, ham_here, sems):
    rows, tile, _ = ham.shape
    copies = [
        pltpu.make_async_copy(ham.at[q], ham_here.at[q], sems.at[q]) for q in range(rows)
    ]
    for copy in copies:
        copy.start()
    fill_table(ham_table, ham_cols, ham_count)
    for q in range(rows):
        copies[q].wait()
        for pair in range(ham_table.shape[1] // 2):
            hi, lo = split(pair_at(ham_here.at[q], ham_table, q, pair))
            a[pair, q * tile : (q + 1) * tile, 0:LANES] = hi
            a[pair, q * tile : (q + 1) * tile, LANES : 2 * LANES] = hi
            a[pair, q * tile : (q + 1) * tile, 2 * LANES : 3 * LANES] = lo


def add_half(step, half, first, dens_table, a, acc_in, chunk, out, b):
    densify_half(chunk, dens_table, half, b, first // LANES)
    pair = shard_of(step) * (dens_table.shape[0] // 2) + half
    for lanes in lane_blocks(out.shape[1]):
        part = times_half(a[pair], b, lanes)
        if acc_in is not None:
            part += acc_in[:, first + lanes.start : first + lanes.stop]
        out[:, lanes] = part


def add_kernel(step, halves, dens_table, a, *rest):
    (acc, b), chunks = rest[-2:], rest[-2 - len(halves) : -2]
    before = rest[0] if step > 0 else None
    for half, chunk in zip(halves, chunks):
        add_half(step, half, 0, dens_table, a, before, chunk, acc, b)
        before = acc


def last_kernel(step, half, first, dens_table, a, acc_in, chunk, m_hi, m_lo, p, above, below, b):
    add_half(step, half, first, dens_table, a, acc_in, chunk, p, b)
    weigh(below, m_hi, m_lo, 2, p)
    weigh(above, m_hi, m_lo, 0, p)


def margin_kernel(over, hi_out, lo_out):
    rows, tile, _ = over.shape
    for s in range(3):
        for j in range(rows):
            for pair in range(rows // 2):
                at = (s * rows + j) * tile
                lanes = slice(at // LANES * LANES, at // LANES * LANES + LANES)
                v0, v1 = over[2 * pair, :, lanes], over[2 * pair + 1, :, lanes]
                if at % LANES == 0:
                    v1 = pltpu.roll(v1, LANES // 2, 1)
                else:
                    v0 = pltpu.roll(v0, LANES // 2, 1)
                hi, lo = split(jnp.where(low_lanes(tile), v0, v1))
                to = slice(pair * LANES, (pair + 1) * LANES)
                hi_out[s, j * tile : (j + 1) * tile, to] = hi
                lo_out[s, j * tile : (j + 1) * tile, to] = lo


def weigh(out, m_hi, m_lo, s, p):
    for lanes in lane_blocks(p.shape[1]):
        hi, lo = split(p[:, lanes])
        out[:, lanes] = (
            jnp.dot(m_hi[s], hi, preferred_element_type=F32)
            + jnp.dot(m_hi[s], lo, preferred_element_type=F32)
            + jnp.dot(m_lo[s], hi, preferred_element_type=F32)
        )


def own_kernel(m_hi, m_lo, *rest):
    parts, (product, window, term, sems) = rest[:-4], rest[-4:]
    rows, tile, width = product.shape
    step = width // len(parts)
    copies = []

    def start(ref, out, at):
        for q in range(rows):
            copies.append(
                pltpu.make_async_copy(
                    ref.at[pl.ds(q * tile, tile)],
                    out.at[q, :, pl.ds(at, step)],
                    sems.at[len(copies)],
                )
            )
            copies[-1].start()

    for i, part in enumerate(parts):
        start(part, product, i * step)
    for i, part in enumerate(parts):
        weigh(term.at[i], m_hi, m_lo, 1, part)
        start(term.at[i], window, width + i * step)
    for copy in copies:
        copy.wait()


def arrived_kernel(at, above, below, window_in, window, sems):
    rows, tile, triple = window.shape
    copies = [
        pltpu.make_async_copy(
            term.at[pl.ds(q * tile, tile)],
            window.at[q, :, pl.ds(start + at, term.shape[1])],
            sems.at[i, q],
        )
        for i, (term, start) in enumerate(((above, 0), (below, triple // 3 * 2)))
        for q in range(rows)
    ]
    for copy in copies:
        copy.start()
    for copy in copies:
        copy.wait()


def call(kernel, name, out_shape, in_spaces, out_spaces, scratch, aliases=None):
    return pl.pallas_call(
        kernel,
        name=name,
        out_shape=out_shape,
        in_specs=[pl.BlockSpec(memory_space=s) for s in in_spaces],
        out_specs=jax.tree.map(lambda s: pl.BlockSpec(memory_space=s), out_spaces),
        scratch_shapes=scratch,
        input_output_aliases=aliases or {},
        cost_estimate=pl.CostEstimate(flops=1024, bytes_accessed=1024, transcendentals=0),
        compiler_params=pltpu.CompilerParams(vmem_limit_bytes=24 << 20),
    )


def shards(ham_tiles, ham_cols, ham_count, dens_tiles, dens_cols, dens_count, over_tiles):
    count = lax.axis_size("cross")
    rows, tile, _ = ham_tiles.shape
    blocks = rows * count
    width = blocks * tile
    tall = rows * tile
    per_shard = rows // 2
    sds = jax.ShapeDtypeStruct

    halves = [dens_tiles[2 * h : 2 * h + 2] for h in range(per_shard)]
    *halves, dens_cols = lax.optimization_barrier((*halves, dens_cols))
    arrivals = [halves, [pass_on(h, 1) for h in halves]]
    ham_cols, ham_count, dens_cols, dens_count, ham_tiles = (
        pltpu.with_memory_space_constraint(x, pltpu.HBM)
        for x in (ham_cols, ham_count, dens_cols, dens_count, ham_tiles)
    )
    table = call(
        table_kernel,
        "table",
        sds((rows, blocks), jnp.int32),
        (SMEM, SMEM),
        SMEM,
        [],
    )(dens_cols, dens_count)
    tables = [table] + [pass_on(table, step) for step in range(1, count)]
    m_hi, m_lo = call(
        margin_kernel,
        "margin",
        (sds((3, tall, tall), BF16),) * 2,
        (VMEM,),
        (VMEM, VMEM),
        [],
    )(over_tiles)
    a = call(
        ham_kernel,
        "ham",
        sds((blocks // 2, tall, 3 * LANES), BF16),
        (SMEM, SMEM, pltpu.HBM),
        VMEM,
        [
            pltpu.SMEM((rows, blocks), jnp.int32),
            VMEM(ham_tiles.shape, F32),
            pltpu.SemaphoreType.DMA((rows,)),
        ],
    )(ham_cols, ham_count, ham_tiles)

    def add(step, chunks, acc):
        return call(
            functools.partial(add_kernel, step, list(range(len(chunks)))),
            "add%d" % step,
            sds((tall, width), F32),
            (SMEM,) + (VMEM,) * (1 + len(chunks) + (step > 0)),
            VMEM,
            [VMEM((4 * tile, width), BF16)],
        )(tables[step], a, *([acc] if step > 0 else []), *chunks)

    acc = None
    for step in range(1, count - 1):
        now = arrivals[-1]
        if step == 1:
            now[0], a = lax.optimization_barrier((now[0], a))
            now[-1], *tables = lax.optimization_barrier((now[-1], *tables))
        else:
            now[0], acc = lax.optimization_barrier((now[0], acc))
        if step == 2:
            now[-1], m_hi, m_lo = lax.optimization_barrier((now[-1], m_hi, m_lo))
        acc = add(step - 1, arrivals[-2], acc)
        arrivals.append([pass_on(h, 1) for h in now])
    acc = add(count - 2, arrivals[-2], acc)
    acc = add(count - 1, arrivals[-1][:-1], acc)

    sides = 2
    piece = width // sides
    parts, befores, afters = [], [], []
    for side in range(sides):
        part, above, below = call(
            functools.partial(last_kernel, count - 1, per_shard - 1, side * piece),
            "last%d" % side,
            [sds((tall, piece), F32)] * 3,
            (SMEM,) + (VMEM,) * 5,
            [VMEM] * 3,
            [VMEM((4 * tile, piece), BF16)],
        )(tables[-1], a, acc, arrivals[-1][-1], m_hi, m_lo)
        if side + 1 < sides:
            part, acc = lax.optimization_barrier((part, acc))
        parts.append(part)
        befores.append(rotate(below, 1))
        afters.append(rotate(above, -1))
    product, window = call(
        own_kernel,
        "own",
        (sds((rows, tile, width), F32), sds((rows, tile, 3 * width), F32)),
        (VMEM,) * (2 + sides),
        (pl.ANY, pl.ANY),
        [VMEM((sides, tall, piece), F32), pltpu.SemaphoreType.DMA((2 * sides * rows,))],
    )(m_hi, m_lo, *parts)
    for side in range(sides):
        window = call(
            functools.partial(arrived_kernel, side * piece),
            "arrived%d" % side,
            sds((rows, tile, 3 * width), F32),
            (VMEM, VMEM, pl.ANY),
            pl.ANY,
            [pltpu.SemaphoreType.DMA((2, rows))],
            {2: 0},
        )(befores[side], afters[side], window)
    return (product, window)


def solution(mesh):
    whole = P(AXES)
    return jax.shard_map(
        shards,
        mesh=mesh,
        in_specs=(whole,) * 7,
        out_specs=(whole, whole),
        check_vma=False,
    )
```

time: 77.6 us -> 68.2 us (0.88)
  waiting for transfers between devices: 40.4 us -> 31.9 us
  starting transfers between devices: 18.1 us -> 16.6 us
    ppermute x13, waiting for transfers between devices: 40.4 us -> 31.9 us  [permute(): lax.ppermute(x, AXES, [(flat(*place), flat(*target(*place))) for place in...]
    ppermute x13, starting transfers between devices: 18.1 us -> 16.6 us  [permute(): lax.ppermute(x, AXES, [(flat(*place), flat(*target(*place))) for place in...]
    slice x0 -> x1, local copies, waits for them, and re-layouts: none -> 1.14 us  [shards(): halves = [dens_tiles[2 * h:2 * h + 2] for h in range(per_shard)]]
    unnamed x4 -> x2, local copies, waits for them, and re-layouts: 1.14 us -> 0.01 us
    pallas_call x9 -> x8, Pallas kernels: 11 us -> 11.5 us  [the longest x4 6.16 us: add(): call(functools.partial(add_kernel, step, list(range(len(chunks)))), 'add%...]
  transfers between devices with their start and end apart: 13 -> 13, of which waited for: 6 -> 10; matrix products, arithmetic and copies ran while one was open for 0% -> 0% of each run, Pallas kernels for 21% -> 22%
where the time goes in v7:
time: 68.2 us; the launch traced here: 67.7 us
  waiting for transfers between devices  31.9 us (47%)
  Pallas kernels  17.4 us (26%)
  starting transfers between devices  16.6 us (24%)
  local copies, waits for them, and re-layouts  1.14 us (2%)
  between operations  0.76 us (1%)
    ppermute x13, waiting for transfers between devices, permute(): lax.ppermute(x, AXES, [(flat(*place), flat(*target(*place))) for place in...  31.9 us
    ppermute x13, starting transfers between devices, permute(): lax.ppermute(x, AXES, [(flat(*place), flat(*target(*place))) for place in...  16.6 us
    pallas_call x4, Pallas kernels, add(): call(functools.partial(add_kernel, step, list(range(len(chunks)))), 'add%...  6.16 us
    pallas_call x2, Pallas kernels, shards(): call(functools.partial(last_kernel, count - 1, per_shard - 1, side * piec...  3.28 us
    pallas_call x1, Pallas kernels, shards(): call(ham_kernel, 'ham', sds((blocks // 2, tall, 3 * LANES), BF16), (SMEM,...  2.51 us
    pallas_call x2, Pallas kernels, shards(): call(functools.partial(arrived_kernel, side * piece), 'arrived%d' % side,...  2.05 us
    pallas_call x1, Pallas kernels, shards(): call(own_kernel, 'own', (sds((rows, tile, width), F32), sds((rows, tile,...  1.7 us
    pallas_call x1, Pallas kernels, shards(): call(table_kernel, 'table', sds((rows, blocks), jnp.int32), (SMEM, SMEM),...  1.4 us
  transfers between devices with their start and end apart: 13, of which 10 were waited for; matrix products, arithmetic and copies ran while one was open for 0% of the time, Pallas kernels for 22%

profile of v7, /device:TPU:0, one launch (start us, length us, event | category | flops | bytes accessed | tf_op | source)
XLA Modules:
  0.0 67.7 jit_solution(4373085425462976171)
XLA Ops:
  0.6 0.0 copy-start
  0.6 1.1 %fusion = (f32[2,64,512]{2,1,0:T(8,128)S(1)}, f32[2,64,512]{2,1,0:T(8,128)S(1)}) fusion(f32[4,64,512]{2,1,0:T(8,128)} %param.10), kind=kLoop, calls=%fused_computation | loop fusion | bytes 1048576 | tf_op jit(solution)/shard_map/slice | solution.py:244
  1.8 3.1 %collective-permute-start.5 = (f32[2,64,512]{2,1,0:T(8,128)S(1)}, f32[2,64,512]{2,1,0:T(8,128)S(1)}, u32[]{:S(2)}, u32[]{:S(2)}) collective-permute-start(f32[2,64,512]{2,1,0:T(8,128)S(1)} %get-tuple-element.37.rest_0_), channel_id=1, source_target_pairs={{0,1},{1,3},{2,0},{3,2},{4,5},{5,7},{6,4},{7,6},{8,9},{9,11},{10,8... | collective-permute-start | bytes 786440 | tf_op jit(solution)/shard_map/ppermute | solution.py:24
  4.9 2.6 %collective-permute-start = (f32[2,64,512]{2,1,0:T(8,128)S(1)}, f32[2,64,512]{2,1,0:T(8,128)S(1)}, u32[]{:S(2)}, u32[]{:S(2)}) collective-permute-start(f32[2,64,512]{2,1,0:T(8,128)S(1)} %get-tuple-element.29.rest_1_), channel_id=1, source_target_pairs={{0,1},{1,3},{2,0},{3,2},{4,5},{5,7},{6,4},{7,6},{8,9},{9,11},{10,8... | collective-permute-start | bytes 786440 | tf_op jit(solution)/shard_map/ppermute | solution.py:24
  7.4 1.4 %table.1.dens_table = s32[4,16]{1,0:T(4,128)S(1)} custom-call(s32[4,8]{1,0:T(4,128)} %columns, s32[4]{0:T(128)} %counts.1), custom_call_target="tpu_custom_call" | custom-call | flops 1024 | bytes 1024 | tf_op jit(solution)/shard_map/table/pallas_call | solution.py:251
  8.9 0.4 collective-permute-start.3
  9.2 2.5 %collective-permute-start.2 = (s32[4,16]{1,0:T(4,128)S(1)}, s32[4,16]{1,0:T(4,128)S(1)}, u32[]{:S(2)}, u32[]{:S(2)}) collective-permute-start(s32[4,16]{1,0:T(4,128)S(1)} %table.1.dens_table), channel_id=1, source_target_pairs={{0,3},{1,2},{2,1},{3,0},{4,7},{5,6},{6,5},{7,4},{8,11},{9,10},{10,... | collective-permute-start | bytes 776 | tf_op jit(solution)/shard_map/ppermute | solution.py:24
  11.7 0.0 collective-permute-start.1
  11.7 2.5 %ham.2.a = bf16[8,256,384]{2,1,0:T(8,128)(2,1)S(1)} custom-call(s32[4,12]{1,0:T(4,128)} %ham_cols.1, s32[4]{0:T(128)} %ham_count.1, f32[4,64,768]{2,1,0:T(8,128)} %ham.3), custom_call_target="tpu_custom_call" | custom-call | flops 1024 | bytes 1024 | tf_op jit(solution)/shard_map/ham/pallas_call | solution.py:268
  14.2 0.0 collective-permute-done.5.rest_1_
  14.2 2.0 %collective-permute-start.6 = (f32[2,64,512]{2,1,0:T(8,128)S(1)}, f32[2,64,512]{2,1,0:T(8,128)S(1)}, u32[]{:S(2)}, u32[]{:S(2)}) collective-permute-start(f32[2,64,512]{2,1,0:T(8,128)S(1)} %collective-permute-done.5.rest_1_), channel_id=1, source_target_pairs={{0,1},{1,3},{2,0},{3,2},{4,5},{5,7},{6,4},{7,6},{8,9},{9,11},{10,8... | collective-permute-start | bytes 786440 | tf_op jit(solution)/shard_map/ppermute | solution.py:24
  16.2 1.0 %collective-permute-done.3.dens_table = s32[4,16]{1,0:T(4,128)S(1)} collective-permute-done((s32[4,16]{1,0:T(4,128)S(1)}, s32[4,16]{1,0:T(4,128)S(1)}, u32[]{:S(2)}, u32[]{:S(2)}) %collective-permute-start.3) | collective-permute-done | bytes 288 | tf_op jit(solution)/shard_map/ppermute | solution.py:24
  17.2 3.0 %collective-permute-done.2.dens_table = s32[4,16]{1,0:T(4,128)S(1)} collective-permute-done((s32[4,16]{1,0:T(4,128)S(1)}, s32[4,16]{1,0:T(4,128)S(1)}, u32[]{:S(2)}, u32[]{:S(2)}) %collective-permute-start.2) | collective-permute-done | bytes 288 | tf_op jit(solution)/shard_map/ppermute | solution.py:24
  20.2 0.0 collective-permute-done.1.dens_table
  20.2 0.0 collective-permute-done.rest_2_
  20.2 0.6 collective-permute-start.4
  20.8 0.0 copy-done
  20.8 0.3 margin.1
  21.1 1.6 %add0.1.rest_0_ = f32[256,1024]{1,0:T(8,128)S(1)} custom-call(s32[4,16]{1,0:T(4,128)S(1)} %table.1.dens_table, bf16[8,256,384]{2,1,0:T(8,128)(2,1)S(1)} %ham.2.a, f32[2,64,512]{2,1,0:T(8,128)S(1)} %get-tuple-element.37.rest_0_, f32[2,64,512]{2,1,0:T(8,128)S(1)} %get-tuple-element.29.rest_1_), custom_call_target="tpu_custom_call" | custom-call | flops 1024 | bytes 1024 | tf_op jit(solution)/shard_map/add0/pallas_call | solution.py:282
  22.7 1.8 %collective-permute-done.6.rest_1_ = f32[2,64,512]{2,1,0:T(8,128)S(1)} collective-permute-done((f32[2,64,512]{2,1,0:T(8,128)S(1)}, f32[2,64,512]{2,1,0:T(8,128)S(1)}, u32[]{:S(2)}, u32[]{:S(2)}) %collective-permute-start.6) | collective-permute-done | bytes 262176 | tf_op jit(solution)/shard_map/ppermute | solution.py:24
  24.5 1.1 %collective-permute-start.7 = (f32[2,64,512]{2,1,0:T(8,128)S(1)}, f32[2,64,512]{2,1,0:T(8,128)S(1)}, u32[]{:S(2)}, u32[]{:S(2)}) collective-permute-start(f32[2,64,512]{2,1,0:T(8,128)S(1)} %collective-permute-done.6.rest_1_), channel_id=1, source_target_pairs={{0,1},{1,3},{2,0},{3,2},{4,5},{5,7},{6,4},{7,6},{8,9},{9,11},{10,8... | collective-permute-start | bytes 786440 | tf_op jit(solution)/shard_map/ppermute | solution.py:24
  25.6 4.8 %collective-permute-done.4.rest_2_ = f32[2,64,512]{2,1,0:T(8,128)S(1)} collective-permute-done((f32[2,64,512]{2,1,0:T(8,128)S(1)}, f32[2,64,512]{2,1,0:T(8,128)S(1)}, u32[]{:S(2)}, u32[]{:S(2)}) %collective-permute-start.4) | collective-permute-done | bytes 262176 | tf_op jit(solution)/shard_map/ppermute | solution.py:24
  30.4 0.8 %collective-permute-start.8 = (f32[2,64,512]{2,1,0:T(8,128)S(1)}, f32[2,64,512]{2,1,0:T(8,128)S(1)}, u32[]{:S(2)}, u32[]{:S(2)}) collective-permute-start(f32[2,64,512]{2,1,0:T(8,128)S(1)} %collective-permute-done.4.rest_2_), channel_id=1, source_target_pairs={{0,1},{1,3},{2,0},{3,2},{4,5},{5,7},{6,4},{7,6},{8,9},{9,11},{10,8... | collective-permute-start | bytes 786440 | tf_op jit(solution)/shard_map/ppermute | solution.py:24
  31.2 1.6 %add1.1.rest_0_ = f32[256,1024]{1,0:T(8,128)S(1)} custom-call(s32[4,16]{1,0:T(4,128)S(1)} %collective-permute-done.1.dens_table, bf16[8,256,384]{2,1,0:T(8,128)(2,1)S(1)} %ham.2.a, f32[256,1024]{1,0:T(8,128)S(1)} %add0.1.rest_0_, f32[2,64,512]{2,1,0:T(8,128)S(1)} %collective-permute-done.5.rest_1_, f32[2,64,512]{2,1,0:T(8,128)S(1)} %collective-permute-done.rest_2_), custom_call_target="tpu_custom_call" | custom-call | flops 1024 | bytes 1024 | tf_op jit(solution)/shard_map/add1/pallas_call | solution.py:282
  32.8 1.6 %add2.1.rest_0_ = f32[256,1024]{1,0:T(8,128)S(1)} custom-call(s32[4,16]{1,0:T(4,128)S(1)} %collective-permute-done.2.dens_table, bf16[8,256,384]{2,1,0:T(8,128)(2,1)S(1)} %ham.2.a, f32[256,1024]{1,0:T(8,128)S(1)} %add1.1.rest_0_, f32[2,64,512]{2,1,0:T(8,128)S(1)} %collective-permute-done.6.rest_1_, f32[2,64,512]{2,1,0:T(8,128)S(1)} %collective-permute-done.4.rest_2_), custom_call_target="tpu_custom_call" | custom-call | flops 1024 | bytes 1024 | tf_op jit(solution)/shard_map/add2/pallas_call | solution.py:282
  34.5 1.5 %collective-permute-done.7.rest_1_ = f32[2,64,512]{2,1,0:T(8,128)S(1)} collective-permute-done((f32[2,64,512]{2,1,0:T(8,128)S(1)}, f32[2,64,512]{2,1,0:T(8,128)S(1)}, u32[]{:S(2)}, u32[]{:S(2)}) %collective-permute-start.7) | collective-permute-done | bytes 262176 | tf_op jit(solution)/shard_map/ppermute | solution.py:24
  36.0 1.3 %add3.1.acc_in = f32[256,1024]{1,0:T(8,128)S(1)} custom-call(s32[4,16]{1,0:T(4,128)S(1)} %collective-permute-done.3.dens_table, bf16[8,256,384]{2,1,0:T(8,128)(2,1)S(1)} %ham.2.a, f32[256,1024]{1,0:T(8,128)S(1)} %add2.1.rest_0_, f32[2,64,512]{2,1,0:T(8,128)S(1)} %collective-permute-done.7.rest_1_), custom_call_target="tpu_custom_call" | custom-call | flops 1024 | bytes 1024 | tf_op jit(solution)/shard_map/add3/pallas_call | solution.py:282
  37.2 3.2 %collective-permute-done.8.chunk = f32[2,64,512]{2,1,0:T(8,128)S(1)} collective-permute-done((f32[2,64,512]{2,1,0:T(8,128)S(1)}, f32[2,64,512]{2,1,0:T(8,128)S(1)}, u32[]{:S(2)}, u32[]{:S(2)}) %collective-permute-start.8) | collective-permute-done | bytes 262176 | tf_op jit(solution)/shard_map/ppermute | solution.py:24
  40.4 1.6 %last0.1 = (f32[256,512]{1,0:T(8,128)S(1)}, f32[256,512]{1,0:T(8,128)S(1)}, f32[256,512]{1,0:T(8,128)S(1)}) custom-call(s32[4,16]{1,0:T(4,128)S(1)} %collective-permute-done.3.dens_table, bf16[8,256,384]{2,1,0:T(8,128)(2,1)S(1)} %ham.2.a, f32[256,1024]{1,0:T(8,128)S(1)} %add3.1.acc_in, f32[2,64,512]{2,1,0:T(8,128)S(1)} %collective-permute-done.8.chunk, ...), custom_call_target="tpu_custom_call" | custom-call | flops 1024 | bytes 1024 | tf_op jit(solution)/shard_map/last0/pallas_call | solution.py:310
  42.1 0.1 collective-permute-start.11
  42.1 1.7 %collective-permute-start.12 = (f32[256,512]{1,0:T(8,128)S(1)}, f32[256,512]{1,0:T(8,128)S(1)}, u32[]{:S(2)}, u32[]{:S(2)}) collective-permute-start(f32[256,512]{1,0:T(8,128)S(1)} %get-tuple-element.54), channel_id=1, source_target_pairs={{0,12},{1,13},{2,14},{3,15},{4,0},{5,1},{6,2},{7,3},{8,4},{9,5},{1... | collective-permute-start | bytes 1572872 | tf_op jit(solution)/shard_map/ppermute | solution.py:24
  43.9 1.6 %last1.1 = (f32[256,512]{1,0:T(8,128)S(1)}, f32[256,512]{1,0:T(8,128)S(1)}, f32[256,512]{1,0:T(8,128)S(1)}) custom-call(s32[4,16]{1,0:T(4,128)S(1)} %collective-permute-done.3.dens_table, bf16[8,256,384]{2,1,0:T(8,128)(2,1)S(1)} %ham.2.a, f32[256,1024]{1,0:T(8,128)S(1)} %add3.1.acc_in, f32[2,64,512]{2,1,0:T(8,128)S(1)} %collective-permute-done.8.chunk, ...), custom_call_target="tpu_custom_call" | custom-call | flops 1024 | bytes 1024 | tf_op jit(solution)/shard_map/last1/pallas_call | solution.py:310
  45.5 0.1 collective-permute-start.9
  45.6 1.7 %collective-permute-start.10 = (f32[256,512]{1,0:T(8,128)S(1)}, f32[256,512]{1,0:T(8,128)S(1)}, u32[]{:S(2)}, u32[]{:S(2)}) collective-permute-start(f32[256,512]{1,0:T(8,128)S(1)} %get-tuple-element.52), channel_id=1, source_target_pairs={{0,12},{1,13},{2,14},{3,15},{4,0},{5,1},{6,2},{7,3},{8,4},{9,5},{1... | collective-permute-start | bytes 1572872 | tf_op jit(solution)/shard_map/ppermute | solution.py:24
  47.3 1.7 %own.1 = (f32[4,64,1024]{2,1,0:T(8,128)}, f32[4,64,3072]{2,1,0:T(8,128)}) custom-call(bf16[3,256,256]{2,1,0:T(8,128)(2,1)S(1)} %get-tuple-element.34.m_hi, bf16[3,256,256]{2,1,0:T(8,128)(2,1)S(1)} %get-tuple-element.35.m_lo, f32[256,512]{1,0:T(8,128)S(1)} %get-tuple-element.47.rest_0_, f32[256,512]{1,0:T(8,128)S(1)} %get-tuple-element.49.rest_1_), custom_call_target="tpu_custom_call" | custom-call | flops 1024 | bytes 1024 | tf_op jit(solution)/shard_map/own/pallas_call | solution.py:323
  49.0 5.4 %collective-permute-done.11.above = f32[256,512]{1,0:T(8,128)S(1)} collective-permute-done((f32[256,512]{1,0:T(8,128)S(1)}, f32[256,512]{1,0:T(8,128)S(1)}, u32[]{:S(2)}, u32[]{:S(2)}) %collective-permute-start.11) | collective-permute-done | bytes 524320 | tf_op jit(solution)/shard_map/ppermute | solution.py:24
  54.5 1.7 %collective-permute-done.12.below = f32[256,512]{1,0:T(8,128)S(1)} collective-permute-done((f32[256,512]{1,0:T(8,128)S(1)}, f32[256,512]{1,0:T(8,128)S(1)}, u32[]{:S(2)}, u32[]{:S(2)}) %collective-permute-start.12) | collective-permute-done | bytes 524320 | tf_op jit(solution)/shard_map/ppermute | solution.py:24
  56.2 1.0 %arrived0.1.window_in = f32[4,64,3072]{2,1,0:T(8,128)} custom-call(f32[256,512]{1,0:T(8,128)S(1)} %collective-permute-done.11.above, f32[256,512]{1,0:T(8,128)S(1)} %collective-permute-done.12.below, f32[4,64,3072]{2,1,0:T(8,128)} %get-tuple-element.55.window_in), custom_call_target="tpu_custom_call", output_to_operand_aliasing={{}: (2, {})} | custom-call | flops 1024 | bytes 1024 | tf_op jit(solution)/shard_map/arrived0/pallas_call | solution.py:332
  57.2 8.5 %collective-permute-done.9.above = f32[256,512]{1,0:T(8,128)S(1)} collective-permute-done((f32[256,512]{1,0:T(8,128)S(1)}, f32[256,512]{1,0:T(8,128)S(1)}, u32[]{:S(2)}, u32[]{:S(2)}) %collective-permute-start.9) | collective-permute-done | bytes 524320 | tf_op jit(solution)/shard_map/ppermute | solution.py:24
  65.7 1.0 %collective-permute-done.10.below = f32[256,512]{1,0:T(8,128)S(1)} collective-permute-done((f32[256,512]{1,0:T(8,128)S(1)}, f32[256,512]{1,0:T(8,128)S(1)}, u32[]{:S(2)}, u32[]{:S(2)}) %collective-permute-start.10) | collective-permute-done | bytes 524320 | tf_op jit(solution)/shard_map/ppermute | solution.py:24
  66.7 1.0 %arrived1.1 = f32[4,64,3072]{2,1,0:T(8,128)} custom-call(f32[256,512]{1,0:T(8,128)S(1)} %collective-permute-done.9.above, f32[256,512]{1,0:T(8,128)S(1)} %collective-permute-done.10.below, f32[4,64,3072]{2,1,0:T(8,128)} %arrived0.1.window_in), custom_call_target="tpu_custom_call", output_to_operand_aliasing={{}: (2, {})} | custom-call | flops 1024 | bytes 1024 | tf_op jit(solution)/shard_map/arrived1/pallas_call | solution.py:332
Async XLA Ops:
  0.6 20.2 %copy-start = (f32[4,64,768]{2,1,0:T(8,128)S(1)}, f32[4,64,768]{2,1,0:T(8,128)}, u32[]{:S(2)}) copy-start(f32[4,64,768]{2,1,0:T(8,128)} %over.1) | copy-start | bytes 2359300
  1.8 12.5 %collective-permute-start.5 = (f32[2,64,512]{2,1,0:T(8,128)S(1)}, f32[2,64,512]{2,1,0:T(8,128)S(1)}, u32[]{:S(2)}, u32[]{:S(2)}) collective-permute-start(f32[2,64,512]{2,1,0:T(8,128)S(1)} %get-tuple-element.37.rest_0_), channel_id=1, source_target_pairs={{0,1},{1,3},{2,0},{3,2},{4,5},{5,7},{6,4},{7,6},{8,9},{9,11},{10,8... | collective-permute-start | bytes 786440 | tf_op jit(solution)/shard_map/ppermute | solution.py:24
  4.9 15.4 %collective-permute-start = (f32[2,64,512]{2,1,0:T(8,128)S(1)}, f32[2,64,512]{2,1,0:T(8,128)S(1)}, u32[]{:S(2)}, u32[]{:S(2)}) collective-permute-start(f32[2,64,512]{2,1,0:T(8,128)S(1)} %get-tuple-element.29.rest_1_), channel_id=1, source_target_pairs={{0,1},{1,3},{2,0},{3,2},{4,5},{5,7},{6,4},{7,6},{8,9},{9,11},{10,8... | collective-permute-start | bytes 786440 | tf_op jit(solution)/shard_map/ppermute | solution.py:24
  8.9 8.4 %collective-permute-start.3 = (s32[4,16]{1,0:T(4,128)S(1)}, s32[4,16]{1,0:T(4,128)S(1)}, u32[]{:S(2)}, u32[]{:S(2)}) collective-permute-start(s32[4,16]{1,0:T(4,128)S(1)} %table.1.dens_table), channel_id=1, source_target_pairs={{0,2},{1,0},{2,3},{3,1},{4,6},{5,4},{6,7},{7,5},{8,10},{9,8},{10,1... | collective-permute-start | bytes 776 | tf_op jit(solution)/shard_map/ppermute | solution.py:24
  9.2 11.0 %collective-permute-start.2 = (s32[4,16]{1,0:T(4,128)S(1)}, s32[4,16]{1,0:T(4,128)S(1)}, u32[]{:S(2)}, u32[]{:S(2)}) collective-permute-start(s32[4,16]{1,0:T(4,128)S(1)} %table.1.dens_table), channel_id=1, source_target_pairs={{0,3},{1,2},{2,1},{3,0},{4,7},{5,6},{6,5},{7,4},{8,11},{9,10},{10,... | collective-permute-start | bytes 776 | tf_op jit(solution)/shard_map/ppermute | solution.py:24
  11.7 8.5 %collective-permute-start.1 = (s32[4,16]{1,0:T(4,128)S(1)}, s32[4,16]{1,0:T(4,128)S(1)}, u32[]{:S(2)}, u32[]{:S(2)}) collective-permute-start(s32[4,16]{1,0:T(4,128)S(1)} %table.1.dens_table), channel_id=1, source_target_pairs={{0,1},{1,3},{2,0},{3,2},{4,5},{5,7},{6,4},{7,6},{8,9},{9,11},{10,8... | collective-permute-start | bytes 776 | tf_op jit(solution)/shard_map/ppermute | solution.py:24
  14.2 10.2 %collective-permute-start.6 = (f32[2,64,512]{2,1,0:T(8,128)S(1)}, f32[2,64,512]{2,1,0:T(8,128)S(1)}, u32[]{:S(2)}, u32[]{:S(2)}) collective-permute-start(f32[2,64,512]{2,1,0:T(8,128)S(1)} %collective-permute-done.5.rest_1_), channel_id=1, source_target_pairs={{0,1},{1,3},{2,0},{3,2},{4,5},{5,7},{6,4},{7,6},{8,9},{9,11},{10,8... | collective-permute-start | bytes 786440 | tf_op jit(solution)/shard_map/ppermute | solution.py:24
  20.2 10.1 %collective-permute-start.4 = (f32[2,64,512]{2,1,0:T(8,128)S(1)}, f32[2,64,512]{2,1,0:T(8,128)S(1)}, u32[]{:S(2)}, u32[]{:S(2)}) collective-permute-start(f32[2,64,512]{2,1,0:T(8,128)S(1)} %collective-permute-done.rest_2_), channel_id=1, source_target_pairs={{0,1},{1,3},{2,0},{3,2},{4,5},{5,7},{6,4},{7,6},{8,9},{9,11},{10,8... | collective-permute-start | bytes 786440 | tf_op jit(solution)/shard_map/ppermute | solution.py:24
  24.5 11.5 %collective-permute-start.7 = (f32[2,64,512]{2,1,0:T(8,128)S(1)}, f32[2,64,512]{2,1,0:T(8,128)S(1)}, u32[]{:S(2)}, u32[]{:S(2)}) collective-permute-start(f32[2,64,512]{2,1,0:T(8,128)S(1)} %collective-permute-done.6.rest_1_), channel_id=1, source_target_pairs={{0,1},{1,3},{2,0},{3,2},{4,5},{5,7},{6,4},{7,6},{8,9},{9,11},{10,8... | collective-permute-start | bytes 786440 | tf_op jit(solution)/shard_map/ppermute | solution.py:24
  30.4 10.1 %collective-permute-start.8 = (f32[2,64,512]{2,1,0:T(8,128)S(1)}, f32[2,64,512]{2,1,0:T(8,128)S(1)}, u32[]{:S(2)}, u32[]{:S(2)}) collective-permute-start(f32[2,64,512]{2,1,0:T(8,128)S(1)} %collective-permute-done.4.rest_2_), channel_id=1, source_target_pairs={{0,1},{1,3},{2,0},{3,2},{4,5},{5,7},{6,4},{7,6},{8,9},{9,11},{10,8... | collective-permute-start | bytes 786440 | tf_op jit(solution)/shard_map/ppermute | solution.py:24
  42.1 12.4 %collective-permute-start.11 = (f32[256,512]{1,0:T(8,128)S(1)}, f32[256,512]{1,0:T(8,128)S(1)}, u32[]{:S(2)}, u32[]{:S(2)}) collective-permute-start(f32[256,512]{1,0:T(8,128)S(1)} %get-tuple-element.53), channel_id=1, source_target_pairs={{0,4},{1,5},{2,6},{3,7},{4,8},{5,9},{6,10},{7,11},{8,12},{9,13},{1... | collective-permute-start | bytes 1572872 | tf_op jit(solution)/shard_map/ppermute | solution.py:24
  42.1 14.0 %collective-permute-start.12 = (f32[256,512]{1,0:T(8,128)S(1)}, f32[256,512]{1,0:T(8,128)S(1)}, u32[]{:S(2)}, u32[]{:S(2)}) collective-permute-start(f32[256,512]{1,0:T(8,128)S(1)} %get-tuple-element.54), channel_id=1, source_target_pairs={{0,12},{1,13},{2,14},{3,15},{4,0},{5,1},{6,2},{7,3},{8,4},{9,5},{1... | collective-permute-start | bytes 1572872 | tf_op jit(solution)/shard_map/ppermute | solution.py:24
  45.5 20.2 %collective-permute-start.9 = (f32[256,512]{1,0:T(8,128)S(1)}, f32[256,512]{1,0:T(8,128)S(1)}, u32[]{:S(2)}, u32[]{:S(2)}) collective-permute-start(f32[256,512]{1,0:T(8,128)S(1)} %get-tuple-element.51), channel_id=1, source_target_pairs={{0,4},{1,5},{2,6},{3,7},{4,8},{5,9},{6,10},{7,11},{8,12},{9,13},{1... | collective-permute-start | bytes 1572872 | tf_op jit(solution)/shard_map/ppermute | solution.py:24
  45.6 21.1 %collective-permute-start.10 = (f32[256,512]{1,0:T(8,128)S(1)}, f32[256,512]{1,0:T(8,128)S(1)}, u32[]{:S(2)}, u32[]{:S(2)}) collective-permute-start(f32[256,512]{1,0:T(8,128)S(1)} %get-tuple-element.52), channel_id=1, source_target_pairs={{0,12},{1,13},{2,14},{3,15},{4,0},{5,1},{6,2},{7,3},{8,4},{9,5},{1... | collective-permute-start | bytes 1572872 | tf_op jit(solution)/shard_map/ppermute | solution.py:24

commit v8 on v7

--- a/solution.py
+++ b/solution.py
@@ -141,15 +141,54 @@
         before = acc
 
 
-def last_kernel(step, half, first, dens_table, a, acc_in, chunk, m_hi, m_lo, p, above, below, b):
-    add_half(step, half, first, dens_table, a, acc_in, chunk, p, b)
-    weigh(below, m_hi, m_lo, 2, p)
-    weigh(above, m_hi, m_lo, 0, p)
+def pick_kernel(half, dens_table, pick):
+    rows, deep, width = pick.shape
+    here = lax.broadcasted_iota(jnp.int32, (deep, LANES), 0)
+    lane = lax.broadcasted_iota(jnp.int32, (deep, LANES), 1)
+    block = LANES // 2
+    for r in range(rows):
+        for pair in range(width // LANES):
+            codes = [dens_table[2 * half + r, 2 * pair + side] for side in range(2)]
+            wanted = jnp.where(
+                lane < block, codes[0] * block - block, codes[1] * block - LANES
+            )
+            pick[r, :, pair * LANES : (pair + 1) * LANES] = jnp.where(
+                here == lane + wanted, 1.0, 0.0
+            ).astype(BF16)
+
+
+def last_kernel(step, half, first, a, acc_in, chunk, pick, m_hi, m_lo, p, above, below, b):
+    rows, tile, _ = chunk.shape
+    width = p.shape[1]
+    for r in range(rows):
+        hi, lo = split(chunk[r])
+        placed = jnp.dot(
+            jnp.concatenate([hi, lo], axis=0),
+            pick[r, :, first : first + width],
+            preferred_element_type=F32,
+        ).astype(BF16)
+        b[r * tile : (r + 1) * tile, :] = placed[:tile]
+        b[(rows + r) * tile : (rows + r + 1) * tile, :] = placed[tile:]
+    pair = shard_of(step) * (a.shape[0] // lax.axis_size("cross")) + half
+    tall = p.shape[0]
+    both_hi = m_hi[0:2].reshape(2 * tall, tall)
+    both_lo = m_lo[0:2].reshape(2 * tall, tall)
+    for lanes in lane_blocks(width):
+        part = acc_in[:, first + lanes.start : first + lanes.stop] + times_half(a[pair], b, lanes)
+        p[:, lanes] = part
+        hi, lo = split(part)
+        terms = (
+            jnp.dot(both_hi, hi, preferred_element_type=F32)
+            + jnp.dot(both_hi, lo, preferred_element_type=F32)
+            + jnp.dot(both_lo, hi, preferred_element_type=F32)
+        )
+        above[:, lanes] = terms[:tall]
+        below[:, lanes] = terms[tall:]
 
 
 def margin_kernel(over, hi_out, lo_out):
     rows, tile, _ = over.shape
-    for s in range(3):
+    for place, s in enumerate((0, 2, 1)):
         for j in range(rows):
             for pair in range(rows // 2):
                 at = (s * rows + j) * tile
@@ -161,8 +200,8 @@
                     v0 = pltpu.roll(v0, LANES // 2, 1)
                 hi, lo = split(jnp.where(low_lanes(tile), v0, v1))
                 to = slice(pair * LANES, (pair + 1) * LANES)
-                hi_out[s, j * tile : (j + 1) * tile, to] = hi
-                lo_out[s, j * tile : (j + 1) * tile, to] = lo
+                hi_out[place, j * tile : (j + 1) * tile, to] = hi
+                lo_out[place, j * tile : (j + 1) * tile, to] = lo
 
 
 def weigh(out, m_hi, m_lo, s, p):
@@ -178,7 +217,6 @@
 def own_kernel(m_hi, m_lo, *rest):
     parts, (product, window, term, sems) = rest[:-4], rest[-4:]
     rows, tile, width = product.shape
-    step = width // len(parts)
     copies = []
 
     def start(ref, out, at):
@@ -186,17 +224,22 @@
             copies.append(
                 pltpu.make_async_copy(
                     ref.at[pl.ds(q * tile, tile)],
-                    out.at[q, :, pl.ds(at, step)],
+                    out.at[q, :, pl.ds(at, ref.shape[1])],
                     sems.at[len(copies)],
                 )
             )
             copies[-1].start()
 
-    for i, part in enumerate(parts):
-        start(part, product, i * step)
-    for i, part in enumerate(parts):
-        weigh(term.at[i], m_hi, m_lo, 1, part)
-        start(term.at[i], window, width + i * step)
+    at = 0
+    for part in parts:
+        start(part, product, at)
+        at += part.shape[1]
+    at = 0
+    for part in parts:
+        here = term.at[:, pl.ds(at, part.shape[1])]
+        weigh(here, m_hi, m_lo, 2, part)
+        start(here, window, width + at)
+        at += part.shape[1]
     for copy in copies:
         copy.wait()
 
@@ -288,6 +331,7 @@
             [VMEM((4 * tile, width), BF16)],
         )(tables[step], a, *([acc] if step > 0 else []), *chunks)
 
+    pieces = (width // 2, width // 2)
     acc = None
     for step in range(1, count - 1):
         now = arrivals[-1]
@@ -297,25 +341,31 @@
         else:
             now[0], acc = lax.optimization_barrier((now[0], acc))
         if step == 2:
-            now[-1], m_hi, m_lo = lax.optimization_barrier((now[-1], m_hi, m_lo))
+            pick = call(
+                functools.partial(pick_kernel, per_shard - 1),
+                "pick",
+                sds((2, dens_tiles.shape[2], width), BF16),
+                (SMEM,),
+                VMEM,
+                [],
+            )(tables[-1])
+            now[-1], m_hi, m_lo, pick = lax.optimization_barrier((now[-1], m_hi, m_lo, pick))
         acc = add(step - 1, arrivals[-2], acc)
         arrivals.append([pass_on(h, 1) for h in now])
     acc = add(count - 2, arrivals[-2], acc)
     acc = add(count - 1, arrivals[-1][:-1], acc)
 
-    sides = 2
-    piece = width // sides
     parts, befores, afters = [], [], []
-    for side in range(sides):
+    for i, piece in enumerate(pieces):
         part, above, below = call(
-            functools.partial(last_kernel, count - 1, per_shard - 1, side * piece),
-            "last%d" % side,
+            functools.partial(last_kernel, count - 1, per_shard - 1, sum(pieces[:i])),
+            "last%d" % i,
             [sds((tall, piece), F32)] * 3,
-            (SMEM,) + (VMEM,) * 5,
+            (VMEM,) * 6,
             [VMEM] * 3,
             [VMEM((4 * tile, piece), BF16)],
-        )(tables[-1], a, acc, arrivals[-1][-1], m_hi, m_lo)
-        if side + 1 < sides:
+        )(a, acc, arrivals[-1][-1], pick, m_hi, m_lo)
+        if i + 1 < len(pieces):
             part, acc = lax.optimization_barrier((part, acc))
         parts.append(part)
         befores.append(rotate(below, 1))
@@ -324,20 +374,20 @@
         own_kernel,
         "own",
         (sds((rows, tile, width), F32), sds((rows, tile, 3 * width), F32)),
-        (VMEM,) * (2 + sides),
+        (VMEM,) * (2 + len(pieces)),
         (pl.ANY, pl.ANY),
-        [VMEM((sides, tall, piece), F32), pltpu.SemaphoreType.DMA((2 * sides * rows,))],
+        [VMEM((tall, width), F32), pltpu.SemaphoreType.DMA((2 * len(pieces) * rows,))],
     )(m_hi, m_lo, *parts)
-    for side in range(sides):
+    for i in range(len(pieces)):
         window = call(
-            functools.partial(arrived_kernel, side * piece),
-            "arrived%d" % side,
+            functools.partial(arrived_kernel, sum(pieces[:i])),
+            "arrived%d" % i,
             sds((rows, tile, 3 * width), F32),
             (VMEM, VMEM, pl.ANY),
             pl.ANY,
             [pltpu.SemaphoreType.DMA((2, rows))],
             {2: 0},
-        )(befores[side], afters[side], window)
+        )(befores[i], afters[i], window)
     return (product, window)
 
 

time: 68.2 us -> 67.8 us (level)
  waiting for transfers between devices: 31.9 us -> 30.4 us
  starting transfers between devices: 16.6 us -> 17.4 us
    ppermute x13, waiting for transfers between devices: 31.9 us -> 30.4 us  [permute(): lax.ppermute(x, AXES, [(flat(*place), flat(*target(*place))) for place in...]
    ppermute x13, starting transfers between devices: 16.6 us -> 17.4 us  [permute(): lax.ppermute(x, AXES, [(flat(*place), flat(*target(*place))) for place in...]
    pallas_call x4 -> x5, Pallas kernels: 5.32 us -> 5.57 us  [the longest x2 2.4 us: shards(): call(functools.partial(last_kernel, count - 1, per_shard - 1, sum(pieces[...]
  transfers between devices with their start and end apart: 13 -> 13, of which waited for: 10 -> 10; matrix products, arithmetic and copies ran while one was open for 0% -> 0% of each run, Pallas kernels for 22% -> 23%
where the time goes in v8:
time: 67.8 us; the launch traced here: 67.2 us
  waiting for transfers between devices  30.4 us (45%)
  Pallas kernels  17.5 us (26%)
  starting transfers between devices  17.4 us (26%)
  local copies, waits for them, and re-layouts  1.14 us (2%)
  between operations  0.76 us (1%)
    ppermute x13, waiting for transfers between devices, permute(): lax.ppermute(x, AXES, [(flat(*place), flat(*target(*place))) for place in...  30.4 us
    ppermute x13, starting transfers between devices, permute(): lax.ppermute(x, AXES, [(flat(*place), flat(*target(*place))) for place in...  17.4 us
    pallas_call x4, Pallas kernels, add(): call(functools.partial(add_kernel, step, list(range(len(chunks)))), 'add%...  6.11 us
    pallas_call x1, Pallas kernels, shards(): call(ham_kernel, 'ham', sds((blocks // 2, tall, 3 * LANES), BF16), (SMEM,...  2.5 us
    pallas_call x2, Pallas kernels, shards(): call(functools.partial(last_kernel, count - 1, per_shard - 1, sum(pieces[...  2.4 us
    pallas_call x2, Pallas kernels, shards(): call(functools.partial(arrived_kernel, sum(pieces[:i])), 'arrived%d' % i,...  2.05 us
    pallas_call x1, Pallas kernels, shards(): call(own_kernel, 'own', (sds((rows, tile, width), F32), sds((rows, tile,...  1.69 us
    pallas_call x1, Pallas kernels, shards(): call(table_kernel, 'table', sds((rows, blocks), jnp.int32), (SMEM, SMEM),...  1.4 us
  transfers between devices with their start and end apart: 13, of which 10 were waited for; matrix products, arithmetic and copies ran while one was open for 0% of the time, Pallas kernels for 23%

profile of v8, /device:TPU:0, one launch (start us, length us, event | category | flops | bytes accessed | tf_op | source)
XLA Modules:
  0.0 67.2 jit_solution(3137986443544159039)
XLA Ops:
  0.6 0.0 copy-start
  0.6 1.1 %fusion = (f32[2,64,512]{2,1,0:T(8,128)S(1)}, f32[2,64,512]{2,1,0:T(8,128)S(1)}) fusion(f32[4,64,512]{2,1,0:T(8,128)} %param.10), kind=kLoop, calls=%fused_computation | loop fusion | bytes 1048576 | tf_op jit(solution)/shard_map/slice | solution.py:287
  1.8 3.1 %collective-permute-start.5 = (f32[2,64,512]{2,1,0:T(8,128)S(1)}, f32[2,64,512]{2,1,0:T(8,128)S(1)}, u32[]{:S(2)}, u32[]{:S(2)}) collective-permute-start(f32[2,64,512]{2,1,0:T(8,128)S(1)} %get-tuple-element.38.rest_0_), channel_id=1, source_target_pairs={{0,1},{1,3},{2,0},{3,2},{4,5},{5,7},{6,4},{7,6},{8,9},{9,11},{10,8... | collective-permute-start | bytes 786440 | tf_op jit(solution)/shard_map/ppermute | solution.py:24
  4.9 2.6 %collective-permute-start = (f32[2,64,512]{2,1,0:T(8,128)S(1)}, f32[2,64,512]{2,1,0:T(8,128)S(1)}, u32[]{:S(2)}, u32[]{:S(2)}) collective-permute-start(f32[2,64,512]{2,1,0:T(8,128)S(1)} %get-tuple-element.30.rest_1_), channel_id=1, source_target_pairs={{0,1},{1,3},{2,0},{3,2},{4,5},{5,7},{6,4},{7,6},{8,9},{9,11},{10,8... | collective-permute-start | bytes 786440 | tf_op jit(solution)/shard_map/ppermute | solution.py:24
  7.4 1.4 %table.1.dens_table = s32[4,16]{1,0:T(4,128)S(1)} custom-call(s32[4,8]{1,0:T(4,128)} %columns, s32[4]{0:T(128)} %counts.1), custom_call_target="tpu_custom_call" | custom-call | flops 1024 | bytes 1024 | tf_op jit(solution)/shard_map/table/pallas_call | solution.py:294
  8.9 0.4 collective-permute-start.3
  9.2 2.5 %collective-permute-start.2 = (s32[4,16]{1,0:T(4,128)S(1)}, s32[4,16]{1,0:T(4,128)S(1)}, u32[]{:S(2)}, u32[]{:S(2)}) collective-permute-start(s32[4,16]{1,0:T(4,128)S(1)} %table.1.dens_table), channel_id=1, source_target_pairs={{0,3},{1,2},{2,1},{3,0},{4,7},{5,6},{6,5},{7,4},{8,11},{9,10},{10,... | collective-permute-start | bytes 776 | tf_op jit(solution)/shard_map/ppermute | solution.py:24
  11.7 0.0 collective-permute-start.1
  11.7 2.5 %ham.2.a = bf16[8,256,384]{2,1,0:T(8,128)(2,1)S(1)} custom-call(s32[4,12]{1,0:T(4,128)} %ham_cols.1, s32[4]{0:T(128)} %ham_count.1, f32[4,64,768]{2,1,0:T(8,128)} %ham.3), custom_call_target="tpu_custom_call" | custom-call | flops 1024 | bytes 1024 | tf_op jit(solution)/shard_map/ham/pallas_call | solution.py:311
  14.2 0.0 collective-permute-done.5.rest_1_
  14.2 2.0 %collective-permute-start.6 = (f32[2,64,512]{2,1,0:T(8,128)S(1)}, f32[2,64,512]{2,1,0:T(8,128)S(1)}, u32[]{:S(2)}, u32[]{:S(2)}) collective-permute-start(f32[2,64,512]{2,1,0:T(8,128)S(1)} %collective-permute-done.5.rest_1_), channel_id=1, source_target_pairs={{0,1},{1,3},{2,0},{3,2},{4,5},{5,7},{6,4},{7,6},{8,9},{9,11},{10,8... | collective-permute-start | bytes 786440 | tf_op jit(solution)/shard_map/ppermute | solution.py:24
  16.2 1.0 %collective-permute-done.3.dens_table = s32[4,16]{1,0:T(4,128)S(1)} collective-permute-done((s32[4,16]{1,0:T(4,128)S(1)}, s32[4,16]{1,0:T(4,128)S(1)}, u32[]{:S(2)}, u32[]{:S(2)}) %collective-permute-start.3) | collective-permute-done | bytes 288 | tf_op jit(solution)/shard_map/ppermute | solution.py:24
  17.2 3.0 %collective-permute-done.2.dens_table = s32[4,16]{1,0:T(4,128)S(1)} collective-permute-done((s32[4,16]{1,0:T(4,128)S(1)}, s32[4,16]{1,0:T(4,128)S(1)}, u32[]{:S(2)}, u32[]{:S(2)}) %collective-permute-start.2) | collective-permute-done | bytes 288 | tf_op jit(solution)/shard_map/ppermute | solution.py:24
  20.2 0.0 collective-permute-done.1.dens_table
  20.2 0.0 collective-permute-done.rest_2_
  20.2 0.6 collective-permute-start.4
  20.8 0.0 copy-done
  20.8 0.3 margin.1
  21.1 1.1 %pick.1 = bf16[2,512,1024]{2,1,0:T(8,128)(2,1)S(1)} custom-call(s32[4,16]{1,0:T(4,128)S(1)} %collective-permute-done.3.dens_table), custom_call_target="tpu_custom_call" | custom-call | flops 1024 | bytes 1024 | tf_op jit(solution)/shard_map/pick/pallas_call | solution.py:344
  22.2 1.6 %add0.1.rest_0_ = f32[256,1024]{1,0:T(8,128)S(1)} custom-call(s32[4,16]{1,0:T(4,128)S(1)} %table.1.dens_table, bf16[8,256,384]{2,1,0:T(8,128)(2,1)S(1)} %ham.2.a, f32[2,64,512]{2,1,0:T(8,128)S(1)} %get-tuple-element.38.rest_0_, f32[2,64,512]{2,1,0:T(8,128)S(1)} %get-tuple-element.30.rest_1_), custom_call_target="tpu_custom_call" | custom-call | flops 1024 | bytes 1024 | tf_op jit(solution)/shard_map/add0/pallas_call | solution.py:325
  23.8 0.7 %collective-permute-done.6.rest_1_ = f32[2,64,512]{2,1,0:T(8,128)S(1)} collective-permute-done((f32[2,64,512]{2,1,0:T(8,128)S(1)}, f32[2,64,512]{2,1,0:T(8,128)S(1)}, u32[]{:S(2)}, u32[]{:S(2)}) %collective-permute-start.6) | collective-permute-done | bytes 262176 | tf_op jit(solution)/shard_map/ppermute | solution.py:24
  24.5 1.9 %collective-permute-start.7 = (f32[2,64,512]{2,1,0:T(8,128)S(1)}, f32[2,64,512]{2,1,0:T(8,128)S(1)}, u32[]{:S(2)}, u32[]{:S(2)}) collective-permute-start(f32[2,64,512]{2,1,0:T(8,128)S(1)} %collective-permute-done.6.rest_1_), channel_id=1, source_target_pairs={{0,1},{1,3},{2,0},{3,2},{4,5},{5,7},{6,4},{7,6},{8,9},{9,11},{10,8... | collective-permute-start | bytes 786440 | tf_op jit(solution)/shard_map/ppermute | solution.py:24
  26.4 3.9 %collective-permute-done.4.rest_2_ = f32[2,64,512]{2,1,0:T(8,128)S(1)} collective-permute-done((f32[2,64,512]{2,1,0:T(8,128)S(1)}, f32[2,64,512]{2,1,0:T(8,128)S(1)}, u32[]{:S(2)}, u32[]{:S(2)}) %collective-permute-start.4) | collective-permute-done | bytes 262176 | tf_op jit(solution)/shard_map/ppermute | solution.py:24
  30.4 0.8 %collective-permute-start.8 = (f32[2,64,512]{2,1,0:T(8,128)S(1)}, f32[2,64,512]{2,1,0:T(8,128)S(1)}, u32[]{:S(2)}, u32[]{:S(2)}) collective-permute-start(f32[2,64,512]{2,1,0:T(8,128)S(1)} %collective-permute-done.4.rest_2_), channel_id=1, source_target_pairs={{0,1},{1,3},{2,0},{3,2},{4,5},{5,7},{6,4},{7,6},{8,9},{9,11},{10,8... | collective-permute-start | bytes 786440 | tf_op jit(solution)/shard_map/ppermute | solution.py:24
  31.2 1.6 %add1.1.rest_0_ = f32[256,1024]{1,0:T(8,128)S(1)} custom-call(s32[4,16]{1,0:T(4,128)S(1)} %collective-permute-done.1.dens_table, bf16[8,256,384]{2,1,0:T(8,128)(2,1)S(1)} %ham.2.a, f32[256,1024]{1,0:T(8,128)S(1)} %add0.1.rest_0_, f32[2,64,512]{2,1,0:T(8,128)S(1)} %collective-permute-done.5.rest_1_, f32[2,64,512]{2,1,0:T(8,128)S(1)} %collective-permute-done.rest_2_), custom_call_target="tpu_custom_call" | custom-call | flops 1024 | bytes 1024 | tf_op jit(solution)/shard_map/add1/pallas_call | solution.py:325
  32.8 1.6 %add2.1.rest_0_ = f32[256,1024]{1,0:T(8,128)S(1)} custom-call(s32[4,16]{1,0:T(4,128)S(1)} %collective-permute-done.2.dens_table, bf16[8,256,384]{2,1,0:T(8,128)(2,1)S(1)} %ham.2.a, f32[256,1024]{1,0:T(8,128)S(1)} %add1.1.rest_0_, f32[2,64,512]{2,1,0:T(8,128)S(1)} %collective-permute-done.6.rest_1_, f32[2,64,512]{2,1,0:T(8,128)S(1)} %collective-permute-done.4.rest_2_), custom_call_target="tpu_custom_call" | custom-call | flops 1024 | bytes 1024 | tf_op jit(solution)/shard_map/add2/pallas_call | solution.py:325
  34.5 1.5 %collective-permute-done.7.rest_1_ = f32[2,64,512]{2,1,0:T(8,128)S(1)} collective-permute-done((f32[2,64,512]{2,1,0:T(8,128)S(1)}, f32[2,64,512]{2,1,0:T(8,128)S(1)}, u32[]{:S(2)}, u32[]{:S(2)}) %collective-permute-start.7) | collective-permute-done | bytes 262176 | tf_op jit(solution)/shard_map/ppermute | solution.py:24
  36.0 1.2 %add3.1.acc_in = f32[256,1024]{1,0:T(8,128)S(1)} custom-call(s32[4,16]{1,0:T(4,128)S(1)} %collective-permute-done.3.dens_table, bf16[8,256,384]{2,1,0:T(8,128)(2,1)S(1)} %ham.2.a, f32[256,1024]{1,0:T(8,128)S(1)} %add2.1.rest_0_, f32[2,64,512]{2,1,0:T(8,128)S(1)} %collective-permute-done.7.rest_1_), custom_call_target="tpu_custom_call" | custom-call | flops 1024 | bytes 1024 | tf_op jit(solution)/shard_map/add3/pallas_call | solution.py:325
  37.2 3.2 %collective-permute-done.8.chunk = f32[2,64,512]{2,1,0:T(8,128)S(1)} collective-permute-done((f32[2,64,512]{2,1,0:T(8,128)S(1)}, f32[2,64,512]{2,1,0:T(8,128)S(1)}, u32[]{:S(2)}, u32[]{:S(2)}) %collective-permute-start.8) | collective-permute-done | bytes 262176 | tf_op jit(solution)/shard_map/ppermute | solution.py:24
  40.4 1.2 %last0.1 = (f32[256,512]{1,0:T(8,128)S(1)}, f32[256,512]{1,0:T(8,128)S(1)}, f32[256,512]{1,0:T(8,128)S(1)}) custom-call(bf16[8,256,384]{2,1,0:T(8,128)(2,1)S(1)} %ham.2.a, f32[256,1024]{1,0:T(8,128)S(1)} %add3.1.acc_in, f32[2,64,512]{2,1,0:T(8,128)S(1)} %collective-permute-done.8.chunk, bf16[2,512,1024]{2,1,0:T(8,128)(2,1)S(1)} %pick.1, ...), custom_call_target="tpu_custom_call" | custom-call | flops 1024 | bytes 1024 | tf_op jit(solution)/shard_map/last0/pallas_call | solution.py:360
  41.6 0.1 collective-permute-start.11
  41.7 1.7 %collective-permute-start.12 = (f32[256,512]{1,0:T(8,128)S(1)}, f32[256,512]{1,0:T(8,128)S(1)}, u32[]{:S(2)}, u32[]{:S(2)}) collective-permute-start(f32[256,512]{1,0:T(8,128)S(1)} %get-tuple-element.56), channel_id=1, source_target_pairs={{0,12},{1,13},{2,14},{3,15},{4,0},{5,1},{6,2},{7,3},{8,4},{9,5},{1... | collective-permute-start | bytes 1572872 | tf_op jit(solution)/shard_map/ppermute | solution.py:24
  43.4 1.2 %last1.1 = (f32[256,512]{1,0:T(8,128)S(1)}, f32[256,512]{1,0:T(8,128)S(1)}, f32[256,512]{1,0:T(8,128)S(1)}) custom-call(bf16[8,256,384]{2,1,0:T(8,128)(2,1)S(1)} %ham.2.a, f32[256,1024]{1,0:T(8,128)S(1)} %add3.1.acc_in, f32[2,64,512]{2,1,0:T(8,128)S(1)} %collective-permute-done.8.chunk, bf16[2,512,1024]{2,1,0:T(8,128)(2,1)S(1)} %pick.1, ...), custom_call_target="tpu_custom_call" | custom-call | flops 1024 | bytes 1024 | tf_op jit(solution)/shard_map/last1/pallas_call | solution.py:360
  44.7 0.1 collective-permute-start.9
  44.7 1.7 %collective-permute-start.10 = (f32[256,512]{1,0:T(8,128)S(1)}, f32[256,512]{1,0:T(8,128)S(1)}, u32[]{:S(2)}, u32[]{:S(2)}) collective-permute-start(f32[256,512]{1,0:T(8,128)S(1)} %get-tuple-element.54), channel_id=1, source_target_pairs={{0,12},{1,13},{2,14},{3,15},{4,0},{5,1},{6,2},{7,3},{8,4},{9,5},{1... | collective-permute-start | bytes 1572872 | tf_op jit(solution)/shard_map/ppermute | solution.py:24
  46.5 1.7 %own.1 = (f32[4,64,1024]{2,1,0:T(8,128)}, f32[4,64,3072]{2,1,0:T(8,128)}) custom-call(bf16[3,256,256]{2,1,0:T(8,128)(2,1)S(1)} %get-tuple-element.36.m_hi, bf16[3,256,256]{2,1,0:T(8,128)(2,1)S(1)} %get-tuple-element.37.m_lo, f32[256,512]{1,0:T(8,128)S(1)} %get-tuple-element.49.rest_0_, f32[256,512]{1,0:T(8,128)S(1)} %get-tuple-element.51.rest_1_), custom_call_target="tpu_custom_call" | custom-call | flops 1024 | bytes 1024 | tf_op jit(solution)/shard_map/own/pallas_call | solution.py:373
  48.2 5.9 %collective-permute-done.11.above = f32[256,512]{1,0:T(8,128)S(1)} collective-permute-done((f32[256,512]{1,0:T(8,128)S(1)}, f32[256,512]{1,0:T(8,128)S(1)}, u32[]{:S(2)}, u32[]{:S(2)}) %collective-permute-start.11) | collective-permute-done | bytes 524320 | tf_op jit(solution)/shard_map/ppermute | solution.py:24
  54.0 1.7 %collective-permute-done.12.below = f32[256,512]{1,0:T(8,128)S(1)} collective-permute-done((f32[256,512]{1,0:T(8,128)S(1)}, f32[256,512]{1,0:T(8,128)S(1)}, u32[]{:S(2)}, u32[]{:S(2)}) %collective-permute-start.12) | collective-permute-done | bytes 524320 | tf_op jit(solution)/shard_map/ppermute | solution.py:24
  55.7 1.0 %arrived0.1.window_in = f32[4,64,3072]{2,1,0:T(8,128)} custom-call(f32[256,512]{1,0:T(8,128)S(1)} %collective-permute-done.11.above, f32[256,512]{1,0:T(8,128)S(1)} %collective-permute-done.12.below, f32[4,64,3072]{2,1,0:T(8,128)} %get-tuple-element.57.window_in), custom_call_target="tpu_custom_call", output_to_operand_aliasing={{}: (2, {})} | custom-call | flops 1024 | bytes 1024 | tf_op jit(solution)/shard_map/arrived0/pallas_call | solution.py:382
  56.8 8.5 %collective-permute-done.9.above = f32[256,512]{1,0:T(8,128)S(1)} collective-permute-done((f32[256,512]{1,0:T(8,128)S(1)}, f32[256,512]{1,0:T(8,128)S(1)}, u32[]{:S(2)}, u32[]{:S(2)}) %collective-permute-start.9) | collective-permute-done | bytes 524320 | tf_op jit(solution)/shard_map/ppermute | solution.py:24
  65.3 1.0 %collective-permute-done.10.below = f32[256,512]{1,0:T(8,128)S(1)} collective-permute-done((f32[256,512]{1,0:T(8,128)S(1)}, f32[256,512]{1,0:T(8,128)S(1)}, u32[]{:S(2)}, u32[]{:S(2)}) %collective-permute-start.10) | collective-permute-done | bytes 524320 | tf_op jit(solution)/shard_map/ppermute | solution.py:24
  66.2 1.0 %arrived1.1 = f32[4,64,3072]{2,1,0:T(8,128)} custom-call(f32[256,512]{1,0:T(8,128)S(1)} %collective-permute-done.9.above, f32[256,512]{1,0:T(8,128)S(1)} %collective-permute-done.10.below, f32[4,64,3072]{2,1,0:T(8,128)} %arrived0.1.window_in), custom_call_target="tpu_custom_call", output_to_operand_aliasing={{}: (2, {})} | custom-call | flops 1024 | bytes 1024 | tf_op jit(solution)/shard_map/arrived1/pallas_call | solution.py:382
Async XLA Ops:
  0.6 20.2 %copy-start = (f32[4,64,768]{2,1,0:T(8,128)S(1)}, f32[4,64,768]{2,1,0:T(8,128)}, u32[]{:S(2)}) copy-start(f32[4,64,768]{2,1,0:T(8,128)} %over.1) | copy-start | bytes 2359300
  1.8 12.5 %collective-permute-start.5 = (f32[2,64,512]{2,1,0:T(8,128)S(1)}, f32[2,64,512]{2,1,0:T(8,128)S(1)}, u32[]{:S(2)}, u32[]{:S(2)}) collective-permute-start(f32[2,64,512]{2,1,0:T(8,128)S(1)} %get-tuple-element.38.rest_0_), channel_id=1, source_target_pairs={{0,1},{1,3},{2,0},{3,2},{4,5},{5,7},{6,4},{7,6},{8,9},{9,11},{10,8... | collective-permute-start | bytes 786440 | tf_op jit(solution)/shard_map/ppermute | solution.py:24
  4.9 15.4 %collective-permute-start = (f32[2,64,512]{2,1,0:T(8,128)S(1)}, f32[2,64,512]{2,1,0:T(8,128)S(1)}, u32[]{:S(2)}, u32[]{:S(2)}) collective-permute-start(f32[2,64,512]{2,1,0:T(8,128)S(1)} %get-tuple-element.30.rest_1_), channel_id=1, source_target_pairs={{0,1},{1,3},{2,0},{3,2},{4,5},{5,7},{6,4},{7,6},{8,9},{9,11},{10,8... | collective-permute-start | bytes 786440 | tf_op jit(solution)/shard_map/ppermute | solution.py:24
  8.9 8.4 %collective-permute-start.3 = (s32[4,16]{1,0:T(4,128)S(1)}, s32[4,16]{1,0:T(4,128)S(1)}, u32[]{:S(2)}, u32[]{:S(2)}) collective-permute-start(s32[4,16]{1,0:T(4,128)S(1)} %table.1.dens_table), channel_id=1, source_target_pairs={{0,2},{1,0},{2,3},{3,1},{4,6},{5,4},{6,7},{7,5},{8,10},{9,8},{10,1... | collective-permute-start | bytes 776 | tf_op jit(solution)/shard_map/ppermute | solution.py:24
  9.2 11.0 %collective-permute-start.2 = (s32[4,16]{1,0:T(4,128)S(1)}, s32[4,16]{1,0:T(4,128)S(1)}, u32[]{:S(2)}, u32[]{:S(2)}) collective-permute-start(s32[4,16]{1,0:T(4,128)S(1)} %table.1.dens_table), channel_id=1, source_target_pairs={{0,3},{1,2},{2,1},{3,0},{4,7},{5,6},{6,5},{7,4},{8,11},{9,10},{10,... | collective-permute-start | bytes 776 | tf_op jit(solution)/shard_map/ppermute | solution.py:24
  11.7 8.5 %collective-permute-start.1 = (s32[4,16]{1,0:T(4,128)S(1)}, s32[4,16]{1,0:T(4,128)S(1)}, u32[]{:S(2)}, u32[]{:S(2)}) collective-permute-start(s32[4,16]{1,0:T(4,128)S(1)} %table.1.dens_table), channel_id=1, source_target_pairs={{0,1},{1,3},{2,0},{3,2},{4,5},{5,7},{6,4},{7,6},{8,9},{9,11},{10,8... | collective-permute-start | bytes 776 | tf_op jit(solution)/shard_map/ppermute | solution.py:24
  14.2 10.2 %collective-permute-start.6 = (f32[2,64,512]{2,1,0:T(8,128)S(1)}, f32[2,64,512]{2,1,0:T(8,128)S(1)}, u32[]{:S(2)}, u32[]{:S(2)}) collective-permute-start(f32[2,64,512]{2,1,0:T(8,128)S(1)} %collective-permute-done.5.rest_1_), channel_id=1, source_target_pairs={{0,1},{1,3},{2,0},{3,2},{4,5},{5,7},{6,4},{7,6},{8,9},{9,11},{10,8... | collective-permute-start | bytes 786440 | tf_op jit(solution)/shard_map/ppermute | solution.py:24
  20.2 10.1 %collective-permute-start.4 = (f32[2,64,512]{2,1,0:T(8,128)S(1)}, f32[2,64,512]{2,1,0:T(8,128)S(1)}, u32[]{:S(2)}, u32[]{:S(2)}) collective-permute-start(f32[2,64,512]{2,1,0:T(8,128)S(1)} %collective-permute-done.rest_2_), channel_id=1, source_target_pairs={{0,1},{1,3},{2,0},{3,2},{4,5},{5,7},{6,4},{7,6},{8,9},{9,11},{10,8... | collective-permute-start | bytes 786440 | tf_op jit(solution)/shard_map/ppermute | solution.py:24
  24.5 11.5 %collective-permute-start.7 = (f32[2,64,512]{2,1,0:T(8,128)S(1)}, f32[2,64,512]{2,1,0:T(8,128)S(1)}, u32[]{:S(2)}, u32[]{:S(2)}) collective-permute-start(f32[2,64,512]{2,1,0:T(8,128)S(1)} %collective-permute-done.6.rest_1_), channel_id=1, source_target_pairs={{0,1},{1,3},{2,0},{3,2},{4,5},{5,7},{6,4},{7,6},{8,9},{9,11},{10,8... | collective-permute-start | bytes 786440 | tf_op jit(solution)/shard_map/ppermute | solution.py:24
  30.4 10.1 %collective-permute-start.8 = (f32[2,64,512]{2,1,0:T(8,128)S(1)}, f32[2,64,512]{2,1,0:T(8,128)S(1)}, u32[]{:S(2)}, u32[]{:S(2)}) collective-permute-start(f32[2,64,512]{2,1,0:T(8,128)S(1)} %collective-permute-done.4.rest_2_), channel_id=1, source_target_pairs={{0,1},{1,3},{2,0},{3,2},{4,5},{5,7},{6,4},{7,6},{8,9},{9,11},{10,8... | collective-permute-start | bytes 786440 | tf_op jit(solution)/shard_map/ppermute | solution.py:24
  41.6 12.4 %collective-permute-start.11 = (f32[256,512]{1,0:T(8,128)S(1)}, f32[256,512]{1,0:T(8,128)S(1)}, u32[]{:S(2)}, u32[]{:S(2)}) collective-permute-start(f32[256,512]{1,0:T(8,128)S(1)} %get-tuple-element.55), channel_id=1, source_target_pairs={{0,4},{1,5},{2,6},{3,7},{4,8},{5,9},{6,10},{7,11},{8,12},{9,13},{1... | collective-permute-start | bytes 1572872 | tf_op jit(solution)/shard_map/ppermute | solution.py:24
  41.7 14.0 %collective-permute-start.12 = (f32[256,512]{1,0:T(8,128)S(1)}, f32[256,512]{1,0:T(8,128)S(1)}, u32[]{:S(2)}, u32[]{:S(2)}) collective-permute-start(f32[256,512]{1,0:T(8,128)S(1)} %get-tuple-element.56), channel_id=1, source_target_pairs={{0,12},{1,13},{2,14},{3,15},{4,0},{5,1},{6,2},{7,3},{8,4},{9,5},{1... | collective-permute-start | bytes 1572872 | tf_op jit(solution)/shard_map/ppermute | solution.py:24
  44.7 20.6 %collective-permute-start.9 = (f32[256,512]{1,0:T(8,128)S(1)}, f32[256,512]{1,0:T(8,128)S(1)}, u32[]{:S(2)}, u32[]{:S(2)}) collective-permute-start(f32[256,512]{1,0:T(8,128)S(1)} %get-tuple-element.53), channel_id=1, source_target_pairs={{0,4},{1,5},{2,6},{3,7},{4,8},{5,9},{6,10},{7,11},{8,12},{9,13},{1... | collective-permute-start | bytes 1572872 | tf_op jit(solution)/shard_map/ppermute | solution.py:24
  44.7 21.5 %collective-permute-start.10 = (f32[256,512]{1,0:T(8,128)S(1)}, f32[256,512]{1,0:T(8,128)S(1)}, u32[]{:S(2)}, u32[]{:S(2)}) collective-permute-start(f32[256,512]{1,0:T(8,128)S(1)} %get-tuple-element.54), channel_id=1, source_target_pairs={{0,12},{1,13},{2,14},{3,15},{4,0},{5,1},{6,2},{7,3},{8,4},{9,5},{1... | collective-permute-start | bytes 1572872 | tf_op jit(solution)/shard_map/ppermute | solution.py:24

commit v9 on v8

--- a/solution.py
+++ b/solution.py
@@ -57,6 +57,18 @@
             @pl.when(slot < counts[r])
             def _(r=r, slot=slot):
                 table[r, columns[r, slot]] = slot + 1
+
+
+def cut_kernel(dens, *rest):
+    halves, sems = rest[:-1], rest[-1]
+    copies = [
+        pltpu.make_async_copy(dens.at[pl.ds(2 * h, 2)], half, sems.at[h])
+        for h, half in enumerate(halves)
+    ]
+    for copy in copies:
+        copy.start()
+    for copy in copies:
+        copy.wait()
 
 
 def table_kernel(columns, counts, table):
@@ -284,7 +296,14 @@
     per_shard = rows // 2
     sds = jax.ShapeDtypeStruct
 
-    halves = [dens_tiles[2 * h : 2 * h + 2] for h in range(per_shard)]
+    halves = call(
+        cut_kernel,
+        "cut",
+        [sds((2, tile, dens_tiles.shape[2]), F32)] * per_shard,
+        (pltpu.HBM,),
+        [VMEM] * per_shard,
+        [pltpu.SemaphoreType.DMA((per_shard,))],
+    )(pltpu.with_memory_space_constraint(dens_tiles, pltpu.HBM))
     *halves, dens_cols = lax.optimization_barrier((*halves, dens_cols))
     arrivals = [halves, [pass_on(h, 1) for h in halves]]
     ham_cols, ham_count, dens_cols, dens_count, ham_tiles = (
@@ -331,7 +350,7 @@
             [VMEM((4 * tile, width), BF16)],
         )(tables[step], a, *([acc] if step > 0 else []), *chunks)
 
-    pieces = (width // 2, width // 2)
+    pieces = (width // 4,) * 4
     acc = None
     for step in range(1, count - 1):
         now = arrivals[-1]

time: 67.8 us -> 67.3 us (level)
  waiting for transfers between devices: 30.4 us -> 23.8 us
  Pallas kernels: 17.5 us -> 21.2 us
  starting transfers between devices: 17.4 us -> 20.9 us
  local copies, waits for them, and re-layouts: 1.14 us -> 0.01 us
    ppermute x13 -> x17, waiting for transfers between devices: 30.4 us -> 23.8 us  [permute(): lax.ppermute(x, AXES, [(flat(*place), flat(*target(*place))) for place in...]
    ppermute x13 -> x17, starting transfers between devices: 17.4 us -> 20.9 us  [permute(): lax.ppermute(x, AXES, [(flat(*place), flat(*target(*place))) for place in...]
    pallas_call x2 -> x4, Pallas kernels: 2.05 us -> 3.4 us  [shards(): call(functools.partial(arrived_kernel, sum(pieces[:i])), 'arrived%d' % i,...]
    pallas_call x2 -> x4, Pallas kernels: 2.4 us -> 3.56 us  [shards(): call(functools.partial(last_kernel, count - 1, per_shard - 1, sum(pieces[...]
    slice x1 -> x0, local copies, waits for them, and re-layouts: 1.14 us -> none  [shards(): halves = [dens_tiles[2 * h:2 * h + 2] for h in range(per_shard)]]
    pallas_call x0 -> x1, Pallas kernels: none -> 1.12 us  [shards(): call(cut_kernel, 'cut', [sds((2, tile, dens_tiles.shape[2]), F32)] * per_...]
  transfers between devices with their start and end apart: 13 -> 17, of which waited for: 10 -> 11; matrix products, arithmetic and copies ran while one was open for 0% -> 0% of each run, Pallas kernels for 23% -> 27%
where the time goes in v9:
time: 67.3 us; the launch traced here: 66.7 us
  waiting for transfers between devices  23.8 us (35%)
  Pallas kernels  21.2 us (32%)
  starting transfers between devices  20.9 us (31%)
  between operations  0.83 us (1%)
    ppermute x17, waiting for transfers between devices, permute(): lax.ppermute(x, AXES, [(flat(*place), flat(*target(*place))) for place in...  23.8 us
    ppermute x17, starting transfers between devices, permute(): lax.ppermute(x, AXES, [(flat(*place), flat(*target(*place))) for place in...  20.9 us
    pallas_call x4, Pallas kernels, add(): call(functools.partial(add_kernel, step, list(range(len(chunks)))), 'add%...  6.15 us
    pallas_call x4, Pallas kernels, shards(): call(functools.partial(last_kernel, count - 1, per_shard - 1, sum(pieces[...  3.56 us
    pallas_call x4, Pallas kernels, shards(): call(functools.partial(arrived_kernel, sum(pieces[:i])), 'arrived%d' % i,...  3.4 us
    pallas_call x1, Pallas kernels, shards(): call(ham_kernel, 'ham', sds((blocks // 2, tall, 3 * LANES), BF16), (SMEM,...  2.51 us
    pallas_call x1, Pallas kernels, shards(): call(own_kernel, 'own', (sds((rows, tile, width), F32), sds((rows, tile,...  1.66 us
    pallas_call x1, Pallas kernels, shards(): call(table_kernel, 'table', sds((rows, blocks), jnp.int32), (SMEM, SMEM),...  1.4 us
  transfers between devices with their start and end apart: 17, of which 11 were waited for; matrix products, arithmetic and copies ran while one was open for 0% of the time, Pallas kernels for 27%

profile of v9, /device:TPU:0, one launch (start us, length us, event | category | flops | bytes accessed | tf_op | source)
XLA Modules:
  0.0 66.7 jit_solution(15166266749098890687)
XLA Ops:
  0.6 1.1 %cut.1 = (f32[2,64,512]{2,1,0:T(8,128)S(1)}, f32[2,64,512]{2,1,0:T(8,128)S(1)}) custom-call(f32[4,64,512]{2,1,0:T(8,128)} %dens.1), custom_call_target="tpu_custom_call" | custom-call | flops 1024 | bytes 1024 | tf_op jit(solution)/shard_map/cut/pallas_call | solution.py:299
  1.8 3.1 %collective-permute-start.5 = (f32[2,64,512]{2,1,0:T(8,128)S(1)}, f32[2,64,512]{2,1,0:T(8,128)S(1)}, u32[]{:S(2)}, u32[]{:S(2)}) collective-permute-start(f32[2,64,512]{2,1,0:T(8,128)S(1)} %get-tuple-element.52.rest_0_), channel_id=1, source_target_pairs={{0,1},{1,3},{2,0},{3,2},{4,5},{5,7},{6,4},{7,6},{8,9},{9,11},{10,8... | collective-permute-start | bytes 786440 | tf_op jit(solution)/shard_map/ppermute | solution.py:24
  4.8 2.6 %collective-permute-start = (f32[2,64,512]{2,1,0:T(8,128)S(1)}, f32[2,64,512]{2,1,0:T(8,128)S(1)}, u32[]{:S(2)}, u32[]{:S(2)}) collective-permute-start(f32[2,64,512]{2,1,0:T(8,128)S(1)} %get-tuple-element.44.rest_1_), channel_id=1, source_target_pairs={{0,1},{1,3},{2,0},{3,2},{4,5},{5,7},{6,4},{7,6},{8,9},{9,11},{10,8... | collective-permute-start | bytes 786440 | tf_op jit(solution)/shard_map/ppermute | solution.py:24
  7.4 1.4 %table.1.dens_table = s32[4,16]{1,0:T(4,128)S(1)} custom-call(s32[4,8]{1,0:T(4,128)} %columns, s32[4]{0:T(128)} %counts.1), custom_call_target="tpu_custom_call" | custom-call | flops 1024 | bytes 1024 | tf_op jit(solution)/shard_map/table/pallas_call | solution.py:313
  8.8 0.4 collective-permute-start.3
  9.2 2.5 %collective-permute-start.2 = (s32[4,16]{1,0:T(4,128)S(1)}, s32[4,16]{1,0:T(4,128)S(1)}, u32[]{:S(2)}, u32[]{:S(2)}) collective-permute-start(s32[4,16]{1,0:T(4,128)S(1)} %table.1.dens_table), channel_id=1, source_target_pairs={{0,3},{1,2},{2,1},{3,0},{4,7},{5,6},{6,5},{7,4},{8,11},{9,10},{10,... | collective-permute-start | bytes 776 | tf_op jit(solution)/shard_map/ppermute | solution.py:24
  11.7 0.0 collective-permute-start.1
  11.7 2.5 %ham.2.a = bf16[8,256,384]{2,1,0:T(8,128)(2,1)S(1)} custom-call(s32[4,12]{1,0:T(4,128)} %ham_cols.1, s32[4]{0:T(128)} %ham_count.1, f32[4,64,768]{2,1,0:T(8,128)} %ham.3), custom_call_target="tpu_custom_call" | custom-call | flops 1024 | bytes 1024 | tf_op jit(solution)/shard_map/ham/pallas_call | solution.py:330
  14.2 0.0 collective-permute-done.5.rest_1_
  14.2 2.0 %collective-permute-start.6 = (f32[2,64,512]{2,1,0:T(8,128)S(1)}, f32[2,64,512]{2,1,0:T(8,128)S(1)}, u32[]{:S(2)}, u32[]{:S(2)}) collective-permute-start(f32[2,64,512]{2,1,0:T(8,128)S(1)} %collective-permute-done.5.rest_1_), channel_id=1, source_target_pairs={{0,1},{1,3},{2,0},{3,2},{4,5},{5,7},{6,4},{7,6},{8,9},{9,11},{10,8... | collective-permute-start | bytes 786440 | tf_op jit(solution)/shard_map/ppermute | solution.py:24
  16.2 1.0 %collective-permute-done.3.dens_table = s32[4,16]{1,0:T(4,128)S(1)} collective-permute-done((s32[4,16]{1,0:T(4,128)S(1)}, s32[4,16]{1,0:T(4,128)S(1)}, u32[]{:S(2)}, u32[]{:S(2)}) %collective-permute-start.3) | collective-permute-done | bytes 288 | tf_op jit(solution)/shard_map/ppermute | solution.py:24
  17.2 3.0 %collective-permute-done.2.dens_table = s32[4,16]{1,0:T(4,128)S(1)} collective-permute-done((s32[4,16]{1,0:T(4,128)S(1)}, s32[4,16]{1,0:T(4,128)S(1)}, u32[]{:S(2)}, u32[]{:S(2)}) %collective-permute-start.2) | collective-permute-done | bytes 288 | tf_op jit(solution)/shard_map/ppermute | solution.py:24
  20.2 0.6 collective-permute-start.4
  20.8 0.3 margin.1
  21.1 1.1 %pick.1 = bf16[2,512,1024]{2,1,0:T(8,128)(2,1)S(1)} custom-call(s32[4,16]{1,0:T(4,128)S(1)} %collective-permute-done.3.dens_table), custom_call_target="tpu_custom_call" | custom-call | flops 1024 | bytes 1024 | tf_op jit(solution)/shard_map/pick/pallas_call | solution.py:363
  22.2 1.6 %add0.1.rest_0_ = f32[256,1024]{1,0:T(8,128)S(1)} custom-call(s32[4,16]{1,0:T(4,128)S(1)} %table.1.dens_table, bf16[8,256,384]{2,1,0:T(8,128)(2,1)S(1)} %ham.2.a, f32[2,64,512]{2,1,0:T(8,128)S(1)} %get-tuple-element.52.rest_0_, f32[2,64,512]{2,1,0:T(8,128)S(1)} %get-tuple-element.44.rest_1_), custom_call_target="tpu_custom_call" | custom-call | flops 1024 | bytes 1024 | tf_op jit(solution)/shard_map/add0/pallas_call | solution.py:344
  23.8 0.7 collective-permute-done.6.rest_1_
  24.5 1.9 %collective-permute-start.7 = (f32[2,64,512]{2,1,0:T(8,128)S(1)}, f32[2,64,512]{2,1,0:T(8,128)S(1)}, u32[]{:S(2)}, u32[]{:S(2)}) collective-permute-start(f32[2,64,512]{2,1,0:T(8,128)S(1)} %collective-permute-done.6.rest_1_), channel_id=1, source_target_pairs={{0,1},{1,3},{2,0},{3,2},{4,5},{5,7},{6,4},{7,6},{8,9},{9,11},{10,8... | collective-permute-start | bytes 786440 | tf_op jit(solution)/shard_map/ppermute | solution.py:24
  26.4 3.9 %collective-permute-done.4.rest_2_ = f32[2,64,512]{2,1,0:T(8,128)S(1)} collective-permute-done((f32[2,64,512]{2,1,0:T(8,128)S(1)}, f32[2,64,512]{2,1,0:T(8,128)S(1)}, u32[]{:S(2)}, u32[]{:S(2)}) %collective-permute-start.4) | collective-permute-done | bytes 262176 | tf_op jit(solution)/shard_map/ppermute | solution.py:24
  30.3 0.8 %collective-permute-start.8 = (f32[2,64,512]{2,1,0:T(8,128)S(1)}, f32[2,64,512]{2,1,0:T(8,128)S(1)}, u32[]{:S(2)}, u32[]{:S(2)}) collective-permute-start(f32[2,64,512]{2,1,0:T(8,128)S(1)} %collective-permute-done.4.rest_2_), channel_id=1, source_target_pairs={{0,1},{1,3},{2,0},{3,2},{4,5},{5,7},{6,4},{7,6},{8,9},{9,11},{10,8... | collective-permute-start | bytes 786440 | tf_op jit(solution)/shard_map/ppermute | solution.py:24
  31.2 1.6 %add1.1.rest_0_ = f32[256,1024]{1,0:T(8,128)S(1)} custom-call(s32[4,16]{1,0:T(4,128)S(1)} %collective-permute-done.1.dens_table, bf16[8,256,384]{2,1,0:T(8,128)(2,1)S(1)} %ham.2.a, f32[256,1024]{1,0:T(8,128)S(1)} %add0.1.rest_0_, f32[2,64,512]{2,1,0:T(8,128)S(1)} %collective-permute-done.5.rest_1_, f32[2,64,512]{2,1,0:T(8,128)S(1)} %collective-permute-done.rest_2_), custom_call_target="tpu_custom_call" | custom-call | flops 1024 | bytes 1024 | tf_op jit(solution)/shard_map/add1/pallas_call | solution.py:344
  32.8 1.7 %add2.1.rest_0_ = f32[256,1024]{1,0:T(8,128)S(1)} custom-call(s32[4,16]{1,0:T(4,128)S(1)} %collective-permute-done.2.dens_table, bf16[8,256,384]{2,1,0:T(8,128)(2,1)S(1)} %ham.2.a, f32[256,1024]{1,0:T(8,128)S(1)} %add1.1.rest_0_, f32[2,64,512]{2,1,0:T(8,128)S(1)} %collective-permute-done.6.rest_1_, f32[2,64,512]{2,1,0:T(8,128)S(1)} %collective-permute-done.4.rest_2_), custom_call_target="tpu_custom_call" | custom-call | flops 1024 | bytes 1024 | tf_op jit(solution)/shard_map/add2/pallas_call | solution.py:344
  34.5 1.5 %collective-permute-done.7.rest_1_ = f32[2,64,512]{2,1,0:T(8,128)S(1)} collective-permute-done((f32[2,64,512]{2,1,0:T(8,128)S(1)}, f32[2,64,512]{2,1,0:T(8,128)S(1)}, u32[]{:S(2)}, u32[]{:S(2)}) %collective-permute-start.7) | collective-permute-done | bytes 262176 | tf_op jit(solution)/shard_map/ppermute | solution.py:24
  36.0 1.2 %add3.1.acc_in = f32[256,1024]{1,0:T(8,128)S(1)} custom-call(s32[4,16]{1,0:T(4,128)S(1)} %collective-permute-done.3.dens_table, bf16[8,256,384]{2,1,0:T(8,128)(2,1)S(1)} %ham.2.a, f32[256,1024]{1,0:T(8,128)S(1)} %add2.1.rest_0_, f32[2,64,512]{2,1,0:T(8,128)S(1)} %collective-permute-done.7.rest_1_), custom_call_target="tpu_custom_call" | custom-call | flops 1024 | bytes 1024 | tf_op jit(solution)/shard_map/add3/pallas_call | solution.py:344
  37.2 3.2 %collective-permute-done.8.chunk = f32[2,64,512]{2,1,0:T(8,128)S(1)} collective-permute-done((f32[2,64,512]{2,1,0:T(8,128)S(1)}, f32[2,64,512]{2,1,0:T(8,128)S(1)}, u32[]{:S(2)}, u32[]{:S(2)}) %collective-permute-start.8) | collective-permute-done | bytes 262176 | tf_op jit(solution)/shard_map/ppermute | solution.py:24
  40.4 0.9 %last0.1 = (f32[256,256]{1,0:T(8,128)S(1)}, f32[256,256]{1,0:T(8,128)S(1)}, f32[256,256]{1,0:T(8,128)S(1)}) custom-call(bf16[8,256,384]{2,1,0:T(8,128)(2,1)S(1)} %ham.2.a, f32[256,1024]{1,0:T(8,128)S(1)} %add3.1.acc_in, f32[2,64,512]{2,1,0:T(8,128)S(1)} %collective-permute-done.8.chunk, bf16[2,512,1024]{2,1,0:T(8,128)(2,1)S(1)} %pick.1, ...), custom_call_target="tpu_custom_call" | custom-call | flops 1024 | bytes 1024 | tf_op jit(solution)/shard_map/last0/pallas_call | solution.py:379
  41.3 0.1 collective-permute-start.15
  41.4 1.7 %collective-permute-start.16 = (f32[256,256]{1,0:T(8,128)S(1)}, f32[256,256]{1,0:T(8,128)S(1)}, u32[]{:S(2)}, u32[]{:S(2)}) collective-permute-start(f32[256,256]{1,0:T(8,128)S(1)} %get-tuple-element.80), channel_id=1, source_target_pairs={{0,12},{1,13},{2,14},{3,15},{4,0},{5,1},{6,2},{7,3},{8,4},{9,5},{1... | collective-permute-start | bytes 786440 | tf_op jit(solution)/shard_map/ppermute | solution.py:24
  43.1 0.9 %last1.1 = (f32[256,256]{1,0:T(8,128)S(1)}, f32[256,256]{1,0:T(8,128)S(1)}, f32[256,256]{1,0:T(8,128)S(1)}) custom-call(bf16[8,256,384]{2,1,0:T(8,128)(2,1)S(1)} %ham.2.a, f32[256,1024]{1,0:T(8,128)S(1)} %add3.1.acc_in, f32[2,64,512]{2,1,0:T(8,128)S(1)} %collective-permute-done.8.chunk, bf16[2,512,1024]{2,1,0:T(8,128)(2,1)S(1)} %pick.1, ...), custom_call_target="tpu_custom_call" | custom-call | flops 1024 | bytes 1024 | tf_op jit(solution)/shard_map/last1/pallas_call | solution.py:379
  44.0 0.1 collective-permute-start.13
  44.1 1.7 %collective-permute-start.14 = (f32[256,256]{1,0:T(8,128)S(1)}, f32[256,256]{1,0:T(8,128)S(1)}, u32[]{:S(2)}, u32[]{:S(2)}) collective-permute-start(f32[256,256]{1,0:T(8,128)S(1)} %get-tuple-element.78), channel_id=1, source_target_pairs={{0,12},{1,13},{2,14},{3,15},{4,0},{5,1},{6,2},{7,3},{8,4},{9,5},{1... | collective-permute-start | bytes 786440 | tf_op jit(solution)/shard_map/ppermute | solution.py:24
  45.8 0.9 %last2.1 = (f32[256,256]{1,0:T(8,128)S(1)}, f32[256,256]{1,0:T(8,128)S(1)}, f32[256,256]{1,0:T(8,128)S(1)}) custom-call(bf16[8,256,384]{2,1,0:T(8,128)(2,1)S(1)} %ham.2.a, f32[256,1024]{1,0:T(8,128)S(1)} %add3.1.acc_in, f32[2,64,512]{2,1,0:T(8,128)S(1)} %collective-permute-done.8.chunk, bf16[2,512,1024]{2,1,0:T(8,128)(2,1)S(1)} %pick.1, ...), custom_call_target="tpu_custom_call" | custom-call | flops 1024 | bytes 1024 | tf_op jit(solution)/shard_map/last2/pallas_call | solution.py:379
  46.7 0.9 %last3.1 = (f32[256,256]{1,0:T(8,128)S(1)}, f32[256,256]{1,0:T(8,128)S(1)}, f32[256,256]{1,0:T(8,128)S(1)}) custom-call(bf16[8,256,384]{2,1,0:T(8,128)(2,1)S(1)} %ham.2.a, f32[256,1024]{1,0:T(8,128)S(1)} %add3.1.acc_in, f32[2,64,512]{2,1,0:T(8,128)S(1)} %collective-permute-done.8.chunk, bf16[2,512,1024]{2,1,0:T(8,128)(2,1)S(1)} %pick.1, ...), custom_call_target="tpu_custom_call" | custom-call | flops 1024 | bytes 1024 | tf_op jit(solution)/shard_map/last3/pallas_call | solution.py:379
  47.6 0.1 collective-permute-start.9
  47.7 0.4 collective-permute-done.15.above
  48.1 1.2 %collective-permute-start.11 = (f32[256,256]{1,0:T(8,128)S(1)}, f32[256,256]{1,0:T(8,128)S(1)}, u32[]{:S(2)}, u32[]{:S(2)}) collective-permute-start(f32[256,256]{1,0:T(8,128)S(1)} %get-tuple-element.75), channel_id=1, source_target_pairs={{0,4},{1,5},{2,6},{3,7},{4,8},{5,9},{6,10},{7,11},{8,12},{9,13},{1... | collective-permute-start | bytes 786440 | tf_op jit(solution)/shard_map/ppermute | solution.py:24
  49.3 0.5 collective-permute-done.16.below
  49.8 2.2 %collective-permute-start.12 = (f32[256,256]{1,0:T(8,128)S(1)}, f32[256,256]{1,0:T(8,128)S(1)}, u32[]{:S(2)}, u32[]{:S(2)}) collective-permute-start(f32[256,256]{1,0:T(8,128)S(1)} %get-tuple-element.76), channel_id=1, source_target_pairs={{0,12},{1,13},{2,14},{3,15},{4,0},{5,1},{6,2},{7,3},{8,4},{9,5},{1... | collective-permute-start | bytes 786440 | tf_op jit(solution)/shard_map/ppermute | solution.py:24
  52.0 1.7 %collective-permute-done.13.above = f32[256,256]{1,0:T(8,128)S(1)} collective-permute-done((f32[256,256]{1,0:T(8,128)S(1)}, f32[256,256]{1,0:T(8,128)S(1)}, u32[]{:S(2)}, u32[]{:S(2)}) %collective-permute-start.13) | collective-permute-done | bytes 262176 | tf_op jit(solution)/shard_map/ppermute | solution.py:24
  53.7 0.0 collective-permute-start.10
  53.7 1.7 %own.1 = (f32[4,64,1024]{2,1,0:T(8,128)}, f32[4,64,3072]{2,1,0:T(8,128)}) custom-call(bf16[3,256,256]{2,1,0:T(8,128)(2,1)S(1)} %get-tuple-element.50.m_hi, bf16[3,256,256]{2,1,0:T(8,128)(2,1)S(1)} %get-tuple-element.51.m_lo, f32[256,256]{1,0:T(8,128)S(1)} %get-tuple-element.63.rest_0_, f32[256,256]{1,0:T(8,128)S(1)} %get-tuple-element.66.rest_1_, ...), custom_call_target="tpu_custom_call" | custom-call | flops 1024 | bytes 1024 | tf_op jit(solution)/shard_map/own/pallas_call | solution.py:392
  55.4 0.9 %arrived0.1.window_in = f32[4,64,3072]{2,1,0:T(8,128)} custom-call(f32[256,256]{1,0:T(8,128)S(1)} %collective-permute-done.15.above, f32[256,256]{1,0:T(8,128)S(1)} %collective-permute-done.16.below, f32[4,64,3072]{2,1,0:T(8,128)} %get-tuple-element.81.window_in), custom_call_target="tpu_custom_call", output_to_operand_aliasing={{}: (2, {})} | custom-call | flops 1024 | bytes 1024 | tf_op jit(solution)/shard_map/arrived0/pallas_call | solution.py:401
  56.2 0.9 %arrived1.1.window_in = f32[4,64,3072]{2,1,0:T(8,128)} custom-call(f32[256,256]{1,0:T(8,128)S(1)} %collective-permute-done.13.above, f32[256,256]{1,0:T(8,128)S(1)} %collective-permute-done.14.below, f32[4,64,3072]{2,1,0:T(8,128)} %arrived0.1.window_in), custom_call_target="tpu_custom_call", output_to_operand_aliasing={{}: (2, {})} | custom-call | flops 1024 | bytes 1024 | tf_op jit(solution)/shard_map/arrived1/pallas_call | solution.py:401
  57.1 7.8 %collective-permute-done.11.above = f32[256,256]{1,0:T(8,128)S(1)} collective-permute-done((f32[256,256]{1,0:T(8,128)S(1)}, f32[256,256]{1,0:T(8,128)S(1)}, u32[]{:S(2)}, u32[]{:S(2)}) %collective-permute-start.11) | collective-permute-done | bytes 262176 | tf_op jit(solution)/shard_map/ppermute | solution.py:24
  64.9 0.0 collective-permute-done.12.below
  64.9 0.8 %arrived2.1.window_in = f32[4,64,3072]{2,1,0:T(8,128)} custom-call(f32[256,256]{1,0:T(8,128)S(1)} %collective-permute-done.11.above, f32[256,256]{1,0:T(8,128)S(1)} %collective-permute-done.12.below, f32[4,64,3072]{2,1,0:T(8,128)} %arrived1.1.window_in), custom_call_target="tpu_custom_call", output_to_operand_aliasing={{}: (2, {})} | custom-call | flops 1024 | bytes 1024 | tf_op jit(solution)/shard_map/arrived2/pallas_call | solution.py:401
  65.8 0.1 collective-permute-done.10.below
  65.9 0.8 %arrived3.1 = f32[4,64,3072]{2,1,0:T(8,128)} custom-call(f32[256,256]{1,0:T(8,128)S(1)} %collective-permute-done.9.above, f32[256,256]{1,0:T(8,128)S(1)} %collective-permute-done.10.below, f32[4,64,3072]{2,1,0:T(8,128)} %arrived2.1.window_in), custom_call_target="tpu_custom_call", output_to_operand_aliasing={{}: (2, {})} | custom-call | flops 1024 | bytes 1024 | tf_op jit(solution)/shard_map/arrived3/pallas_call | solution.py:401
  (6 shorter events, 0.0 us)
Async XLA Ops:
  0.6 20.2 %copy-start = (f32[4,64,768]{2,1,0:T(8,128)S(1)}, f32[4,64,768]{2,1,0:T(8,128)}, u32[]{:S(2)}) copy-start(f32[4,64,768]{2,1,0:T(8,128)} %over.1) | copy-start | bytes 2359300
  1.8 12.5 %collective-permute-start.5 = (f32[2,64,512]{2,1,0:T(8,128)S(1)}, f32[2,64,512]{2,1,0:T(8,128)S(1)}, u32[]{:S(2)}, u32[]{:S(2)}) collective-permute-start(f32[2,64,512]{2,1,0:T(8,128)S(1)} %get-tuple-element.52.rest_0_), channel_id=1, source_target_pairs={{0,1},{1,3},{2,0},{3,2},{4,5},{5,7},{6,4},{7,6},{8,9},{9,11},{10,8... | collective-permute-start | bytes 786440 | tf_op jit(solution)/shard_map/ppermute | solution.py:24
  4.8 15.4 %collective-permute-start = (f32[2,64,512]{2,1,0:T(8,128)S(1)}, f32[2,64,512]{2,1,0:T(8,128)S(1)}, u32[]{:S(2)}, u32[]{:S(2)}) collective-permute-start(f32[2,64,512]{2,1,0:T(8,128)S(1)} %get-tuple-element.44.rest_1_), channel_id=1, source_target_pairs={{0,1},{1,3},{2,0},{3,2},{4,5},{5,7},{6,4},{7,6},{8,9},{9,11},{10,8... | collective-permute-start | bytes 786440 | tf_op jit(solution)/shard_map/ppermute | solution.py:24
  8.8 8.4 %collective-permute-start.3 = (s32[4,16]{1,0:T(4,128)S(1)}, s32[4,16]{1,0:T(4,128)S(1)}, u32[]{:S(2)}, u32[]{:S(2)}) collective-permute-start(s32[4,16]{1,0:T(4,128)S(1)} %table.1.dens_table), channel_id=1, source_target_pairs={{0,2},{1,0},{2,3},{3,1},{4,6},{5,4},{6,7},{7,5},{8,10},{9,8},{10,1... | collective-permute-start | bytes 776 | tf_op jit(solution)/shard_map/ppermute | solution.py:24
  9.2 11.0 %collective-permute-start.2 = (s32[4,16]{1,0:T(4,128)S(1)}, s32[4,16]{1,0:T(4,128)S(1)}, u32[]{:S(2)}, u32[]{:S(2)}) collective-permute-start(s32[4,16]{1,0:T(4,128)S(1)} %table.1.dens_table), channel_id=1, source_target_pairs={{0,3},{1,2},{2,1},{3,0},{4,7},{5,6},{6,5},{7,4},{8,11},{9,10},{10,... | collective-permute-start | bytes 776 | tf_op jit(solution)/shard_map/ppermute | solution.py:24
  11.7 8.5 %collective-permute-start.1 = (s32[4,16]{1,0:T(4,128)S(1)}, s32[4,16]{1,0:T(4,128)S(1)}, u32[]{:S(2)}, u32[]{:S(2)}) collective-permute-start(s32[4,16]{1,0:T(4,128)S(1)} %table.1.dens_table), channel_id=1, source_target_pairs={{0,1},{1,3},{2,0},{3,2},{4,5},{5,7},{6,4},{7,6},{8,9},{9,11},{10,8... | collective-permute-start | bytes 776 | tf_op jit(solution)/shard_map/ppermute | solution.py:24
  14.2 10.2 %collective-permute-start.6 = (f32[2,64,512]{2,1,0:T(8,128)S(1)}, f32[2,64,512]{2,1,0:T(8,128)S(1)}, u32[]{:S(2)}, u32[]{:S(2)}) collective-permute-start(f32[2,64,512]{2,1,0:T(8,128)S(1)} %collective-permute-done.5.rest_1_), channel_id=1, source_target_pairs={{0,1},{1,3},{2,0},{3,2},{4,5},{5,7},{6,4},{7,6},{8,9},{9,11},{10,8... | collective-permute-start | bytes 786440 | tf_op jit(solution)/shard_map/ppermute | solution.py:24
  20.2 10.1 %collective-permute-start.4 = (f32[2,64,512]{2,1,0:T(8,128)S(1)}, f32[2,64,512]{2,1,0:T(8,128)S(1)}, u32[]{:S(2)}, u32[]{:S(2)}) collective-permute-start(f32[2,64,512]{2,1,0:T(8,128)S(1)} %collective-permute-done.rest_2_), channel_id=1, source_target_pairs={{0,1},{1,3},{2,0},{3,2},{4,5},{5,7},{6,4},{7,6},{8,9},{9,11},{10,8... | collective-permute-start | bytes 786440 | tf_op jit(solution)/shard_map/ppermute | solution.py:24
  24.5 11.5 %collective-permute-start.7 = (f32[2,64,512]{2,1,0:T(8,128)S(1)}, f32[2,64,512]{2,1,0:T(8,128)S(1)}, u32[]{:S(2)}, u32[]{:S(2)}) collective-permute-start(f32[2,64,512]{2,1,0:T(8,128)S(1)} %collective-permute-done.6.rest_1_), channel_id=1, source_target_pairs={{0,1},{1,3},{2,0},{3,2},{4,5},{5,7},{6,4},{7,6},{8,9},{9,11},{10,8... | collective-permute-start | bytes 786440 | tf_op jit(solution)/shard_map/ppermute | solution.py:24
  30.3 10.1 %collective-permute-start.8 = (f32[2,64,512]{2,1,0:T(8,128)S(1)}, f32[2,64,512]{2,1,0:T(8,128)S(1)}, u32[]{:S(2)}, u32[]{:S(2)}) collective-permute-start(f32[2,64,512]{2,1,0:T(8,128)S(1)} %collective-permute-done.4.rest_2_), channel_id=1, source_target_pairs={{0,1},{1,3},{2,0},{3,2},{4,5},{5,7},{6,4},{7,6},{8,9},{9,11},{10,8... | collective-permute-start | bytes 786440 | tf_op jit(solution)/shard_map/ppermute | solution.py:24
  41.3 6.8 %collective-permute-start.15 = (f32[256,256]{1,0:T(8,128)S(1)}, f32[256,256]{1,0:T(8,128)S(1)}, u32[]{:S(2)}, u32[]{:S(2)}) collective-permute-start(f32[256,256]{1,0:T(8,128)S(1)} %get-tuple-element.79), channel_id=1, source_target_pairs={{0,4},{1,5},{2,6},{3,7},{4,8},{5,9},{6,10},{7,11},{8,12},{9,13},{1... | collective-permute-start | bytes 786440 | tf_op jit(solution)/shard_map/ppermute | solution.py:24
  41.4 8.4 %collective-permute-start.16 = (f32[256,256]{1,0:T(8,128)S(1)}, f32[256,256]{1,0:T(8,128)S(1)}, u32[]{:S(2)}, u32[]{:S(2)}) collective-permute-start(f32[256,256]{1,0:T(8,128)S(1)} %get-tuple-element.80), channel_id=1, source_target_pairs={{0,12},{1,13},{2,14},{3,15},{4,0},{5,1},{6,2},{7,3},{8,4},{9,5},{1... | collective-permute-start | bytes 786440 | tf_op jit(solution)/shard_map/ppermute | solution.py:24
  44.0 9.7 %collective-permute-start.13 = (f32[256,256]{1,0:T(8,128)S(1)}, f32[256,256]{1,0:T(8,128)S(1)}, u32[]{:S(2)}, u32[]{:S(2)}) collective-permute-start(f32[256,256]{1,0:T(8,128)S(1)} %get-tuple-element.77), channel_id=1, source_target_pairs={{0,4},{1,5},{2,6},{3,7},{4,8},{5,9},{6,10},{7,11},{8,12},{9,13},{1... | collective-permute-start | bytes 786440 | tf_op jit(solution)/shard_map/ppermute | solution.py:24
  44.1 12.1 %collective-permute-start.14 = (f32[256,256]{1,0:T(8,128)S(1)}, f32[256,256]{1,0:T(8,128)S(1)}, u32[]{:S(2)}, u32[]{:S(2)}) collective-permute-start(f32[256,256]{1,0:T(8,128)S(1)} %get-tuple-element.78), channel_id=1, source_target_pairs={{0,12},{1,13},{2,14},{3,15},{4,0},{5,1},{6,2},{7,3},{8,4},{9,5},{1... | collective-permute-start | bytes 786440 | tf_op jit(solution)/shard_map/ppermute | solution.py:24
  47.6 18.2 %collective-permute-start.9 = (f32[256,256]{1,0:T(8,128)S(1)}, f32[256,256]{1,0:T(8,128)S(1)}, u32[]{:S(2)}, u32[]{:S(2)}) collective-permute-start(f32[256,256]{1,0:T(8,128)S(1)} %get-tuple-element.73), channel_id=1, source_target_pairs={{0,4},{1,5},{2,6},{3,7},{4,8},{5,9},{6,10},{7,11},{8,12},{9,13},{1... | collective-permute-start | bytes 786440 | tf_op jit(solution)/shard_map/ppermute | solution.py:24
  48.1 16.9 %collective-permute-start.11 = (f32[256,256]{1,0:T(8,128)S(1)}, f32[256,256]{1,0:T(8,128)S(1)}, u32[]{:S(2)}, u32[]{:S(2)}) collective-permute-start(f32[256,256]{1,0:T(8,128)S(1)} %get-tuple-element.75), channel_id=1, source_target_pairs={{0,4},{1,5},{2,6},{3,7},{4,8},{5,9},{6,10},{7,11},{8,12},{9,13},{1... | collective-permute-start | bytes 786440 | tf_op jit(solution)/shard_map/ppermute | solution.py:24
  49.8 15.1 %collective-permute-start.12 = (f32[256,256]{1,0:T(8,128)S(1)}, f32[256,256]{1,0:T(8,128)S(1)}, u32[]{:S(2)}, u32[]{:S(2)}) collective-permute-start(f32[256,256]{1,0:T(8,128)S(1)} %get-tuple-element.76), channel_id=1, source_target_pairs={{0,12},{1,13},{2,14},{3,15},{4,0},{5,1},{6,2},{7,3},{8,4},{9,5},{1... | collective-permute-start | bytes 786440 | tf_op jit(solution)/shard_map/ppermute | solution.py:24
  53.7 12.2 %collective-permute-start.10 = (f32[256,256]{1,0:T(8,128)S(1)}, f32[256,256]{1,0:T(8,128)S(1)}, u32[]{:S(2)}, u32[]{:S(2)}) collective-permute-start(f32[256,256]{1,0:T(8,128)S(1)} %get-tuple-element.74), channel_id=1, source_target_pairs={{0,12},{1,13},{2,14},{3,15},{4,0},{5,1},{6,2},{7,3},{8,4},{9,5},{1... | collective-permute-start | bytes 786440 | tf_op jit(solution)/shard_map/ppermute | solution.py:24

commit v10 on v9

--- a/solution.py
+++ b/solution.py
@@ -169,7 +169,7 @@
             ).astype(BF16)
 
 
-def last_kernel(step, half, first, a, acc_in, chunk, pick, m_hi, m_lo, p, above, below, b):
+def last_kernel(step, half, first, a, acc_in, chunk, pick, m_hi, m_lo, p, below, b):
     rows, tile, _ = chunk.shape
     width = p.shape[1]
     for r in range(rows):
@@ -182,25 +182,24 @@
         b[r * tile : (r + 1) * tile, :] = placed[:tile]
         b[(rows + r) * tile : (rows + r + 1) * tile, :] = placed[tile:]
     pair = shard_of(step) * (a.shape[0] // lax.axis_size("cross")) + half
-    tall = p.shape[0]
-    both_hi = m_hi[0:2].reshape(2 * tall, tall)
-    both_lo = m_lo[0:2].reshape(2 * tall, tall)
     for lanes in lane_blocks(width):
         part = acc_in[:, first + lanes.start : first + lanes.stop] + times_half(a[pair], b, lanes)
         p[:, lanes] = part
-        hi, lo = split(part)
-        terms = (
-            jnp.dot(both_hi, hi, preferred_element_type=F32)
-            + jnp.dot(both_hi, lo, preferred_element_type=F32)
-            + jnp.dot(both_lo, hi, preferred_element_type=F32)
-        )
-        above[:, lanes] = terms[:tall]
-        below[:, lanes] = terms[tall:]
+        weigh(below.at[:, lanes], m_hi, m_lo, 2, part)
+
+
+def above_kernel(count, m_hi, m_lo, *rest):
+    parts, outs = rest[:count], rest[count:]
+    step = parts[0].shape[1]
+    per_out = outs[0].shape[1] // step
+    for i, part in enumerate(parts):
+        lanes = pl.ds(i % per_out * step, step)
+        weigh(outs[i // per_out].at[:, lanes], m_hi, m_lo, 0, part[...])
 
 
 def margin_kernel(over, hi_out, lo_out):
     rows, tile, _ = over.shape
-    for place, s in enumerate((0, 2, 1)):
+    for s in range(3):
         for j in range(rows):
             for pair in range(rows // 2):
                 at = (s * rows + j) * tile
@@ -212,18 +211,17 @@
                     v0 = pltpu.roll(v0, LANES // 2, 1)
                 hi, lo = split(jnp.where(low_lanes(tile), v0, v1))
                 to = slice(pair * LANES, (pair + 1) * LANES)
-                hi_out[place, j * tile : (j + 1) * tile, to] = hi
-                lo_out[place, j * tile : (j + 1) * tile, to] = lo
+                hi_out[s, j * tile : (j + 1) * tile, to] = hi
+                lo_out[s, j * tile : (j + 1) * tile, to] = lo
 
 
 def weigh(out, m_hi, m_lo, s, p):
-    for lanes in lane_blocks(p.shape[1]):
-        hi, lo = split(p[:, lanes])
-        out[:, lanes] = (
-            jnp.dot(m_hi[s], hi, preferred_element_type=F32)
-            + jnp.dot(m_hi[s], lo, preferred_element_type=F32)
-            + jnp.dot(m_lo[s], hi, preferred_element_type=F32)
-        )
+    hi, lo = split(p)
+    out[...] = (
+        jnp.dot(m_hi[s], hi, preferred_element_type=F32)
+        + jnp.dot(m_hi[s], lo, preferred_element_type=F32)
+        + jnp.dot(m_lo[s], hi, preferred_element_type=F32)
+    )
 
 
 def own_kernel(m_hi, m_lo, *rest):
@@ -249,26 +247,28 @@
     at = 0
     for part in parts:
         here = term.at[:, pl.ds(at, part.shape[1])]
-        weigh(here, m_hi, m_lo, 2, part)
+        weigh(here, m_hi, m_lo, 1, part[...])
         start(here, window, width + at)
         at += part.shape[1]
     for copy in copies:
         copy.wait()
 
 
-def arrived_kernel(at, above, below, window_in, window, sems):
-    rows, tile, triple = window.shape
-    copies = [
-        pltpu.make_async_copy(
-            term.at[pl.ds(q * tile, tile)],
-            window.at[q, :, pl.ds(start + at, term.shape[1])],
-            sems.at[i, q],
-        )
-        for i, (term, start) in enumerate(((above, 0), (below, triple // 3 * 2)))
-        for q in range(rows)
-    ]
-    for copy in copies:
-        copy.start()
+def arrived_kernel(at, count, *rest):
+    terms, (window_in, window, sems) = rest[:count], rest[count:]
+    rows, tile, _ = window.shape
+    copies = []
+    for term in terms:
+        for q in range(rows):
+            copies.append(
+                pltpu.make_async_copy(
+                    term.at[pl.ds(q * tile, tile)],
+                    window.at[q, :, pl.ds(at, term.shape[1])],
+                    sems.at[len(copies)],
+                )
+            )
+            copies[-1].start()
+        at += term.shape[1]
     for copy in copies:
         copy.wait()
 
@@ -350,7 +350,7 @@
             [VMEM((4 * tile, width), BF16)],
         )(tables[step], a, *([acc] if step > 0 else []), *chunks)
 
-    pieces = (width // 4,) * 4
+    pieces = (width // 2,) * 2
     acc = None
     for step in range(1, count - 1):
         now = arrivals[-1]
@@ -374,21 +374,32 @@
     acc = add(count - 2, arrivals[-2], acc)
     acc = add(count - 1, arrivals[-1][:-1], acc)
 
-    parts, befores, afters = [], [], []
+    parts, befores = [], []
     for i, piece in enumerate(pieces):
-        part, above, below = call(
+        part, below = call(
             functools.partial(last_kernel, count - 1, per_shard - 1, sum(pieces[:i])),
             "last%d" % i,
-            [sds((tall, piece), F32)] * 3,
+            [sds((tall, piece), F32)] * 2,
             (VMEM,) * 6,
-            [VMEM] * 3,
+            [VMEM] * 2,
             [VMEM((4 * tile, piece), BF16)],
         )(a, acc, arrivals[-1][-1], pick, m_hi, m_lo)
         if i + 1 < len(pieces):
             part, acc = lax.optimization_barrier((part, acc))
         parts.append(part)
         befores.append(rotate(below, 1))
-        afters.append(rotate(above, -1))
+    outs = 2
+    above = call(
+        functools.partial(above_kernel, len(parts)),
+        "above",
+        [sds((tall, width // outs), F32)] * outs,
+        (VMEM,) * (2 + len(parts)),
+        [VMEM] * outs,
+        [],
+    )(m_hi, m_lo, *parts)
+    above = list(above)
+    above[0], *befores[:-1] = lax.optimization_barrier((above[0], *befores[:-1]))
+    afters = [rotate(term, -1) for term in above]
     product, window = call(
         own_kernel,
         "own",
@@ -397,16 +408,18 @@
         (pl.ANY, pl.ANY),
         [VMEM((tall, width), F32), pltpu.SemaphoreType.DMA((2 * len(pieces) * rows,))],
     )(m_hi, m_lo, *parts)
-    for i in range(len(pieces)):
+    arrived = [(0, befores)]
+    arrived += [(2 * width + i * (width // outs), [term]) for i, term in enumerate(afters)]
+    for i, (at, terms) in enumerate(arrived):
         window = call(
-            functools.partial(arrived_kernel, sum(pieces[:i])),
+            functools.partial(arrived_kernel, at, len(terms)),
             "arrived%d" % i,
             sds((rows, tile, 3 * width), F32),
-            (VMEM, VMEM, pl.ANY),
+            (VMEM,) * len(terms) + (pl.ANY,),
             pl.ANY,
-            [pltpu.SemaphoreType.DMA((2, rows))],
-            {2: 0},
-        )(befores[i], afters[i], window)
+            [pltpu.SemaphoreType.DMA((len(terms) * rows,))],
+            {len(terms): 0},
+        )(*terms, window)
     return (product, window)
 
 

time: 67.3 us -> 67.5 us (level)
  waiting for transfers between devices: 23.8 us -> 29.2 us
  starting transfers between devices: 20.9 us -> 17.2 us
  Pallas kernels: 21.2 us -> 19.8 us
    ppermute x17 -> x13, waiting for transfers between devices: 23.8 us -> 29.2 us  [permute(): lax.ppermute(x, AXES, [(flat(*place), flat(*target(*place))) for place in...]
    ppermute x17 -> x13, starting transfers between devices: 20.9 us -> 17.2 us  [permute(): lax.ppermute(x, AXES, [(flat(*place), flat(*target(*place))) for place in...]
    pallas_call x4 -> x2, Pallas kernels: 3.56 us -> 2.38 us  [shards(): call(functools.partial(last_kernel, count - 1, per_shard - 1, sum(pieces[...]
  transfers between devices with their start and end apart: 17 -> 13, of which waited for: 11 -> 10; matrix products, arithmetic and copies ran while one was open for 0% -> 0% of each run, Pallas kernels for 27% -> 25%
where the time goes in v10:
time: 67.5 us; the launch traced here: 67 us
  waiting for transfers between devices  29.2 us (43%)
  Pallas kernels  19.8 us (29%)
  starting transfers between devices  17.2 us (25%)
  between operations  0.78 us (1%)
    ppermute x13, waiting for transfers between devices, permute(): lax.ppermute(x, AXES, [(flat(*place), flat(*target(*place))) for place in...  29.2 us
    ppermute x13, starting transfers between devices, permute(): lax.ppermute(x, AXES, [(flat(*place), flat(*target(*place))) for place in...  17.2 us
    pallas_call x4, Pallas kernels, add(): call(functools.partial(add_kernel, step, list(range(len(chunks)))), 'add%...  6.09 us
    pallas_call x3, Pallas kernels, shards(): call(functools.partial(arrived_kernel, at, len(terms)), 'arrived%d' % i,...  2.66 us
    pallas_call x1, Pallas kernels, shards(): call(ham_kernel, 'ham', sds((blocks // 2, tall, 3 * LANES), BF16), (SMEM,...  2.51 us
    pallas_call x2, Pallas kernels, shards(): call(functools.partial(last_kernel, count - 1, per_shard - 1, sum(pieces[...  2.38 us
    pallas_call x1, Pallas kernels, shards(): call(own_kernel, 'own', (sds((rows, tile, width), F32), sds((rows, tile,...  1.69 us
    pallas_call x1, Pallas kernels, shards(): call(table_kernel, 'table', sds((rows, blocks), jnp.int32), (SMEM, SMEM),...  1.4 us
  transfers between devices with their start and end apart: 13, of which 10 were waited for; matrix products, arithmetic and copies ran while one was open for 0% of the time, Pallas kernels for 25%

profile of v10, /device:TPU:0, one launch (start us, length us, event | category | flops | bytes accessed | tf_op | source)
XLA Modules:
  0.0 67.0 jit_solution(11993574402168666222)
XLA Ops:
  0.6 0.0 copy-start
  0.6 1.1 %cut.1 = (f32[2,64,512]{2,1,0:T(8,128)S(1)}, f32[2,64,512]{2,1,0:T(8,128)S(1)}) custom-call(f32[4,64,512]{2,1,0:T(8,128)} %dens.1), custom_call_target="tpu_custom_call" | custom-call | flops 1024 | bytes 1024 | tf_op jit(solution)/shard_map/cut/pallas_call | solution.py:299
  1.8 3.1 %collective-permute-start.5 = (f32[2,64,512]{2,1,0:T(8,128)S(1)}, f32[2,64,512]{2,1,0:T(8,128)S(1)}, u32[]{:S(2)}, u32[]{:S(2)}) collective-permute-start(f32[2,64,512]{2,1,0:T(8,128)S(1)} %get-tuple-element.44.rest_0_), channel_id=1, source_target_pairs={{0,1},{1,3},{2,0},{3,2},{4,5},{5,7},{6,4},{7,6},{8,9},{9,11},{10,8... | collective-permute-start | bytes 786440 | tf_op jit(solution)/shard_map/ppermute | solution.py:24
  4.8 2.6 %collective-permute-start = (f32[2,64,512]{2,1,0:T(8,128)S(1)}, f32[2,64,512]{2,1,0:T(8,128)S(1)}, u32[]{:S(2)}, u32[]{:S(2)}) collective-permute-start(f32[2,64,512]{2,1,0:T(8,128)S(1)} %get-tuple-element.36.rest_1_), channel_id=1, source_target_pairs={{0,1},{1,3},{2,0},{3,2},{4,5},{5,7},{6,4},{7,6},{8,9},{9,11},{10,8... | collective-permute-start | bytes 786440 | tf_op jit(solution)/shard_map/ppermute | solution.py:24
  7.4 1.4 %table.1.dens_table = s32[4,16]{1,0:T(4,128)S(1)} custom-call(s32[4,8]{1,0:T(4,128)} %columns, s32[4]{0:T(128)} %counts.1), custom_call_target="tpu_custom_call" | custom-call | flops 1024 | bytes 1024 | tf_op jit(solution)/shard_map/table/pallas_call | solution.py:313
  8.8 0.4 collective-permute-start.3
  9.2 2.5 %collective-permute-start.2 = (s32[4,16]{1,0:T(4,128)S(1)}, s32[4,16]{1,0:T(4,128)S(1)}, u32[]{:S(2)}, u32[]{:S(2)}) collective-permute-start(s32[4,16]{1,0:T(4,128)S(1)} %table.1.dens_table), channel_id=1, source_target_pairs={{0,3},{1,2},{2,1},{3,0},{4,7},{5,6},{6,5},{7,4},{8,11},{9,10},{10,... | collective-permute-start | bytes 776 | tf_op jit(solution)/shard_map/ppermute | solution.py:24
  11.7 0.0 collective-permute-start.1
  11.7 2.5 %ham.2.a = bf16[8,256,384]{2,1,0:T(8,128)(2,1)S(1)} custom-call(s32[4,12]{1,0:T(4,128)} %ham_cols.1, s32[4]{0:T(128)} %ham_count.1, f32[4,64,768]{2,1,0:T(8,128)} %ham.3), custom_call_target="tpu_custom_call" | custom-call | flops 1024 | bytes 1024 | tf_op jit(solution)/shard_map/ham/pallas_call | solution.py:330
  14.2 0.0 collective-permute-done.5.rest_1_
  14.2 2.0 %collective-permute-start.6 = (f32[2,64,512]{2,1,0:T(8,128)S(1)}, f32[2,64,512]{2,1,0:T(8,128)S(1)}, u32[]{:S(2)}, u32[]{:S(2)}) collective-permute-start(f32[2,64,512]{2,1,0:T(8,128)S(1)} %collective-permute-done.5.rest_1_), channel_id=1, source_target_pairs={{0,1},{1,3},{2,0},{3,2},{4,5},{5,7},{6,4},{7,6},{8,9},{9,11},{10,8... | collective-permute-start | bytes 786440 | tf_op jit(solution)/shard_map/ppermute | solution.py:24
  16.2 1.0 %collective-permute-done.3.dens_table = s32[4,16]{1,0:T(4,128)S(1)} collective-permute-done((s32[4,16]{1,0:T(4,128)S(1)}, s32[4,16]{1,0:T(4,128)S(1)}, u32[]{:S(2)}, u32[]{:S(2)}) %collective-permute-start.3) | collective-permute-done | bytes 288 | tf_op jit(solution)/shard_map/ppermute | solution.py:24
  17.2 3.0 %collective-permute-done.2.dens_table = s32[4,16]{1,0:T(4,128)S(1)} collective-permute-done((s32[4,16]{1,0:T(4,128)S(1)}, s32[4,16]{1,0:T(4,128)S(1)}, u32[]{:S(2)}, u32[]{:S(2)}) %collective-permute-start.2) | collective-permute-done | bytes 288 | tf_op jit(solution)/shard_map/ppermute | solution.py:24
  20.2 0.0 collective-permute-done.1.dens_table
  20.2 0.0 collective-permute-done.rest_2_
  20.2 0.6 collective-permute-start.4
  20.8 0.0 copy-done
  20.8 0.3 margin.1
  21.1 1.1 %pick.1 = bf16[2,512,1024]{2,1,0:T(8,128)(2,1)S(1)} custom-call(s32[4,16]{1,0:T(4,128)S(1)} %collective-permute-done.3.dens_table), custom_call_target="tpu_custom_call" | custom-call | flops 1024 | bytes 1024 | tf_op jit(solution)/shard_map/pick/pallas_call | solution.py:363
  22.2 1.6 %add0.1.rest_0_ = f32[256,1024]{1,0:T(8,128)S(1)} custom-call(s32[4,16]{1,0:T(4,128)S(1)} %table.1.dens_table, bf16[8,256,384]{2,1,0:T(8,128)(2,1)S(1)} %ham.2.a, f32[2,64,512]{2,1,0:T(8,128)S(1)} %get-tuple-element.44.rest_0_, f32[2,64,512]{2,1,0:T(8,128)S(1)} %get-tuple-element.36.rest_1_), custom_call_target="tpu_custom_call" | custom-call | flops 1024 | bytes 1024 | tf_op jit(solution)/shard_map/add0/pallas_call | solution.py:344
  23.8 0.7 %collective-permute-done.6.rest_1_ = f32[2,64,512]{2,1,0:T(8,128)S(1)} collective-permute-done((f32[2,64,512]{2,1,0:T(8,128)S(1)}, f32[2,64,512]{2,1,0:T(8,128)S(1)}, u32[]{:S(2)}, u32[]{:S(2)}) %collective-permute-start.6) | collective-permute-done | bytes 262176 | tf_op jit(solution)/shard_map/ppermute | solution.py:24
  24.5 1.9 %collective-permute-start.7 = (f32[2,64,512]{2,1,0:T(8,128)S(1)}, f32[2,64,512]{2,1,0:T(8,128)S(1)}, u32[]{:S(2)}, u32[]{:S(2)}) collective-permute-start(f32[2,64,512]{2,1,0:T(8,128)S(1)} %collective-permute-done.6.rest_1_), channel_id=1, source_target_pairs={{0,1},{1,3},{2,0},{3,2},{4,5},{5,7},{6,4},{7,6},{8,9},{9,11},{10,8... | collective-permute-start | bytes 786440 | tf_op jit(solution)/shard_map/ppermute | solution.py:24
  26.4 3.9 %collective-permute-done.4.rest_2_ = f32[2,64,512]{2,1,0:T(8,128)S(1)} collective-permute-done((f32[2,64,512]{2,1,0:T(8,128)S(1)}, f32[2,64,512]{2,1,0:T(8,128)S(1)}, u32[]{:S(2)}, u32[]{:S(2)}) %collective-permute-start.4) | collective-permute-done | bytes 262176 | tf_op jit(solution)/shard_map/ppermute | solution.py:24
  30.3 0.8 %collective-permute-start.8 = (f32[2,64,512]{2,1,0:T(8,128)S(1)}, f32[2,64,512]{2,1,0:T(8,128)S(1)}, u32[]{:S(2)}, u32[]{:S(2)}) collective-permute-start(f32[2,64,512]{2,1,0:T(8,128)S(1)} %collective-permute-done.4.rest_2_), channel_id=1, source_target_pairs={{0,1},{1,3},{2,0},{3,2},{4,5},{5,7},{6,4},{7,6},{8,9},{9,11},{10,8... | collective-permute-start | bytes 786440 | tf_op jit(solution)/shard_map/ppermute | solution.py:24
  31.2 1.6 %add1.1.rest_0_ = f32[256,1024]{1,0:T(8,128)S(1)} custom-call(s32[4,16]{1,0:T(4,128)S(1)} %collective-permute-done.1.dens_table, bf16[8,256,384]{2,1,0:T(8,128)(2,1)S(1)} %ham.2.a, f32[256,1024]{1,0:T(8,128)S(1)} %add0.1.rest_0_, f32[2,64,512]{2,1,0:T(8,128)S(1)} %collective-permute-done.5.rest_1_, f32[2,64,512]{2,1,0:T(8,128)S(1)} %collective-permute-done.rest_2_), custom_call_target="tpu_custom_call" | custom-call | flops 1024 | bytes 1024 | tf_op jit(solution)/shard_map/add1/pallas_call | solution.py:344
  32.8 1.6 %add2.1.rest_0_ = f32[256,1024]{1,0:T(8,128)S(1)} custom-call(s32[4,16]{1,0:T(4,128)S(1)} %collective-permute-done.2.dens_table, bf16[8,256,384]{2,1,0:T(8,128)(2,1)S(1)} %ham.2.a, f32[256,1024]{1,0:T(8,128)S(1)} %add1.1.rest_0_, f32[2,64,512]{2,1,0:T(8,128)S(1)} %collective-permute-done.6.rest_1_, f32[2,64,512]{2,1,0:T(8,128)S(1)} %collective-permute-done.4.rest_2_), custom_call_target="tpu_custom_call" | custom-call | flops 1024 | bytes 1024 | tf_op jit(solution)/shard_map/add2/pallas_call | solution.py:344
  34.4 1.5 %collective-permute-done.7.rest_1_ = f32[2,64,512]{2,1,0:T(8,128)S(1)} collective-permute-done((f32[2,64,512]{2,1,0:T(8,128)S(1)}, f32[2,64,512]{2,1,0:T(8,128)S(1)}, u32[]{:S(2)}, u32[]{:S(2)}) %collective-permute-start.7) | collective-permute-done | bytes 262176 | tf_op jit(solution)/shard_map/ppermute | solution.py:24
  36.0 1.2 %add3.1.acc_in = f32[256,1024]{1,0:T(8,128)S(1)} custom-call(s32[4,16]{1,0:T(4,128)S(1)} %collective-permute-done.3.dens_table, bf16[8,256,384]{2,1,0:T(8,128)(2,1)S(1)} %ham.2.a, f32[256,1024]{1,0:T(8,128)S(1)} %add2.1.rest_0_, f32[2,64,512]{2,1,0:T(8,128)S(1)} %collective-permute-done.7.rest_1_), custom_call_target="tpu_custom_call" | custom-call | flops 1024 | bytes 1024 | tf_op jit(solution)/shard_map/add3/pallas_call | solution.py:344
  37.2 3.2 %collective-permute-done.8.chunk = f32[2,64,512]{2,1,0:T(8,128)S(1)} collective-permute-done((f32[2,64,512]{2,1,0:T(8,128)S(1)}, f32[2,64,512]{2,1,0:T(8,128)S(1)}, u32[]{:S(2)}, u32[]{:S(2)}) %collective-permute-start.8) | collective-permute-done | bytes 262176 | tf_op jit(solution)/shard_map/ppermute | solution.py:24
  40.4 1.2 %last0.1 = (f32[256,512]{1,0:T(8,128)S(1)}, f32[256,512]{1,0:T(8,128)S(1)}) custom-call(bf16[8,256,384]{2,1,0:T(8,128)(2,1)S(1)} %ham.2.a, f32[256,1024]{1,0:T(8,128)S(1)} %add3.1.acc_in, f32[2,64,512]{2,1,0:T(8,128)S(1)} %collective-permute-done.8.chunk, bf16[2,512,1024]{2,1,0:T(8,128)(2,1)S(1)} %pick.1, bf16[3,256,256]{2,1,0:T(8,128)(2,1)S(1)} %get-tuple-element.42.m_hi, ...), custom_call_target="tpu_custom_call" | custom-call | flops 1024 | bytes 1024 | tf_op jit(solution)/shard_map/last0/pallas_call | solution.py:379
  41.6 0.1 collective-permute-start.10
  41.7 1.2 %last1.1 = (f32[256,512]{1,0:T(8,128)S(1)}, f32[256,512]{1,0:T(8,128)S(1)}) custom-call(bf16[8,256,384]{2,1,0:T(8,128)(2,1)S(1)} %ham.2.a, f32[256,1024]{1,0:T(8,128)S(1)} %add3.1.acc_in, f32[2,64,512]{2,1,0:T(8,128)S(1)} %collective-permute-done.8.chunk, bf16[2,512,1024]{2,1,0:T(8,128)(2,1)S(1)} %pick.1, bf16[3,256,256]{2,1,0:T(8,128)(2,1)S(1)} %get-tuple-element.42.m_hi, ...), custom_call_target="tpu_custom_call" | custom-call | flops 1024 | bytes 1024 | tf_op jit(solution)/shard_map/last1/pallas_call | solution.py:379
  42.9 1.7 %collective-permute-start.12 = (f32[256,512]{1,0:T(8,128)S(1)}, f32[256,512]{1,0:T(8,128)S(1)}, u32[]{:S(2)}, u32[]{:S(2)}) collective-permute-start(f32[256,512]{1,0:T(8,128)S(1)} %get-tuple-element.64), channel_id=1, source_target_pairs={{0,4},{1,5},{2,6},{3,7},{4,8},{5,9},{6,10},{7,11},{8,12},{9,13},{1... | collective-permute-start | bytes 1572872 | tf_op jit(solution)/shard_map/ppermute | solution.py:24
  44.6 0.6 above.1
  45.2 5.1 %collective-permute-done.10.rest_0_ = f32[256,512]{1,0:T(8,128)S(1)} collective-permute-done((f32[256,512]{1,0:T(8,128)S(1)}, f32[256,512]{1,0:T(8,128)S(1)}, u32[]{:S(2)}, u32[]{:S(2)}) %collective-permute-start.10) | collective-permute-done | bytes 524320 | tf_op jit(solution)/shard_map/ppermute | solution.py:24
  50.3 0.0 collective-permute-start.11
  50.3 1.7 %collective-permute-start.9 = (f32[256,512]{1,0:T(8,128)S(1)}, f32[256,512]{1,0:T(8,128)S(1)}, u32[]{:S(2)}, u32[]{:S(2)}) collective-permute-start(f32[256,512]{1,0:T(8,128)S(1)} %get-tuple-element.59), channel_id=1, source_target_pairs={{0,12},{1,13},{2,14},{3,15},{4,0},{5,1},{6,2},{7,3},{8,4},{9,5},{1... | collective-permute-start | bytes 1572872 | tf_op jit(solution)/shard_map/ppermute | solution.py:24
  51.9 1.7 %own.1 = (f32[4,64,1024]{2,1,0:T(8,128)}, f32[4,64,3072]{2,1,0:T(8,128)}) custom-call(bf16[3,256,256]{2,1,0:T(8,128)(2,1)S(1)} %get-tuple-element.42.m_hi, bf16[3,256,256]{2,1,0:T(8,128)(2,1)S(1)} %get-tuple-element.43.m_lo, f32[256,512]{1,0:T(8,128)S(1)} %get-tuple-element.55.rest_0_, f32[256,512]{1,0:T(8,128)S(1)} %get-tuple-element.57.rest_1_), custom_call_target="tpu_custom_call" | custom-call | flops 1024 | bytes 1024 | tf_op jit(solution)/shard_map/own/pallas_call | solution.py:403
  53.6 4.7 %collective-permute-done.12.rest_1_ = f32[256,512]{1,0:T(8,128)S(1)} collective-permute-done((f32[256,512]{1,0:T(8,128)S(1)}, f32[256,512]{1,0:T(8,128)S(1)}, u32[]{:S(2)}, u32[]{:S(2)}) %collective-permute-start.12) | collective-permute-done | bytes 524320 | tf_op jit(solution)/shard_map/ppermute | solution.py:24
  58.4 1.0 %arrived0.1.rest_1_ = f32[4,64,3072]{2,1,0:T(8,128)} custom-call(f32[256,512]{1,0:T(8,128)S(1)} %collective-permute-done.10.rest_0_, f32[256,512]{1,0:T(8,128)S(1)} %collective-permute-done.12.rest_1_, f32[4,64,3072]{2,1,0:T(8,128)} %get-tuple-element.65.rest_2_), custom_call_target="tpu_custom_call", output_to_operand_aliasing={{}: (2, {})} | custom-call | flops 1024 | bytes 1024 | tf_op jit(solution)/shard_map/arrived0/pallas_call | solution.py:414
  59.4 1.2 %collective-permute-done.11.rest_0_ = f32[256,512]{1,0:T(8,128)S(1)} collective-permute-done((f32[256,512]{1,0:T(8,128)S(1)}, f32[256,512]{1,0:T(8,128)S(1)}, u32[]{:S(2)}, u32[]{:S(2)}) %collective-permute-start.11) | collective-permute-done | bytes 524320 | tf_op jit(solution)/shard_map/ppermute | solution.py:24
  60.6 0.8 %arrived1.1.rest_1_ = f32[4,64,3072]{2,1,0:T(8,128)} custom-call(f32[256,512]{1,0:T(8,128)S(1)} %collective-permute-done.11.rest_0_, f32[4,64,3072]{2,1,0:T(8,128)} %arrived0.1.rest_1_), custom_call_target="tpu_custom_call", output_to_operand_aliasing={{}: (1, {})} | custom-call | flops 1024 | bytes 1024 | tf_op jit(solution)/shard_map/arrived1/pallas_call | solution.py:414
  61.4 4.8 %collective-permute-done.9.rest_0_ = f32[256,512]{1,0:T(8,128)S(1)} collective-permute-done((f32[256,512]{1,0:T(8,128)S(1)}, f32[256,512]{1,0:T(8,128)S(1)}, u32[]{:S(2)}, u32[]{:S(2)}) %collective-permute-start.9) | collective-permute-done | bytes 524320 | tf_op jit(solution)/shard_map/ppermute | solution.py:24
  66.2 0.8 %arrived2.1 = f32[4,64,3072]{2,1,0:T(8,128)} custom-call(f32[256,512]{1,0:T(8,128)S(1)} %collective-permute-done.9.rest_0_, f32[4,64,3072]{2,1,0:T(8,128)} %arrived1.1.rest_1_), custom_call_target="tpu_custom_call", output_to_operand_aliasing={{}: (1, {})} | custom-call | flops 1024 | bytes 1024 | tf_op jit(solution)/shard_map/arrived2/pallas_call | solution.py:414
Async XLA Ops:
  0.6 20.2 %copy-start = (f32[4,64,768]{2,1,0:T(8,128)S(1)}, f32[4,64,768]{2,1,0:T(8,128)}, u32[]{:S(2)}) copy-start(f32[4,64,768]{2,1,0:T(8,128)} %over.1) | copy-start | bytes 2359300
  1.8 12.5 %collective-permute-start.5 = (f32[2,64,512]{2,1,0:T(8,128)S(1)}, f32[2,64,512]{2,1,0:T(8,128)S(1)}, u32[]{:S(2)}, u32[]{:S(2)}) collective-permute-start(f32[2,64,512]{2,1,0:T(8,128)S(1)} %get-tuple-element.44.rest_0_), channel_id=1, source_target_pairs={{0,1},{1,3},{2,0},{3,2},{4,5},{5,7},{6,4},{7,6},{8,9},{9,11},{10,8... | collective-permute-start | bytes 786440 | tf_op jit(solution)/shard_map/ppermute | solution.py:24
  4.8 15.4 %collective-permute-start = (f32[2,64,512]{2,1,0:T(8,128)S(1)}, f32[2,64,512]{2,1,0:T(8,128)S(1)}, u32[]{:S(2)}, u32[]{:S(2)}) collective-permute-start(f32[2,64,512]{2,1,0:T(8,128)S(1)} %get-tuple-element.36.rest_1_), channel_id=1, source_target_pairs={{0,1},{1,3},{2,0},{3,2},{4,5},{5,7},{6,4},{7,6},{8,9},{9,11},{10,8... | collective-permute-start | bytes 786440 | tf_op jit(solution)/shard_map/ppermute | solution.py:24
  8.8 8.4 %collective-permute-start.3 = (s32[4,16]{1,0:T(4,128)S(1)}, s32[4,16]{1,0:T(4,128)S(1)}, u32[]{:S(2)}, u32[]{:S(2)}) collective-permute-start(s32[4,16]{1,0:T(4,128)S(1)} %table.1.dens_table), channel_id=1, source_target_pairs={{0,2},{1,0},{2,3},{3,1},{4,6},{5,4},{6,7},{7,5},{8,10},{9,8},{10,1... | collective-permute-start | bytes 776 | tf_op jit(solution)/shard_map/ppermute | solution.py:24
  9.2 11.0 %collective-permute-start.2 = (s32[4,16]{1,0:T(4,128)S(1)}, s32[4,16]{1,0:T(4,128)S(1)}, u32[]{:S(2)}, u32[]{:S(2)}) collective-permute-start(s32[4,16]{1,0:T(4,128)S(1)} %table.1.dens_table), channel_id=1, source_target_pairs={{0,3},{1,2},{2,1},{3,0},{4,7},{5,6},{6,5},{7,4},{8,11},{9,10},{10,... | collective-permute-start | bytes 776 | tf_op jit(solution)/shard_map/ppermute | solution.py:24
  11.7 8.5 %collective-permute-start.1 = (s32[4,16]{1,0:T(4,128)S(1)}, s32[4,16]{1,0:T(4,128)S(1)}, u32[]{:S(2)}, u32[]{:S(2)}) collective-permute-start(s32[4,16]{1,0:T(4,128)S(1)} %table.1.dens_table), channel_id=1, source_target_pairs={{0,1},{1,3},{2,0},{3,2},{4,5},{5,7},{6,4},{7,6},{8,9},{9,11},{10,8... | collective-permute-start | bytes 776 | tf_op jit(solution)/shard_map/ppermute | solution.py:24
  14.2 10.2 %collective-permute-start.6 = (f32[2,64,512]{2,1,0:T(8,128)S(1)}, f32[2,64,512]{2,1,0:T(8,128)S(1)}, u32[]{:S(2)}, u32[]{:S(2)}) collective-permute-start(f32[2,64,512]{2,1,0:T(8,128)S(1)} %collective-permute-done.5.rest_1_), channel_id=1, source_target_pairs={{0,1},{1,3},{2,0},{3,2},{4,5},{5,7},{6,4},{7,6},{8,9},{9,11},{10,8... | collective-permute-start | bytes 786440 | tf_op jit(solution)/shard_map/ppermute | solution.py:24
  20.2 10.1 %collective-permute-start.4 = (f32[2,64,512]{2,1,0:T(8,128)S(1)}, f32[2,64,512]{2,1,0:T(8,128)S(1)}, u32[]{:S(2)}, u32[]{:S(2)}) collective-permute-start(f32[2,64,512]{2,1,0:T(8,128)S(1)} %collective-permute-done.rest_2_), channel_id=1, source_target_pairs={{0,1},{1,3},{2,0},{3,2},{4,5},{5,7},{6,4},{7,6},{8,9},{9,11},{10,8... | collective-permute-start | bytes 786440 | tf_op jit(solution)/shard_map/ppermute | solution.py:24
  24.5 11.5 %collective-permute-start.7 = (f32[2,64,512]{2,1,0:T(8,128)S(1)}, f32[2,64,512]{2,1,0:T(8,128)S(1)}, u32[]{:S(2)}, u32[]{:S(2)}) collective-permute-start(f32[2,64,512]{2,1,0:T(8,128)S(1)} %collective-permute-done.6.rest_1_), channel_id=1, source_target_pairs={{0,1},{1,3},{2,0},{3,2},{4,5},{5,7},{6,4},{7,6},{8,9},{9,11},{10,8... | collective-permute-start | bytes 786440 | tf_op jit(solution)/shard_map/ppermute | solution.py:24
  30.3 10.1 %collective-permute-start.8 = (f32[2,64,512]{2,1,0:T(8,128)S(1)}, f32[2,64,512]{2,1,0:T(8,128)S(1)}, u32[]{:S(2)}, u32[]{:S(2)}) collective-permute-start(f32[2,64,512]{2,1,0:T(8,128)S(1)} %collective-permute-done.4.rest_2_), channel_id=1, source_target_pairs={{0,1},{1,3},{2,0},{3,2},{4,5},{5,7},{6,4},{7,6},{8,9},{9,11},{10,8... | collective-permute-start | bytes 786440 | tf_op jit(solution)/shard_map/ppermute | solution.py:24
  41.6 8.7 %collective-permute-start.10 = (f32[256,512]{1,0:T(8,128)S(1)}, f32[256,512]{1,0:T(8,128)S(1)}, u32[]{:S(2)}, u32[]{:S(2)}) collective-permute-start(f32[256,512]{1,0:T(8,128)S(1)} %get-tuple-element.61), channel_id=1, source_target_pairs={{0,4},{1,5},{2,6},{3,7},{4,8},{5,9},{6,10},{7,11},{8,12},{9,13},{1... | collective-permute-start | bytes 1572872 | tf_op jit(solution)/shard_map/ppermute | solution.py:24
  42.9 15.5 %collective-permute-start.12 = (f32[256,512]{1,0:T(8,128)S(1)}, f32[256,512]{1,0:T(8,128)S(1)}, u32[]{:S(2)}, u32[]{:S(2)}) collective-permute-start(f32[256,512]{1,0:T(8,128)S(1)} %get-tuple-element.64), channel_id=1, source_target_pairs={{0,4},{1,5},{2,6},{3,7},{4,8},{5,9},{6,10},{7,11},{8,12},{9,13},{1... | collective-permute-start | bytes 1572872 | tf_op jit(solution)/shard_map/ppermute | solution.py:24
  50.3 10.3 %collective-permute-start.11 = (f32[256,512]{1,0:T(8,128)S(1)}, f32[256,512]{1,0:T(8,128)S(1)}, u32[]{:S(2)}, u32[]{:S(2)}) collective-permute-start(f32[256,512]{1,0:T(8,128)S(1)} %get-tuple-element.62), channel_id=1, source_target_pairs={{0,12},{1,13},{2,14},{3,15},{4,0},{5,1},{6,2},{7,3},{8,4},{9,5},{1... | collective-permute-start | bytes 1572872 | tf_op jit(solution)/shard_map/ppermute | solution.py:24
  50.3 15.9 %collective-permute-start.9 = (f32[256,512]{1,0:T(8,128)S(1)}, f32[256,512]{1,0:T(8,128)S(1)}, u32[]{:S(2)}, u32[]{:S(2)}) collective-permute-start(f32[256,512]{1,0:T(8,128)S(1)} %get-tuple-element.59), channel_id=1, source_target_pairs={{0,12},{1,13},{2,14},{3,15},{4,0},{5,1},{6,2},{7,3},{8,4},{9,5},{1... | collective-permute-start | bytes 1572872 | tf_op jit(solution)/shard_map/ppermute | solution.py:24

commit v11 on v8

--- a/solution.py
+++ b/solution.py
@@ -57,6 +57,12 @@
             @pl.when(slot < counts[r])
             def _(r=r, slot=slot):
                 table[r, columns[r, slot]] = slot + 1
+
+
+def cut_kernel(half, dens, out, sem):
+    copy = pltpu.make_async_copy(dens.at[pl.ds(2 * half, 2)], out, sem)
+    copy.start()
+    copy.wait()
 
 
 def table_kernel(columns, counts, table):
@@ -244,7 +250,7 @@
         copy.wait()
 
 
-def arrived_kernel(at, above, below, window_in, window, sems):
+def arrived_kernel(at, below, above, window_in, window, sems):
     rows, tile, triple = window.shape
     copies = [
         pltpu.make_async_copy(
@@ -284,8 +290,20 @@
     per_shard = rows // 2
     sds = jax.ShapeDtypeStruct
 
-    halves = [dens_tiles[2 * h : 2 * h + 2] for h in range(per_shard)]
-    *halves, dens_cols = lax.optimization_barrier((*halves, dens_cols))
+    dens_here = pltpu.with_memory_space_constraint(dens_tiles, pltpu.HBM)
+    halves = []
+    for h in range(per_shard):
+        half = call(
+            functools.partial(cut_kernel, h),
+            "cut%d" % h,
+            sds((2, tile, dens_tiles.shape[2]), F32),
+            (pltpu.HBM,),
+            VMEM,
+            [pltpu.SemaphoreType.DMA],
+        )(dens_here)
+        half, dens_here = lax.optimization_barrier((half, dens_here))
+        halves.append(half)
+    halves[0], dens_cols = lax.optimization_barrier((halves[0], dens_cols))
     arrivals = [halves, [pass_on(h, 1) for h in halves]]
     ham_cols, ham_count, dens_cols, dens_count, ham_tiles = (
         pltpu.with_memory_space_constraint(x, pltpu.HBM)
@@ -331,7 +349,7 @@
             [VMEM((4 * tile, width), BF16)],
         )(tables[step], a, *([acc] if step > 0 else []), *chunks)
 
-    pieces = (width // 2, width // 2)
+    pieces = (width // 4,) * 4
     acc = None
     for step in range(1, count - 1):
         now = arrivals[-1]
@@ -368,8 +386,8 @@
         if i + 1 < len(pieces):
             part, acc = lax.optimization_barrier((part, acc))
         parts.append(part)
+        afters.append(rotate(above, -1))
         befores.append(rotate(below, 1))
-        afters.append(rotate(above, -1))
     product, window = call(
         own_kernel,
         "own",
@@ -387,7 +405,7 @@
             pl.ANY,
             [pltpu.SemaphoreType.DMA((2, rows))],
             {2: 0},
-        )(befores[i], afters[i], window)
+        )(afters[i], befores[i], window)
     return (product, window)
 
 

time: 67.8 us -> 68.4 us (level)
  waiting for transfers between devices: 30.4 us -> 23.1 us
  Pallas kernels: 17.5 us -> 22.1 us
  starting transfers between devices: 17.4 us -> 21.7 us
  local copies, waits for them, and re-layouts: 1.14 us -> 0.01 us
    ppermute x13 -> x17, waiting for transfers between devices: 30.4 us -> 23.1 us  [permute(): lax.ppermute(x, AXES, [(flat(*place), flat(*target(*place))) for place in...]
    ppermute x13 -> x17, starting transfers between devices: 17.4 us -> 21.7 us  [permute(): lax.ppermute(x, AXES, [(flat(*place), flat(*target(*place))) for place in...]
    pallas_call x0 -> x2, Pallas kernels: none -> 1.99 us  [shards(): call(functools.partial(cut_kernel, h), 'cut%d' % h, sds((2, tile, dens_ti...]
    pallas_call x2 -> x4, Pallas kernels: 2.05 us -> 3.4 us  [shards(): call(functools.partial(arrived_kernel, sum(pieces[:i])), 'arrived%d' % i,...]
    pallas_call x2 -> x4, Pallas kernels: 2.4 us -> 3.56 us  [shards(): call(functools.partial(last_kernel, count - 1, per_shard - 1, sum(pieces[...]
    slice x1 -> x0, local copies, waits for them, and re-layouts: 1.14 us -> none  [shards(): halves = [dens_tiles[2 * h:2 * h + 2] for h in range(per_shard)]]
  transfers between devices with their start and end apart: 13 -> 17, of which waited for: 10 -> 9; matrix products, arithmetic and copies ran while one was open for 0% -> 0% of each run, Pallas kernels for 23% -> 29%
where the time goes in v11:
time: 68.4 us; the launch traced here: 67.6 us
  waiting for transfers between devices  23.1 us (34%)
  Pallas kernels  22.1 us (32%)
  starting transfers between devices  21.7 us (32%)
  between operations  0.82 us (1%)
    ppermute x17, waiting for transfers between devices, permute(): lax.ppermute(x, AXES, [(flat(*place), flat(*target(*place))) for place in...  23.1 us
    ppermute x17, starting transfers between devices, permute(): lax.ppermute(x, AXES, [(flat(*place), flat(*target(*place))) for place in...  21.7 us
    pallas_call x4, Pallas kernels, add(): call(functools.partial(add_kernel, step, list(range(len(chunks)))), 'add%...  6.15 us
    pallas_call x4, Pallas kernels, shards(): call(functools.partial(last_kernel, count - 1, per_shard - 1, sum(pieces[...  3.56 us
    pallas_call x4, Pallas kernels, shards(): call(functools.partial(arrived_kernel, sum(pieces[:i])), 'arrived%d' % i,...  3.4 us
    pallas_call x1, Pallas kernels, shards(): call(ham_kernel, 'ham', sds((blocks // 2, tall, 3 * LANES), BF16), (SMEM,...  2.51 us
    pallas_call x2, Pallas kernels, shards(): call(functools.partial(cut_kernel, h), 'cut%d' % h, sds((2, tile, dens_ti...  1.99 us
    pallas_call x1, Pallas kernels, shards(): call(own_kernel, 'own', (sds((rows, tile, width), F32), sds((rows, tile,...  1.66 us
  transfers between devices with their start and end apart: 17, of which 9 were waited for; matrix products, arithmetic and copies ran while one was open for 0% of the time, Pallas kernels for 29%

profile of v11, /device:TPU:0, one launch (start us, length us, event | category | flops | bytes accessed | tf_op | source)
XLA Modules:
  0.0 67.6 jit_solution(11243372264693757261)
XLA Ops:
  0.6 1.0 %cut0.1.rest_0_ = f32[2,64,512]{2,1,0:T(8,128)S(1)} custom-call(f32[4,64,512]{2,1,0:T(8,128)} %dens.2), custom_call_target="tpu_custom_call" | custom-call | flops 1024 | bytes 1024 | tf_op jit(solution)/shard_map/cut0/pallas_call | solution.py:296
  1.7 3.1 %collective-permute-start.5 = (f32[2,64,512]{2,1,0:T(8,128)S(1)}, f32[2,64,512]{2,1,0:T(8,128)S(1)}, u32[]{:S(2)}, u32[]{:S(2)}) collective-permute-start(f32[2,64,512]{2,1,0:T(8,128)S(1)} %cut0.1.rest_0_), channel_id=1, source_target_pairs={{0,1},{1,3},{2,0},{3,2},{4,5},{5,7},{6,4},{7,6},{8,9},{9,11},{10,8... | collective-permute-start | bytes 786440 | tf_op jit(solution)/shard_map/ppermute | solution.py:24
  4.8 1.0 %cut1.1.rest_1_ = f32[2,64,512]{2,1,0:T(8,128)S(1)} custom-call(f32[4,64,512]{2,1,0:T(8,128)} %dens.2), custom_call_target="tpu_custom_call" | custom-call | flops 1024 | bytes 1024 | tf_op jit(solution)/shard_map/cut1/pallas_call | solution.py:296
  5.7 2.6 %collective-permute-start = (f32[2,64,512]{2,1,0:T(8,128)S(1)}, f32[2,64,512]{2,1,0:T(8,128)S(1)}, u32[]{:S(2)}, u32[]{:S(2)}) collective-permute-start(f32[2,64,512]{2,1,0:T(8,128)S(1)} %cut1.1.rest_1_), channel_id=1, source_target_pairs={{0,1},{1,3},{2,0},{3,2},{4,5},{5,7},{6,4},{7,6},{8,9},{9,11},{10,8... | collective-permute-start | bytes 786440 | tf_op jit(solution)/shard_map/ppermute | solution.py:24
  8.4 1.4 %table.1.dens_table = s32[4,16]{1,0:T(4,128)S(1)} custom-call(s32[4,8]{1,0:T(4,128)} %columns, s32[4]{0:T(128)} %counts.1), custom_call_target="tpu_custom_call" | custom-call | flops 1024 | bytes 1024 | tf_op jit(solution)/shard_map/table/pallas_call | solution.py:312
  9.8 0.4 collective-permute-start.3
  10.2 2.5 %collective-permute-start.2 = (s32[4,16]{1,0:T(4,128)S(1)}, s32[4,16]{1,0:T(4,128)S(1)}, u32[]{:S(2)}, u32[]{:S(2)}) collective-permute-start(s32[4,16]{1,0:T(4,128)S(1)} %table.1.dens_table), channel_id=1, source_target_pairs={{0,3},{1,2},{2,1},{3,0},{4,7},{5,6},{6,5},{7,4},{8,11},{9,10},{10,... | collective-permute-start | bytes 776 | tf_op jit(solution)/shard_map/ppermute | solution.py:24
  12.6 0.0 collective-permute-start.1
  12.6 2.5 %ham.2.a = bf16[8,256,384]{2,1,0:T(8,128)(2,1)S(1)} custom-call(s32[4,12]{1,0:T(4,128)} %ham_cols.1, s32[4]{0:T(128)} %ham_count.1, f32[4,64,768]{2,1,0:T(8,128)} %ham.3), custom_call_target="tpu_custom_call" | custom-call | flops 1024 | bytes 1024 | tf_op jit(solution)/shard_map/ham/pallas_call | solution.py:329
  15.2 0.0 collective-permute-done.5.rest_1_
  15.2 2.0 %collective-permute-start.6 = (f32[2,64,512]{2,1,0:T(8,128)S(1)}, f32[2,64,512]{2,1,0:T(8,128)S(1)}, u32[]{:S(2)}, u32[]{:S(2)}) collective-permute-start(f32[2,64,512]{2,1,0:T(8,128)S(1)} %collective-permute-done.5.rest_1_), channel_id=1, source_target_pairs={{0,1},{1,3},{2,0},{3,2},{4,5},{5,7},{6,4},{7,6},{8,9},{9,11},{10,8... | collective-permute-start | bytes 786440 | tf_op jit(solution)/shard_map/ppermute | solution.py:24
  17.1 0.0 collective-permute-done.3.dens_table
  17.1 2.2 %collective-permute-done.2.dens_table = s32[4,16]{1,0:T(4,128)S(1)} collective-permute-done((s32[4,16]{1,0:T(4,128)S(1)}, s32[4,16]{1,0:T(4,128)S(1)}, u32[]{:S(2)}, u32[]{:S(2)}) %collective-permute-start.2) | collective-permute-done | bytes 288 | tf_op jit(solution)/shard_map/ppermute | solution.py:24
  19.3 0.6 collective-permute-start.4
  19.9 0.3 margin.1
  20.1 1.1 %pick.1 = bf16[2,512,1024]{2,1,0:T(8,128)(2,1)S(1)} custom-call(s32[4,16]{1,0:T(4,128)S(1)} %collective-permute-done.3.dens_table), custom_call_target="tpu_custom_call" | custom-call | flops 1024 | bytes 1024 | tf_op jit(solution)/shard_map/pick/pallas_call | solution.py:362
  21.3 1.6 %add0.1.rest_0_ = f32[256,1024]{1,0:T(8,128)S(1)} custom-call(s32[4,16]{1,0:T(4,128)S(1)} %table.1.dens_table, bf16[8,256,384]{2,1,0:T(8,128)(2,1)S(1)} %ham.2.a, f32[2,64,512]{2,1,0:T(8,128)S(1)} %cut0.1.rest_0_, f32[2,64,512]{2,1,0:T(8,128)S(1)} %cut1.1.rest_1_), custom_call_target="tpu_custom_call" | custom-call | flops 1024 | bytes 1024 | tf_op jit(solution)/shard_map/add0/pallas_call | solution.py:343
  22.9 2.5 %collective-permute-done.6.rest_1_ = f32[2,64,512]{2,1,0:T(8,128)S(1)} collective-permute-done((f32[2,64,512]{2,1,0:T(8,128)S(1)}, f32[2,64,512]{2,1,0:T(8,128)S(1)}, u32[]{:S(2)}, u32[]{:S(2)}) %collective-permute-start.6) | collective-permute-done | bytes 262176 | tf_op jit(solution)/shard_map/ppermute | solution.py:24
  25.4 1.0 %collective-permute-start.7 = (f32[2,64,512]{2,1,0:T(8,128)S(1)}, f32[2,64,512]{2,1,0:T(8,128)S(1)}, u32[]{:S(2)}, u32[]{:S(2)}) collective-permute-start(f32[2,64,512]{2,1,0:T(8,128)S(1)} %collective-permute-done.6.rest_1_), channel_id=1, source_target_pairs={{0,1},{1,3},{2,0},{3,2},{4,5},{5,7},{6,4},{7,6},{8,9},{9,11},{10,8... | collective-permute-start | bytes 786440 | tf_op jit(solution)/shard_map/ppermute | solution.py:24
  26.4 4.6 %collective-permute-done.4.rest_2_ = f32[2,64,512]{2,1,0:T(8,128)S(1)} collective-permute-done((f32[2,64,512]{2,1,0:T(8,128)S(1)}, f32[2,64,512]{2,1,0:T(8,128)S(1)}, u32[]{:S(2)}, u32[]{:S(2)}) %collective-permute-start.4) | collective-permute-done | bytes 262176 | tf_op jit(solution)/shard_map/ppermute | solution.py:24
  31.0 1.0 %collective-permute-start.8 = (f32[2,64,512]{2,1,0:T(8,128)S(1)}, f32[2,64,512]{2,1,0:T(8,128)S(1)}, u32[]{:S(2)}, u32[]{:S(2)}) collective-permute-start(f32[2,64,512]{2,1,0:T(8,128)S(1)} %collective-permute-done.4.rest_2_), channel_id=1, source_target_pairs={{0,1},{1,3},{2,0},{3,2},{4,5},{5,7},{6,4},{7,6},{8,9},{9,11},{10,8... | collective-permute-start | bytes 786440 | tf_op jit(solution)/shard_map/ppermute | solution.py:24
  32.0 1.6 %add1.1.rest_0_ = f32[256,1024]{1,0:T(8,128)S(1)} custom-call(s32[4,16]{1,0:T(4,128)S(1)} %collective-permute-done.1.dens_table, bf16[8,256,384]{2,1,0:T(8,128)(2,1)S(1)} %ham.2.a, f32[256,1024]{1,0:T(8,128)S(1)} %add0.1.rest_0_, f32[2,64,512]{2,1,0:T(8,128)S(1)} %collective-permute-done.5.rest_1_, f32[2,64,512]{2,1,0:T(8,128)S(1)} %collective-permute-done.rest_2_), custom_call_target="tpu_custom_call" | custom-call | flops 1024 | bytes 1024 | tf_op jit(solution)/shard_map/add1/pallas_call | solution.py:343
  33.6 1.6 %add2.1.rest_0_ = f32[256,1024]{1,0:T(8,128)S(1)} custom-call(s32[4,16]{1,0:T(4,128)S(1)} %collective-permute-done.2.dens_table, bf16[8,256,384]{2,1,0:T(8,128)(2,1)S(1)} %ham.2.a, f32[256,1024]{1,0:T(8,128)S(1)} %add1.1.rest_0_, f32[2,64,512]{2,1,0:T(8,128)S(1)} %collective-permute-done.6.rest_1_, f32[2,64,512]{2,1,0:T(8,128)S(1)} %collective-permute-done.4.rest_2_), custom_call_target="tpu_custom_call" | custom-call | flops 1024 | bytes 1024 | tf_op jit(solution)/shard_map/add2/pallas_call | solution.py:343
  35.3 1.3 %collective-permute-done.7.rest_1_ = f32[2,64,512]{2,1,0:T(8,128)S(1)} collective-permute-done((f32[2,64,512]{2,1,0:T(8,128)S(1)}, f32[2,64,512]{2,1,0:T(8,128)S(1)}, u32[]{:S(2)}, u32[]{:S(2)}) %collective-permute-start.7) | collective-permute-done | bytes 262176 | tf_op jit(solution)/shard_map/ppermute | solution.py:24
  36.6 1.3 %add3.1.acc_in = f32[256,1024]{1,0:T(8,128)S(1)} custom-call(s32[4,16]{1,0:T(4,128)S(1)} %collective-permute-done.3.dens_table, bf16[8,256,384]{2,1,0:T(8,128)(2,1)S(1)} %ham.2.a, f32[256,1024]{1,0:T(8,128)S(1)} %add2.1.rest_0_, f32[2,64,512]{2,1,0:T(8,128)S(1)} %collective-permute-done.7.rest_1_), custom_call_target="tpu_custom_call" | custom-call | flops 1024 | bytes 1024 | tf_op jit(solution)/shard_map/add3/pallas_call | solution.py:343
  37.9 2.5 %collective-permute-done.8.chunk = f32[2,64,512]{2,1,0:T(8,128)S(1)} collective-permute-done((f32[2,64,512]{2,1,0:T(8,128)S(1)}, f32[2,64,512]{2,1,0:T(8,128)S(1)}, u32[]{:S(2)}, u32[]{:S(2)}) %collective-permute-start.8) | collective-permute-done | bytes 262176 | tf_op jit(solution)/shard_map/ppermute | solution.py:24
  40.3 0.9 %last0.1 = (f32[256,256]{1,0:T(8,128)S(1)}, f32[256,256]{1,0:T(8,128)S(1)}, f32[256,256]{1,0:T(8,128)S(1)}) custom-call(bf16[8,256,384]{2,1,0:T(8,128)(2,1)S(1)} %ham.2.a, f32[256,1024]{1,0:T(8,128)S(1)} %add3.1.acc_in, f32[2,64,512]{2,1,0:T(8,128)S(1)} %collective-permute-done.8.chunk, bf16[2,512,1024]{2,1,0:T(8,128)(2,1)S(1)} %pick.1, ...), custom_call_target="tpu_custom_call" | custom-call | flops 1024 | bytes 1024 | tf_op jit(solution)/shard_map/last0/pallas_call | solution.py:378
  41.2 0.1 collective-permute-start.15
  41.3 0.5 collective-permute-start.16
  41.8 0.9 %last1.1 = (f32[256,256]{1,0:T(8,128)S(1)}, f32[256,256]{1,0:T(8,128)S(1)}, f32[256,256]{1,0:T(8,128)S(1)}) custom-call(bf16[8,256,384]{2,1,0:T(8,128)(2,1)S(1)} %ham.2.a, f32[256,1024]{1,0:T(8,128)S(1)} %add3.1.acc_in, f32[2,64,512]{2,1,0:T(8,128)S(1)} %collective-permute-done.8.chunk, bf16[2,512,1024]{2,1,0:T(8,128)(2,1)S(1)} %pick.1, ...), custom_call_target="tpu_custom_call" | custom-call | flops 1024 | bytes 1024 | tf_op jit(solution)/shard_map/last1/pallas_call | solution.py:378
  42.7 1.4 %collective-permute-start.13 = (f32[256,256]{1,0:T(8,128)S(1)}, f32[256,256]{1,0:T(8,128)S(1)}, u32[]{:S(2)}, u32[]{:S(2)}) collective-permute-start(f32[256,256]{1,0:T(8,128)S(1)} %get-tuple-element.77), channel_id=1, source_target_pairs={{0,12},{1,13},{2,14},{3,15},{4,0},{5,1},{6,2},{7,3},{8,4},{9,5},{1... | collective-permute-start | bytes 786440 | tf_op jit(solution)/shard_map/ppermute | solution.py:24
  44.1 0.0 collective-permute-start.14
  44.1 0.9 %last2.1 = (f32[256,256]{1,0:T(8,128)S(1)}, f32[256,256]{1,0:T(8,128)S(1)}, f32[256,256]{1,0:T(8,128)S(1)}) custom-call(bf16[8,256,384]{2,1,0:T(8,128)(2,1)S(1)} %ham.2.a, f32[256,1024]{1,0:T(8,128)S(1)} %add3.1.acc_in, f32[2,64,512]{2,1,0:T(8,128)S(1)} %collective-permute-done.8.chunk, bf16[2,512,1024]{2,1,0:T(8,128)(2,1)S(1)} %pick.1, ...), custom_call_target="tpu_custom_call" | custom-call | flops 1024 | bytes 1024 | tf_op jit(solution)/shard_map/last2/pallas_call | solution.py:378
  45.0 0.9 %last3.1 = (f32[256,256]{1,0:T(8,128)S(1)}, f32[256,256]{1,0:T(8,128)S(1)}, f32[256,256]{1,0:T(8,128)S(1)}) custom-call(bf16[8,256,384]{2,1,0:T(8,128)(2,1)S(1)} %ham.2.a, f32[256,1024]{1,0:T(8,128)S(1)} %add3.1.acc_in, f32[2,64,512]{2,1,0:T(8,128)S(1)} %collective-permute-done.8.chunk, bf16[2,512,1024]{2,1,0:T(8,128)(2,1)S(1)} %pick.1, ...), custom_call_target="tpu_custom_call" | custom-call | flops 1024 | bytes 1024 | tf_op jit(solution)/shard_map/last3/pallas_call | solution.py:378
  45.8 1.8 %collective-permute-start.9 = (f32[256,256]{1,0:T(8,128)S(1)}, f32[256,256]{1,0:T(8,128)S(1)}, u32[]{:S(2)}, u32[]{:S(2)}) collective-permute-start(f32[256,256]{1,0:T(8,128)S(1)} %get-tuple-element.73), channel_id=1, source_target_pairs={{0,12},{1,13},{2,14},{3,15},{4,0},{5,1},{6,2},{7,3},{8,4},{9,5},{1... | collective-permute-start | bytes 786440 | tf_op jit(solution)/shard_map/ppermute | solution.py:24
  47.6 1.5 %collective-permute-start.11 = (f32[256,256]{1,0:T(8,128)S(1)}, f32[256,256]{1,0:T(8,128)S(1)}, u32[]{:S(2)}, u32[]{:S(2)}) collective-permute-start(f32[256,256]{1,0:T(8,128)S(1)} %get-tuple-element.75), channel_id=1, source_target_pairs={{0,12},{1,13},{2,14},{3,15},{4,0},{5,1},{6,2},{7,3},{8,4},{9,5},{1... | collective-permute-start | bytes 786440 | tf_op jit(solution)/shard_map/ppermute | solution.py:24
  49.2 0.8 %collective-permute-done.16.above = f32[256,256]{1,0:T(8,128)S(1)} collective-permute-done((f32[256,256]{1,0:T(8,128)S(1)}, f32[256,256]{1,0:T(8,128)S(1)}, u32[]{:S(2)}, u32[]{:S(2)}) %collective-permute-start.16) | collective-permute-done | bytes 262176 | tf_op jit(solution)/shard_map/ppermute | solution.py:24
  49.9 0.2 collective-permute-start.12
  50.1 2.5 %collective-permute-done.13.below = f32[256,256]{1,0:T(8,128)S(1)} collective-permute-done((f32[256,256]{1,0:T(8,128)S(1)}, f32[256,256]{1,0:T(8,128)S(1)}, u32[]{:S(2)}, u32[]{:S(2)}) %collective-permute-start.13) | collective-permute-done | bytes 262176 | tf_op jit(solution)/shard_map/ppermute | solution.py:24
  52.6 3.1 %collective-permute-start.10 = (f32[256,256]{1,0:T(8,128)S(1)}, f32[256,256]{1,0:T(8,128)S(1)}, u32[]{:S(2)}, u32[]{:S(2)}) collective-permute-start(f32[256,256]{1,0:T(8,128)S(1)} %get-tuple-element.74), channel_id=1, source_target_pairs={{0,4},{1,5},{2,6},{3,7},{4,8},{5,9},{6,10},{7,11},{8,12},{9,13},{1... | collective-permute-start | bytes 786440 | tf_op jit(solution)/shard_map/ppermute | solution.py:24
  55.7 1.7 %own.1 = (f32[4,64,1024]{2,1,0:T(8,128)}, f32[4,64,3072]{2,1,0:T(8,128)}) custom-call(bf16[3,256,256]{2,1,0:T(8,128)(2,1)S(1)} %get-tuple-element.50.m_hi, bf16[3,256,256]{2,1,0:T(8,128)(2,1)S(1)} %get-tuple-element.51.m_lo, f32[256,256]{1,0:T(8,128)S(1)} %get-tuple-element.63.rest_0_, f32[256,256]{1,0:T(8,128)S(1)} %get-tuple-element.66.rest_1_, ...), custom_call_target="tpu_custom_call" | custom-call | flops 1024 | bytes 1024 | tf_op jit(solution)/shard_map/own/pallas_call | solution.py:391
  57.4 0.9 %arrived0.1.window_in = f32[4,64,3072]{2,1,0:T(8,128)} custom-call(f32[256,256]{1,0:T(8,128)S(1)} %collective-permute-done.15.below, f32[256,256]{1,0:T(8,128)S(1)} %collective-permute-done.16.above, f32[4,64,3072]{2,1,0:T(8,128)} %get-tuple-element.81.window_in), custom_call_target="tpu_custom_call", output_to_operand_aliasing={{}: (2, {})} | custom-call | flops 1024 | bytes 1024 | tf_op jit(solution)/shard_map/arrived0/pallas_call | solution.py:400
  58.3 0.0 collective-permute-done.14.above
  58.3 0.9 %arrived1.1.window_in = f32[4,64,3072]{2,1,0:T(8,128)} custom-call(f32[256,256]{1,0:T(8,128)S(1)} %collective-permute-done.13.below, f32[256,256]{1,0:T(8,128)S(1)} %collective-permute-done.14.above, f32[4,64,3072]{2,1,0:T(8,128)} %arrived0.1.window_in), custom_call_target="tpu_custom_call", output_to_operand_aliasing={{}: (2, {})} | custom-call | flops 1024 | bytes 1024 | tf_op jit(solution)/shard_map/arrived1/pallas_call | solution.py:400
  59.1 4.7 %collective-permute-done.11.below = f32[256,256]{1,0:T(8,128)S(1)} collective-permute-done((f32[256,256]{1,0:T(8,128)S(1)}, f32[256,256]{1,0:T(8,128)S(1)}, u32[]{:S(2)}, u32[]{:S(2)}) %collective-permute-start.11) | collective-permute-done | bytes 262176 | tf_op jit(solution)/shard_map/ppermute | solution.py:24
  63.8 0.8 %arrived2.1.window_in = f32[4,64,3072]{2,1,0:T(8,128)} custom-call(f32[256,256]{1,0:T(8,128)S(1)} %collective-permute-done.11.below, f32[256,256]{1,0:T(8,128)S(1)} %collective-permute-done.12.above, f32[4,64,3072]{2,1,0:T(8,128)} %arrived1.1.window_in), custom_call_target="tpu_custom_call", output_to_operand_aliasing={{}: (2, {})} | custom-call | flops 1024 | bytes 1024 | tf_op jit(solution)/shard_map/arrived2/pallas_call | solution.py:400
  64.7 2.1 %collective-permute-done.10.above = f32[256,256]{1,0:T(8,128)S(1)} collective-permute-done((f32[256,256]{1,0:T(8,128)S(1)}, f32[256,256]{1,0:T(8,128)S(1)}, u32[]{:S(2)}, u32[]{:S(2)}) %collective-permute-start.10) | collective-permute-done | bytes 262176 | tf_op jit(solution)/shard_map/ppermute | solution.py:24
  66.8 0.8 %arrived3.1 = f32[4,64,3072]{2,1,0:T(8,128)} custom-call(f32[256,256]{1,0:T(8,128)S(1)} %collective-permute-done.9.below, f32[256,256]{1,0:T(8,128)S(1)} %collective-permute-done.10.above, f32[4,64,3072]{2,1,0:T(8,128)} %arrived2.1.window_in), custom_call_target="tpu_custom_call", output_to_operand_aliasing={{}: (2, {})} | custom-call | flops 1024 | bytes 1024 | tf_op jit(solution)/shard_map/arrived3/pallas_call | solution.py:400
  (7 shorter events, 0.0 us)
Async XLA Ops:
  0.6 19.2 %copy-start = (f32[4,64,768]{2,1,0:T(8,128)S(1)}, f32[4,64,768]{2,1,0:T(8,128)}, u32[]{:S(2)}) copy-start(f32[4,64,768]{2,1,0:T(8,128)} %over.1) | copy-start | bytes 2359300
  1.7 13.5 %collective-permute-start.5 = (f32[2,64,512]{2,1,0:T(8,128)S(1)}, f32[2,64,512]{2,1,0:T(8,128)S(1)}, u32[]{:S(2)}, u32[]{:S(2)}) collective-permute-start(f32[2,64,512]{2,1,0:T(8,128)S(1)} %cut0.1.rest_0_), channel_id=1, source_target_pairs={{0,1},{1,3},{2,0},{3,2},{4,5},{5,7},{6,4},{7,6},{8,9},{9,11},{10,8... | collective-permute-start | bytes 786440 | tf_op jit(solution)/shard_map/ppermute | solution.py:24
  5.7 13.6 %collective-permute-start = (f32[2,64,512]{2,1,0:T(8,128)S(1)}, f32[2,64,512]{2,1,0:T(8,128)S(1)}, u32[]{:S(2)}, u32[]{:S(2)}) collective-permute-start(f32[2,64,512]{2,1,0:T(8,128)S(1)} %cut1.1.rest_1_), channel_id=1, source_target_pairs={{0,1},{1,3},{2,0},{3,2},{4,5},{5,7},{6,4},{7,6},{8,9},{9,11},{10,8... | collective-permute-start | bytes 786440 | tf_op jit(solution)/shard_map/ppermute | solution.py:24
  9.8 7.4 %collective-permute-start.3 = (s32[4,16]{1,0:T(4,128)S(1)}, s32[4,16]{1,0:T(4,128)S(1)}, u32[]{:S(2)}, u32[]{:S(2)}) collective-permute-start(s32[4,16]{1,0:T(4,128)S(1)} %table.1.dens_table), channel_id=1, source_target_pairs={{0,2},{1,0},{2,3},{3,1},{4,6},{5,4},{6,7},{7,5},{8,10},{9,8},{10,1... | collective-permute-start | bytes 776 | tf_op jit(solution)/shard_map/ppermute | solution.py:24
  10.2 9.1 %collective-permute-start.2 = (s32[4,16]{1,0:T(4,128)S(1)}, s32[4,16]{1,0:T(4,128)S(1)}, u32[]{:S(2)}, u32[]{:S(2)}) collective-permute-start(s32[4,16]{1,0:T(4,128)S(1)} %table.1.dens_table), channel_id=1, source_target_pairs={{0,3},{1,2},{2,1},{3,0},{4,7},{5,6},{6,5},{7,4},{8,11},{9,10},{10,... | collective-permute-start | bytes 776 | tf_op jit(solution)/shard_map/ppermute | solution.py:24
  12.6 6.6 %collective-permute-start.1 = (s32[4,16]{1,0:T(4,128)S(1)}, s32[4,16]{1,0:T(4,128)S(1)}, u32[]{:S(2)}, u32[]{:S(2)}) collective-permute-start(s32[4,16]{1,0:T(4,128)S(1)} %table.1.dens_table), channel_id=1, source_target_pairs={{0,1},{1,3},{2,0},{3,2},{4,5},{5,7},{6,4},{7,6},{8,9},{9,11},{10,8... | collective-permute-start | bytes 776 | tf_op jit(solution)/shard_map/ppermute | solution.py:24
  15.2 10.2 %collective-permute-start.6 = (f32[2,64,512]{2,1,0:T(8,128)S(1)}, f32[2,64,512]{2,1,0:T(8,128)S(1)}, u32[]{:S(2)}, u32[]{:S(2)}) collective-permute-start(f32[2,64,512]{2,1,0:T(8,128)S(1)} %collective-permute-done.5.rest_1_), channel_id=1, source_target_pairs={{0,1},{1,3},{2,0},{3,2},{4,5},{5,7},{6,4},{7,6},{8,9},{9,11},{10,8... | collective-permute-start | bytes 786440 | tf_op jit(solution)/shard_map/ppermute | solution.py:24
  19.3 11.7 %collective-permute-start.4 = (f32[2,64,512]{2,1,0:T(8,128)S(1)}, f32[2,64,512]{2,1,0:T(8,128)S(1)}, u32[]{:S(2)}, u32[]{:S(2)}) collective-permute-start(f32[2,64,512]{2,1,0:T(8,128)S(1)} %collective-permute-done.rest_2_), channel_id=1, source_target_pairs={{0,1},{1,3},{2,0},{3,2},{4,5},{5,7},{6,4},{7,6},{8,9},{9,11},{10,8... | collective-permute-start | bytes 786440 | tf_op jit(solution)/shard_map/ppermute | solution.py:24
  25.4 11.2 %collective-permute-start.7 = (f32[2,64,512]{2,1,0:T(8,128)S(1)}, f32[2,64,512]{2,1,0:T(8,128)S(1)}, u32[]{:S(2)}, u32[]{:S(2)}) collective-permute-start(f32[2,64,512]{2,1,0:T(8,128)S(1)} %collective-permute-done.6.rest_1_), channel_id=1, source_target_pairs={{0,1},{1,3},{2,0},{3,2},{4,5},{5,7},{6,4},{7,6},{8,9},{9,11},{10,8... | collective-permute-start | bytes 786440 | tf_op jit(solution)/shard_map/ppermute | solution.py:24
  31.0 9.4 %collective-permute-start.8 = (f32[2,64,512]{2,1,0:T(8,128)S(1)}, f32[2,64,512]{2,1,0:T(8,128)S(1)}, u32[]{:S(2)}, u32[]{:S(2)}) collective-permute-start(f32[2,64,512]{2,1,0:T(8,128)S(1)} %collective-permute-done.4.rest_2_), channel_id=1, source_target_pairs={{0,1},{1,3},{2,0},{3,2},{4,5},{5,7},{6,4},{7,6},{8,9},{9,11},{10,8... | collective-permute-start | bytes 786440 | tf_op jit(solution)/shard_map/ppermute | solution.py:24
  41.2 6.4 %collective-permute-start.15 = (f32[256,256]{1,0:T(8,128)S(1)}, f32[256,256]{1,0:T(8,128)S(1)}, u32[]{:S(2)}, u32[]{:S(2)}) collective-permute-start(f32[256,256]{1,0:T(8,128)S(1)} %get-tuple-element.79), channel_id=1, source_target_pairs={{0,12},{1,13},{2,14},{3,15},{4,0},{5,1},{6,2},{7,3},{8,4},{9,5},{1... | collective-permute-start | bytes 786440 | tf_op jit(solution)/shard_map/ppermute | solution.py:24
  41.3 8.6 %collective-permute-start.16 = (f32[256,256]{1,0:T(8,128)S(1)}, f32[256,256]{1,0:T(8,128)S(1)}, u32[]{:S(2)}, u32[]{:S(2)}) collective-permute-start(f32[256,256]{1,0:T(8,128)S(1)} %get-tuple-element.80), channel_id=1, source_target_pairs={{0,4},{1,5},{2,6},{3,7},{4,8},{5,9},{6,10},{7,11},{8,12},{9,13},{1... | collective-permute-start | bytes 786440 | tf_op jit(solution)/shard_map/ppermute | solution.py:24
  42.7 9.9 %collective-permute-start.13 = (f32[256,256]{1,0:T(8,128)S(1)}, f32[256,256]{1,0:T(8,128)S(1)}, u32[]{:S(2)}, u32[]{:S(2)}) collective-permute-start(f32[256,256]{1,0:T(8,128)S(1)} %get-tuple-element.77), channel_id=1, source_target_pairs={{0,12},{1,13},{2,14},{3,15},{4,0},{5,1},{6,2},{7,3},{8,4},{9,5},{1... | collective-permute-start | bytes 786440 | tf_op jit(solution)/shard_map/ppermute | solution.py:24
  44.1 14.2 %collective-permute-start.14 = (f32[256,256]{1,0:T(8,128)S(1)}, f32[256,256]{1,0:T(8,128)S(1)}, u32[]{:S(2)}, u32[]{:S(2)}) collective-permute-start(f32[256,256]{1,0:T(8,128)S(1)} %get-tuple-element.78), channel_id=1, source_target_pairs={{0,4},{1,5},{2,6},{3,7},{4,8},{5,9},{6,10},{7,11},{8,12},{9,13},{1... | collective-permute-start | bytes 786440 | tf_op jit(solution)/shard_map/ppermute | solution.py:24
  45.8 18.8 %collective-permute-start.9 = (f32[256,256]{1,0:T(8,128)S(1)}, f32[256,256]{1,0:T(8,128)S(1)}, u32[]{:S(2)}, u32[]{:S(2)}) collective-permute-start(f32[256,256]{1,0:T(8,128)S(1)} %get-tuple-element.73), channel_id=1, source_target_pairs={{0,12},{1,13},{2,14},{3,15},{4,0},{5,1},{6,2},{7,3},{8,4},{9,5},{1... | collective-permute-start | bytes 786440 | tf_op jit(solution)/shard_map/ppermute | solution.py:24
  47.6 16.2 %collective-permute-start.11 = (f32[256,256]{1,0:T(8,128)S(1)}, f32[256,256]{1,0:T(8,128)S(1)}, u32[]{:S(2)}, u32[]{:S(2)}) collective-permute-start(f32[256,256]{1,0:T(8,128)S(1)} %get-tuple-element.75), channel_id=1, source_target_pairs={{0,12},{1,13},{2,14},{3,15},{4,0},{5,1},{6,2},{7,3},{8,4},{9,5},{1... | collective-permute-start | bytes 786440 | tf_op jit(solution)/shard_map/ppermute | solution.py:24
  49.9 13.9 %collective-permute-start.12 = (f32[256,256]{1,0:T(8,128)S(1)}, f32[256,256]{1,0:T(8,128)S(1)}, u32[]{:S(2)}, u32[]{:S(2)}) collective-permute-start(f32[256,256]{1,0:T(8,128)S(1)} %get-tuple-element.76), channel_id=1, source_target_pairs={{0,4},{1,5},{2,6},{3,7},{4,8},{5,9},{6,10},{7,11},{8,12},{9,13},{1... | collective-permute-start | bytes 786440 | tf_op jit(solution)/shard_map/ppermute | solution.py:24
  52.6 14.2 %collective-permute-start.10 = (f32[256,256]{1,0:T(8,128)S(1)}, f32[256,256]{1,0:T(8,128)S(1)}, u32[]{:S(2)}, u32[]{:S(2)}) collective-permute-start(f32[256,256]{1,0:T(8,128)S(1)} %get-tuple-element.74), channel_id=1, source_target_pairs={{0,4},{1,5},{2,6},{3,7},{4,8},{5,9},{6,10},{7,11},{8,12},{9,13},{1... | collective-permute-start | bytes 786440 | tf_op jit(solution)/shard_map/ppermute | solution.py:24

commit v12 on v11

--- a/solution.py
+++ b/solution.py
@@ -349,7 +349,7 @@
             [VMEM((4 * tile, width), BF16)],
         )(tables[step], a, *([acc] if step > 0 else []), *chunks)
 
-    pieces = (width // 4,) * 4
+    pieces = (width // 2, width // 2)
     acc = None
     for step in range(1, count - 1):
         now = arrivals[-1]

time: 68.4 us -> 68.3 us (level)
  waiting for transfers between devices: 23.1 us -> 32.7 us
  starting transfers between devices: 21.7 us -> 15 us
  Pallas kernels: 22.1 us -> 19.5 us
    ppermute x17 -> x13, waiting for transfers between devices: 23.1 us -> 32.7 us  [permute(): lax.ppermute(x, AXES, [(flat(*place), flat(*target(*place))) for place in...]
    ppermute x17 -> x13, starting transfers between devices: 21.7 us -> 15 us  [permute(): lax.ppermute(x, AXES, [(flat(*place), flat(*target(*place))) for place in...]
    pallas_call x4 -> x2, Pallas kernels: 3.4 us -> 2.05 us  [shards(): call(functools.partial(arrived_kernel, sum(pieces[:i])), 'arrived%d' % i,...]
    pallas_call x4 -> x2, Pallas kernels: 3.56 us -> 2.4 us  [shards(): call(functools.partial(last_kernel, count - 1, per_shard - 1, sum(pieces[...]
  transfers between devices with their start and end apart: 17 -> 13, of which waited for: 9 -> 9; matrix products, arithmetic and copies ran while one was open for 0% -> 0% of each run, Pallas kernels for 29% -> 24%
where the time goes in v12:
time: 68.3 us; the launch traced here: 68.1 us
  waiting for transfers between devices  32.7 us (48%)
  Pallas kernels  19.5 us (29%)
  starting transfers between devices  15 us (22%)
  between operations  0.77 us (1%)
    ppermute x13, waiting for transfers between devices, permute(): lax.ppermute(x, AXES, [(flat(*place), flat(*target(*place))) for place in...  32.7 us
    ppermute x13, starting transfers between devices, permute(): lax.ppermute(x, AXES, [(flat(*place), flat(*target(*place))) for place in...  15 us
    pallas_call x4, Pallas kernels, add(): call(functools.partial(add_kernel, step, list(range(len(chunks)))), 'add%...  6.12 us
    pallas_call x1, Pallas kernels, shards(): call(ham_kernel, 'ham', sds((blocks // 2, tall, 3 * LANES), BF16), (SMEM,...  2.51 us
    pallas_call x2, Pallas kernels, shards(): call(functools.partial(last_kernel, count - 1, per_shard - 1, sum(pieces[...  2.4 us
    pallas_call x2, Pallas kernels, shards(): call(functools.partial(arrived_kernel, sum(pieces[:i])), 'arrived%d' % i,...  2.05 us
    pallas_call x2, Pallas kernels, shards(): call(functools.partial(cut_kernel, h), 'cut%d' % h, sds((2, tile, dens_ti...  1.99 us
    pallas_call x1, Pallas kernels, shards(): call(own_kernel, 'own', (sds((rows, tile, width), F32), sds((rows, tile,...  1.69 us
  transfers between devices with their start and end apart: 13, of which 9 were waited for; matrix products, arithmetic and copies ran while one was open for 0% of the time, Pallas kernels for 24%

profile of v12, /device:TPU:0, one launch (start us, length us, event | category | flops | bytes accessed | tf_op | source)
XLA Modules:
  0.0 68.1 jit_solution(925389061715427963)
XLA Ops:
  0.6 0.0 copy-start
  0.6 1.0 %cut0.1.rest_0_ = f32[2,64,512]{2,1,0:T(8,128)S(1)} custom-call(f32[4,64,512]{2,1,0:T(8,128)} %dens.2), custom_call_target="tpu_custom_call" | custom-call | flops 1024 | bytes 1024 | tf_op jit(solution)/shard_map/cut0/pallas_call | solution.py:296
  1.7 3.1 %collective-permute-start.5 = (f32[2,64,512]{2,1,0:T(8,128)S(1)}, f32[2,64,512]{2,1,0:T(8,128)S(1)}, u32[]{:S(2)}, u32[]{:S(2)}) collective-permute-start(f32[2,64,512]{2,1,0:T(8,128)S(1)} %cut0.1.rest_0_), channel_id=1, source_target_pairs={{0,1},{1,3},{2,0},{3,2},{4,5},{5,7},{6,4},{7,6},{8,9},{9,11},{10,8... | collective-permute-start | bytes 786440 | tf_op jit(solution)/shard_map/ppermute | solution.py:24
  4.8 1.0 %cut1.1.rest_1_ = f32[2,64,512]{2,1,0:T(8,128)S(1)} custom-call(f32[4,64,512]{2,1,0:T(8,128)} %dens.2), custom_call_target="tpu_custom_call" | custom-call | flops 1024 | bytes 1024 | tf_op jit(solution)/shard_map/cut1/pallas_call | solution.py:296
  5.7 2.6 %collective-permute-start = (f32[2,64,512]{2,1,0:T(8,128)S(1)}, f32[2,64,512]{2,1,0:T(8,128)S(1)}, u32[]{:S(2)}, u32[]{:S(2)}) collective-permute-start(f32[2,64,512]{2,1,0:T(8,128)S(1)} %cut1.1.rest_1_), channel_id=1, source_target_pairs={{0,1},{1,3},{2,0},{3,2},{4,5},{5,7},{6,4},{7,6},{8,9},{9,11},{10,8... | collective-permute-start | bytes 786440 | tf_op jit(solution)/shard_map/ppermute | solution.py:24
  8.4 1.4 %table.1.dens_table = s32[4,16]{1,0:T(4,128)S(1)} custom-call(s32[4,8]{1,0:T(4,128)} %columns, s32[4]{0:T(128)} %counts.1), custom_call_target="tpu_custom_call" | custom-call | flops 1024 | bytes 1024 | tf_op jit(solution)/shard_map/table/pallas_call | solution.py:312
  9.8 0.4 collective-permute-start.3
  10.2 2.5 %collective-permute-start.2 = (s32[4,16]{1,0:T(4,128)S(1)}, s32[4,16]{1,0:T(4,128)S(1)}, u32[]{:S(2)}, u32[]{:S(2)}) collective-permute-start(s32[4,16]{1,0:T(4,128)S(1)} %table.1.dens_table), channel_id=1, source_target_pairs={{0,3},{1,2},{2,1},{3,0},{4,7},{5,6},{6,5},{7,4},{8,11},{9,10},{10,... | collective-permute-start | bytes 776 | tf_op jit(solution)/shard_map/ppermute | solution.py:24
  12.6 0.0 collective-permute-start.1
  12.6 2.5 %ham.2.a = bf16[8,256,384]{2,1,0:T(8,128)(2,1)S(1)} custom-call(s32[4,12]{1,0:T(4,128)} %ham_cols.1, s32[4]{0:T(128)} %ham_count.1, f32[4,64,768]{2,1,0:T(8,128)} %ham.3), custom_call_target="tpu_custom_call" | custom-call | flops 1024 | bytes 1024 | tf_op jit(solution)/shard_map/ham/pallas_call | solution.py:329
  15.2 0.0 collective-permute-done.5.rest_1_
  15.2 2.0 %collective-permute-start.6 = (f32[2,64,512]{2,1,0:T(8,128)S(1)}, f32[2,64,512]{2,1,0:T(8,128)S(1)}, u32[]{:S(2)}, u32[]{:S(2)}) collective-permute-start(f32[2,64,512]{2,1,0:T(8,128)S(1)} %collective-permute-done.5.rest_1_), channel_id=1, source_target_pairs={{0,1},{1,3},{2,0},{3,2},{4,5},{5,7},{6,4},{7,6},{8,9},{9,11},{10,8... | collective-permute-start | bytes 786440 | tf_op jit(solution)/shard_map/ppermute | solution.py:24
  17.1 0.0 collective-permute-done.3.dens_table
  17.1 2.2 %collective-permute-done.2.dens_table = s32[4,16]{1,0:T(4,128)S(1)} collective-permute-done((s32[4,16]{1,0:T(4,128)S(1)}, s32[4,16]{1,0:T(4,128)S(1)}, u32[]{:S(2)}, u32[]{:S(2)}) %collective-permute-start.2) | collective-permute-done | bytes 288 | tf_op jit(solution)/shard_map/ppermute | solution.py:24
  19.3 0.0 collective-permute-done.1.dens_table
  19.3 0.0 collective-permute-done.rest_2_
  19.3 0.6 collective-permute-start.4
  19.9 0.0 copy-done
  19.9 0.3 margin.1
  20.1 1.1 %pick.1 = bf16[2,512,1024]{2,1,0:T(8,128)(2,1)S(1)} custom-call(s32[4,16]{1,0:T(4,128)S(1)} %collective-permute-done.3.dens_table), custom_call_target="tpu_custom_call" | custom-call | flops 1024 | bytes 1024 | tf_op jit(solution)/shard_map/pick/pallas_call | solution.py:362
  21.3 1.6 %add0.1.rest_0_ = f32[256,1024]{1,0:T(8,128)S(1)} custom-call(s32[4,16]{1,0:T(4,128)S(1)} %table.1.dens_table, bf16[8,256,384]{2,1,0:T(8,128)(2,1)S(1)} %ham.2.a, f32[2,64,512]{2,1,0:T(8,128)S(1)} %cut0.1.rest_0_, f32[2,64,512]{2,1,0:T(8,128)S(1)} %cut1.1.rest_1_), custom_call_target="tpu_custom_call" | custom-call | flops 1024 | bytes 1024 | tf_op jit(solution)/shard_map/add0/pallas_call | solution.py:343
  22.9 2.5 %collective-permute-done.6.rest_1_ = f32[2,64,512]{2,1,0:T(8,128)S(1)} collective-permute-done((f32[2,64,512]{2,1,0:T(8,128)S(1)}, f32[2,64,512]{2,1,0:T(8,128)S(1)}, u32[]{:S(2)}, u32[]{:S(2)}) %collective-permute-start.6) | collective-permute-done | bytes 262176 | tf_op jit(solution)/shard_map/ppermute | solution.py:24
  25.4 1.0 %collective-permute-start.7 = (f32[2,64,512]{2,1,0:T(8,128)S(1)}, f32[2,64,512]{2,1,0:T(8,128)S(1)}, u32[]{:S(2)}, u32[]{:S(2)}) collective-permute-start(f32[2,64,512]{2,1,0:T(8,128)S(1)} %collective-permute-done.6.rest_1_), channel_id=1, source_target_pairs={{0,1},{1,3},{2,0},{3,2},{4,5},{5,7},{6,4},{7,6},{8,9},{9,11},{10,8... | collective-permute-start | bytes 786440 | tf_op jit(solution)/shard_map/ppermute | solution.py:24
  26.4 4.6 %collective-permute-done.4.rest_2_ = f32[2,64,512]{2,1,0:T(8,128)S(1)} collective-permute-done((f32[2,64,512]{2,1,0:T(8,128)S(1)}, f32[2,64,512]{2,1,0:T(8,128)S(1)}, u32[]{:S(2)}, u32[]{:S(2)}) %collective-permute-start.4) | collective-permute-done | bytes 262176 | tf_op jit(solution)/shard_map/ppermute | solution.py:24
  31.0 1.0 %collective-permute-start.8 = (f32[2,64,512]{2,1,0:T(8,128)S(1)}, f32[2,64,512]{2,1,0:T(8,128)S(1)}, u32[]{:S(2)}, u32[]{:S(2)}) collective-permute-start(f32[2,64,512]{2,1,0:T(8,128)S(1)} %collective-permute-done.4.rest_2_), channel_id=1, source_target_pairs={{0,1},{1,3},{2,0},{3,2},{4,5},{5,7},{6,4},{7,6},{8,9},{9,11},{10,8... | collective-permute-start | bytes 786440 | tf_op jit(solution)/shard_map/ppermute | solution.py:24
  32.0 1.6 %add1.1.rest_0_ = f32[256,1024]{1,0:T(8,128)S(1)} custom-call(s32[4,16]{1,0:T(4,128)S(1)} %collective-permute-done.1.dens_table, bf16[8,256,384]{2,1,0:T(8,128)(2,1)S(1)} %ham.2.a, f32[256,1024]{1,0:T(8,128)S(1)} %add0.1.rest_0_, f32[2,64,512]{2,1,0:T(8,128)S(1)} %collective-permute-done.5.rest_1_, f32[2,64,512]{2,1,0:T(8,128)S(1)} %collective-permute-done.rest_2_), custom_call_target="tpu_custom_call" | custom-call | flops 1024 | bytes 1024 | tf_op jit(solution)/shard_map/add1/pallas_call | solution.py:343
  33.6 1.6 %add2.1.rest_0_ = f32[256,1024]{1,0:T(8,128)S(1)} custom-call(s32[4,16]{1,0:T(4,128)S(1)} %collective-permute-done.2.dens_table, bf16[8,256,384]{2,1,0:T(8,128)(2,1)S(1)} %ham.2.a, f32[256,1024]{1,0:T(8,128)S(1)} %add1.1.rest_0_, f32[2,64,512]{2,1,0:T(8,128)S(1)} %collective-permute-done.6.rest_1_, f32[2,64,512]{2,1,0:T(8,128)S(1)} %collective-permute-done.4.rest_2_), custom_call_target="tpu_custom_call" | custom-call | flops 1024 | bytes 1024 | tf_op jit(solution)/shard_map/add2/pallas_call | solution.py:343
  35.3 1.3 %collective-permute-done.7.rest_1_ = f32[2,64,512]{2,1,0:T(8,128)S(1)} collective-permute-done((f32[2,64,512]{2,1,0:T(8,128)S(1)}, f32[2,64,512]{2,1,0:T(8,128)S(1)}, u32[]{:S(2)}, u32[]{:S(2)}) %collective-permute-start.7) | collective-permute-done | bytes 262176 | tf_op jit(solution)/shard_map/ppermute | solution.py:24
  36.6 1.2 %add3.1.acc_in = f32[256,1024]{1,0:T(8,128)S(1)} custom-call(s32[4,16]{1,0:T(4,128)S(1)} %collective-permute-done.3.dens_table, bf16[8,256,384]{2,1,0:T(8,128)(2,1)S(1)} %ham.2.a, f32[256,1024]{1,0:T(8,128)S(1)} %add2.1.rest_0_, f32[2,64,512]{2,1,0:T(8,128)S(1)} %collective-permute-done.7.rest_1_), custom_call_target="tpu_custom_call" | custom-call | flops 1024 | bytes 1024 | tf_op jit(solution)/shard_map/add3/pallas_call | solution.py:343
  37.9 2.5 %collective-permute-done.8.chunk = f32[2,64,512]{2,1,0:T(8,128)S(1)} collective-permute-done((f32[2,64,512]{2,1,0:T(8,128)S(1)}, f32[2,64,512]{2,1,0:T(8,128)S(1)}, u32[]{:S(2)}, u32[]{:S(2)}) %collective-permute-start.8) | collective-permute-done | bytes 262176 | tf_op jit(solution)/shard_map/ppermute | solution.py:24
  40.3 1.2 %last0.1 = (f32[256,512]{1,0:T(8,128)S(1)}, f32[256,512]{1,0:T(8,128)S(1)}, f32[256,512]{1,0:T(8,128)S(1)}) custom-call(bf16[8,256,384]{2,1,0:T(8,128)(2,1)S(1)} %ham.2.a, f32[256,1024]{1,0:T(8,128)S(1)} %add3.1.acc_in, f32[2,64,512]{2,1,0:T(8,128)S(1)} %collective-permute-done.8.chunk, bf16[2,512,1024]{2,1,0:T(8,128)(2,1)S(1)} %pick.1, ...), custom_call_target="tpu_custom_call" | custom-call | flops 1024 | bytes 1024 | tf_op jit(solution)/shard_map/last0/pallas_call | solution.py:378
  41.5 0.1 collective-permute-start.11
  41.6 0.5 collective-permute-start.12
  42.1 1.2 %last1.1 = (f32[256,512]{1,0:T(8,128)S(1)}, f32[256,512]{1,0:T(8,128)S(1)}, f32[256,512]{1,0:T(8,128)S(1)}) custom-call(bf16[8,256,384]{2,1,0:T(8,128)(2,1)S(1)} %ham.2.a, f32[256,1024]{1,0:T(8,128)S(1)} %add3.1.acc_in, f32[2,64,512]{2,1,0:T(8,128)S(1)} %collective-permute-done.8.chunk, bf16[2,512,1024]{2,1,0:T(8,128)(2,1)S(1)} %pick.1, ...), custom_call_target="tpu_custom_call" | custom-call | flops 1024 | bytes 1024 | tf_op jit(solution)/shard_map/last1/pallas_call | solution.py:378
  43.3 1.4 %collective-permute-start.9 = (f32[256,512]{1,0:T(8,128)S(1)}, f32[256,512]{1,0:T(8,128)S(1)}, u32[]{:S(2)}, u32[]{:S(2)}) collective-permute-start(f32[256,512]{1,0:T(8,128)S(1)} %get-tuple-element.57), channel_id=1, source_target_pairs={{0,12},{1,13},{2,14},{3,15},{4,0},{5,1},{6,2},{7,3},{8,4},{9,5},{1... | collective-permute-start | bytes 1572872 | tf_op jit(solution)/shard_map/ppermute | solution.py:24
  44.7 0.0 collective-permute-start.10
  44.7 1.7 %own.1 = (f32[4,64,1024]{2,1,0:T(8,128)}, f32[4,64,3072]{2,1,0:T(8,128)}) custom-call(bf16[3,256,256]{2,1,0:T(8,128)(2,1)S(1)} %get-tuple-element.40.m_hi, bf16[3,256,256]{2,1,0:T(8,128)(2,1)S(1)} %get-tuple-element.41.m_lo, f32[256,512]{1,0:T(8,128)S(1)} %get-tuple-element.53.rest_0_, f32[256,512]{1,0:T(8,128)S(1)} %get-tuple-element.55.rest_1_), custom_call_target="tpu_custom_call" | custom-call | flops 1024 | bytes 1024 | tf_op jit(solution)/shard_map/own/pallas_call | solution.py:391
  46.4 6.5 %collective-permute-done.11.below = f32[256,512]{1,0:T(8,128)S(1)} collective-permute-done((f32[256,512]{1,0:T(8,128)S(1)}, f32[256,512]{1,0:T(8,128)S(1)}, u32[]{:S(2)}, u32[]{:S(2)}) %collective-permute-start.11) | collective-permute-done | bytes 524320 | tf_op jit(solution)/shard_map/ppermute | solution.py:24
  52.9 3.0 %collective-permute-done.12.above = f32[256,512]{1,0:T(8,128)S(1)} collective-permute-done((f32[256,512]{1,0:T(8,128)S(1)}, f32[256,512]{1,0:T(8,128)S(1)}, u32[]{:S(2)}, u32[]{:S(2)}) %collective-permute-start.12) | collective-permute-done | bytes 524320 | tf_op jit(solution)/shard_map/ppermute | solution.py:24
  55.9 1.0 %arrived0.1.window_in = f32[4,64,3072]{2,1,0:T(8,128)} custom-call(f32[256,512]{1,0:T(8,128)S(1)} %collective-permute-done.11.below, f32[256,512]{1,0:T(8,128)S(1)} %collective-permute-done.12.above, f32[4,64,3072]{2,1,0:T(8,128)} %get-tuple-element.61.window_in), custom_call_target="tpu_custom_call", output_to_operand_aliasing={{}: (2, {})} | custom-call | flops 1024 | bytes 1024 | tf_op jit(solution)/shard_map/arrived0/pallas_call | solution.py:400
  56.9 7.2 %collective-permute-done.9.below = f32[256,512]{1,0:T(8,128)S(1)} collective-permute-done((f32[256,512]{1,0:T(8,128)S(1)}, f32[256,512]{1,0:T(8,128)S(1)}, u32[]{:S(2)}, u32[]{:S(2)}) %collective-permute-start.9) | collective-permute-done | bytes 524320 | tf_op jit(solution)/shard_map/ppermute | solution.py:24
  64.1 3.0 %collective-permute-done.10.above = f32[256,512]{1,0:T(8,128)S(1)} collective-permute-done((f32[256,512]{1,0:T(8,128)S(1)}, f32[256,512]{1,0:T(8,128)S(1)}, u32[]{:S(2)}, u32[]{:S(2)}) %collective-permute-start.10) | collective-permute-done | bytes 524320 | tf_op jit(solution)/shard_map/ppermute | solution.py:24
  67.1 1.0 %arrived1.1 = f32[4,64,3072]{2,1,0:T(8,128)} custom-call(f32[256,512]{1,0:T(8,128)S(1)} %collective-permute-done.9.below, f32[256,512]{1,0:T(8,128)S(1)} %collective-permute-done.10.above, f32[4,64,3072]{2,1,0:T(8,128)} %arrived0.1.window_in), custom_call_target="tpu_custom_call", output_to_operand_aliasing={{}: (2, {})} | custom-call | flops 1024 | bytes 1024 | tf_op jit(solution)/shard_map/arrived1/pallas_call | solution.py:400
Async XLA Ops:
  0.6 19.2 %copy-start = (f32[4,64,768]{2,1,0:T(8,128)S(1)}, f32[4,64,768]{2,1,0:T(8,128)}, u32[]{:S(2)}) copy-start(f32[4,64,768]{2,1,0:T(8,128)} %over.1) | copy-start | bytes 2359300
  1.7 13.5 %collective-permute-start.5 = (f32[2,64,512]{2,1,0:T(8,128)S(1)}, f32[2,64,512]{2,1,0:T(8,128)S(1)}, u32[]{:S(2)}, u32[]{:S(2)}) collective-permute-start(f32[2,64,512]{2,1,0:T(8,128)S(1)} %cut0.1.rest_0_), channel_id=1, source_target_pairs={{0,1},{1,3},{2,0},{3,2},{4,5},{5,7},{6,4},{7,6},{8,9},{9,11},{10,8... | collective-permute-start | bytes 786440 | tf_op jit(solution)/shard_map/ppermute | solution.py:24
  5.7 13.6 %collective-permute-start = (f32[2,64,512]{2,1,0:T(8,128)S(1)}, f32[2,64,512]{2,1,0:T(8,128)S(1)}, u32[]{:S(2)}, u32[]{:S(2)}) collective-permute-start(f32[2,64,512]{2,1,0:T(8,128)S(1)} %cut1.1.rest_1_), channel_id=1, source_target_pairs={{0,1},{1,3},{2,0},{3,2},{4,5},{5,7},{6,4},{7,6},{8,9},{9,11},{10,8... | collective-permute-start | bytes 786440 | tf_op jit(solution)/shard_map/ppermute | solution.py:24
  9.8 7.4 %collective-permute-start.3 = (s32[4,16]{1,0:T(4,128)S(1)}, s32[4,16]{1,0:T(4,128)S(1)}, u32[]{:S(2)}, u32[]{:S(2)}) collective-permute-start(s32[4,16]{1,0:T(4,128)S(1)} %table.1.dens_table), channel_id=1, source_target_pairs={{0,2},{1,0},{2,3},{3,1},{4,6},{5,4},{6,7},{7,5},{8,10},{9,8},{10,1... | collective-permute-start | bytes 776 | tf_op jit(solution)/shard_map/ppermute | solution.py:24
  10.2 9.1 %collective-permute-start.2 = (s32[4,16]{1,0:T(4,128)S(1)}, s32[4,16]{1,0:T(4,128)S(1)}, u32[]{:S(2)}, u32[]{:S(2)}) collective-permute-start(s32[4,16]{1,0:T(4,128)S(1)} %table.1.dens_table), channel_id=1, source_target_pairs={{0,3},{1,2},{2,1},{3,0},{4,7},{5,6},{6,5},{7,4},{8,11},{9,10},{10,... | collective-permute-start | bytes 776 | tf_op jit(solution)/shard_map/ppermute | solution.py:24
  12.6 6.6 %collective-permute-start.1 = (s32[4,16]{1,0:T(4,128)S(1)}, s32[4,16]{1,0:T(4,128)S(1)}, u32[]{:S(2)}, u32[]{:S(2)}) collective-permute-start(s32[4,16]{1,0:T(4,128)S(1)} %table.1.dens_table), channel_id=1, source_target_pairs={{0,1},{1,3},{2,0},{3,2},{4,5},{5,7},{6,4},{7,6},{8,9},{9,11},{10,8... | collective-permute-start | bytes 776 | tf_op jit(solution)/shard_map/ppermute | solution.py:24
  15.2 10.2 %collective-permute-start.6 = (f32[2,64,512]{2,1,0:T(8,128)S(1)}, f32[2,64,512]{2,1,0:T(8,128)S(1)}, u32[]{:S(2)}, u32[]{:S(2)}) collective-permute-start(f32[2,64,512]{2,1,0:T(8,128)S(1)} %collective-permute-done.5.rest_1_), channel_id=1, source_target_pairs={{0,1},{1,3},{2,0},{3,2},{4,5},{5,7},{6,4},{7,6},{8,9},{9,11},{10,8... | collective-permute-start | bytes 786440 | tf_op jit(solution)/shard_map/ppermute | solution.py:24
  19.3 11.7 %collective-permute-start.4 = (f32[2,64,512]{2,1,0:T(8,128)S(1)}, f32[2,64,512]{2,1,0:T(8,128)S(1)}, u32[]{:S(2)}, u32[]{:S(2)}) collective-permute-start(f32[2,64,512]{2,1,0:T(8,128)S(1)} %collective-permute-done.rest_2_), channel_id=1, source_target_pairs={{0,1},{1,3},{2,0},{3,2},{4,5},{5,7},{6,4},{7,6},{8,9},{9,11},{10,8... | collective-permute-start | bytes 786440 | tf_op jit(solution)/shard_map/ppermute | solution.py:24
  25.4 11.2 %collective-permute-start.7 = (f32[2,64,512]{2,1,0:T(8,128)S(1)}, f32[2,64,512]{2,1,0:T(8,128)S(1)}, u32[]{:S(2)}, u32[]{:S(2)}) collective-permute-start(f32[2,64,512]{2,1,0:T(8,128)S(1)} %collective-permute-done.6.rest_1_), channel_id=1, source_target_pairs={{0,1},{1,3},{2,0},{3,2},{4,5},{5,7},{6,4},{7,6},{8,9},{9,11},{10,8... | collective-permute-start | bytes 786440 | tf_op jit(solution)/shard_map/ppermute | solution.py:24
  31.0 9.4 %collective-permute-start.8 = (f32[2,64,512]{2,1,0:T(8,128)S(1)}, f32[2,64,512]{2,1,0:T(8,128)S(1)}, u32[]{:S(2)}, u32[]{:S(2)}) collective-permute-start(f32[2,64,512]{2,1,0:T(8,128)S(1)} %collective-permute-done.4.rest_2_), channel_id=1, source_target_pairs={{0,1},{1,3},{2,0},{3,2},{4,5},{5,7},{6,4},{7,6},{8,9},{9,11},{10,8... | collective-permute-start | bytes 786440 | tf_op jit(solution)/shard_map/ppermute | solution.py:24
  41.5 11.3 %collective-permute-start.11 = (f32[256,512]{1,0:T(8,128)S(1)}, f32[256,512]{1,0:T(8,128)S(1)}, u32[]{:S(2)}, u32[]{:S(2)}) collective-permute-start(f32[256,512]{1,0:T(8,128)S(1)} %get-tuple-element.59), channel_id=1, source_target_pairs={{0,12},{1,13},{2,14},{3,15},{4,0},{5,1},{6,2},{7,3},{8,4},{9,5},{1... | collective-permute-start | bytes 1572872 | tf_op jit(solution)/shard_map/ppermute | solution.py:24
  41.6 14.2 %collective-permute-start.12 = (f32[256,512]{1,0:T(8,128)S(1)}, f32[256,512]{1,0:T(8,128)S(1)}, u32[]{:S(2)}, u32[]{:S(2)}) collective-permute-start(f32[256,512]{1,0:T(8,128)S(1)} %get-tuple-element.60), channel_id=1, source_target_pairs={{0,4},{1,5},{2,6},{3,7},{4,8},{5,9},{6,10},{7,11},{8,12},{9,13},{1... | collective-permute-start | bytes 1572872 | tf_op jit(solution)/shard_map/ppermute | solution.py:24
  43.3 20.8 %collective-permute-start.9 = (f32[256,512]{1,0:T(8,128)S(1)}, f32[256,512]{1,0:T(8,128)S(1)}, u32[]{:S(2)}, u32[]{:S(2)}) collective-permute-start(f32[256,512]{1,0:T(8,128)S(1)} %get-tuple-element.57), channel_id=1, source_target_pairs={{0,12},{1,13},{2,14},{3,15},{4,0},{5,1},{6,2},{7,3},{8,4},{9,5},{1... | collective-permute-start | bytes 1572872 | tf_op jit(solution)/shard_map/ppermute | solution.py:24
  44.7 22.4 %collective-permute-start.10 = (f32[256,512]{1,0:T(8,128)S(1)}, f32[256,512]{1,0:T(8,128)S(1)}, u32[]{:S(2)}, u32[]{:S(2)}) collective-permute-start(f32[256,512]{1,0:T(8,128)S(1)} %get-tuple-element.58), channel_id=1, source_target_pairs={{0,4},{1,5},{2,6},{3,7},{4,8},{5,9},{6,10},{7,11},{8,12},{9,13},{1... | collective-permute-start | bytes 1572872 | tf_op jit(solution)/shard_map/ppermute | solution.py:24

commit v13 on v12

--- a/solution.py
+++ b/solution.py
@@ -109,7 +109,7 @@
 
 
 def lane_blocks(width, step=256):
-    return [slice(i, i + step) for i in range(0, width, step)]
+    return [slice(i, min(i + step, width)) for i in range(0, width, step)]
 
 
 def ham_kernel(ham_cols, ham_count, ham, a, ham_table, ham_here, sems):
@@ -250,7 +250,7 @@
         copy.wait()
 
 
-def arrived_kernel(at, below, above, window_in, window, sems):
+def arrived_kernel(at, above, below, window_in, window, sems):
     rows, tile, triple = window.shape
     copies = [
         pltpu.make_async_copy(
@@ -349,7 +349,7 @@
             [VMEM((4 * tile, width), BF16)],
         )(tables[step], a, *([acc] if step > 0 else []), *chunks)
 
-    pieces = (width // 2, width // 2)
+    pieces = (width * 3 // 8, width * 3 // 8, width // 4)
     acc = None
     for step in range(1, count - 1):
         now = arrivals[-1]
@@ -386,8 +386,8 @@
         if i + 1 < len(pieces):
             part, acc = lax.optimization_barrier((part, acc))
         parts.append(part)
+        befores.append(rotate(below, 1))
         afters.append(rotate(above, -1))
-        befores.append(rotate(below, 1))
     product, window = call(
         own_kernel,
         "own",
@@ -405,7 +405,7 @@
             pl.ANY,
             [pltpu.SemaphoreType.DMA((2, rows))],
             {2: 0},
-        )(afters[i], befores[i], window)
+        )(befores[i], afters[i], window)
     return (product, window)
 
 

time: 68.3 us -> 67.5 us (0.988)
  waiting for transfers between devices: 32.7 us -> 28.3 us
  starting transfers between devices: 15 us -> 16.8 us
  Pallas kernels: 19.5 us -> 21.1 us
    ppermute x13 -> x15, waiting for transfers between devices: 32.7 us -> 28.3 us  [permute(): lax.ppermute(x, AXES, [(flat(*place), flat(*target(*place))) for place in...]
    ppermute x13 -> x15, starting transfers between devices: 15 us -> 16.8 us  [permute(): lax.ppermute(x, AXES, [(flat(*place), flat(*target(*place))) for place in...]
    pallas_call x2 -> x3, Pallas kernels: 2.4 us -> 3.2 us  [shards(): call(functools.partial(last_kernel, count - 1, per_shard - 1, sum(pieces[...]
    pallas_call x2 -> x3, Pallas kernels: 2.05 us -> 2.72 us  [shards(): call(functools.partial(arrived_kernel, sum(pieces[:i])), 'arrived%d' % i,...]
  transfers between devices with their start and end apart: 13 -> 15, of which waited for: 9 -> 10; matrix products, arithmetic and copies ran while one was open for 0% -> 0% of each run, Pallas kernels for 24% -> 27%
where the time goes in v13:
time: 67.5 us; the launch traced here: 66.9 us
  waiting for transfers between devices  28.3 us (42%)
  Pallas kernels  21.1 us (31%)
  starting transfers between devices  16.8 us (25%)
  between operations  0.8 us (1%)
    ppermute x15, waiting for transfers between devices, permute(): lax.ppermute(x, AXES, [(flat(*place), flat(*target(*place))) for place in...  28.3 us
    ppermute x15, starting transfers between devices, permute(): lax.ppermute(x, AXES, [(flat(*place), flat(*target(*place))) for place in...  16.8 us
    pallas_call x4, Pallas kernels, add(): call(functools.partial(add_kernel, step, list(range(len(chunks)))), 'add%...  6.14 us
    pallas_call x3, Pallas kernels, shards(): call(functools.partial(last_kernel, count - 1, per_shard - 1, sum(pieces[...  3.2 us
    pallas_call x3, Pallas kernels, shards(): call(functools.partial(arrived_kernel, sum(pieces[:i])), 'arrived%d' % i,...  2.72 us
    pallas_call x1, Pallas kernels, shards(): call(ham_kernel, 'ham', sds((blocks // 2, tall, 3 * LANES), BF16), (SMEM,...  2.5 us
    pallas_call x2, Pallas kernels, shards(): call(functools.partial(cut_kernel, h), 'cut%d' % h, sds((2, tile, dens_ti...  1.99 us
    pallas_call x1, Pallas kernels, shards(): call(own_kernel, 'own', (sds((rows, tile, width), F32), sds((rows, tile,...  1.71 us
  transfers between devices with their start and end apart: 15, of which 10 were waited for; matrix products, arithmetic and copies ran while one was open for 0% of the time, Pallas kernels for 27%

profile of v13, /device:TPU:0, one launch (start us, length us, event | category | flops | bytes accessed | tf_op | source)
XLA Modules:
  0.0 66.9 jit_solution(11465564673293554942)
XLA Ops:
  0.6 0.0 copy-start
  0.6 1.0 %cut0.1.rest_0_ = f32[2,64,512]{2,1,0:T(8,128)S(1)} custom-call(f32[4,64,512]{2,1,0:T(8,128)} %dens.2), custom_call_target="tpu_custom_call" | custom-call | flops 1024 | bytes 1024 | tf_op jit(solution)/shard_map/cut0/pallas_call | solution.py:296
  1.7 3.1 %collective-permute-start.5 = (f32[2,64,512]{2,1,0:T(8,128)S(1)}, f32[2,64,512]{2,1,0:T(8,128)S(1)}, u32[]{:S(2)}, u32[]{:S(2)}) collective-permute-start(f32[2,64,512]{2,1,0:T(8,128)S(1)} %cut0.1.rest_0_), channel_id=1, source_target_pairs={{0,1},{1,3},{2,0},{3,2},{4,5},{5,7},{6,4},{7,6},{8,9},{9,11},{10,8... | collective-permute-start | bytes 786440 | tf_op jit(solution)/shard_map/ppermute | solution.py:24
  4.8 1.0 %cut1.1.rest_1_ = f32[2,64,512]{2,1,0:T(8,128)S(1)} custom-call(f32[4,64,512]{2,1,0:T(8,128)} %dens.2), custom_call_target="tpu_custom_call" | custom-call | flops 1024 | bytes 1024 | tf_op jit(solution)/shard_map/cut1/pallas_call | solution.py:296
  5.7 2.6 %collective-permute-start = (f32[2,64,512]{2,1,0:T(8,128)S(1)}, f32[2,64,512]{2,1,0:T(8,128)S(1)}, u32[]{:S(2)}, u32[]{:S(2)}) collective-permute-start(f32[2,64,512]{2,1,0:T(8,128)S(1)} %cut1.1.rest_1_), channel_id=1, source_target_pairs={{0,1},{1,3},{2,0},{3,2},{4,5},{5,7},{6,4},{7,6},{8,9},{9,11},{10,8... | collective-permute-start | bytes 786440 | tf_op jit(solution)/shard_map/ppermute | solution.py:24
  8.4 1.4 %table.1.dens_table = s32[4,16]{1,0:T(4,128)S(1)} custom-call(s32[4,8]{1,0:T(4,128)} %columns, s32[4]{0:T(128)} %counts.1), custom_call_target="tpu_custom_call" | custom-call | flops 1024 | bytes 1024 | tf_op jit(solution)/shard_map/table/pallas_call | solution.py:312
  9.8 0.4 collective-permute-start.3
  10.2 2.5 %collective-permute-start.2 = (s32[4,16]{1,0:T(4,128)S(1)}, s32[4,16]{1,0:T(4,128)S(1)}, u32[]{:S(2)}, u32[]{:S(2)}) collective-permute-start(s32[4,16]{1,0:T(4,128)S(1)} %table.1.dens_table), channel_id=1, source_target_pairs={{0,3},{1,2},{2,1},{3,0},{4,7},{5,6},{6,5},{7,4},{8,11},{9,10},{10,... | collective-permute-start | bytes 776 | tf_op jit(solution)/shard_map/ppermute | solution.py:24
  12.6 0.0 collective-permute-start.1
  12.6 2.5 %ham.2.a = bf16[8,256,384]{2,1,0:T(8,128)(2,1)S(1)} custom-call(s32[4,12]{1,0:T(4,128)} %ham_cols.1, s32[4]{0:T(128)} %ham_count.1, f32[4,64,768]{2,1,0:T(8,128)} %ham.3), custom_call_target="tpu_custom_call" | custom-call | flops 1024 | bytes 1024 | tf_op jit(solution)/shard_map/ham/pallas_call | solution.py:329
  15.2 0.0 collective-permute-done.5.rest_1_
  15.2 2.0 %collective-permute-start.6 = (f32[2,64,512]{2,1,0:T(8,128)S(1)}, f32[2,64,512]{2,1,0:T(8,128)S(1)}, u32[]{:S(2)}, u32[]{:S(2)}) collective-permute-start(f32[2,64,512]{2,1,0:T(8,128)S(1)} %collective-permute-done.5.rest_1_), channel_id=1, source_target_pairs={{0,1},{1,3},{2,0},{3,2},{4,5},{5,7},{6,4},{7,6},{8,9},{9,11},{10,8... | collective-permute-start | bytes 786440 | tf_op jit(solution)/shard_map/ppermute | solution.py:24
  17.1 0.0 collective-permute-done.3.dens_table
  17.1 2.2 %collective-permute-done.2.dens_table = s32[4,16]{1,0:T(4,128)S(1)} collective-permute-done((s32[4,16]{1,0:T(4,128)S(1)}, s32[4,16]{1,0:T(4,128)S(1)}, u32[]{:S(2)}, u32[]{:S(2)}) %collective-permute-start.2) | collective-permute-done | bytes 288 | tf_op jit(solution)/shard_map/ppermute | solution.py:24
  19.3 0.0 collective-permute-done.1.dens_table
  19.3 0.0 collective-permute-done.rest_2_
  19.3 0.6 collective-permute-start.4
  19.9 0.3 margin.1
  20.1 1.1 %pick.1 = bf16[2,512,1024]{2,1,0:T(8,128)(2,1)S(1)} custom-call(s32[4,16]{1,0:T(4,128)S(1)} %collective-permute-done.3.dens_table), custom_call_target="tpu_custom_call" | custom-call | flops 1024 | bytes 1024 | tf_op jit(solution)/shard_map/pick/pallas_call | solution.py:362
  21.3 1.6 %add0.1.rest_0_ = f32[256,1024]{1,0:T(8,128)S(1)} custom-call(s32[4,16]{1,0:T(4,128)S(1)} %table.1.dens_table, bf16[8,256,384]{2,1,0:T(8,128)(2,1)S(1)} %ham.2.a, f32[2,64,512]{2,1,0:T(8,128)S(1)} %cut0.1.rest_0_, f32[2,64,512]{2,1,0:T(8,128)S(1)} %cut1.1.rest_1_), custom_call_target="tpu_custom_call" | custom-call | flops 1024 | bytes 1024 | tf_op jit(solution)/shard_map/add0/pallas_call | solution.py:343
  22.9 2.5 %collective-permute-done.6.rest_1_ = f32[2,64,512]{2,1,0:T(8,128)S(1)} collective-permute-done((f32[2,64,512]{2,1,0:T(8,128)S(1)}, f32[2,64,512]{2,1,0:T(8,128)S(1)}, u32[]{:S(2)}, u32[]{:S(2)}) %collective-permute-start.6) | collective-permute-done | bytes 262176 | tf_op jit(solution)/shard_map/ppermute | solution.py:24
  25.4 1.0 %collective-permute-start.7 = (f32[2,64,512]{2,1,0:T(8,128)S(1)}, f32[2,64,512]{2,1,0:T(8,128)S(1)}, u32[]{:S(2)}, u32[]{:S(2)}) collective-permute-start(f32[2,64,512]{2,1,0:T(8,128)S(1)} %collective-permute-done.6.rest_1_), channel_id=1, source_target_pairs={{0,1},{1,3},{2,0},{3,2},{4,5},{5,7},{6,4},{7,6},{8,9},{9,11},{10,8... | collective-permute-start | bytes 786440 | tf_op jit(solution)/shard_map/ppermute | solution.py:24
  26.4 4.6 %collective-permute-done.4.rest_2_ = f32[2,64,512]{2,1,0:T(8,128)S(1)} collective-permute-done((f32[2,64,512]{2,1,0:T(8,128)S(1)}, f32[2,64,512]{2,1,0:T(8,128)S(1)}, u32[]{:S(2)}, u32[]{:S(2)}) %collective-permute-start.4) | collective-permute-done | bytes 262176 | tf_op jit(solution)/shard_map/ppermute | solution.py:24
  31.0 1.0 %collective-permute-start.8 = (f32[2,64,512]{2,1,0:T(8,128)S(1)}, f32[2,64,512]{2,1,0:T(8,128)S(1)}, u32[]{:S(2)}, u32[]{:S(2)}) collective-permute-start(f32[2,64,512]{2,1,0:T(8,128)S(1)} %collective-permute-done.4.rest_2_), channel_id=1, source_target_pairs={{0,1},{1,3},{2,0},{3,2},{4,5},{5,7},{6,4},{7,6},{8,9},{9,11},{10,8... | collective-permute-start | bytes 786440 | tf_op jit(solution)/shard_map/ppermute | solution.py:24
  32.0 1.6 %add1.1.rest_0_ = f32[256,1024]{1,0:T(8,128)S(1)} custom-call(s32[4,16]{1,0:T(4,128)S(1)} %collective-permute-done.1.dens_table, bf16[8,256,384]{2,1,0:T(8,128)(2,1)S(1)} %ham.2.a, f32[256,1024]{1,0:T(8,128)S(1)} %add0.1.rest_0_, f32[2,64,512]{2,1,0:T(8,128)S(1)} %collective-permute-done.5.rest_1_, f32[2,64,512]{2,1,0:T(8,128)S(1)} %collective-permute-done.rest_2_), custom_call_target="tpu_custom_call" | custom-call | flops 1024 | bytes 1024 | tf_op jit(solution)/shard_map/add1/pallas_call | solution.py:343
  33.6 1.7 %add2.1.rest_0_ = f32[256,1024]{1,0:T(8,128)S(1)} custom-call(s32[4,16]{1,0:T(4,128)S(1)} %collective-permute-done.2.dens_table, bf16[8,256,384]{2,1,0:T(8,128)(2,1)S(1)} %ham.2.a, f32[256,1024]{1,0:T(8,128)S(1)} %add1.1.rest_0_, f32[2,64,512]{2,1,0:T(8,128)S(1)} %collective-permute-done.6.rest_1_, f32[2,64,512]{2,1,0:T(8,128)S(1)} %collective-permute-done.4.rest_2_), custom_call_target="tpu_custom_call" | custom-call | flops 1024 | bytes 1024 | tf_op jit(solution)/shard_map/add2/pallas_call | solution.py:343
  35.3 1.3 %collective-permute-done.7.rest_1_ = f32[2,64,512]{2,1,0:T(8,128)S(1)} collective-permute-done((f32[2,64,512]{2,1,0:T(8,128)S(1)}, f32[2,64,512]{2,1,0:T(8,128)S(1)}, u32[]{:S(2)}, u32[]{:S(2)}) %collective-permute-start.7) | collective-permute-done | bytes 262176 | tf_op jit(solution)/shard_map/ppermute | solution.py:24
  36.6 1.2 %add3.1.acc_in = f32[256,1024]{1,0:T(8,128)S(1)} custom-call(s32[4,16]{1,0:T(4,128)S(1)} %collective-permute-done.3.dens_table, bf16[8,256,384]{2,1,0:T(8,128)(2,1)S(1)} %ham.2.a, f32[256,1024]{1,0:T(8,128)S(1)} %add2.1.rest_0_, f32[2,64,512]{2,1,0:T(8,128)S(1)} %collective-permute-done.7.rest_1_), custom_call_target="tpu_custom_call" | custom-call | flops 1024 | bytes 1024 | tf_op jit(solution)/shard_map/add3/pallas_call | solution.py:343
  37.9 2.5 %collective-permute-done.8.chunk = f32[2,64,512]{2,1,0:T(8,128)S(1)} collective-permute-done((f32[2,64,512]{2,1,0:T(8,128)S(1)}, f32[2,64,512]{2,1,0:T(8,128)S(1)}, u32[]{:S(2)}, u32[]{:S(2)}) %collective-permute-start.8) | collective-permute-done | bytes 262176 | tf_op jit(solution)/shard_map/ppermute | solution.py:24
  40.3 1.2 %last0.1 = (f32[256,384]{1,0:T(8,128)S(1)}, f32[256,384]{1,0:T(8,128)S(1)}, f32[256,384]{1,0:T(8,128)S(1)}) custom-call(bf16[8,256,384]{2,1,0:T(8,128)(2,1)S(1)} %ham.2.a, f32[256,1024]{1,0:T(8,128)S(1)} %add3.1.acc_in, f32[2,64,512]{2,1,0:T(8,128)S(1)} %collective-permute-done.8.chunk, bf16[2,512,1024]{2,1,0:T(8,128)(2,1)S(1)} %pick.1, ...), custom_call_target="tpu_custom_call" | custom-call | flops 1024 | bytes 1024 | tf_op jit(solution)/shard_map/last0/pallas_call | solution.py:378
  41.5 0.1 collective-permute-start.13
  41.6 1.7 %collective-permute-start.14 = (f32[256,384]{1,0:T(8,128)S(1)}, f32[256,384]{1,0:T(8,128)S(1)}, u32[]{:S(2)}, u32[]{:S(2)}) collective-permute-start(f32[256,384]{1,0:T(8,128)S(1)} %get-tuple-element.70), channel_id=1, source_target_pairs={{0,12},{1,13},{2,14},{3,15},{4,0},{5,1},{6,2},{7,3},{8,4},{9,5},{1... | collective-permute-start | bytes 1179656 | tf_op jit(solution)/shard_map/ppermute | solution.py:24
  43.3 1.2 %last1.1 = (f32[256,384]{1,0:T(8,128)S(1)}, f32[256,384]{1,0:T(8,128)S(1)}, f32[256,384]{1,0:T(8,128)S(1)}) custom-call(bf16[8,256,384]{2,1,0:T(8,128)(2,1)S(1)} %ham.2.a, f32[256,1024]{1,0:T(8,128)S(1)} %add3.1.acc_in, f32[2,64,512]{2,1,0:T(8,128)S(1)} %collective-permute-done.8.chunk, bf16[2,512,1024]{2,1,0:T(8,128)(2,1)S(1)} %pick.1, ...), custom_call_target="tpu_custom_call" | custom-call | flops 1024 | bytes 1024 | tf_op jit(solution)/shard_map/last1/pallas_call | solution.py:378
  44.5 0.1 collective-permute-start.11
  44.5 1.7 %collective-permute-start.12 = (f32[256,384]{1,0:T(8,128)S(1)}, f32[256,384]{1,0:T(8,128)S(1)}, u32[]{:S(2)}, u32[]{:S(2)}) collective-permute-start(f32[256,384]{1,0:T(8,128)S(1)} %get-tuple-element.68), channel_id=1, source_target_pairs={{0,12},{1,13},{2,14},{3,15},{4,0},{5,1},{6,2},{7,3},{8,4},{9,5},{1... | collective-permute-start | bytes 1179656 | tf_op jit(solution)/shard_map/ppermute | solution.py:24
  46.3 0.9 %last2.1 = (f32[256,256]{1,0:T(8,128)S(1)}, f32[256,256]{1,0:T(8,128)S(1)}, f32[256,256]{1,0:T(8,128)S(1)}) custom-call(bf16[8,256,384]{2,1,0:T(8,128)(2,1)S(1)} %ham.2.a, f32[256,1024]{1,0:T(8,128)S(1)} %add3.1.acc_in, f32[2,64,512]{2,1,0:T(8,128)S(1)} %collective-permute-done.8.chunk, bf16[2,512,1024]{2,1,0:T(8,128)(2,1)S(1)} %pick.1, ...), custom_call_target="tpu_custom_call" | custom-call | flops 1024 | bytes 1024 | tf_op jit(solution)/shard_map/last2/pallas_call | solution.py:378
  47.1 0.1 collective-permute-start.9
  47.2 3.8 %collective-permute-done.13.above = f32[256,384]{1,0:T(8,128)S(1)} collective-permute-done((f32[256,384]{1,0:T(8,128)S(1)}, f32[256,384]{1,0:T(8,128)S(1)}, u32[]{:S(2)}, u32[]{:S(2)}) %collective-permute-start.13) | collective-permute-done | bytes 393248 | tf_op jit(solution)/shard_map/ppermute | solution.py:24
  51.1 0.0 collective-permute-start.10
  51.1 1.7 %own.1 = (f32[4,64,1024]{2,1,0:T(8,128)}, f32[4,64,3072]{2,1,0:T(8,128)}) custom-call(bf16[3,256,256]{2,1,0:T(8,128)(2,1)S(1)} %get-tuple-element.45.m_hi, bf16[3,256,256]{2,1,0:T(8,128)(2,1)S(1)} %get-tuple-element.46.m_lo, f32[256,384]{1,0:T(8,128)S(1)} %get-tuple-element.58.rest_0_, f32[256,384]{1,0:T(8,128)S(1)} %get-tuple-element.61.rest_1_, ...), custom_call_target="tpu_custom_call" | custom-call | flops 1024 | bytes 1024 | tf_op jit(solution)/shard_map/own/pallas_call | solution.py:391
  52.8 0.0 collective-permute-done.14.below
  52.8 0.9 %arrived0.1.window_in = f32[4,64,3072]{2,1,0:T(8,128)} custom-call(f32[256,384]{1,0:T(8,128)S(1)} %collective-permute-done.13.above, f32[256,384]{1,0:T(8,128)S(1)} %collective-permute-done.14.below, f32[4,64,3072]{2,1,0:T(8,128)} %get-tuple-element.71.window_in), custom_call_target="tpu_custom_call", output_to_operand_aliasing={{}: (2, {})} | custom-call | flops 1024 | bytes 1024 | tf_op jit(solution)/shard_map/arrived0/pallas_call | solution.py:400
  53.7 5.7 %collective-permute-done.11.above = f32[256,384]{1,0:T(8,128)S(1)} collective-permute-done((f32[256,384]{1,0:T(8,128)S(1)}, f32[256,384]{1,0:T(8,128)S(1)}, u32[]{:S(2)}, u32[]{:S(2)}) %collective-permute-start.11) | collective-permute-done | bytes 393248 | tf_op jit(solution)/shard_map/ppermute | solution.py:24
  59.5 1.7 %collective-permute-done.12.below = f32[256,384]{1,0:T(8,128)S(1)} collective-permute-done((f32[256,384]{1,0:T(8,128)S(1)}, f32[256,384]{1,0:T(8,128)S(1)}, u32[]{:S(2)}, u32[]{:S(2)}) %collective-permute-start.12) | collective-permute-done | bytes 393248 | tf_op jit(solution)/shard_map/ppermute | solution.py:24
  61.2 0.9 %arrived1.1.window_in = f32[4,64,3072]{2,1,0:T(8,128)} custom-call(f32[256,384]{1,0:T(8,128)S(1)} %collective-permute-done.11.above, f32[256,384]{1,0:T(8,128)S(1)} %collective-permute-done.12.below, f32[4,64,3072]{2,1,0:T(8,128)} %arrived0.1.window_in), custom_call_target="tpu_custom_call", output_to_operand_aliasing={{}: (2, {})} | custom-call | flops 1024 | bytes 1024 | tf_op jit(solution)/shard_map/arrived1/pallas_call | solution.py:400
  62.1 3.0 %collective-permute-done.9.above = f32[256,256]{1,0:T(8,128)S(1)} collective-permute-done((f32[256,256]{1,0:T(8,128)S(1)}, f32[256,256]{1,0:T(8,128)S(1)}, u32[]{:S(2)}, u32[]{:S(2)}) %collective-permute-start.9) | collective-permute-done | bytes 262176 | tf_op jit(solution)/shard_map/ppermute | solution.py:24
  65.1 1.0 %collective-permute-done.10.below = f32[256,256]{1,0:T(8,128)S(1)} collective-permute-done((f32[256,256]{1,0:T(8,128)S(1)}, f32[256,256]{1,0:T(8,128)S(1)}, u32[]{:S(2)}, u32[]{:S(2)}) %collective-permute-start.10) | collective-permute-done | bytes 262176 | tf_op jit(solution)/shard_map/ppermute | solution.py:24
  66.1 0.8 %arrived2.1 = f32[4,64,3072]{2,1,0:T(8,128)} custom-call(f32[256,256]{1,0:T(8,128)S(1)} %collective-permute-done.9.above, f32[256,256]{1,0:T(8,128)S(1)} %collective-permute-done.10.below, f32[4,64,3072]{2,1,0:T(8,128)} %arrived1.1.window_in), custom_call_target="tpu_custom_call", output_to_operand_aliasing={{}: (2, {})} | custom-call | flops 1024 | bytes 1024 | tf_op jit(solution)/shard_map/arrived2/pallas_call | solution.py:400
  (1 shorter events, 0.0 us)
Async XLA Ops:
  0.6 19.2 %copy-start = (f32[4,64,768]{2,1,0:T(8,128)S(1)}, f32[4,64,768]{2,1,0:T(8,128)}, u32[]{:S(2)}) copy-start(f32[4,64,768]{2,1,0:T(8,128)} %over.1) | copy-start | bytes 2359300
  1.7 13.5 %collective-permute-start.5 = (f32[2,64,512]{2,1,0:T(8,128)S(1)}, f32[2,64,512]{2,1,0:T(8,128)S(1)}, u32[]{:S(2)}, u32[]{:S(2)}) collective-permute-start(f32[2,64,512]{2,1,0:T(8,128)S(1)} %cut0.1.rest_0_), channel_id=1, source_target_pairs={{0,1},{1,3},{2,0},{3,2},{4,5},{5,7},{6,4},{7,6},{8,9},{9,11},{10,8... | collective-permute-start | bytes 786440 | tf_op jit(solution)/shard_map/ppermute | solution.py:24
  5.7 13.6 %collective-permute-start = (f32[2,64,512]{2,1,0:T(8,128)S(1)}, f32[2,64,512]{2,1,0:T(8,128)S(1)}, u32[]{:S(2)}, u32[]{:S(2)}) collective-permute-start(f32[2,64,512]{2,1,0:T(8,128)S(1)} %cut1.1.rest_1_), channel_id=1, source_target_pairs={{0,1},{1,3},{2,0},{3,2},{4,5},{5,7},{6,4},{7,6},{8,9},{9,11},{10,8... | collective-permute-start | bytes 786440 | tf_op jit(solution)/shard_map/ppermute | solution.py:24
  9.8 7.4 %collective-permute-start.3 = (s32[4,16]{1,0:T(4,128)S(1)}, s32[4,16]{1,0:T(4,128)S(1)}, u32[]{:S(2)}, u32[]{:S(2)}) collective-permute-start(s32[4,16]{1,0:T(4,128)S(1)} %table.1.dens_table), channel_id=1, source_target_pairs={{0,2},{1,0},{2,3},{3,1},{4,6},{5,4},{6,7},{7,5},{8,10},{9,8},{10,1... | collective-permute-start | bytes 776 | tf_op jit(solution)/shard_map/ppermute | solution.py:24
  10.2 9.1 %collective-permute-start.2 = (s32[4,16]{1,0:T(4,128)S(1)}, s32[4,16]{1,0:T(4,128)S(1)}, u32[]{:S(2)}, u32[]{:S(2)}) collective-permute-start(s32[4,16]{1,0:T(4,128)S(1)} %table.1.dens_table), channel_id=1, source_target_pairs={{0,3},{1,2},{2,1},{3,0},{4,7},{5,6},{6,5},{7,4},{8,11},{9,10},{10,... | collective-permute-start | bytes 776 | tf_op jit(solution)/shard_map/ppermute | solution.py:24
  12.6 6.6 %collective-permute-start.1 = (s32[4,16]{1,0:T(4,128)S(1)}, s32[4,16]{1,0:T(4,128)S(1)}, u32[]{:S(2)}, u32[]{:S(2)}) collective-permute-start(s32[4,16]{1,0:T(4,128)S(1)} %table.1.dens_table), channel_id=1, source_target_pairs={{0,1},{1,3},{2,0},{3,2},{4,5},{5,7},{6,4},{7,6},{8,9},{9,11},{10,8... | collective-permute-start | bytes 776 | tf_op jit(solution)/shard_map/ppermute | solution.py:24
  15.2 10.2 %collective-permute-start.6 = (f32[2,64,512]{2,1,0:T(8,128)S(1)}, f32[2,64,512]{2,1,0:T(8,128)S(1)}, u32[]{:S(2)}, u32[]{:S(2)}) collective-permute-start(f32[2,64,512]{2,1,0:T(8,128)S(1)} %collective-permute-done.5.rest_1_), channel_id=1, source_target_pairs={{0,1},{1,3},{2,0},{3,2},{4,5},{5,7},{6,4},{7,6},{8,9},{9,11},{10,8... | collective-permute-start | bytes 786440 | tf_op jit(solution)/shard_map/ppermute | solution.py:24
  19.3 11.7 %collective-permute-start.4 = (f32[2,64,512]{2,1,0:T(8,128)S(1)}, f32[2,64,512]{2,1,0:T(8,128)S(1)}, u32[]{:S(2)}, u32[]{:S(2)}) collective-permute-start(f32[2,64,512]{2,1,0:T(8,128)S(1)} %collective-permute-done.rest_2_), channel_id=1, source_target_pairs={{0,1},{1,3},{2,0},{3,2},{4,5},{5,7},{6,4},{7,6},{8,9},{9,11},{10,8... | collective-permute-start | bytes 786440 | tf_op jit(solution)/shard_map/ppermute | solution.py:24
  25.4 11.2 %collective-permute-start.7 = (f32[2,64,512]{2,1,0:T(8,128)S(1)}, f32[2,64,512]{2,1,0:T(8,128)S(1)}, u32[]{:S(2)}, u32[]{:S(2)}) collective-permute-start(f32[2,64,512]{2,1,0:T(8,128)S(1)} %collective-permute-done.6.rest_1_), channel_id=1, source_target_pairs={{0,1},{1,3},{2,0},{3,2},{4,5},{5,7},{6,4},{7,6},{8,9},{9,11},{10,8... | collective-permute-start | bytes 786440 | tf_op jit(solution)/shard_map/ppermute | solution.py:24
  31.0 9.4 %collective-permute-start.8 = (f32[2,64,512]{2,1,0:T(8,128)S(1)}, f32[2,64,512]{2,1,0:T(8,128)S(1)}, u32[]{:S(2)}, u32[]{:S(2)}) collective-permute-start(f32[2,64,512]{2,1,0:T(8,128)S(1)} %collective-permute-done.4.rest_2_), channel_id=1, source_target_pairs={{0,1},{1,3},{2,0},{3,2},{4,5},{5,7},{6,4},{7,6},{8,9},{9,11},{10,8... | collective-permute-start | bytes 786440 | tf_op jit(solution)/shard_map/ppermute | solution.py:24
  41.5 9.6 %collective-permute-start.13 = (f32[256,384]{1,0:T(8,128)S(1)}, f32[256,384]{1,0:T(8,128)S(1)}, u32[]{:S(2)}, u32[]{:S(2)}) collective-permute-start(f32[256,384]{1,0:T(8,128)S(1)} %get-tuple-element.69), channel_id=1, source_target_pairs={{0,4},{1,5},{2,6},{3,7},{4,8},{5,9},{6,10},{7,11},{8,12},{9,13},{1... | collective-permute-start | bytes 1179656 | tf_op jit(solution)/shard_map/ppermute | solution.py:24
  41.6 11.2 %collective-permute-start.14 = (f32[256,384]{1,0:T(8,128)S(1)}, f32[256,384]{1,0:T(8,128)S(1)}, u32[]{:S(2)}, u32[]{:S(2)}) collective-permute-start(f32[256,384]{1,0:T(8,128)S(1)} %get-tuple-element.70), channel_id=1, source_target_pairs={{0,12},{1,13},{2,14},{3,15},{4,0},{5,1},{6,2},{7,3},{8,4},{9,5},{1... | collective-permute-start | bytes 1179656 | tf_op jit(solution)/shard_map/ppermute | solution.py:24
  44.5 15.0 %collective-permute-start.11 = (f32[256,384]{1,0:T(8,128)S(1)}, f32[256,384]{1,0:T(8,128)S(1)}, u32[]{:S(2)}, u32[]{:S(2)}) collective-permute-start(f32[256,384]{1,0:T(8,128)S(1)} %get-tuple-element.67), channel_id=1, source_target_pairs={{0,4},{1,5},{2,6},{3,7},{4,8},{5,9},{6,10},{7,11},{8,12},{9,13},{1... | collective-permute-start | bytes 1179656 | tf_op jit(solution)/shard_map/ppermute | solution.py:24
  44.5 16.7 %collective-permute-start.12 = (f32[256,384]{1,0:T(8,128)S(1)}, f32[256,384]{1,0:T(8,128)S(1)}, u32[]{:S(2)}, u32[]{:S(2)}) collective-permute-start(f32[256,384]{1,0:T(8,128)S(1)} %get-tuple-element.68), channel_id=1, source_target_pairs={{0,12},{1,13},{2,14},{3,15},{4,0},{5,1},{6,2},{7,3},{8,4},{9,5},{1... | collective-permute-start | bytes 1179656 | tf_op jit(solution)/shard_map/ppermute | solution.py:24
  47.1 18.0 %collective-permute-start.9 = (f32[256,256]{1,0:T(8,128)S(1)}, f32[256,256]{1,0:T(8,128)S(1)}, u32[]{:S(2)}, u32[]{:S(2)}) collective-permute-start(f32[256,256]{1,0:T(8,128)S(1)} %get-tuple-element.65), channel_id=1, source_target_pairs={{0,4},{1,5},{2,6},{3,7},{4,8},{5,9},{6,10},{7,11},{8,12},{9,13},{1... | collective-permute-start | bytes 786440 | tf_op jit(solution)/shard_map/ppermute | solution.py:24
  51.1 15.0 %collective-permute-start.10 = (f32[256,256]{1,0:T(8,128)S(1)}, f32[256,256]{1,0:T(8,128)S(1)}, u32[]{:S(2)}, u32[]{:S(2)}) collective-permute-start(f32[256,256]{1,0:T(8,128)S(1)} %get-tuple-element.66), channel_id=1, source_target_pairs={{0,12},{1,13},{2,14},{3,15},{4,0},{5,1},{6,2},{7,3},{8,4},{9,5},{1... | collective-permute-start | bytes 786440 | tf_op jit(solution)/shard_map/ppermute | solution.py:24

commit v14 on v13

--- a/solution.py
+++ b/solution.py
@@ -349,7 +349,7 @@
             [VMEM((4 * tile, width), BF16)],
         )(tables[step], a, *([acc] if step > 0 else []), *chunks)
 
-    pieces = (width * 3 // 8, width * 3 // 8, width // 4)
+    pieces = (width // 4,) * 4
     acc = None
     for step in range(1, count - 1):
         now = arrivals[-1]

time: 67.5 us -> 67.2 us (level)
  waiting for transfers between devices: 28.3 us -> 23.6 us
  starting transfers between devices: 16.8 us -> 20.2 us
  Pallas kernels: 21.1 us -> 22 us
    ppermute x15 -> x17, waiting for transfers between devices: 28.3 us -> 23.6 us  [permute(): lax.ppermute(x, AXES, [(flat(*place), flat(*target(*place))) for place in...]
    ppermute x15 -> x17, starting transfers between devices: 16.8 us -> 20.2 us  [permute(): lax.ppermute(x, AXES, [(flat(*place), flat(*target(*place))) for place in...]
    pallas_call x3 -> x4, Pallas kernels: 2.72 us -> 3.4 us  [shards(): call(functools.partial(arrived_kernel, sum(pieces[:i])), 'arrived%d' % i,...]
    pallas_call x3 -> x4, Pallas kernels: 3.2 us -> 3.56 us  [shards(): call(functools.partial(last_kernel, count - 1, per_shard - 1, sum(pieces[...]
  transfers between devices with their start and end apart: 15 -> 17, of which waited for: 10 -> 10; matrix products, arithmetic and copies ran while one was open for 0% -> 0% of each run, Pallas kernels for 27% -> 29%
where the time goes in v14:
time: 67.2 us; the launch traced here: 66.7 us
  waiting for transfers between devices  23.6 us (35%)
  Pallas kernels  22 us (33%)
  starting transfers between devices  20.2 us (30%)
  between operations  0.84 us (1%)
    ppermute x17, waiting for transfers between devices, permute(): lax.ppermute(x, AXES, [(flat(*place), flat(*target(*place))) for place in...  23.6 us
    ppermute x17, starting transfers between devices, permute(): lax.ppermute(x, AXES, [(flat(*place), flat(*target(*place))) for place in...  20.2 us
    pallas_call x4, Pallas kernels, add(): call(functools.partial(add_kernel, step, list(range(len(chunks)))), 'add%...  6.14 us
    pallas_call x4, Pallas kernels, shards(): call(functools.partial(last_kernel, count - 1, per_shard - 1, sum(pieces[...  3.56 us
    pallas_call x4, Pallas kernels, shards(): call(functools.partial(arrived_kernel, sum(pieces[:i])), 'arrived%d' % i,...  3.4 us
    pallas_call x1, Pallas kernels, shards(): call(ham_kernel, 'ham', sds((blocks // 2, tall, 3 * LANES), BF16), (SMEM,...  2.51 us
    pallas_call x2, Pallas kernels, shards(): call(functools.partial(cut_kernel, h), 'cut%d' % h, sds((2, tile, dens_ti...  1.99 us
    pallas_call x1, Pallas kernels, shards(): call(own_kernel, 'own', (sds((rows, tile, width), F32), sds((rows, tile,...  1.66 us
  transfers between devices with their start and end apart: 17, of which 10 were waited for; matrix products, arithmetic and copies ran while one was open for 0% of the time, Pallas kernels for 29%

profile of v14, /device:TPU:0, one launch (start us, length us, event | category | flops | bytes accessed | tf_op | source)
XLA Modules:
  0.0 66.7 jit_solution(1199256057068192689)
XLA Ops:
  0.6 1.0 %cut0.1.rest_0_ = f32[2,64,512]{2,1,0:T(8,128)S(1)} custom-call(f32[4,64,512]{2,1,0:T(8,128)} %dens.2), custom_call_target="tpu_custom_call" | custom-call | flops 1024 | bytes 1024 | tf_op jit(solution)/shard_map/cut0/pallas_call | solution.py:296
  1.7 3.1 %collective-permute-start.5 = (f32[2,64,512]{2,1,0:T(8,128)S(1)}, f32[2,64,512]{2,1,0:T(8,128)S(1)}, u32[]{:S(2)}, u32[]{:S(2)}) collective-permute-start(f32[2,64,512]{2,1,0:T(8,128)S(1)} %cut0.1.rest_0_), channel_id=1, source_target_pairs={{0,1},{1,3},{2,0},{3,2},{4,5},{5,7},{6,4},{7,6},{8,9},{9,11},{10,8... | collective-permute-start | bytes 786440 | tf_op jit(solution)/shard_map/ppermute | solution.py:24
  4.8 1.0 %cut1.1.rest_1_ = f32[2,64,512]{2,1,0:T(8,128)S(1)} custom-call(f32[4,64,512]{2,1,0:T(8,128)} %dens.2), custom_call_target="tpu_custom_call" | custom-call | flops 1024 | bytes 1024 | tf_op jit(solution)/shard_map/cut1/pallas_call | solution.py:296
  5.7 2.6 %collective-permute-start = (f32[2,64,512]{2,1,0:T(8,128)S(1)}, f32[2,64,512]{2,1,0:T(8,128)S(1)}, u32[]{:S(2)}, u32[]{:S(2)}) collective-permute-start(f32[2,64,512]{2,1,0:T(8,128)S(1)} %cut1.1.rest_1_), channel_id=1, source_target_pairs={{0,1},{1,3},{2,0},{3,2},{4,5},{5,7},{6,4},{7,6},{8,9},{9,11},{10,8... | collective-permute-start | bytes 786440 | tf_op jit(solution)/shard_map/ppermute | solution.py:24
  8.4 1.4 %table.1.dens_table = s32[4,16]{1,0:T(4,128)S(1)} custom-call(s32[4,8]{1,0:T(4,128)} %columns, s32[4]{0:T(128)} %counts.1), custom_call_target="tpu_custom_call" | custom-call | flops 1024 | bytes 1024 | tf_op jit(solution)/shard_map/table/pallas_call | solution.py:312
  9.8 0.4 collective-permute-start.3
  10.2 2.5 %collective-permute-start.2 = (s32[4,16]{1,0:T(4,128)S(1)}, s32[4,16]{1,0:T(4,128)S(1)}, u32[]{:S(2)}, u32[]{:S(2)}) collective-permute-start(s32[4,16]{1,0:T(4,128)S(1)} %table.1.dens_table), channel_id=1, source_target_pairs={{0,3},{1,2},{2,1},{3,0},{4,7},{5,6},{6,5},{7,4},{8,11},{9,10},{10,... | collective-permute-start | bytes 776 | tf_op jit(solution)/shard_map/ppermute | solution.py:24
  12.6 0.0 collective-permute-start.1
  12.6 2.5 %ham.2.a = bf16[8,256,384]{2,1,0:T(8,128)(2,1)S(1)} custom-call(s32[4,12]{1,0:T(4,128)} %ham_cols.1, s32[4]{0:T(128)} %ham_count.1, f32[4,64,768]{2,1,0:T(8,128)} %ham.3), custom_call_target="tpu_custom_call" | custom-call | flops 1024 | bytes 1024 | tf_op jit(solution)/shard_map/ham/pallas_call | solution.py:329
  15.2 2.0 %collective-permute-start.6 = (f32[2,64,512]{2,1,0:T(8,128)S(1)}, f32[2,64,512]{2,1,0:T(8,128)S(1)}, u32[]{:S(2)}, u32[]{:S(2)}) collective-permute-start(f32[2,64,512]{2,1,0:T(8,128)S(1)} %collective-permute-done.5.rest_1_), channel_id=1, source_target_pairs={{0,1},{1,3},{2,0},{3,2},{4,5},{5,7},{6,4},{7,6},{8,9},{9,11},{10,8... | collective-permute-start | bytes 786440 | tf_op jit(solution)/shard_map/ppermute | solution.py:24
  17.1 0.0 collective-permute-done.3.dens_table
  17.1 2.2 %collective-permute-done.2.dens_table = s32[4,16]{1,0:T(4,128)S(1)} collective-permute-done((s32[4,16]{1,0:T(4,128)S(1)}, s32[4,16]{1,0:T(4,128)S(1)}, u32[]{:S(2)}, u32[]{:S(2)}) %collective-permute-start.2) | collective-permute-done | bytes 288 | tf_op jit(solution)/shard_map/ppermute | solution.py:24
  19.3 0.0 collective-permute-done.1.dens_table
  19.3 0.0 collective-permute-done.rest_2_
  19.3 0.6 collective-permute-start.4
  19.9 0.3 margin.1
  20.1 1.1 %pick.1 = bf16[2,512,1024]{2,1,0:T(8,128)(2,1)S(1)} custom-call(s32[4,16]{1,0:T(4,128)S(1)} %collective-permute-done.3.dens_table), custom_call_target="tpu_custom_call" | custom-call | flops 1024 | bytes 1024 | tf_op jit(solution)/shard_map/pick/pallas_call | solution.py:362
  21.3 1.6 %add0.1.rest_0_ = f32[256,1024]{1,0:T(8,128)S(1)} custom-call(s32[4,16]{1,0:T(4,128)S(1)} %table.1.dens_table, bf16[8,256,384]{2,1,0:T(8,128)(2,1)S(1)} %ham.2.a, f32[2,64,512]{2,1,0:T(8,128)S(1)} %cut0.1.rest_0_, f32[2,64,512]{2,1,0:T(8,128)S(1)} %cut1.1.rest_1_), custom_call_target="tpu_custom_call" | custom-call | flops 1024 | bytes 1024 | tf_op jit(solution)/shard_map/add0/pallas_call | solution.py:343
  22.9 2.4 %collective-permute-done.6.rest_1_ = f32[2,64,512]{2,1,0:T(8,128)S(1)} collective-permute-done((f32[2,64,512]{2,1,0:T(8,128)S(1)}, f32[2,64,512]{2,1,0:T(8,128)S(1)}, u32[]{:S(2)}, u32[]{:S(2)}) %collective-permute-start.6) | collective-permute-done | bytes 262176 | tf_op jit(solution)/shard_map/ppermute | solution.py:24
  25.4 1.0 %collective-permute-start.7 = (f32[2,64,512]{2,1,0:T(8,128)S(1)}, f32[2,64,512]{2,1,0:T(8,128)S(1)}, u32[]{:S(2)}, u32[]{:S(2)}) collective-permute-start(f32[2,64,512]{2,1,0:T(8,128)S(1)} %collective-permute-done.6.rest_1_), channel_id=1, source_target_pairs={{0,1},{1,3},{2,0},{3,2},{4,5},{5,7},{6,4},{7,6},{8,9},{9,11},{10,8... | collective-permute-start | bytes 786440 | tf_op jit(solution)/shard_map/ppermute | solution.py:24
  26.4 4.6 %collective-permute-done.4.rest_2_ = f32[2,64,512]{2,1,0:T(8,128)S(1)} collective-permute-done((f32[2,64,512]{2,1,0:T(8,128)S(1)}, f32[2,64,512]{2,1,0:T(8,128)S(1)}, u32[]{:S(2)}, u32[]{:S(2)}) %collective-permute-start.4) | collective-permute-done | bytes 262176 | tf_op jit(solution)/shard_map/ppermute | solution.py:24
  31.0 1.0 %collective-permute-start.8 = (f32[2,64,512]{2,1,0:T(8,128)S(1)}, f32[2,64,512]{2,1,0:T(8,128)S(1)}, u32[]{:S(2)}, u32[]{:S(2)}) collective-permute-start(f32[2,64,512]{2,1,0:T(8,128)S(1)} %collective-permute-done.4.rest_2_), channel_id=1, source_target_pairs={{0,1},{1,3},{2,0},{3,2},{4,5},{5,7},{6,4},{7,6},{8,9},{9,11},{10,8... | collective-permute-start | bytes 786440 | tf_op jit(solution)/shard_map/ppermute | solution.py:24
  32.0 1.6 %add1.1.rest_0_ = f32[256,1024]{1,0:T(8,128)S(1)} custom-call(s32[4,16]{1,0:T(4,128)S(1)} %collective-permute-done.1.dens_table, bf16[8,256,384]{2,1,0:T(8,128)(2,1)S(1)} %ham.2.a, f32[256,1024]{1,0:T(8,128)S(1)} %add0.1.rest_0_, f32[2,64,512]{2,1,0:T(8,128)S(1)} %collective-permute-done.5.rest_1_, f32[2,64,512]{2,1,0:T(8,128)S(1)} %collective-permute-done.rest_2_), custom_call_target="tpu_custom_call" | custom-call | flops 1024 | bytes 1024 | tf_op jit(solution)/shard_map/add1/pallas_call | solution.py:343
  33.6 1.6 %add2.1.rest_0_ = f32[256,1024]{1,0:T(8,128)S(1)} custom-call(s32[4,16]{1,0:T(4,128)S(1)} %collective-permute-done.2.dens_table, bf16[8,256,384]{2,1,0:T(8,128)(2,1)S(1)} %ham.2.a, f32[256,1024]{1,0:T(8,128)S(1)} %add1.1.rest_0_, f32[2,64,512]{2,1,0:T(8,128)S(1)} %collective-permute-done.6.rest_1_, f32[2,64,512]{2,1,0:T(8,128)S(1)} %collective-permute-done.4.rest_2_), custom_call_target="tpu_custom_call" | custom-call | flops 1024 | bytes 1024 | tf_op jit(solution)/shard_map/add2/pallas_call | solution.py:343
  35.3 1.3 %collective-permute-done.7.rest_1_ = f32[2,64,512]{2,1,0:T(8,128)S(1)} collective-permute-done((f32[2,64,512]{2,1,0:T(8,128)S(1)}, f32[2,64,512]{2,1,0:T(8,128)S(1)}, u32[]{:S(2)}, u32[]{:S(2)}) %collective-permute-start.7) | collective-permute-done | bytes 262176 | tf_op jit(solution)/shard_map/ppermute | solution.py:24
  36.6 1.2 %add3.1.acc_in = f32[256,1024]{1,0:T(8,128)S(1)} custom-call(s32[4,16]{1,0:T(4,128)S(1)} %collective-permute-done.3.dens_table, bf16[8,256,384]{2,1,0:T(8,128)(2,1)S(1)} %ham.2.a, f32[256,1024]{1,0:T(8,128)S(1)} %add2.1.rest_0_, f32[2,64,512]{2,1,0:T(8,128)S(1)} %collective-permute-done.7.rest_1_), custom_call_target="tpu_custom_call" | custom-call | flops 1024 | bytes 1024 | tf_op jit(solution)/shard_map/add3/pallas_call | solution.py:343
  37.9 2.5 %collective-permute-done.8.chunk = f32[2,64,512]{2,1,0:T(8,128)S(1)} collective-permute-done((f32[2,64,512]{2,1,0:T(8,128)S(1)}, f32[2,64,512]{2,1,0:T(8,128)S(1)}, u32[]{:S(2)}, u32[]{:S(2)}) %collective-permute-start.8) | collective-permute-done | bytes 262176 | tf_op jit(solution)/shard_map/ppermute | solution.py:24
  40.3 0.9 %last0.1 = (f32[256,256]{1,0:T(8,128)S(1)}, f32[256,256]{1,0:T(8,128)S(1)}, f32[256,256]{1,0:T(8,128)S(1)}) custom-call(bf16[8,256,384]{2,1,0:T(8,128)(2,1)S(1)} %ham.2.a, f32[256,1024]{1,0:T(8,128)S(1)} %add3.1.acc_in, f32[2,64,512]{2,1,0:T(8,128)S(1)} %collective-permute-done.8.chunk, bf16[2,512,1024]{2,1,0:T(8,128)(2,1)S(1)} %pick.1, ...), custom_call_target="tpu_custom_call" | custom-call | flops 1024 | bytes 1024 | tf_op jit(solution)/shard_map/last0/pallas_call | solution.py:378
  41.2 0.1 collective-permute-start.15
  41.3 1.7 %collective-permute-start.16 = (f32[256,256]{1,0:T(8,128)S(1)}, f32[256,256]{1,0:T(8,128)S(1)}, u32[]{:S(2)}, u32[]{:S(2)}) collective-permute-start(f32[256,256]{1,0:T(8,128)S(1)} %get-tuple-element.80), channel_id=1, source_target_pairs={{0,12},{1,13},{2,14},{3,15},{4,0},{5,1},{6,2},{7,3},{8,4},{9,5},{1... | collective-permute-start | bytes 786440 | tf_op jit(solution)/shard_map/ppermute | solution.py:24
  43.0 0.9 %last1.1 = (f32[256,256]{1,0:T(8,128)S(1)}, f32[256,256]{1,0:T(8,128)S(1)}, f32[256,256]{1,0:T(8,128)S(1)}) custom-call(bf16[8,256,384]{2,1,0:T(8,128)(2,1)S(1)} %ham.2.a, f32[256,1024]{1,0:T(8,128)S(1)} %add3.1.acc_in, f32[2,64,512]{2,1,0:T(8,128)S(1)} %collective-permute-done.8.chunk, bf16[2,512,1024]{2,1,0:T(8,128)(2,1)S(1)} %pick.1, ...), custom_call_target="tpu_custom_call" | custom-call | flops 1024 | bytes 1024 | tf_op jit(solution)/shard_map/last1/pallas_call | solution.py:378
  43.9 0.1 collective-permute-start.13
  44.0 1.7 %collective-permute-start.14 = (f32[256,256]{1,0:T(8,128)S(1)}, f32[256,256]{1,0:T(8,128)S(1)}, u32[]{:S(2)}, u32[]{:S(2)}) collective-permute-start(f32[256,256]{1,0:T(8,128)S(1)} %get-tuple-element.78), channel_id=1, source_target_pairs={{0,12},{1,13},{2,14},{3,15},{4,0},{5,1},{6,2},{7,3},{8,4},{9,5},{1... | collective-permute-start | bytes 786440 | tf_op jit(solution)/shard_map/ppermute | solution.py:24
  45.7 0.9 %last2.1 = (f32[256,256]{1,0:T(8,128)S(1)}, f32[256,256]{1,0:T(8,128)S(1)}, f32[256,256]{1,0:T(8,128)S(1)}) custom-call(bf16[8,256,384]{2,1,0:T(8,128)(2,1)S(1)} %ham.2.a, f32[256,1024]{1,0:T(8,128)S(1)} %add3.1.acc_in, f32[2,64,512]{2,1,0:T(8,128)S(1)} %collective-permute-done.8.chunk, bf16[2,512,1024]{2,1,0:T(8,128)(2,1)S(1)} %pick.1, ...), custom_call_target="tpu_custom_call" | custom-call | flops 1024 | bytes 1024 | tf_op jit(solution)/shard_map/last2/pallas_call | solution.py:378
  46.6 0.9 %last3.1 = (f32[256,256]{1,0:T(8,128)S(1)}, f32[256,256]{1,0:T(8,128)S(1)}, f32[256,256]{1,0:T(8,128)S(1)}) custom-call(bf16[8,256,384]{2,1,0:T(8,128)(2,1)S(1)} %ham.2.a, f32[256,1024]{1,0:T(8,128)S(1)} %add3.1.acc_in, f32[2,64,512]{2,1,0:T(8,128)S(1)} %collective-permute-done.8.chunk, bf16[2,512,1024]{2,1,0:T(8,128)(2,1)S(1)} %pick.1, ...), custom_call_target="tpu_custom_call" | custom-call | flops 1024 | bytes 1024 | tf_op jit(solution)/shard_map/last3/pallas_call | solution.py:378
  47.5 0.1 collective-permute-start.9
  47.6 0.4 collective-permute-done.15.above
  48.0 1.2 %collective-permute-start.11 = (f32[256,256]{1,0:T(8,128)S(1)}, f32[256,256]{1,0:T(8,128)S(1)}, u32[]{:S(2)}, u32[]{:S(2)}) collective-permute-start(f32[256,256]{1,0:T(8,128)S(1)} %get-tuple-element.75), channel_id=1, source_target_pairs={{0,4},{1,5},{2,6},{3,7},{4,8},{5,9},{6,10},{7,11},{8,12},{9,13},{1... | collective-permute-start | bytes 786440 | tf_op jit(solution)/shard_map/ppermute | solution.py:24
  49.2 0.5 collective-permute-done.16.below
  49.7 2.2 %collective-permute-start.12 = (f32[256,256]{1,0:T(8,128)S(1)}, f32[256,256]{1,0:T(8,128)S(1)}, u32[]{:S(2)}, u32[]{:S(2)}) collective-permute-start(f32[256,256]{1,0:T(8,128)S(1)} %get-tuple-element.76), channel_id=1, source_target_pairs={{0,12},{1,13},{2,14},{3,15},{4,0},{5,1},{6,2},{7,3},{8,4},{9,5},{1... | collective-permute-start | bytes 786440 | tf_op jit(solution)/shard_map/ppermute | solution.py:24
  51.9 1.7 %collective-permute-done.13.above = f32[256,256]{1,0:T(8,128)S(1)} collective-permute-done((f32[256,256]{1,0:T(8,128)S(1)}, f32[256,256]{1,0:T(8,128)S(1)}, u32[]{:S(2)}, u32[]{:S(2)}) %collective-permute-start.13) | collective-permute-done | bytes 262176 | tf_op jit(solution)/shard_map/ppermute | solution.py:24
  53.6 1.7 %own.1 = (f32[4,64,1024]{2,1,0:T(8,128)}, f32[4,64,3072]{2,1,0:T(8,128)}) custom-call(bf16[3,256,256]{2,1,0:T(8,128)(2,1)S(1)} %get-tuple-element.50.m_hi, bf16[3,256,256]{2,1,0:T(8,128)(2,1)S(1)} %get-tuple-element.51.m_lo, f32[256,256]{1,0:T(8,128)S(1)} %get-tuple-element.63.rest_0_, f32[256,256]{1,0:T(8,128)S(1)} %get-tuple-element.66.rest_1_, ...), custom_call_target="tpu_custom_call" | custom-call | flops 1024 | bytes 1024 | tf_op jit(solution)/shard_map/own/pallas_call | solution.py:391
  55.3 0.9 %arrived0.1.window_in = f32[4,64,3072]{2,1,0:T(8,128)} custom-call(f32[256,256]{1,0:T(8,128)S(1)} %collective-permute-done.15.above, f32[256,256]{1,0:T(8,128)S(1)} %collective-permute-done.16.below, f32[4,64,3072]{2,1,0:T(8,128)} %get-tuple-element.81.window_in), custom_call_target="tpu_custom_call", output_to_operand_aliasing={{}: (2, {})} | custom-call | flops 1024 | bytes 1024 | tf_op jit(solution)/shard_map/arrived0/pallas_call | solution.py:400
  56.2 0.9 %arrived1.1.window_in = f32[4,64,3072]{2,1,0:T(8,128)} custom-call(f32[256,256]{1,0:T(8,128)S(1)} %collective-permute-done.13.above, f32[256,256]{1,0:T(8,128)S(1)} %collective-permute-done.14.below, f32[4,64,3072]{2,1,0:T(8,128)} %arrived0.1.window_in), custom_call_target="tpu_custom_call", output_to_operand_aliasing={{}: (2, {})} | custom-call | flops 1024 | bytes 1024 | tf_op jit(solution)/shard_map/arrived1/pallas_call | solution.py:400
  57.0 7.8 %collective-permute-done.11.above = f32[256,256]{1,0:T(8,128)S(1)} collective-permute-done((f32[256,256]{1,0:T(8,128)S(1)}, f32[256,256]{1,0:T(8,128)S(1)}, u32[]{:S(2)}, u32[]{:S(2)}) %collective-permute-start.11) | collective-permute-done | bytes 262176 | tf_op jit(solution)/shard_map/ppermute | solution.py:24
  64.8 0.8 %arrived2.1.window_in = f32[4,64,3072]{2,1,0:T(8,128)} custom-call(f32[256,256]{1,0:T(8,128)S(1)} %collective-permute-done.11.above, f32[256,256]{1,0:T(8,128)S(1)} %collective-permute-done.12.below, f32[4,64,3072]{2,1,0:T(8,128)} %arrived1.1.window_in), custom_call_target="tpu_custom_call", output_to_operand_aliasing={{}: (2, {})} | custom-call | flops 1024 | bytes 1024 | tf_op jit(solution)/shard_map/arrived2/pallas_call | solution.py:400
  65.7 0.1 collective-permute-done.10.below
  65.8 0.8 %arrived3.1 = f32[4,64,3072]{2,1,0:T(8,128)} custom-call(f32[256,256]{1,0:T(8,128)S(1)} %collective-permute-done.9.above, f32[256,256]{1,0:T(8,128)S(1)} %collective-permute-done.10.below, f32[4,64,3072]{2,1,0:T(8,128)} %arrived2.1.window_in), custom_call_target="tpu_custom_call", output_to_operand_aliasing={{}: (2, {})} | custom-call | flops 1024 | bytes 1024 | tf_op jit(solution)/shard_map/arrived3/pallas_call | solution.py:400
  (7 shorter events, 0.0 us)
Async XLA Ops:
  0.6 19.2 %copy-start = (f32[4,64,768]{2,1,0:T(8,128)S(1)}, f32[4,64,768]{2,1,0:T(8,128)}, u32[]{:S(2)}) copy-start(f32[4,64,768]{2,1,0:T(8,128)} %over.1) | copy-start | bytes 2359300
  1.7 13.5 %collective-permute-start.5 = (f32[2,64,512]{2,1,0:T(8,128)S(1)}, f32[2,64,512]{2,1,0:T(8,128)S(1)}, u32[]{:S(2)}, u32[]{:S(2)}) collective-permute-start(f32[2,64,512]{2,1,0:T(8,128)S(1)} %cut0.1.rest_0_), channel_id=1, source_target_pairs={{0,1},{1,3},{2,0},{3,2},{4,5},{5,7},{6,4},{7,6},{8,9},{9,11},{10,8... | collective-permute-start | bytes 786440 | tf_op jit(solution)/shard_map/ppermute | solution.py:24
  5.7 13.6 %collective-permute-start = (f32[2,64,512]{2,1,0:T(8,128)S(1)}, f32[2,64,512]{2,1,0:T(8,128)S(1)}, u32[]{:S(2)}, u32[]{:S(2)}) collective-permute-start(f32[2,64,512]{2,1,0:T(8,128)S(1)} %cut1.1.rest_1_), channel_id=1, source_target_pairs={{0,1},{1,3},{2,0},{3,2},{4,5},{5,7},{6,4},{7,6},{8,9},{9,11},{10,8... | collective-permute-start | bytes 786440 | tf_op jit(solution)/shard_map/ppermute | solution.py:24
  9.8 7.4 %collective-permute-start.3 = (s32[4,16]{1,0:T(4,128)S(1)}, s32[4,16]{1,0:T(4,128)S(1)}, u32[]{:S(2)}, u32[]{:S(2)}) collective-permute-start(s32[4,16]{1,0:T(4,128)S(1)} %table.1.dens_table), channel_id=1, source_target_pairs={{0,2},{1,0},{2,3},{3,1},{4,6},{5,4},{6,7},{7,5},{8,10},{9,8},{10,1... | collective-permute-start | bytes 776 | tf_op jit(solution)/shard_map/ppermute | solution.py:24
  10.2 9.1 %collective-permute-start.2 = (s32[4,16]{1,0:T(4,128)S(1)}, s32[4,16]{1,0:T(4,128)S(1)}, u32[]{:S(2)}, u32[]{:S(2)}) collective-permute-start(s32[4,16]{1,0:T(4,128)S(1)} %table.1.dens_table), channel_id=1, source_target_pairs={{0,3},{1,2},{2,1},{3,0},{4,7},{5,6},{6,5},{7,4},{8,11},{9,10},{10,... | collective-permute-start | bytes 776 | tf_op jit(solution)/shard_map/ppermute | solution.py:24
  12.6 6.6 %collective-permute-start.1 = (s32[4,16]{1,0:T(4,128)S(1)}, s32[4,16]{1,0:T(4,128)S(1)}, u32[]{:S(2)}, u32[]{:S(2)}) collective-permute-start(s32[4,16]{1,0:T(4,128)S(1)} %table.1.dens_table), channel_id=1, source_target_pairs={{0,1},{1,3},{2,0},{3,2},{4,5},{5,7},{6,4},{7,6},{8,9},{9,11},{10,8... | collective-permute-start | bytes 776 | tf_op jit(solution)/shard_map/ppermute | solution.py:24
  15.2 10.2 %collective-permute-start.6 = (f32[2,64,512]{2,1,0:T(8,128)S(1)}, f32[2,64,512]{2,1,0:T(8,128)S(1)}, u32[]{:S(2)}, u32[]{:S(2)}) collective-permute-start(f32[2,64,512]{2,1,0:T(8,128)S(1)} %collective-permute-done.5.rest_1_), channel_id=1, source_target_pairs={{0,1},{1,3},{2,0},{3,2},{4,5},{5,7},{6,4},{7,6},{8,9},{9,11},{10,8... | collective-permute-start | bytes 786440 | tf_op jit(solution)/shard_map/ppermute | solution.py:24
  19.3 11.7 %collective-permute-start.4 = (f32[2,64,512]{2,1,0:T(8,128)S(1)}, f32[2,64,512]{2,1,0:T(8,128)S(1)}, u32[]{:S(2)}, u32[]{:S(2)}) collective-permute-start(f32[2,64,512]{2,1,0:T(8,128)S(1)} %collective-permute-done.rest_2_), channel_id=1, source_target_pairs={{0,1},{1,3},{2,0},{3,2},{4,5},{5,7},{6,4},{7,6},{8,9},{9,11},{10,8... | collective-permute-start | bytes 786440 | tf_op jit(solution)/shard_map/ppermute | solution.py:24
  25.4 11.2 %collective-permute-start.7 = (f32[2,64,512]{2,1,0:T(8,128)S(1)}, f32[2,64,512]{2,1,0:T(8,128)S(1)}, u32[]{:S(2)}, u32[]{:S(2)}) collective-permute-start(f32[2,64,512]{2,1,0:T(8,128)S(1)} %collective-permute-done.6.rest_1_), channel_id=1, source_target_pairs={{0,1},{1,3},{2,0},{3,2},{4,5},{5,7},{6,4},{7,6},{8,9},{9,11},{10,8... | collective-permute-start | bytes 786440 | tf_op jit(solution)/shard_map/ppermute | solution.py:24
  31.0 9.4 %collective-permute-start.8 = (f32[2,64,512]{2,1,0:T(8,128)S(1)}, f32[2,64,512]{2,1,0:T(8,128)S(1)}, u32[]{:S(2)}, u32[]{:S(2)}) collective-permute-start(f32[2,64,512]{2,1,0:T(8,128)S(1)} %collective-permute-done.4.rest_2_), channel_id=1, source_target_pairs={{0,1},{1,3},{2,0},{3,2},{4,5},{5,7},{6,4},{7,6},{8,9},{9,11},{10,8... | collective-permute-start | bytes 786440 | tf_op jit(solution)/shard_map/ppermute | solution.py:24
  41.2 6.8 %collective-permute-start.15 = (f32[256,256]{1,0:T(8,128)S(1)}, f32[256,256]{1,0:T(8,128)S(1)}, u32[]{:S(2)}, u32[]{:S(2)}) collective-permute-start(f32[256,256]{1,0:T(8,128)S(1)} %get-tuple-element.79), channel_id=1, source_target_pairs={{0,4},{1,5},{2,6},{3,7},{4,8},{5,9},{6,10},{7,11},{8,12},{9,13},{1... | collective-permute-start | bytes 786440 | tf_op jit(solution)/shard_map/ppermute | solution.py:24
  41.3 8.4 %collective-permute-start.16 = (f32[256,256]{1,0:T(8,128)S(1)}, f32[256,256]{1,0:T(8,128)S(1)}, u32[]{:S(2)}, u32[]{:S(2)}) collective-permute-start(f32[256,256]{1,0:T(8,128)S(1)} %get-tuple-element.80), channel_id=1, source_target_pairs={{0,12},{1,13},{2,14},{3,15},{4,0},{5,1},{6,2},{7,3},{8,4},{9,5},{1... | collective-permute-start | bytes 786440 | tf_op jit(solution)/shard_map/ppermute | solution.py:24
  43.9 9.7 %collective-permute-start.13 = (f32[256,256]{1,0:T(8,128)S(1)}, f32[256,256]{1,0:T(8,128)S(1)}, u32[]{:S(2)}, u32[]{:S(2)}) collective-permute-start(f32[256,256]{1,0:T(8,128)S(1)} %get-tuple-element.77), channel_id=1, source_target_pairs={{0,4},{1,5},{2,6},{3,7},{4,8},{5,9},{6,10},{7,11},{8,12},{9,13},{1... | collective-permute-start | bytes 786440 | tf_op jit(solution)/shard_map/ppermute | solution.py:24
  44.0 12.1 %collective-permute-start.14 = (f32[256,256]{1,0:T(8,128)S(1)}, f32[256,256]{1,0:T(8,128)S(1)}, u32[]{:S(2)}, u32[]{:S(2)}) collective-permute-start(f32[256,256]{1,0:T(8,128)S(1)} %get-tuple-element.78), channel_id=1, source_target_pairs={{0,12},{1,13},{2,14},{3,15},{4,0},{5,1},{6,2},{7,3},{8,4},{9,5},{1... | collective-permute-start | bytes 786440 | tf_op jit(solution)/shard_map/ppermute | solution.py:24
  47.5 18.2 %collective-permute-start.9 = (f32[256,256]{1,0:T(8,128)S(1)}, f32[256,256]{1,0:T(8,128)S(1)}, u32[]{:S(2)}, u32[]{:S(2)}) collective-permute-start(f32[256,256]{1,0:T(8,128)S(1)} %get-tuple-element.73), channel_id=1, source_target_pairs={{0,4},{1,5},{2,6},{3,7},{4,8},{5,9},{6,10},{7,11},{8,12},{9,13},{1... | collective-permute-start | bytes 786440 | tf_op jit(solution)/shard_map/ppermute | solution.py:24
  48.0 16.9 %collective-permute-start.11 = (f32[256,256]{1,0:T(8,128)S(1)}, f32[256,256]{1,0:T(8,128)S(1)}, u32[]{:S(2)}, u32[]{:S(2)}) collective-permute-start(f32[256,256]{1,0:T(8,128)S(1)} %get-tuple-element.75), channel_id=1, source_target_pairs={{0,4},{1,5},{2,6},{3,7},{4,8},{5,9},{6,10},{7,11},{8,12},{9,13},{1... | collective-permute-start | bytes 786440 | tf_op jit(solution)/shard_map/ppermute | solution.py:24
  49.7 15.2 %collective-permute-start.12 = (f32[256,256]{1,0:T(8,128)S(1)}, f32[256,256]{1,0:T(8,128)S(1)}, u32[]{:S(2)}, u32[]{:S(2)}) collective-permute-start(f32[256,256]{1,0:T(8,128)S(1)} %get-tuple-element.76), channel_id=1, source_target_pairs={{0,12},{1,13},{2,14},{3,15},{4,0},{5,1},{6,2},{7,3},{8,4},{9,5},{1... | collective-permute-start | bytes 786440 | tf_op jit(solution)/shard_map/ppermute | solution.py:24
  53.6 12.2 %collective-permute-start.10 = (f32[256,256]{1,0:T(8,128)S(1)}, f32[256,256]{1,0:T(8,128)S(1)}, u32[]{:S(2)}, u32[]{:S(2)}) collective-permute-start(f32[256,256]{1,0:T(8,128)S(1)} %get-tuple-element.74), channel_id=1, source_target_pairs={{0,12},{1,13},{2,14},{3,15},{4,0},{5,1},{6,2},{7,3},{8,4},{9,5},{1... | collective-permute-start | bytes 786440 | tf_op jit(solution)/shard_map/ppermute | solution.py:24

commit v15 on v14

--- a/solution.py
+++ b/solution.py
@@ -250,8 +250,9 @@
         copy.wait()
 
 
-def arrived_kernel(at, above, below, window_in, window, sems):
+def arrived_kernel(at, before_first, one, other, window_in, window, sems):
     rows, tile, triple = window.shape
+    above, below = (one, other) if before_first else (other, one)
     copies = [
         pltpu.make_async_copy(
             term.at[pl.ds(q * tile, tile)],
@@ -386,8 +387,11 @@
         if i + 1 < len(pieces):
             part, acc = lax.optimization_barrier((part, acc))
         parts.append(part)
+        if i == 0:
+            afters.append(rotate(above, -1))
         befores.append(rotate(below, 1))
-        afters.append(rotate(above, -1))
+        if i > 0:
+            afters.append(rotate(above, -1))
     product, window = call(
         own_kernel,
         "own",
@@ -398,14 +402,14 @@
     )(m_hi, m_lo, *parts)
     for i in range(len(pieces)):
         window = call(
-            functools.partial(arrived_kernel, sum(pieces[:i])),
+            functools.partial(arrived_kernel, sum(pieces[:i]), i > 0),
             "arrived%d" % i,
             sds((rows, tile, 3 * width), F32),
             (VMEM, VMEM, pl.ANY),
             pl.ANY,
             [pltpu.SemaphoreType.DMA((2, rows))],
             {2: 0},
-        )(befores[i], afters[i], window)
+        )(*((befores[i], afters[i]) if i > 0 else (afters[i], befores[i])), window)
     return (product, window)
 
 

time: 67.2 us -> 68.8 us (1.024)
  waiting for transfers between devices: 23.6 us -> 26.9 us
  starting transfers between devices: 20.2 us -> 18.7 us
    ppermute x17, waiting for transfers between devices: 23.6 us -> 26.9 us  [permute(): lax.ppermute(x, AXES, [(flat(*place), flat(*target(*place))) for place in...]
    ppermute x17, starting transfers between devices: 20.2 us -> 18.7 us  [permute(): lax.ppermute(x, AXES, [(flat(*place), flat(*target(*place))) for place in...]
  transfers between devices with their start and end apart: 17 -> 17, of which waited for: 10 -> 8; matrix products, arithmetic and copies ran while one was open for 0% -> 0% of each run, Pallas kernels for 29% -> 28%
where the time goes in v15:
time: 68.8 us; the launch traced here: 68.5 us
  waiting for transfers between devices  26.9 us (39%)
  Pallas kernels  22.1 us (32%)
  starting transfers between devices  18.7 us (27%)
  between operations  0.84 us (1%)
    ppermute x17, waiting for transfers between devices, permute(): lax.ppermute(x, AXES, [(flat(*place), flat(*target(*place))) for place in...  26.9 us
    ppermute x17, starting transfers between devices, permute(): lax.ppermute(x, AXES, [(flat(*place), flat(*target(*place))) for place in...  18.7 us
    pallas_call x4, Pallas kernels, add(): call(functools.partial(add_kernel, step, list(range(len(chunks)))), 'add%...  6.14 us
    pallas_call x4, Pallas kernels, shards(): call(functools.partial(last_kernel, count - 1, per_shard - 1, sum(pieces[...  3.56 us
    pallas_call x4, Pallas kernels, shards(): call(functools.partial(arrived_kernel, sum(pieces[:i]), i > 0), 'arrived%...  3.41 us
    pallas_call x1, Pallas kernels, shards(): call(ham_kernel, 'ham', sds((blocks // 2, tall, 3 * LANES), BF16), (SMEM,...  2.51 us
    pallas_call x2, Pallas kernels, shards(): call(functools.partial(cut_kernel, h), 'cut%d' % h, sds((2, tile, dens_ti...  1.99 us
    pallas_call x1, Pallas kernels, shards(): call(own_kernel, 'own', (sds((rows, tile, width), F32), sds((rows, tile,...  1.66 us
  transfers between devices with their start and end apart: 17, of which 8 were waited for; matrix products, arithmetic and copies ran while one was open for 0% of the time, Pallas kernels for 28%

profile of v15, /device:TPU:0, one launch (start us, length us, event | category | flops | bytes accessed | tf_op | source)
XLA Modules:
  0.0 68.5 jit_solution(13334265231640262517)
XLA Ops:
  0.6 1.0 %cut0.1.rest_0_ = f32[2,64,512]{2,1,0:T(8,128)S(1)} custom-call(f32[4,64,512]{2,1,0:T(8,128)} %dens.2), custom_call_target="tpu_custom_call" | custom-call | flops 1024 | bytes 1024 | tf_op jit(solution)/shard_map/cut0/pallas_call | solution.py:297
  1.7 3.1 %collective-permute-start.5 = (f32[2,64,512]{2,1,0:T(8,128)S(1)}, f32[2,64,512]{2,1,0:T(8,128)S(1)}, u32[]{:S(2)}, u32[]{:S(2)}) collective-permute-start(f32[2,64,512]{2,1,0:T(8,128)S(1)} %cut0.1.rest_0_), channel_id=1, source_target_pairs={{0,1},{1,3},{2,0},{3,2},{4,5},{5,7},{6,4},{7,6},{8,9},{9,11},{10,8... | collective-permute-start | bytes 786440 | tf_op jit(solution)/shard_map/ppermute | solution.py:24
  4.8 1.0 %cut1.1.rest_1_ = f32[2,64,512]{2,1,0:T(8,128)S(1)} custom-call(f32[4,64,512]{2,1,0:T(8,128)} %dens.2), custom_call_target="tpu_custom_call" | custom-call | flops 1024 | bytes 1024 | tf_op jit(solution)/shard_map/cut1/pallas_call | solution.py:297
  5.7 2.6 %collective-permute-start = (f32[2,64,512]{2,1,0:T(8,128)S(1)}, f32[2,64,512]{2,1,0:T(8,128)S(1)}, u32[]{:S(2)}, u32[]{:S(2)}) collective-permute-start(f32[2,64,512]{2,1,0:T(8,128)S(1)} %cut1.1.rest_1_), channel_id=1, source_target_pairs={{0,1},{1,3},{2,0},{3,2},{4,5},{5,7},{6,4},{7,6},{8,9},{9,11},{10,8... | collective-permute-start | bytes 786440 | tf_op jit(solution)/shard_map/ppermute | solution.py:24
  8.4 1.4 %table.1.dens_table = s32[4,16]{1,0:T(4,128)S(1)} custom-call(s32[4,8]{1,0:T(4,128)} %columns, s32[4]{0:T(128)} %counts.1), custom_call_target="tpu_custom_call" | custom-call | flops 1024 | bytes 1024 | tf_op jit(solution)/shard_map/table/pallas_call | solution.py:313
  9.8 0.4 collective-permute-start.3
  10.2 2.5 %collective-permute-start.2 = (s32[4,16]{1,0:T(4,128)S(1)}, s32[4,16]{1,0:T(4,128)S(1)}, u32[]{:S(2)}, u32[]{:S(2)}) collective-permute-start(s32[4,16]{1,0:T(4,128)S(1)} %table.1.dens_table), channel_id=1, source_target_pairs={{0,3},{1,2},{2,1},{3,0},{4,7},{5,6},{6,5},{7,4},{8,11},{9,10},{10,... | collective-permute-start | bytes 776 | tf_op jit(solution)/shard_map/ppermute | solution.py:24
  12.6 0.0 collective-permute-start.1
  12.6 2.5 %ham.2.a = bf16[8,256,384]{2,1,0:T(8,128)(2,1)S(1)} custom-call(s32[4,12]{1,0:T(4,128)} %ham_cols.1, s32[4]{0:T(128)} %ham_count.1, f32[4,64,768]{2,1,0:T(8,128)} %ham.3), custom_call_target="tpu_custom_call" | custom-call | flops 1024 | bytes 1024 | tf_op jit(solution)/shard_map/ham/pallas_call | solution.py:330
  15.2 0.0 collective-permute-done.5.rest_1_
  15.2 2.0 %collective-permute-start.6 = (f32[2,64,512]{2,1,0:T(8,128)S(1)}, f32[2,64,512]{2,1,0:T(8,128)S(1)}, u32[]{:S(2)}, u32[]{:S(2)}) collective-permute-start(f32[2,64,512]{2,1,0:T(8,128)S(1)} %collective-permute-done.5.rest_1_), channel_id=1, source_target_pairs={{0,1},{1,3},{2,0},{3,2},{4,5},{5,7},{6,4},{7,6},{8,9},{9,11},{10,8... | collective-permute-start | bytes 786440 | tf_op jit(solution)/shard_map/ppermute | solution.py:24
  17.1 0.0 collective-permute-done.3.dens_table
  17.1 2.2 %collective-permute-done.2.dens_table = s32[4,16]{1,0:T(4,128)S(1)} collective-permute-done((s32[4,16]{1,0:T(4,128)S(1)}, s32[4,16]{1,0:T(4,128)S(1)}, u32[]{:S(2)}, u32[]{:S(2)}) %collective-permute-start.2) | collective-permute-done | bytes 288 | tf_op jit(solution)/shard_map/ppermute | solution.py:24
  19.3 0.0 collective-permute-done.1.dens_table
  19.3 0.6 collective-permute-start.4
  19.9 0.3 margin.1
  20.2 1.1 %pick.1 = bf16[2,512,1024]{2,1,0:T(8,128)(2,1)S(1)} custom-call(s32[4,16]{1,0:T(4,128)S(1)} %collective-permute-done.3.dens_table), custom_call_target="tpu_custom_call" | custom-call | flops 1024 | bytes 1024 | tf_op jit(solution)/shard_map/pick/pallas_call | solution.py:363
  21.3 1.6 %add0.1.rest_0_ = f32[256,1024]{1,0:T(8,128)S(1)} custom-call(s32[4,16]{1,0:T(4,128)S(1)} %table.1.dens_table, bf16[8,256,384]{2,1,0:T(8,128)(2,1)S(1)} %ham.2.a, f32[2,64,512]{2,1,0:T(8,128)S(1)} %cut0.1.rest_0_, f32[2,64,512]{2,1,0:T(8,128)S(1)} %cut1.1.rest_1_), custom_call_target="tpu_custom_call" | custom-call | flops 1024 | bytes 1024 | tf_op jit(solution)/shard_map/add0/pallas_call | solution.py:344
  22.9 2.5 %collective-permute-done.6.rest_1_ = f32[2,64,512]{2,1,0:T(8,128)S(1)} collective-permute-done((f32[2,64,512]{2,1,0:T(8,128)S(1)}, f32[2,64,512]{2,1,0:T(8,128)S(1)}, u32[]{:S(2)}, u32[]{:S(2)}) %collective-permute-start.6) | collective-permute-done | bytes 262176 | tf_op jit(solution)/shard_map/ppermute | solution.py:24
  25.4 1.0 %collective-permute-start.7 = (f32[2,64,512]{2,1,0:T(8,128)S(1)}, f32[2,64,512]{2,1,0:T(8,128)S(1)}, u32[]{:S(2)}, u32[]{:S(2)}) collective-permute-start(f32[2,64,512]{2,1,0:T(8,128)S(1)} %collective-permute-done.6.rest_1_), channel_id=1, source_target_pairs={{0,1},{1,3},{2,0},{3,2},{4,5},{5,7},{6,4},{7,6},{8,9},{9,11},{10,8... | collective-permute-start | bytes 786440 | tf_op jit(solution)/shard_map/ppermute | solution.py:24
  26.4 4.6 %collective-permute-done.4.rest_2_ = f32[2,64,512]{2,1,0:T(8,128)S(1)} collective-permute-done((f32[2,64,512]{2,1,0:T(8,128)S(1)}, f32[2,64,512]{2,1,0:T(8,128)S(1)}, u32[]{:S(2)}, u32[]{:S(2)}) %collective-permute-start.4) | collective-permute-done | bytes 262176 | tf_op jit(solution)/shard_map/ppermute | solution.py:24
  31.0 1.0 %collective-permute-start.8 = (f32[2,64,512]{2,1,0:T(8,128)S(1)}, f32[2,64,512]{2,1,0:T(8,128)S(1)}, u32[]{:S(2)}, u32[]{:S(2)}) collective-permute-start(f32[2,64,512]{2,1,0:T(8,128)S(1)} %collective-permute-done.4.rest_2_), channel_id=1, source_target_pairs={{0,1},{1,3},{2,0},{3,2},{4,5},{5,7},{6,4},{7,6},{8,9},{9,11},{10,8... | collective-permute-start | bytes 786440 | tf_op jit(solution)/shard_map/ppermute | solution.py:24
  32.0 1.6 %add1.1.rest_0_ = f32[256,1024]{1,0:T(8,128)S(1)} custom-call(s32[4,16]{1,0:T(4,128)S(1)} %collective-permute-done.1.dens_table, bf16[8,256,384]{2,1,0:T(8,128)(2,1)S(1)} %ham.2.a, f32[256,1024]{1,0:T(8,128)S(1)} %add0.1.rest_0_, f32[2,64,512]{2,1,0:T(8,128)S(1)} %collective-permute-done.5.rest_1_, f32[2,64,512]{2,1,0:T(8,128)S(1)} %collective-permute-done.rest_2_), custom_call_target="tpu_custom_call" | custom-call | flops 1024 | bytes 1024 | tf_op jit(solution)/shard_map/add1/pallas_call | solution.py:344
  33.6 1.6 %add2.1.rest_0_ = f32[256,1024]{1,0:T(8,128)S(1)} custom-call(s32[4,16]{1,0:T(4,128)S(1)} %collective-permute-done.2.dens_table, bf16[8,256,384]{2,1,0:T(8,128)(2,1)S(1)} %ham.2.a, f32[256,1024]{1,0:T(8,128)S(1)} %add1.1.rest_0_, f32[2,64,512]{2,1,0:T(8,128)S(1)} %collective-permute-done.6.rest_1_, f32[2,64,512]{2,1,0:T(8,128)S(1)} %collective-permute-done.4.rest_2_), custom_call_target="tpu_custom_call" | custom-call | flops 1024 | bytes 1024 | tf_op jit(solution)/shard_map/add2/pallas_call | solution.py:344
  35.3 1.3 %collective-permute-done.7.rest_1_ = f32[2,64,512]{2,1,0:T(8,128)S(1)} collective-permute-done((f32[2,64,512]{2,1,0:T(8,128)S(1)}, f32[2,64,512]{2,1,0:T(8,128)S(1)}, u32[]{:S(2)}, u32[]{:S(2)}) %collective-permute-start.7) | collective-permute-done | bytes 262176 | tf_op jit(solution)/shard_map/ppermute | solution.py:24
  36.6 1.2 %add3.1.acc_in = f32[256,1024]{1,0:T(8,128)S(1)} custom-call(s32[4,16]{1,0:T(4,128)S(1)} %collective-permute-done.3.dens_table, bf16[8,256,384]{2,1,0:T(8,128)(2,1)S(1)} %ham.2.a, f32[256,1024]{1,0:T(8,128)S(1)} %add2.1.rest_0_, f32[2,64,512]{2,1,0:T(8,128)S(1)} %collective-permute-done.7.rest_1_), custom_call_target="tpu_custom_call" | custom-call | flops 1024 | bytes 1024 | tf_op jit(solution)/shard_map/add3/pallas_call | solution.py:344
  37.9 2.5 %collective-permute-done.8.chunk = f32[2,64,512]{2,1,0:T(8,128)S(1)} collective-permute-done((f32[2,64,512]{2,1,0:T(8,128)S(1)}, f32[2,64,512]{2,1,0:T(8,128)S(1)}, u32[]{:S(2)}, u32[]{:S(2)}) %collective-permute-start.8) | collective-permute-done | bytes 262176 | tf_op jit(solution)/shard_map/ppermute | solution.py:24
  40.3 0.9 %last0.1 = (f32[256,256]{1,0:T(8,128)S(1)}, f32[256,256]{1,0:T(8,128)S(1)}, f32[256,256]{1,0:T(8,128)S(1)}) custom-call(bf16[8,256,384]{2,1,0:T(8,128)(2,1)S(1)} %ham.2.a, f32[256,1024]{1,0:T(8,128)S(1)} %add3.1.acc_in, f32[2,64,512]{2,1,0:T(8,128)S(1)} %collective-permute-done.8.chunk, bf16[2,512,1024]{2,1,0:T(8,128)(2,1)S(1)} %pick.1, ...), custom_call_target="tpu_custom_call" | custom-call | flops 1024 | bytes 1024 | tf_op jit(solution)/shard_map/last0/pallas_call | solution.py:379
  41.2 0.1 collective-permute-start.15
  41.3 0.5 collective-permute-start.16
  41.8 0.9 %last1.1 = (f32[256,256]{1,0:T(8,128)S(1)}, f32[256,256]{1,0:T(8,128)S(1)}, f32[256,256]{1,0:T(8,128)S(1)}) custom-call(bf16[8,256,384]{2,1,0:T(8,128)(2,1)S(1)} %ham.2.a, f32[256,1024]{1,0:T(8,128)S(1)} %add3.1.acc_in, f32[2,64,512]{2,1,0:T(8,128)S(1)} %collective-permute-done.8.chunk, bf16[2,512,1024]{2,1,0:T(8,128)(2,1)S(1)} %pick.1, ...), custom_call_target="tpu_custom_call" | custom-call | flops 1024 | bytes 1024 | tf_op jit(solution)/shard_map/last1/pallas_call | solution.py:379
  42.7 1.3 %collective-permute-start.13 = (f32[256,256]{1,0:T(8,128)S(1)}, f32[256,256]{1,0:T(8,128)S(1)}, u32[]{:S(2)}, u32[]{:S(2)}) collective-permute-start(f32[256,256]{1,0:T(8,128)S(1)} %get-tuple-element.77), channel_id=1, source_target_pairs={{0,4},{1,5},{2,6},{3,7},{4,8},{5,9},{6,10},{7,11},{8,12},{9,13},{1... | collective-permute-start | bytes 786440 | tf_op jit(solution)/shard_map/ppermute | solution.py:24
  44.0 0.5 collective-permute-start.14
  44.5 0.9 %last2.1 = (f32[256,256]{1,0:T(8,128)S(1)}, f32[256,256]{1,0:T(8,128)S(1)}, f32[256,256]{1,0:T(8,128)S(1)}) custom-call(bf16[8,256,384]{2,1,0:T(8,128)(2,1)S(1)} %ham.2.a, f32[256,1024]{1,0:T(8,128)S(1)} %add3.1.acc_in, f32[2,64,512]{2,1,0:T(8,128)S(1)} %collective-permute-done.8.chunk, bf16[2,512,1024]{2,1,0:T(8,128)(2,1)S(1)} %pick.1, ...), custom_call_target="tpu_custom_call" | custom-call | flops 1024 | bytes 1024 | tf_op jit(solution)/shard_map/last2/pallas_call | solution.py:379
  45.4 0.9 %last3.1 = (f32[256,256]{1,0:T(8,128)S(1)}, f32[256,256]{1,0:T(8,128)S(1)}, f32[256,256]{1,0:T(8,128)S(1)}) custom-call(bf16[8,256,384]{2,1,0:T(8,128)(2,1)S(1)} %ham.2.a, f32[256,1024]{1,0:T(8,128)S(1)} %add3.1.acc_in, f32[2,64,512]{2,1,0:T(8,128)S(1)} %collective-permute-done.8.chunk, bf16[2,512,1024]{2,1,0:T(8,128)(2,1)S(1)} %pick.1, ...), custom_call_target="tpu_custom_call" | custom-call | flops 1024 | bytes 1024 | tf_op jit(solution)/shard_map/last3/pallas_call | solution.py:379
  46.3 0.1 collective-permute-start.9
  46.3 0.6 collective-permute-done.15.one
  47.0 3.1 %collective-permute-start.11 = (f32[256,256]{1,0:T(8,128)S(1)}, f32[256,256]{1,0:T(8,128)S(1)}, u32[]{:S(2)}, u32[]{:S(2)}) collective-permute-start(f32[256,256]{1,0:T(8,128)S(1)} %get-tuple-element.75), channel_id=1, source_target_pairs={{0,4},{1,5},{2,6},{3,7},{4,8},{5,9},{6,10},{7,11},{8,12},{9,13},{1... | collective-permute-start | bytes 786440 | tf_op jit(solution)/shard_map/ppermute | solution.py:24
  50.1 5.4 %collective-permute-done.13.one = f32[256,256]{1,0:T(8,128)S(1)} collective-permute-done((f32[256,256]{1,0:T(8,128)S(1)}, f32[256,256]{1,0:T(8,128)S(1)}, u32[]{:S(2)}, u32[]{:S(2)}) %collective-permute-start.13) | collective-permute-done | bytes 262176 | tf_op jit(solution)/shard_map/ppermute | solution.py:24
  55.5 1.7 %own.1 = (f32[4,64,1024]{2,1,0:T(8,128)}, f32[4,64,3072]{2,1,0:T(8,128)}) custom-call(bf16[3,256,256]{2,1,0:T(8,128)(2,1)S(1)} %get-tuple-element.50.m_hi, bf16[3,256,256]{2,1,0:T(8,128)(2,1)S(1)} %get-tuple-element.51.m_lo, f32[256,256]{1,0:T(8,128)S(1)} %get-tuple-element.63.rest_0_, f32[256,256]{1,0:T(8,128)S(1)} %get-tuple-element.66.rest_1_, ...), custom_call_target="tpu_custom_call" | custom-call | flops 1024 | bytes 1024 | tf_op jit(solution)/shard_map/own/pallas_call | solution.py:395
  57.2 0.9 %arrived0.1.window_in = f32[4,64,3072]{2,1,0:T(8,128)} custom-call(f32[256,256]{1,0:T(8,128)S(1)} %collective-permute-done.15.one, f32[256,256]{1,0:T(8,128)S(1)} %collective-permute-done.16.other, f32[4,64,3072]{2,1,0:T(8,128)} %get-tuple-element.81.window_in), custom_call_target="tpu_custom_call", output_to_operand_aliasing={{}: (2, {})} | custom-call | flops 1024 | bytes 1024 | tf_op jit(solution)/shard_map/arrived0/pallas_call | solution.py:404
  58.1 0.0 collective-permute-done.14.other
  58.1 0.9 %arrived1.1.window_in = f32[4,64,3072]{2,1,0:T(8,128)} custom-call(f32[256,256]{1,0:T(8,128)S(1)} %collective-permute-done.13.one, f32[256,256]{1,0:T(8,128)S(1)} %collective-permute-done.14.other, f32[4,64,3072]{2,1,0:T(8,128)} %arrived0.1.window_in), custom_call_target="tpu_custom_call", output_to_operand_aliasing={{}: (2, {})} | custom-call | flops 1024 | bytes 1024 | tf_op jit(solution)/shard_map/arrived1/pallas_call | solution.py:404
  59.0 7.8 %collective-permute-done.11.one = f32[256,256]{1,0:T(8,128)S(1)} collective-permute-done((f32[256,256]{1,0:T(8,128)S(1)}, f32[256,256]{1,0:T(8,128)S(1)}, u32[]{:S(2)}, u32[]{:S(2)}) %collective-permute-start.11) | collective-permute-done | bytes 262176 | tf_op jit(solution)/shard_map/ppermute | solution.py:24
  66.8 0.8 %arrived2.1.window_in = f32[4,64,3072]{2,1,0:T(8,128)} custom-call(f32[256,256]{1,0:T(8,128)S(1)} %collective-permute-done.11.one, f32[256,256]{1,0:T(8,128)S(1)} %collective-permute-done.12.other, f32[4,64,3072]{2,1,0:T(8,128)} %arrived1.1.window_in), custom_call_target="tpu_custom_call", output_to_operand_aliasing={{}: (2, {})} | custom-call | flops 1024 | bytes 1024 | tf_op jit(solution)/shard_map/arrived2/pallas_call | solution.py:404
  67.6 0.0 collective-permute-done.9.one
  67.7 0.0 collective-permute-done.10.other
  67.7 0.9 %arrived3.1 = f32[4,64,3072]{2,1,0:T(8,128)} custom-call(f32[256,256]{1,0:T(8,128)S(1)} %collective-permute-done.9.one, f32[256,256]{1,0:T(8,128)S(1)} %collective-permute-done.10.other, f32[4,64,3072]{2,1,0:T(8,128)} %arrived2.1.window_in), custom_call_target="tpu_custom_call", output_to_operand_aliasing={{}: (2, {})} | custom-call | flops 1024 | bytes 1024 | tf_op jit(solution)/shard_map/arrived3/pallas_call | solution.py:404
  (7 shorter events, 0.0 us)
Async XLA Ops:
  0.6 19.2 %copy-start = (f32[4,64,768]{2,1,0:T(8,128)S(1)}, f32[4,64,768]{2,1,0:T(8,128)}, u32[]{:S(2)}) copy-start(f32[4,64,768]{2,1,0:T(8,128)} %over.1) | copy-start | bytes 2359300
  1.7 13.5 %collective-permute-start.5 = (f32[2,64,512]{2,1,0:T(8,128)S(1)}, f32[2,64,512]{2,1,0:T(8,128)S(1)}, u32[]{:S(2)}, u32[]{:S(2)}) collective-permute-start(f32[2,64,512]{2,1,0:T(8,128)S(1)} %cut0.1.rest_0_), channel_id=1, source_target_pairs={{0,1},{1,3},{2,0},{3,2},{4,5},{5,7},{6,4},{7,6},{8,9},{9,11},{10,8... | collective-permute-start | bytes 786440 | tf_op jit(solution)/shard_map/ppermute | solution.py:24
  5.7 13.6 %collective-permute-start = (f32[2,64,512]{2,1,0:T(8,128)S(1)}, f32[2,64,512]{2,1,0:T(8,128)S(1)}, u32[]{:S(2)}, u32[]{:S(2)}) collective-permute-start(f32[2,64,512]{2,1,0:T(8,128)S(1)} %cut1.1.rest_1_), channel_id=1, source_target_pairs={{0,1},{1,3},{2,0},{3,2},{4,5},{5,7},{6,4},{7,6},{8,9},{9,11},{10,8... | collective-permute-start | bytes 786440 | tf_op jit(solution)/shard_map/ppermute | solution.py:24
  9.8 7.4 %collective-permute-start.3 = (s32[4,16]{1,0:T(4,128)S(1)}, s32[4,16]{1,0:T(4,128)S(1)}, u32[]{:S(2)}, u32[]{:S(2)}) collective-permute-start(s32[4,16]{1,0:T(4,128)S(1)} %table.1.dens_table), channel_id=1, source_target_pairs={{0,2},{1,0},{2,3},{3,1},{4,6},{5,4},{6,7},{7,5},{8,10},{9,8},{10,1... | collective-permute-start | bytes 776 | tf_op jit(solution)/shard_map/ppermute | solution.py:24
  10.2 9.1 %collective-permute-start.2 = (s32[4,16]{1,0:T(4,128)S(1)}, s32[4,16]{1,0:T(4,128)S(1)}, u32[]{:S(2)}, u32[]{:S(2)}) collective-permute-start(s32[4,16]{1,0:T(4,128)S(1)} %table.1.dens_table), channel_id=1, source_target_pairs={{0,3},{1,2},{2,1},{3,0},{4,7},{5,6},{6,5},{7,4},{8,11},{9,10},{10,... | collective-permute-start | bytes 776 | tf_op jit(solution)/shard_map/ppermute | solution.py:24
  12.6 6.7 %collective-permute-start.1 = (s32[4,16]{1,0:T(4,128)S(1)}, s32[4,16]{1,0:T(4,128)S(1)}, u32[]{:S(2)}, u32[]{:S(2)}) collective-permute-start(s32[4,16]{1,0:T(4,128)S(1)} %table.1.dens_table), channel_id=1, source_target_pairs={{0,1},{1,3},{2,0},{3,2},{4,5},{5,7},{6,4},{7,6},{8,9},{9,11},{10,8... | collective-permute-start | bytes 776 | tf_op jit(solution)/shard_map/ppermute | solution.py:24
  15.2 10.2 %collective-permute-start.6 = (f32[2,64,512]{2,1,0:T(8,128)S(1)}, f32[2,64,512]{2,1,0:T(8,128)S(1)}, u32[]{:S(2)}, u32[]{:S(2)}) collective-permute-start(f32[2,64,512]{2,1,0:T(8,128)S(1)} %collective-permute-done.5.rest_1_), channel_id=1, source_target_pairs={{0,1},{1,3},{2,0},{3,2},{4,5},{5,7},{6,4},{7,6},{8,9},{9,11},{10,8... | collective-permute-start | bytes 786440 | tf_op jit(solution)/shard_map/ppermute | solution.py:24
  19.3 11.7 %collective-permute-start.4 = (f32[2,64,512]{2,1,0:T(8,128)S(1)}, f32[2,64,512]{2,1,0:T(8,128)S(1)}, u32[]{:S(2)}, u32[]{:S(2)}) collective-permute-start(f32[2,64,512]{2,1,0:T(8,128)S(1)} %collective-permute-done.rest_2_), channel_id=1, source_target_pairs={{0,1},{1,3},{2,0},{3,2},{4,5},{5,7},{6,4},{7,6},{8,9},{9,11},{10,8... | collective-permute-start | bytes 786440 | tf_op jit(solution)/shard_map/ppermute | solution.py:24
  25.4 11.2 %collective-permute-start.7 = (f32[2,64,512]{2,1,0:T(8,128)S(1)}, f32[2,64,512]{2,1,0:T(8,128)S(1)}, u32[]{:S(2)}, u32[]{:S(2)}) collective-permute-start(f32[2,64,512]{2,1,0:T(8,128)S(1)} %collective-permute-done.6.rest_1_), channel_id=1, source_target_pairs={{0,1},{1,3},{2,0},{3,2},{4,5},{5,7},{6,4},{7,6},{8,9},{9,11},{10,8... | collective-permute-start | bytes 786440 | tf_op jit(solution)/shard_map/ppermute | solution.py:24
  31.0 9.4 %collective-permute-start.8 = (f32[2,64,512]{2,1,0:T(8,128)S(1)}, f32[2,64,512]{2,1,0:T(8,128)S(1)}, u32[]{:S(2)}, u32[]{:S(2)}) collective-permute-start(f32[2,64,512]{2,1,0:T(8,128)S(1)} %collective-permute-done.4.rest_2_), channel_id=1, source_target_pairs={{0,1},{1,3},{2,0},{3,2},{4,5},{5,7},{6,4},{7,6},{8,9},{9,11},{10,8... | collective-permute-start | bytes 786440 | tf_op jit(solution)/shard_map/ppermute | solution.py:24
  41.2 5.7 %collective-permute-start.15 = (f32[256,256]{1,0:T(8,128)S(1)}, f32[256,256]{1,0:T(8,128)S(1)}, u32[]{:S(2)}, u32[]{:S(2)}) collective-permute-start(f32[256,256]{1,0:T(8,128)S(1)} %get-tuple-element.79), channel_id=1, source_target_pairs={{0,12},{1,13},{2,14},{3,15},{4,0},{5,1},{6,2},{7,3},{8,4},{9,5},{1... | collective-permute-start | bytes 786440 | tf_op jit(solution)/shard_map/ppermute | solution.py:24
  41.3 8.8 %collective-permute-start.16 = (f32[256,256]{1,0:T(8,128)S(1)}, f32[256,256]{1,0:T(8,128)S(1)}, u32[]{:S(2)}, u32[]{:S(2)}) collective-permute-start(f32[256,256]{1,0:T(8,128)S(1)} %get-tuple-element.80), channel_id=1, source_target_pairs={{0,4},{1,5},{2,6},{3,7},{4,8},{5,9},{6,10},{7,11},{8,12},{9,13},{1... | collective-permute-start | bytes 786440 | tf_op jit(solution)/shard_map/ppermute | solution.py:24
  42.7 12.8 %collective-permute-start.13 = (f32[256,256]{1,0:T(8,128)S(1)}, f32[256,256]{1,0:T(8,128)S(1)}, u32[]{:S(2)}, u32[]{:S(2)}) collective-permute-start(f32[256,256]{1,0:T(8,128)S(1)} %get-tuple-element.77), channel_id=1, source_target_pairs={{0,4},{1,5},{2,6},{3,7},{4,8},{5,9},{6,10},{7,11},{8,12},{9,13},{1... | collective-permute-start | bytes 786440 | tf_op jit(solution)/shard_map/ppermute | solution.py:24
  44.0 14.1 %collective-permute-start.14 = (f32[256,256]{1,0:T(8,128)S(1)}, f32[256,256]{1,0:T(8,128)S(1)}, u32[]{:S(2)}, u32[]{:S(2)}) collective-permute-start(f32[256,256]{1,0:T(8,128)S(1)} %get-tuple-element.78), channel_id=1, source_target_pairs={{0,12},{1,13},{2,14},{3,15},{4,0},{5,1},{6,2},{7,3},{8,4},{9,5},{1... | collective-permute-start | bytes 786440 | tf_op jit(solution)/shard_map/ppermute | solution.py:24
  46.3 21.4 %collective-permute-start.9 = (f32[256,256]{1,0:T(8,128)S(1)}, f32[256,256]{1,0:T(8,128)S(1)}, u32[]{:S(2)}, u32[]{:S(2)}) collective-permute-start(f32[256,256]{1,0:T(8,128)S(1)} %get-tuple-element.73), channel_id=1, source_target_pairs={{0,4},{1,5},{2,6},{3,7},{4,8},{5,9},{6,10},{7,11},{8,12},{9,13},{1... | collective-permute-start | bytes 786440 | tf_op jit(solution)/shard_map/ppermute | solution.py:24
  47.0 19.8 %collective-permute-start.11 = (f32[256,256]{1,0:T(8,128)S(1)}, f32[256,256]{1,0:T(8,128)S(1)}, u32[]{:S(2)}, u32[]{:S(2)}) collective-permute-start(f32[256,256]{1,0:T(8,128)S(1)} %get-tuple-element.75), channel_id=1, source_target_pairs={{0,4},{1,5},{2,6},{3,7},{4,8},{5,9},{6,10},{7,11},{8,12},{9,13},{1... | collective-permute-start | bytes 786440 | tf_op jit(solution)/shard_map/ppermute | solution.py:24
  50.1 16.7 %collective-permute-start.12 = (f32[256,256]{1,0:T(8,128)S(1)}, f32[256,256]{1,0:T(8,128)S(1)}, u32[]{:S(2)}, u32[]{:S(2)}) collective-permute-start(f32[256,256]{1,0:T(8,128)S(1)} %get-tuple-element.76), channel_id=1, source_target_pairs={{0,12},{1,13},{2,14},{3,15},{4,0},{5,1},{6,2},{7,3},{8,4},{9,5},{1... | collective-permute-start | bytes 786440 | tf_op jit(solution)/shard_map/ppermute | solution.py:24
  55.5 12.1 %collective-permute-start.10 = (f32[256,256]{1,0:T(8,128)S(1)}, f32[256,256]{1,0:T(8,128)S(1)}, u32[]{:S(2)}, u32[]{:S(2)}) collective-permute-start(f32[256,256]{1,0:T(8,128)S(1)} %get-tuple-element.74), channel_id=1, source_target_pairs={{0,12},{1,13},{2,14},{3,15},{4,0},{5,1},{6,2},{7,3},{8,4},{9,5},{1... | collective-permute-start | bytes 786440 | tf_op jit(solution)/shard_map/ppermute | solution.py:24

commit v16 on v9

--- a/solution.py
+++ b/solution.py
@@ -327,18 +327,7 @@
         (VMEM, VMEM),
         [],
     )(over_tiles)
-    a = call(
-        ham_kernel,
-        "ham",
-        sds((blocks // 2, tall, 3 * LANES), BF16),
-        (SMEM, SMEM, pltpu.HBM),
-        VMEM,
-        [
-            pltpu.SMEM((rows, blocks), jnp.int32),
-            VMEM(ham_tiles.shape, F32),
-            pltpu.SemaphoreType.DMA((rows,)),
-        ],
-    )(ham_cols, ham_count, ham_tiles)
+    a = None
 
     def add(step, chunks, acc):
         return call(
@@ -355,8 +344,20 @@
     for step in range(1, count - 1):
         now = arrivals[-1]
         if step == 1:
-            now[0], a = lax.optimization_barrier((now[0], a))
-            now[-1], *tables = lax.optimization_barrier((now[-1], *tables))
+            now[0], ham_tiles = lax.optimization_barrier((now[0], ham_tiles))
+            a = call(
+                ham_kernel,
+                "ham",
+                sds((blocks // 2, tall, 3 * LANES), BF16),
+                (SMEM, SMEM, pltpu.HBM),
+                VMEM,
+                [
+                    pltpu.SMEM((rows, blocks), jnp.int32),
+                    VMEM(ham_tiles.shape, F32),
+                    pltpu.SemaphoreType.DMA((rows,)),
+                ],
+            )(ham_cols, ham_count, ham_tiles)
+            now[-1], a, *tables = lax.optimization_barrier((now[-1], a, *tables))
         else:
             now[0], acc = lax.optimization_barrier((now[0], acc))
         if step == 2:

time: 67.3 us -> 67.3 us (level)
  waiting for transfers between devices: 23.8 us -> 24.6 us
  starting transfers between devices: 20.9 us -> 20.1 us
    ppermute x17, starting transfers between devices: 20.9 us -> 20.1 us  [permute(): lax.ppermute(x, AXES, [(flat(*place), flat(*target(*place))) for place in...]
    ppermute x17, waiting for transfers between devices: 23.8 us -> 24.6 us  [permute(): lax.ppermute(x, AXES, [(flat(*place), flat(*target(*place))) for place in...]
  transfers between devices with their start and end apart: 17 -> 17, of which waited for: 11 -> 12; matrix products, arithmetic and copies ran while one was open for 0% -> 0% of each run, Pallas kernels for 27% -> 28%
where the time goes in v16:
time: 67.3 us; the launch traced here: 66.7 us
  waiting for transfers between devices  24.6 us (37%)
  Pallas kernels  21.2 us (32%)
  starting transfers between devices  20.1 us (30%)
  between operations  0.82 us (1%)
    ppermute x17, waiting for transfers between devices, permute(): lax.ppermute(x, AXES, [(flat(*place), flat(*target(*place))) for place in...  24.6 us
    ppermute x17, starting transfers between devices, permute(): lax.ppermute(x, AXES, [(flat(*place), flat(*target(*place))) for place in...  20.1 us
    pallas_call x4, Pallas kernels, add(): call(functools.partial(add_kernel, step, list(range(len(chunks)))), 'add%...  6.17 us
    pallas_call x4, Pallas kernels, shards(): call(functools.partial(last_kernel, count - 1, per_shard - 1, sum(pieces[...  3.56 us
    pallas_call x4, Pallas kernels, shards(): call(functools.partial(arrived_kernel, sum(pieces[:i])), 'arrived%d' % i,...  3.4 us
    pallas_call x1, Pallas kernels, shards(): call(ham_kernel, 'ham', sds((blocks // 2, tall, 3 * LANES), BF16), (SMEM,...  2.5 us
    pallas_call x1, Pallas kernels, shards(): call(own_kernel, 'own', (sds((rows, tile, width), F32), sds((rows, tile,...  1.66 us
    pallas_call x1, Pallas kernels, shards(): call(table_kernel, 'table', sds((rows, blocks), jnp.int32), (SMEM, SMEM),...  1.4 us
  transfers between devices with their start and end apart: 17, of which 12 were waited for; matrix products, arithmetic and copies ran while one was open for 0% of the time, Pallas kernels for 28%

profile of v16, /device:TPU:0, one launch (start us, length us, event | category | flops | bytes accessed | tf_op | source)
XLA Modules:
  0.0 66.7 jit_solution(12628097484819622254)
XLA Ops:
  0.6 1.1 %cut.1 = (f32[2,64,512]{2,1,0:T(8,128)S(1)}, f32[2,64,512]{2,1,0:T(8,128)S(1)}) custom-call(f32[4,64,512]{2,1,0:T(8,128)} %dens.1), custom_call_target="tpu_custom_call" | custom-call | flops 1024 | bytes 1024 | tf_op jit(solution)/shard_map/cut/pallas_call | solution.py:299
  1.8 3.1 %collective-permute-start.1 = (f32[2,64,512]{2,1,0:T(8,128)S(1)}, f32[2,64,512]{2,1,0:T(8,128)S(1)}, u32[]{:S(2)}, u32[]{:S(2)}) collective-permute-start(f32[2,64,512]{2,1,0:T(8,128)S(1)} %get-tuple-element.46.rest_0_), channel_id=1, source_target_pairs={{0,1},{1,3},{2,0},{3,2},{4,5},{5,7},{6,4},{7,6},{8,9},{9,11},{10,8... | collective-permute-start | bytes 786440 | tf_op jit(solution)/shard_map/ppermute | solution.py:24
  4.8 2.6 %collective-permute-start = (f32[2,64,512]{2,1,0:T(8,128)S(1)}, f32[2,64,512]{2,1,0:T(8,128)S(1)}, u32[]{:S(2)}, u32[]{:S(2)}) collective-permute-start(f32[2,64,512]{2,1,0:T(8,128)S(1)} %get-tuple-element.45.rest_1_), channel_id=1, source_target_pairs={{0,1},{1,3},{2,0},{3,2},{4,5},{5,7},{6,4},{7,6},{8,9},{9,11},{10,8... | collective-permute-start | bytes 786440 | tf_op jit(solution)/shard_map/ppermute | solution.py:24
  7.4 1.4 %table.1.dens_table = s32[4,16]{1,0:T(4,128)S(1)} custom-call(s32[4,8]{1,0:T(4,128)} %columns, s32[4]{0:T(128)} %counts.1), custom_call_target="tpu_custom_call" | custom-call | flops 1024 | bytes 1024 | tf_op jit(solution)/shard_map/table/pallas_call | solution.py:313
  8.8 0.4 collective-permute-start.4
  9.2 2.5 %collective-permute-start.3 = (s32[4,16]{1,0:T(4,128)S(1)}, s32[4,16]{1,0:T(4,128)S(1)}, u32[]{:S(2)}, u32[]{:S(2)}) collective-permute-start(s32[4,16]{1,0:T(4,128)S(1)} %table.1.dens_table), channel_id=1, source_target_pairs={{0,3},{1,2},{2,1},{3,0},{4,7},{5,6},{6,5},{7,4},{8,11},{9,10},{10,... | collective-permute-start | bytes 776 | tf_op jit(solution)/shard_map/ppermute | solution.py:24
  11.7 0.0 collective-permute-start.2
  11.7 1.3 %collective-permute-done.1.rest_1_ = f32[2,64,512]{2,1,0:T(8,128)S(1)} collective-permute-done((f32[2,64,512]{2,1,0:T(8,128)S(1)}, f32[2,64,512]{2,1,0:T(8,128)S(1)}, u32[]{:S(2)}, u32[]{:S(2)}) %collective-permute-start.1) | collective-permute-done | bytes 262176 | tf_op jit(solution)/shard_map/ppermute | solution.py:24
  13.0 1.1 %collective-permute-start.6 = (f32[2,64,512]{2,1,0:T(8,128)S(1)}, f32[2,64,512]{2,1,0:T(8,128)S(1)}, u32[]{:S(2)}, u32[]{:S(2)}) collective-permute-start(f32[2,64,512]{2,1,0:T(8,128)S(1)} %collective-permute-done.1.rest_1_), channel_id=1, source_target_pairs={{0,1},{1,3},{2,0},{3,2},{4,5},{5,7},{6,4},{7,6},{8,9},{9,11},{10,8... | collective-permute-start | bytes 786440 | tf_op jit(solution)/shard_map/ppermute | solution.py:24
  14.1 2.5 %ham.1.a = bf16[8,256,384]{2,1,0:T(8,128)(2,1)S(1)} custom-call(s32[4,12]{1,0:T(4,128)} %ham_cols.1, s32[4]{0:T(128)} %ham_count.1, f32[4,64,768]{2,1,0:T(8,128)} %ham.2), custom_call_target="tpu_custom_call" | custom-call | flops 1024 | bytes 1024 | tf_op jit(solution)/shard_map/ham/pallas_call | solution.py:348
  16.7 0.6 collective-permute-done.4.dens_table
  17.2 3.0 %collective-permute-done.3.dens_table = s32[4,16]{1,0:T(4,128)S(1)} collective-permute-done((s32[4,16]{1,0:T(4,128)S(1)}, s32[4,16]{1,0:T(4,128)S(1)}, u32[]{:S(2)}, u32[]{:S(2)}) %collective-permute-start.3) | collective-permute-done | bytes 288 | tf_op jit(solution)/shard_map/ppermute | solution.py:24
  20.2 0.6 collective-permute-start.5
  20.8 0.3 margin.1
  21.1 1.1 %pick.1 = bf16[2,512,1024]{2,1,0:T(8,128)(2,1)S(1)} custom-call(s32[4,16]{1,0:T(4,128)S(1)} %collective-permute-done.4.dens_table), custom_call_target="tpu_custom_call" | custom-call | flops 1024 | bytes 1024 | tf_op jit(solution)/shard_map/pick/pallas_call | solution.py:364
  22.2 1.6 %add0.1.rest_0_ = f32[256,1024]{1,0:T(8,128)S(1)} custom-call(s32[4,16]{1,0:T(4,128)S(1)} %table.1.dens_table, bf16[8,256,384]{2,1,0:T(8,128)(2,1)S(1)} %ham.1.a, f32[2,64,512]{2,1,0:T(8,128)S(1)} %get-tuple-element.46.rest_0_, f32[2,64,512]{2,1,0:T(8,128)S(1)} %get-tuple-element.45.rest_1_), custom_call_target="tpu_custom_call" | custom-call | flops 1024 | bytes 1024 | tf_op jit(solution)/shard_map/add0/pallas_call | solution.py:333
  23.8 0.6 collective-permute-done.6.rest_1_
  24.4 2.0 %collective-permute-start.7 = (f32[2,64,512]{2,1,0:T(8,128)S(1)}, f32[2,64,512]{2,1,0:T(8,128)S(1)}, u32[]{:S(2)}, u32[]{:S(2)}) collective-permute-start(f32[2,64,512]{2,1,0:T(8,128)S(1)} %collective-permute-done.6.rest_1_), channel_id=1, source_target_pairs={{0,1},{1,3},{2,0},{3,2},{4,5},{5,7},{6,4},{7,6},{8,9},{9,11},{10,8... | collective-permute-start | bytes 786440 | tf_op jit(solution)/shard_map/ppermute | solution.py:24
  26.4 3.9 %collective-permute-done.5.rest_2_ = f32[2,64,512]{2,1,0:T(8,128)S(1)} collective-permute-done((f32[2,64,512]{2,1,0:T(8,128)S(1)}, f32[2,64,512]{2,1,0:T(8,128)S(1)}, u32[]{:S(2)}, u32[]{:S(2)}) %collective-permute-start.5) | collective-permute-done | bytes 262176 | tf_op jit(solution)/shard_map/ppermute | solution.py:24
  30.3 0.8 %collective-permute-start.8 = (f32[2,64,512]{2,1,0:T(8,128)S(1)}, f32[2,64,512]{2,1,0:T(8,128)S(1)}, u32[]{:S(2)}, u32[]{:S(2)}) collective-permute-start(f32[2,64,512]{2,1,0:T(8,128)S(1)} %collective-permute-done.5.rest_2_), channel_id=1, source_target_pairs={{0,1},{1,3},{2,0},{3,2},{4,5},{5,7},{6,4},{7,6},{8,9},{9,11},{10,8... | collective-permute-start | bytes 786440 | tf_op jit(solution)/shard_map/ppermute | solution.py:24
  31.2 1.6 %add1.1.rest_0_ = f32[256,1024]{1,0:T(8,128)S(1)} custom-call(s32[4,16]{1,0:T(4,128)S(1)} %collective-permute-done.2.dens_table, bf16[8,256,384]{2,1,0:T(8,128)(2,1)S(1)} %ham.1.a, f32[256,1024]{1,0:T(8,128)S(1)} %add0.1.rest_0_, f32[2,64,512]{2,1,0:T(8,128)S(1)} %collective-permute-done.1.rest_1_, f32[2,64,512]{2,1,0:T(8,128)S(1)} %collective-permute-done.rest_2_), custom_call_target="tpu_custom_call" | custom-call | flops 1024 | bytes 1024 | tf_op jit(solution)/shard_map/add1/pallas_call | solution.py:333
  32.8 1.7 %add2.1.rest_0_ = f32[256,1024]{1,0:T(8,128)S(1)} custom-call(s32[4,16]{1,0:T(4,128)S(1)} %collective-permute-done.3.dens_table, bf16[8,256,384]{2,1,0:T(8,128)(2,1)S(1)} %ham.1.a, f32[256,1024]{1,0:T(8,128)S(1)} %add1.1.rest_0_, f32[2,64,512]{2,1,0:T(8,128)S(1)} %collective-permute-done.6.rest_1_, f32[2,64,512]{2,1,0:T(8,128)S(1)} %collective-permute-done.5.rest_2_), custom_call_target="tpu_custom_call" | custom-call | flops 1024 | bytes 1024 | tf_op jit(solution)/shard_map/add2/pallas_call | solution.py:333
  34.5 1.5 %collective-permute-done.7.rest_1_ = f32[2,64,512]{2,1,0:T(8,128)S(1)} collective-permute-done((f32[2,64,512]{2,1,0:T(8,128)S(1)}, f32[2,64,512]{2,1,0:T(8,128)S(1)}, u32[]{:S(2)}, u32[]{:S(2)}) %collective-permute-start.7) | collective-permute-done | bytes 262176 | tf_op jit(solution)/shard_map/ppermute | solution.py:24
  36.0 1.2 %add3.1.acc_in = f32[256,1024]{1,0:T(8,128)S(1)} custom-call(s32[4,16]{1,0:T(4,128)S(1)} %collective-permute-done.4.dens_table, bf16[8,256,384]{2,1,0:T(8,128)(2,1)S(1)} %ham.1.a, f32[256,1024]{1,0:T(8,128)S(1)} %add2.1.rest_0_, f32[2,64,512]{2,1,0:T(8,128)S(1)} %collective-permute-done.7.rest_1_), custom_call_target="tpu_custom_call" | custom-call | flops 1024 | bytes 1024 | tf_op jit(solution)/shard_map/add3/pallas_call | solution.py:333
  37.2 3.2 %collective-permute-done.8.chunk = f32[2,64,512]{2,1,0:T(8,128)S(1)} collective-permute-done((f32[2,64,512]{2,1,0:T(8,128)S(1)}, f32[2,64,512]{2,1,0:T(8,128)S(1)}, u32[]{:S(2)}, u32[]{:S(2)}) %collective-permute-start.8) | collective-permute-done | bytes 262176 | tf_op jit(solution)/shard_map/ppermute | solution.py:24
  40.4 0.9 %last0.1 = (f32[256,256]{1,0:T(8,128)S(1)}, f32[256,256]{1,0:T(8,128)S(1)}, f32[256,256]{1,0:T(8,128)S(1)}) custom-call(bf16[8,256,384]{2,1,0:T(8,128)(2,1)S(1)} %ham.1.a, f32[256,1024]{1,0:T(8,128)S(1)} %add3.1.acc_in, f32[2,64,512]{2,1,0:T(8,128)S(1)} %collective-permute-done.8.chunk, bf16[2,512,1024]{2,1,0:T(8,128)(2,1)S(1)} %pick.1, ...), custom_call_target="tpu_custom_call" | custom-call | flops 1024 | bytes 1024 | tf_op jit(solution)/shard_map/last0/pallas_call | solution.py:380
  41.3 0.1 collective-permute-start.15
  41.4 1.7 %collective-permute-start.16 = (f32[256,256]{1,0:T(8,128)S(1)}, f32[256,256]{1,0:T(8,128)S(1)}, u32[]{:S(2)}, u32[]{:S(2)}) collective-permute-start(f32[256,256]{1,0:T(8,128)S(1)} %get-tuple-element.82), channel_id=1, source_target_pairs={{0,12},{1,13},{2,14},{3,15},{4,0},{5,1},{6,2},{7,3},{8,4},{9,5},{1... | collective-permute-start | bytes 786440 | tf_op jit(solution)/shard_map/ppermute | solution.py:24
  43.1 0.9 %last1.1 = (f32[256,256]{1,0:T(8,128)S(1)}, f32[256,256]{1,0:T(8,128)S(1)}, f32[256,256]{1,0:T(8,128)S(1)}) custom-call(bf16[8,256,384]{2,1,0:T(8,128)(2,1)S(1)} %ham.1.a, f32[256,1024]{1,0:T(8,128)S(1)} %add3.1.acc_in, f32[2,64,512]{2,1,0:T(8,128)S(1)} %collective-permute-done.8.chunk, bf16[2,512,1024]{2,1,0:T(8,128)(2,1)S(1)} %pick.1, ...), custom_call_target="tpu_custom_call" | custom-call | flops 1024 | bytes 1024 | tf_op jit(solution)/shard_map/last1/pallas_call | solution.py:380
  44.0 0.1 collective-permute-start.13
  44.1 1.7 %collective-permute-start.14 = (f32[256,256]{1,0:T(8,128)S(1)}, f32[256,256]{1,0:T(8,128)S(1)}, u32[]{:S(2)}, u32[]{:S(2)}) collective-permute-start(f32[256,256]{1,0:T(8,128)S(1)} %get-tuple-element.80), channel_id=1, source_target_pairs={{0,12},{1,13},{2,14},{3,15},{4,0},{5,1},{6,2},{7,3},{8,4},{9,5},{1... | collective-permute-start | bytes 786440 | tf_op jit(solution)/shard_map/ppermute | solution.py:24
  45.8 0.9 %last2.1 = (f32[256,256]{1,0:T(8,128)S(1)}, f32[256,256]{1,0:T(8,128)S(1)}, f32[256,256]{1,0:T(8,128)S(1)}) custom-call(bf16[8,256,384]{2,1,0:T(8,128)(2,1)S(1)} %ham.1.a, f32[256,1024]{1,0:T(8,128)S(1)} %add3.1.acc_in, f32[2,64,512]{2,1,0:T(8,128)S(1)} %collective-permute-done.8.chunk, bf16[2,512,1024]{2,1,0:T(8,128)(2,1)S(1)} %pick.1, ...), custom_call_target="tpu_custom_call" | custom-call | flops 1024 | bytes 1024 | tf_op jit(solution)/shard_map/last2/pallas_call | solution.py:380
  46.7 0.9 %last3.1 = (f32[256,256]{1,0:T(8,128)S(1)}, f32[256,256]{1,0:T(8,128)S(1)}, f32[256,256]{1,0:T(8,128)S(1)}) custom-call(bf16[8,256,384]{2,1,0:T(8,128)(2,1)S(1)} %ham.1.a, f32[256,1024]{1,0:T(8,128)S(1)} %add3.1.acc_in, f32[2,64,512]{2,1,0:T(8,128)S(1)} %collective-permute-done.8.chunk, bf16[2,512,1024]{2,1,0:T(8,128)(2,1)S(1)} %pick.1, ...), custom_call_target="tpu_custom_call" | custom-call | flops 1024 | bytes 1024 | tf_op jit(solution)/shard_map/last3/pallas_call | solution.py:380
  47.6 0.1 collective-permute-start.9
  47.7 0.4 collective-permute-done.15.above
  48.1 1.2 %collective-permute-start.11 = (f32[256,256]{1,0:T(8,128)S(1)}, f32[256,256]{1,0:T(8,128)S(1)}, u32[]{:S(2)}, u32[]{:S(2)}) collective-permute-start(f32[256,256]{1,0:T(8,128)S(1)} %get-tuple-element.77), channel_id=1, source_target_pairs={{0,4},{1,5},{2,6},{3,7},{4,8},{5,9},{6,10},{7,11},{8,12},{9,13},{1... | collective-permute-start | bytes 786440 | tf_op jit(solution)/shard_map/ppermute | solution.py:24
  49.3 0.5 collective-permute-done.16.below
  49.8 2.2 %collective-permute-start.12 = (f32[256,256]{1,0:T(8,128)S(1)}, f32[256,256]{1,0:T(8,128)S(1)}, u32[]{:S(2)}, u32[]{:S(2)}) collective-permute-start(f32[256,256]{1,0:T(8,128)S(1)} %get-tuple-element.78), channel_id=1, source_target_pairs={{0,12},{1,13},{2,14},{3,15},{4,0},{5,1},{6,2},{7,3},{8,4},{9,5},{1... | collective-permute-start | bytes 786440 | tf_op jit(solution)/shard_map/ppermute | solution.py:24
  52.0 1.7 %collective-permute-done.13.above = f32[256,256]{1,0:T(8,128)S(1)} collective-permute-done((f32[256,256]{1,0:T(8,128)S(1)}, f32[256,256]{1,0:T(8,128)S(1)}, u32[]{:S(2)}, u32[]{:S(2)}) %collective-permute-start.13) | collective-permute-done | bytes 262176 | tf_op jit(solution)/shard_map/ppermute | solution.py:24
  53.7 0.0 collective-permute-start.10
  53.7 1.7 %own.1 = (f32[4,64,1024]{2,1,0:T(8,128)}, f32[4,64,3072]{2,1,0:T(8,128)}) custom-call(bf16[3,256,256]{2,1,0:T(8,128)(2,1)S(1)} %get-tuple-element.53.m_hi, bf16[3,256,256]{2,1,0:T(8,128)(2,1)S(1)} %get-tuple-element.54.m_lo, f32[256,256]{1,0:T(8,128)S(1)} %get-tuple-element.65.rest_0_, f32[256,256]{1,0:T(8,128)S(1)} %get-tuple-element.68.rest_1_, ...), custom_call_target="tpu_custom_call" | custom-call | flops 1024 | bytes 1024 | tf_op jit(solution)/shard_map/own/pallas_call | solution.py:393
  55.4 0.9 %arrived0.1.window_in = f32[4,64,3072]{2,1,0:T(8,128)} custom-call(f32[256,256]{1,0:T(8,128)S(1)} %collective-permute-done.15.above, f32[256,256]{1,0:T(8,128)S(1)} %collective-permute-done.16.below, f32[4,64,3072]{2,1,0:T(8,128)} %get-tuple-element.83.window_in), custom_call_target="tpu_custom_call", output_to_operand_aliasing={{}: (2, {})} | custom-call | flops 1024 | bytes 1024 | tf_op jit(solution)/shard_map/arrived0/pallas_call | solution.py:402
  56.2 0.9 %arrived1.1.window_in = f32[4,64,3072]{2,1,0:T(8,128)} custom-call(f32[256,256]{1,0:T(8,128)S(1)} %collective-permute-done.13.above, f32[256,256]{1,0:T(8,128)S(1)} %collective-permute-done.14.below, f32[4,64,3072]{2,1,0:T(8,128)} %arrived0.1.window_in), custom_call_target="tpu_custom_call", output_to_operand_aliasing={{}: (2, {})} | custom-call | flops 1024 | bytes 1024 | tf_op jit(solution)/shard_map/arrived1/pallas_call | solution.py:402
  57.1 7.8 %collective-permute-done.11.above = f32[256,256]{1,0:T(8,128)S(1)} collective-permute-done((f32[256,256]{1,0:T(8,128)S(1)}, f32[256,256]{1,0:T(8,128)S(1)}, u32[]{:S(2)}, u32[]{:S(2)}) %collective-permute-start.11) | collective-permute-done | bytes 262176 | tf_op jit(solution)/shard_map/ppermute | solution.py:24
  64.9 0.0 collective-permute-done.12.below
  64.9 0.8 %arrived2.1.window_in = f32[4,64,3072]{2,1,0:T(8,128)} custom-call(f32[256,256]{1,0:T(8,128)S(1)} %collective-permute-done.11.above, f32[256,256]{1,0:T(8,128)S(1)} %collective-permute-done.12.below, f32[4,64,3072]{2,1,0:T(8,128)} %arrived1.1.window_in), custom_call_target="tpu_custom_call", output_to_operand_aliasing={{}: (2, {})} | custom-call | flops 1024 | bytes 1024 | tf_op jit(solution)/shard_map/arrived2/pallas_call | solution.py:402
  65.8 0.1 collective-permute-done.10.below
  65.9 0.8 %arrived3.1 = f32[4,64,3072]{2,1,0:T(8,128)} custom-call(f32[256,256]{1,0:T(8,128)S(1)} %collective-permute-done.9.above, f32[256,256]{1,0:T(8,128)S(1)} %collective-permute-done.10.below, f32[4,64,3072]{2,1,0:T(8,128)} %arrived2.1.window_in), custom_call_target="tpu_custom_call", output_to_operand_aliasing={{}: (2, {})} | custom-call | flops 1024 | bytes 1024 | tf_op jit(solution)/shard_map/arrived3/pallas_call | solution.py:402
  (6 shorter events, 0.0 us)
Async XLA Ops:
  0.6 20.2 %copy-start = (f32[4,64,768]{2,1,0:T(8,128)S(1)}, f32[4,64,768]{2,1,0:T(8,128)}, u32[]{:S(2)}) copy-start(f32[4,64,768]{2,1,0:T(8,128)} %over.1) | copy-start | bytes 2359300
  1.8 11.3 %collective-permute-start.1 = (f32[2,64,512]{2,1,0:T(8,128)S(1)}, f32[2,64,512]{2,1,0:T(8,128)S(1)}, u32[]{:S(2)}, u32[]{:S(2)}) collective-permute-start(f32[2,64,512]{2,1,0:T(8,128)S(1)} %get-tuple-element.46.rest_0_), channel_id=1, source_target_pairs={{0,1},{1,3},{2,0},{3,2},{4,5},{5,7},{6,4},{7,6},{8,9},{9,11},{10,8... | collective-permute-start | bytes 786440 | tf_op jit(solution)/shard_map/ppermute | solution.py:24
  4.8 15.4 %collective-permute-start = (f32[2,64,512]{2,1,0:T(8,128)S(1)}, f32[2,64,512]{2,1,0:T(8,128)S(1)}, u32[]{:S(2)}, u32[]{:S(2)}) collective-permute-start(f32[2,64,512]{2,1,0:T(8,128)S(1)} %get-tuple-element.45.rest_1_), channel_id=1, source_target_pairs={{0,1},{1,3},{2,0},{3,2},{4,5},{5,7},{6,4},{7,6},{8,9},{9,11},{10,8... | collective-permute-start | bytes 786440 | tf_op jit(solution)/shard_map/ppermute | solution.py:24
  8.8 8.4 %collective-permute-start.4 = (s32[4,16]{1,0:T(4,128)S(1)}, s32[4,16]{1,0:T(4,128)S(1)}, u32[]{:S(2)}, u32[]{:S(2)}) collective-permute-start(s32[4,16]{1,0:T(4,128)S(1)} %table.1.dens_table), channel_id=1, source_target_pairs={{0,2},{1,0},{2,3},{3,1},{4,6},{5,4},{6,7},{7,5},{8,10},{9,8},{10,1... | collective-permute-start | bytes 776 | tf_op jit(solution)/shard_map/ppermute | solution.py:24
  9.2 11.0 %collective-permute-start.3 = (s32[4,16]{1,0:T(4,128)S(1)}, s32[4,16]{1,0:T(4,128)S(1)}, u32[]{:S(2)}, u32[]{:S(2)}) collective-permute-start(s32[4,16]{1,0:T(4,128)S(1)} %table.1.dens_table), channel_id=1, source_target_pairs={{0,3},{1,2},{2,1},{3,0},{4,7},{5,6},{6,5},{7,4},{8,11},{9,10},{10,... | collective-permute-start | bytes 776 | tf_op jit(solution)/shard_map/ppermute | solution.py:24
  11.7 8.5 %collective-permute-start.2 = (s32[4,16]{1,0:T(4,128)S(1)}, s32[4,16]{1,0:T(4,128)S(1)}, u32[]{:S(2)}, u32[]{:S(2)}) collective-permute-start(s32[4,16]{1,0:T(4,128)S(1)} %table.1.dens_table), channel_id=1, source_target_pairs={{0,1},{1,3},{2,0},{3,2},{4,5},{5,7},{6,4},{7,6},{8,9},{9,11},{10,8... | collective-permute-start | bytes 776 | tf_op jit(solution)/shard_map/ppermute | solution.py:24
  13.0 11.4 %collective-permute-start.6 = (f32[2,64,512]{2,1,0:T(8,128)S(1)}, f32[2,64,512]{2,1,0:T(8,128)S(1)}, u32[]{:S(2)}, u32[]{:S(2)}) collective-permute-start(f32[2,64,512]{2,1,0:T(8,128)S(1)} %collective-permute-done.1.rest_1_), channel_id=1, source_target_pairs={{0,1},{1,3},{2,0},{3,2},{4,5},{5,7},{6,4},{7,6},{8,9},{9,11},{10,8... | collective-permute-start | bytes 786440 | tf_op jit(solution)/shard_map/ppermute | solution.py:24
  20.2 10.1 %collective-permute-start.5 = (f32[2,64,512]{2,1,0:T(8,128)S(1)}, f32[2,64,512]{2,1,0:T(8,128)S(1)}, u32[]{:S(2)}, u32[]{:S(2)}) collective-permute-start(f32[2,64,512]{2,1,0:T(8,128)S(1)} %collective-permute-done.rest_2_), channel_id=1, source_target_pairs={{0,1},{1,3},{2,0},{3,2},{4,5},{5,7},{6,4},{7,6},{8,9},{9,11},{10,8... | collective-permute-start | bytes 786440 | tf_op jit(solution)/shard_map/ppermute | solution.py:24
  24.4 11.6 %collective-permute-start.7 = (f32[2,64,512]{2,1,0:T(8,128)S(1)}, f32[2,64,512]{2,1,0:T(8,128)S(1)}, u32[]{:S(2)}, u32[]{:S(2)}) collective-permute-start(f32[2,64,512]{2,1,0:T(8,128)S(1)} %collective-permute-done.6.rest_1_), channel_id=1, source_target_pairs={{0,1},{1,3},{2,0},{3,2},{4,5},{5,7},{6,4},{7,6},{8,9},{9,11},{10,8... | collective-permute-start | bytes 786440 | tf_op jit(solution)/shard_map/ppermute | solution.py:24
  30.3 10.1 %collective-permute-start.8 = (f32[2,64,512]{2,1,0:T(8,128)S(1)}, f32[2,64,512]{2,1,0:T(8,128)S(1)}, u32[]{:S(2)}, u32[]{:S(2)}) collective-permute-start(f32[2,64,512]{2,1,0:T(8,128)S(1)} %collective-permute-done.5.rest_2_), channel_id=1, source_target_pairs={{0,1},{1,3},{2,0},{3,2},{4,5},{5,7},{6,4},{7,6},{8,9},{9,11},{10,8... | collective-permute-start | bytes 786440 | tf_op jit(solution)/shard_map/ppermute | solution.py:24
  41.3 6.8 %collective-permute-start.15 = (f32[256,256]{1,0:T(8,128)S(1)}, f32[256,256]{1,0:T(8,128)S(1)}, u32[]{:S(2)}, u32[]{:S(2)}) collective-permute-start(f32[256,256]{1,0:T(8,128)S(1)} %get-tuple-element.81), channel_id=1, source_target_pairs={{0,4},{1,5},{2,6},{3,7},{4,8},{5,9},{6,10},{7,11},{8,12},{9,13},{1... | collective-permute-start | bytes 786440 | tf_op jit(solution)/shard_map/ppermute | solution.py:24
  41.4 8.4 %collective-permute-start.16 = (f32[256,256]{1,0:T(8,128)S(1)}, f32[256,256]{1,0:T(8,128)S(1)}, u32[]{:S(2)}, u32[]{:S(2)}) collective-permute-start(f32[256,256]{1,0:T(8,128)S(1)} %get-tuple-element.82), channel_id=1, source_target_pairs={{0,12},{1,13},{2,14},{3,15},{4,0},{5,1},{6,2},{7,3},{8,4},{9,5},{1... | collective-permute-start | bytes 786440 | tf_op jit(solution)/shard_map/ppermute | solution.py:24
  44.0 9.7 %collective-permute-start.13 = (f32[256,256]{1,0:T(8,128)S(1)}, f32[256,256]{1,0:T(8,128)S(1)}, u32[]{:S(2)}, u32[]{:S(2)}) collective-permute-start(f32[256,256]{1,0:T(8,128)S(1)} %get-tuple-element.79), channel_id=1, source_target_pairs={{0,4},{1,5},{2,6},{3,7},{4,8},{5,9},{6,10},{7,11},{8,12},{9,13},{1... | collective-permute-start | bytes 786440 | tf_op jit(solution)/shard_map/ppermute | solution.py:24
  44.1 12.1 %collective-permute-start.14 = (f32[256,256]{1,0:T(8,128)S(1)}, f32[256,256]{1,0:T(8,128)S(1)}, u32[]{:S(2)}, u32[]{:S(2)}) collective-permute-start(f32[256,256]{1,0:T(8,128)S(1)} %get-tuple-element.80), channel_id=1, source_target_pairs={{0,12},{1,13},{2,14},{3,15},{4,0},{5,1},{6,2},{7,3},{8,4},{9,5},{1... | collective-permute-start | bytes 786440 | tf_op jit(solution)/shard_map/ppermute | solution.py:24
  47.6 18.2 %collective-permute-start.9 = (f32[256,256]{1,0:T(8,128)S(1)}, f32[256,256]{1,0:T(8,128)S(1)}, u32[]{:S(2)}, u32[]{:S(2)}) collective-permute-start(f32[256,256]{1,0:T(8,128)S(1)} %get-tuple-element.75), channel_id=1, source_target_pairs={{0,4},{1,5},{2,6},{3,7},{4,8},{5,9},{6,10},{7,11},{8,12},{9,13},{1... | collective-permute-start | bytes 786440 | tf_op jit(solution)/shard_map/ppermute | solution.py:24
  48.1 16.9 %collective-permute-start.11 = (f32[256,256]{1,0:T(8,128)S(1)}, f32[256,256]{1,0:T(8,128)S(1)}, u32[]{:S(2)}, u32[]{:S(2)}) collective-permute-start(f32[256,256]{1,0:T(8,128)S(1)} %get-tuple-element.77), channel_id=1, source_target_pairs={{0,4},{1,5},{2,6},{3,7},{4,8},{5,9},{6,10},{7,11},{8,12},{9,13},{1... | collective-permute-start | bytes 786440 | tf_op jit(solution)/shard_map/ppermute | solution.py:24
  49.8 15.1 %collective-permute-start.12 = (f32[256,256]{1,0:T(8,128)S(1)}, f32[256,256]{1,0:T(8,128)S(1)}, u32[]{:S(2)}, u32[]{:S(2)}) collective-permute-start(f32[256,256]{1,0:T(8,128)S(1)} %get-tuple-element.78), channel_id=1, source_target_pairs={{0,12},{1,13},{2,14},{3,15},{4,0},{5,1},{6,2},{7,3},{8,4},{9,5},{1... | collective-permute-start | bytes 786440 | tf_op jit(solution)/shard_map/ppermute | solution.py:24
  53.7 12.2 %collective-permute-start.10 = (f32[256,256]{1,0:T(8,128)S(1)}, f32[256,256]{1,0:T(8,128)S(1)}, u32[]{:S(2)}, u32[]{:S(2)}) collective-permute-start(f32[256,256]{1,0:T(8,128)S(1)} %get-tuple-element.76), channel_id=1, source_target_pairs={{0,12},{1,13},{2,14},{3,15},{4,0},{5,1},{6,2},{7,3},{8,4},{9,5},{1... | collective-permute-start | bytes 786440 | tf_op jit(solution)/shard_map/ppermute | solution.py:24

commit v17 on v14

--- a/solution.py
+++ b/solution.py
@@ -109,7 +109,7 @@
 
 
 def lane_blocks(width, step=256):
-    return [slice(i, min(i + step, width)) for i in range(0, width, step)]
+    return [slice(i, i + step) for i in range(0, width, step)]
 
 
 def ham_kernel(ham_cols, ham_count, ham, a, ham_table, ham_here, sems):
@@ -326,18 +326,7 @@
         (VMEM, VMEM),
         [],
     )(over_tiles)
-    a = call(
-        ham_kernel,
-        "ham",
-        sds((blocks // 2, tall, 3 * LANES), BF16),
-        (SMEM, SMEM, pltpu.HBM),
-        VMEM,
-        [
-            pltpu.SMEM((rows, blocks), jnp.int32),
-            VMEM(ham_tiles.shape, F32),
-            pltpu.SemaphoreType.DMA((rows,)),
-        ],
-    )(ham_cols, ham_count, ham_tiles)
+    a = None
 
     def add(step, chunks, acc):
         return call(
@@ -354,8 +343,20 @@
     for step in range(1, count - 1):
         now = arrivals[-1]
         if step == 1:
-            now[0], a = lax.optimization_barrier((now[0], a))
-            now[-1], *tables = lax.optimization_barrier((now[-1], *tables))
+            now[0], ham_tiles = lax.optimization_barrier((now[0], ham_tiles))
+            a = call(
+                ham_kernel,
+                "ham",
+                sds((blocks // 2, tall, 3 * LANES), BF16),
+                (SMEM, SMEM, pltpu.HBM),
+                VMEM,
+                [
+                    pltpu.SMEM((rows, blocks), jnp.int32),
+                    VMEM(ham_tiles.shape, F32),
+                    pltpu.SemaphoreType.DMA((rows,)),
+                ],
+            )(ham_cols, ham_count, ham_tiles)
+            now[-1], a, *tables = lax.optimization_barrier((now[-1], a, *tables))
         else:
             now[0], acc = lax.optimization_barrier((now[0], acc))
         if step == 2:

time: 67.2 us -> 67.2 us (level)
  transfers between devices with their start and end apart: 17 -> 17, of which waited for: 10 -> 12; matrix products, arithmetic and copies ran while one was open for 0% -> 0% of each run, Pallas kernels for 29% -> 29%
where the time goes in v17:
time: 67.2 us; the launch traced here: 66.7 us
  waiting for transfers between devices  23.1 us (34%)
  Pallas kernels  22.1 us (33%)
  starting transfers between devices  20.7 us (31%)
  between operations  0.83 us (1%)
    ppermute x17, waiting for transfers between devices, permute(): lax.ppermute(x, AXES, [(flat(*place), flat(*target(*place))) for place in...  23.1 us
    ppermute x17, starting transfers between devices, permute(): lax.ppermute(x, AXES, [(flat(*place), flat(*target(*place))) for place in...  20.7 us
    pallas_call x4, Pallas kernels, add(): call(functools.partial(add_kernel, step, list(range(len(chunks)))), 'add%...  6.16 us
    pallas_call x4, Pallas kernels, shards(): call(functools.partial(last_kernel, count - 1, per_shard - 1, sum(pieces[...  3.56 us
    pallas_call x4, Pallas kernels, shards(): call(functools.partial(arrived_kernel, sum(pieces[:i])), 'arrived%d' % i,...  3.4 us
    pallas_call x1, Pallas kernels, shards(): call(ham_kernel, 'ham', sds((blocks // 2, tall, 3 * LANES), BF16), (SMEM,...  2.51 us
    pallas_call x2, Pallas kernels, shards(): call(functools.partial(cut_kernel, h), 'cut%d' % h, sds((2, tile, dens_ti...  1.99 us
    pallas_call x1, Pallas kernels, shards(): call(own_kernel, 'own', (sds((rows, tile, width), F32), sds((rows, tile,...  1.66 us
  transfers between devices with their start and end apart: 17, of which 12 were waited for; matrix products, arithmetic and copies ran while one was open for 0% of the time, Pallas kernels for 29%

profile of v17, /device:TPU:0, one launch (start us, length us, event | category | flops | bytes accessed | tf_op | source)
XLA Modules:
  0.0 66.7 jit_solution(14116311321888209370)
XLA Ops:
  0.6 1.0 %cut0.1.rest_0_ = f32[2,64,512]{2,1,0:T(8,128)S(1)} custom-call(f32[4,64,512]{2,1,0:T(8,128)} %dens.2), custom_call_target="tpu_custom_call" | custom-call | flops 1024 | bytes 1024 | tf_op jit(solution)/shard_map/cut0/pallas_call | solution.py:296
  1.7 3.1 %collective-permute-start.1 = (f32[2,64,512]{2,1,0:T(8,128)S(1)}, f32[2,64,512]{2,1,0:T(8,128)S(1)}, u32[]{:S(2)}, u32[]{:S(2)}) collective-permute-start(f32[2,64,512]{2,1,0:T(8,128)S(1)} %cut0.1.rest_0_), channel_id=1, source_target_pairs={{0,1},{1,3},{2,0},{3,2},{4,5},{5,7},{6,4},{7,6},{8,9},{9,11},{10,8... | collective-permute-start | bytes 786440 | tf_op jit(solution)/shard_map/ppermute | solution.py:24
  4.8 1.0 %cut1.1.rest_1_ = f32[2,64,512]{2,1,0:T(8,128)S(1)} custom-call(f32[4,64,512]{2,1,0:T(8,128)} %dens.2), custom_call_target="tpu_custom_call" | custom-call | flops 1024 | bytes 1024 | tf_op jit(solution)/shard_map/cut1/pallas_call | solution.py:296
  5.7 2.6 %collective-permute-start = (f32[2,64,512]{2,1,0:T(8,128)S(1)}, f32[2,64,512]{2,1,0:T(8,128)S(1)}, u32[]{:S(2)}, u32[]{:S(2)}) collective-permute-start(f32[2,64,512]{2,1,0:T(8,128)S(1)} %cut1.1.rest_1_), channel_id=1, source_target_pairs={{0,1},{1,3},{2,0},{3,2},{4,5},{5,7},{6,4},{7,6},{8,9},{9,11},{10,8... | collective-permute-start | bytes 786440 | tf_op jit(solution)/shard_map/ppermute | solution.py:24
  8.4 1.4 %table.1.dens_table = s32[4,16]{1,0:T(4,128)S(1)} custom-call(s32[4,8]{1,0:T(4,128)} %columns, s32[4]{0:T(128)} %counts.1), custom_call_target="tpu_custom_call" | custom-call | flops 1024 | bytes 1024 | tf_op jit(solution)/shard_map/table/pallas_call | solution.py:312
  9.8 0.4 collective-permute-start.4
  10.2 2.5 %collective-permute-start.3 = (s32[4,16]{1,0:T(4,128)S(1)}, s32[4,16]{1,0:T(4,128)S(1)}, u32[]{:S(2)}, u32[]{:S(2)}) collective-permute-start(s32[4,16]{1,0:T(4,128)S(1)} %table.1.dens_table), channel_id=1, source_target_pairs={{0,3},{1,2},{2,1},{3,0},{4,7},{5,6},{6,5},{7,4},{8,11},{9,10},{10,... | collective-permute-start | bytes 776 | tf_op jit(solution)/shard_map/ppermute | solution.py:24
  12.6 0.0 collective-permute-start.2
  12.6 0.3 collective-permute-done.1.rest_1_
  12.9 1.6 %collective-permute-start.6 = (f32[2,64,512]{2,1,0:T(8,128)S(1)}, f32[2,64,512]{2,1,0:T(8,128)S(1)}, u32[]{:S(2)}, u32[]{:S(2)}) collective-permute-start(f32[2,64,512]{2,1,0:T(8,128)S(1)} %collective-permute-done.1.rest_1_), channel_id=1, source_target_pairs={{0,1},{1,3},{2,0},{3,2},{4,5},{5,7},{6,4},{7,6},{8,9},{9,11},{10,8... | collective-permute-start | bytes 786440 | tf_op jit(solution)/shard_map/ppermute | solution.py:24
  14.6 2.5 %ham.1.a = bf16[8,256,384]{2,1,0:T(8,128)(2,1)S(1)} custom-call(s32[4,12]{1,0:T(4,128)} %ham_cols.1, s32[4]{0:T(128)} %ham_count.1, f32[4,64,768]{2,1,0:T(8,128)} %ham.2), custom_call_target="tpu_custom_call" | custom-call | flops 1024 | bytes 1024 | tf_op jit(solution)/shard_map/ham/pallas_call | solution.py:347
  17.1 0.1 collective-permute-done.4.dens_table
  17.1 3.0 %collective-permute-done.3.dens_table = s32[4,16]{1,0:T(4,128)S(1)} collective-permute-done((s32[4,16]{1,0:T(4,128)S(1)}, s32[4,16]{1,0:T(4,128)S(1)}, u32[]{:S(2)}, u32[]{:S(2)}) %collective-permute-start.3) | collective-permute-done | bytes 288 | tf_op jit(solution)/shard_map/ppermute | solution.py:24
  20.1 0.6 collective-permute-start.5
  20.7 0.3 margin.1
  21.0 1.1 %pick.1 = bf16[2,512,1024]{2,1,0:T(8,128)(2,1)S(1)} custom-call(s32[4,16]{1,0:T(4,128)S(1)} %collective-permute-done.4.dens_table), custom_call_target="tpu_custom_call" | custom-call | flops 1024 | bytes 1024 | tf_op jit(solution)/shard_map/pick/pallas_call | solution.py:363
  22.1 1.6 %add0.1.rest_0_ = f32[256,1024]{1,0:T(8,128)S(1)} custom-call(s32[4,16]{1,0:T(4,128)S(1)} %table.1.dens_table, bf16[8,256,384]{2,1,0:T(8,128)(2,1)S(1)} %ham.1.a, f32[2,64,512]{2,1,0:T(8,128)S(1)} %cut0.1.rest_0_, f32[2,64,512]{2,1,0:T(8,128)S(1)} %cut1.1.rest_1_), custom_call_target="tpu_custom_call" | custom-call | flops 1024 | bytes 1024 | tf_op jit(solution)/shard_map/add0/pallas_call | solution.py:332
  23.7 0.6 collective-permute-done.6.rest_1_
  24.3 2.0 %collective-permute-start.7 = (f32[2,64,512]{2,1,0:T(8,128)S(1)}, f32[2,64,512]{2,1,0:T(8,128)S(1)}, u32[]{:S(2)}, u32[]{:S(2)}) collective-permute-start(f32[2,64,512]{2,1,0:T(8,128)S(1)} %collective-permute-done.6.rest_1_), channel_id=1, source_target_pairs={{0,1},{1,3},{2,0},{3,2},{4,5},{5,7},{6,4},{7,6},{8,9},{9,11},{10,8... | collective-permute-start | bytes 786440 | tf_op jit(solution)/shard_map/ppermute | solution.py:24
  26.3 3.9 %collective-permute-done.5.rest_2_ = f32[2,64,512]{2,1,0:T(8,128)S(1)} collective-permute-done((f32[2,64,512]{2,1,0:T(8,128)S(1)}, f32[2,64,512]{2,1,0:T(8,128)S(1)}, u32[]{:S(2)}, u32[]{:S(2)}) %collective-permute-start.5) | collective-permute-done | bytes 262176 | tf_op jit(solution)/shard_map/ppermute | solution.py:24
  30.3 0.8 %collective-permute-start.8 = (f32[2,64,512]{2,1,0:T(8,128)S(1)}, f32[2,64,512]{2,1,0:T(8,128)S(1)}, u32[]{:S(2)}, u32[]{:S(2)}) collective-permute-start(f32[2,64,512]{2,1,0:T(8,128)S(1)} %collective-permute-done.5.rest_2_), channel_id=1, source_target_pairs={{0,1},{1,3},{2,0},{3,2},{4,5},{5,7},{6,4},{7,6},{8,9},{9,11},{10,8... | collective-permute-start | bytes 786440 | tf_op jit(solution)/shard_map/ppermute | solution.py:24
  31.1 1.6 %add1.1.rest_0_ = f32[256,1024]{1,0:T(8,128)S(1)} custom-call(s32[4,16]{1,0:T(4,128)S(1)} %collective-permute-done.2.dens_table, bf16[8,256,384]{2,1,0:T(8,128)(2,1)S(1)} %ham.1.a, f32[256,1024]{1,0:T(8,128)S(1)} %add0.1.rest_0_, f32[2,64,512]{2,1,0:T(8,128)S(1)} %collective-permute-done.1.rest_1_, f32[2,64,512]{2,1,0:T(8,128)S(1)} %collective-permute-done.rest_2_), custom_call_target="tpu_custom_call" | custom-call | flops 1024 | bytes 1024 | tf_op jit(solution)/shard_map/add1/pallas_call | solution.py:332
  32.7 1.6 %add2.1.rest_0_ = f32[256,1024]{1,0:T(8,128)S(1)} custom-call(s32[4,16]{1,0:T(4,128)S(1)} %collective-permute-done.3.dens_table, bf16[8,256,384]{2,1,0:T(8,128)(2,1)S(1)} %ham.1.a, f32[256,1024]{1,0:T(8,128)S(1)} %add1.1.rest_0_, f32[2,64,512]{2,1,0:T(8,128)S(1)} %collective-permute-done.6.rest_1_, f32[2,64,512]{2,1,0:T(8,128)S(1)} %collective-permute-done.5.rest_2_), custom_call_target="tpu_custom_call" | custom-call | flops 1024 | bytes 1024 | tf_op jit(solution)/shard_map/add2/pallas_call | solution.py:332
  34.4 1.5 %collective-permute-done.7.rest_1_ = f32[2,64,512]{2,1,0:T(8,128)S(1)} collective-permute-done((f32[2,64,512]{2,1,0:T(8,128)S(1)}, f32[2,64,512]{2,1,0:T(8,128)S(1)}, u32[]{:S(2)}, u32[]{:S(2)}) %collective-permute-start.7) | collective-permute-done | bytes 262176 | tf_op jit(solution)/shard_map/ppermute | solution.py:24
  35.9 1.2 %add3.1.acc_in = f32[256,1024]{1,0:T(8,128)S(1)} custom-call(s32[4,16]{1,0:T(4,128)S(1)} %collective-permute-done.4.dens_table, bf16[8,256,384]{2,1,0:T(8,128)(2,1)S(1)} %ham.1.a, f32[256,1024]{1,0:T(8,128)S(1)} %add2.1.rest_0_, f32[2,64,512]{2,1,0:T(8,128)S(1)} %collective-permute-done.7.rest_1_), custom_call_target="tpu_custom_call" | custom-call | flops 1024 | bytes 1024 | tf_op jit(solution)/shard_map/add3/pallas_call | solution.py:332
  37.1 3.2 %collective-permute-done.8.chunk = f32[2,64,512]{2,1,0:T(8,128)S(1)} collective-permute-done((f32[2,64,512]{2,1,0:T(8,128)S(1)}, f32[2,64,512]{2,1,0:T(8,128)S(1)}, u32[]{:S(2)}, u32[]{:S(2)}) %collective-permute-start.8) | collective-permute-done | bytes 262176 | tf_op jit(solution)/shard_map/ppermute | solution.py:24
  40.3 0.9 %last0.1 = (f32[256,256]{1,0:T(8,128)S(1)}, f32[256,256]{1,0:T(8,128)S(1)}, f32[256,256]{1,0:T(8,128)S(1)}) custom-call(bf16[8,256,384]{2,1,0:T(8,128)(2,1)S(1)} %ham.1.a, f32[256,1024]{1,0:T(8,128)S(1)} %add3.1.acc_in, f32[2,64,512]{2,1,0:T(8,128)S(1)} %collective-permute-done.8.chunk, bf16[2,512,1024]{2,1,0:T(8,128)(2,1)S(1)} %pick.1, ...), custom_call_target="tpu_custom_call" | custom-call | flops 1024 | bytes 1024 | tf_op jit(solution)/shard_map/last0/pallas_call | solution.py:379
  41.2 0.1 collective-permute-start.15
  41.3 1.7 %collective-permute-start.16 = (f32[256,256]{1,0:T(8,128)S(1)}, f32[256,256]{1,0:T(8,128)S(1)}, u32[]{:S(2)}, u32[]{:S(2)}) collective-permute-start(f32[256,256]{1,0:T(8,128)S(1)} %get-tuple-element.82), channel_id=1, source_target_pairs={{0,12},{1,13},{2,14},{3,15},{4,0},{5,1},{6,2},{7,3},{8,4},{9,5},{1... | collective-permute-start | bytes 786440 | tf_op jit(solution)/shard_map/ppermute | solution.py:24
  43.0 0.9 %last1.1 = (f32[256,256]{1,0:T(8,128)S(1)}, f32[256,256]{1,0:T(8,128)S(1)}, f32[256,256]{1,0:T(8,128)S(1)}) custom-call(bf16[8,256,384]{2,1,0:T(8,128)(2,1)S(1)} %ham.1.a, f32[256,1024]{1,0:T(8,128)S(1)} %add3.1.acc_in, f32[2,64,512]{2,1,0:T(8,128)S(1)} %collective-permute-done.8.chunk, bf16[2,512,1024]{2,1,0:T(8,128)(2,1)S(1)} %pick.1, ...), custom_call_target="tpu_custom_call" | custom-call | flops 1024 | bytes 1024 | tf_op jit(solution)/shard_map/last1/pallas_call | solution.py:379
  43.9 0.1 collective-permute-start.13
  44.0 1.7 %collective-permute-start.14 = (f32[256,256]{1,0:T(8,128)S(1)}, f32[256,256]{1,0:T(8,128)S(1)}, u32[]{:S(2)}, u32[]{:S(2)}) collective-permute-start(f32[256,256]{1,0:T(8,128)S(1)} %get-tuple-element.80), channel_id=1, source_target_pairs={{0,12},{1,13},{2,14},{3,15},{4,0},{5,1},{6,2},{7,3},{8,4},{9,5},{1... | collective-permute-start | bytes 786440 | tf_op jit(solution)/shard_map/ppermute | solution.py:24
  45.7 0.9 %last2.1 = (f32[256,256]{1,0:T(8,128)S(1)}, f32[256,256]{1,0:T(8,128)S(1)}, f32[256,256]{1,0:T(8,128)S(1)}) custom-call(bf16[8,256,384]{2,1,0:T(8,128)(2,1)S(1)} %ham.1.a, f32[256,1024]{1,0:T(8,128)S(1)} %add3.1.acc_in, f32[2,64,512]{2,1,0:T(8,128)S(1)} %collective-permute-done.8.chunk, bf16[2,512,1024]{2,1,0:T(8,128)(2,1)S(1)} %pick.1, ...), custom_call_target="tpu_custom_call" | custom-call | flops 1024 | bytes 1024 | tf_op jit(solution)/shard_map/last2/pallas_call | solution.py:379
  46.6 0.9 %last3.1 = (f32[256,256]{1,0:T(8,128)S(1)}, f32[256,256]{1,0:T(8,128)S(1)}, f32[256,256]{1,0:T(8,128)S(1)}) custom-call(bf16[8,256,384]{2,1,0:T(8,128)(2,1)S(1)} %ham.1.a, f32[256,1024]{1,0:T(8,128)S(1)} %add3.1.acc_in, f32[2,64,512]{2,1,0:T(8,128)S(1)} %collective-permute-done.8.chunk, bf16[2,512,1024]{2,1,0:T(8,128)(2,1)S(1)} %pick.1, ...), custom_call_target="tpu_custom_call" | custom-call | flops 1024 | bytes 1024 | tf_op jit(solution)/shard_map/last3/pallas_call | solution.py:379
  47.5 0.1 collective-permute-start.9
  47.6 0.4 collective-permute-done.15.above
  48.0 1.2 %collective-permute-start.11 = (f32[256,256]{1,0:T(8,128)S(1)}, f32[256,256]{1,0:T(8,128)S(1)}, u32[]{:S(2)}, u32[]{:S(2)}) collective-permute-start(f32[256,256]{1,0:T(8,128)S(1)} %get-tuple-element.77), channel_id=1, source_target_pairs={{0,4},{1,5},{2,6},{3,7},{4,8},{5,9},{6,10},{7,11},{8,12},{9,13},{1... | collective-permute-start | bytes 786440 | tf_op jit(solution)/shard_map/ppermute | solution.py:24
  49.2 0.5 collective-permute-done.16.below
  49.7 2.2 %collective-permute-start.12 = (f32[256,256]{1,0:T(8,128)S(1)}, f32[256,256]{1,0:T(8,128)S(1)}, u32[]{:S(2)}, u32[]{:S(2)}) collective-permute-start(f32[256,256]{1,0:T(8,128)S(1)} %get-tuple-element.78), channel_id=1, source_target_pairs={{0,12},{1,13},{2,14},{3,15},{4,0},{5,1},{6,2},{7,3},{8,4},{9,5},{1... | collective-permute-start | bytes 786440 | tf_op jit(solution)/shard_map/ppermute | solution.py:24
  51.9 1.7 %collective-permute-done.13.above = f32[256,256]{1,0:T(8,128)S(1)} collective-permute-done((f32[256,256]{1,0:T(8,128)S(1)}, f32[256,256]{1,0:T(8,128)S(1)}, u32[]{:S(2)}, u32[]{:S(2)}) %collective-permute-start.13) | collective-permute-done | bytes 262176 | tf_op jit(solution)/shard_map/ppermute | solution.py:24
  53.6 0.0 collective-permute-start.10
  53.6 1.7 %own.1 = (f32[4,64,1024]{2,1,0:T(8,128)}, f32[4,64,3072]{2,1,0:T(8,128)}) custom-call(bf16[3,256,256]{2,1,0:T(8,128)(2,1)S(1)} %get-tuple-element.53.m_hi, bf16[3,256,256]{2,1,0:T(8,128)(2,1)S(1)} %get-tuple-element.54.m_lo, f32[256,256]{1,0:T(8,128)S(1)} %get-tuple-element.65.rest_0_, f32[256,256]{1,0:T(8,128)S(1)} %get-tuple-element.68.rest_1_, ...), custom_call_target="tpu_custom_call" | custom-call | flops 1024 | bytes 1024 | tf_op jit(solution)/shard_map/own/pallas_call | solution.py:392
  55.3 0.9 %arrived0.1.window_in = f32[4,64,3072]{2,1,0:T(8,128)} custom-call(f32[256,256]{1,0:T(8,128)S(1)} %collective-permute-done.15.above, f32[256,256]{1,0:T(8,128)S(1)} %collective-permute-done.16.below, f32[4,64,3072]{2,1,0:T(8,128)} %get-tuple-element.83.window_in), custom_call_target="tpu_custom_call", output_to_operand_aliasing={{}: (2, {})} | custom-call | flops 1024 | bytes 1024 | tf_op jit(solution)/shard_map/arrived0/pallas_call | solution.py:401
  56.2 0.9 %arrived1.1.window_in = f32[4,64,3072]{2,1,0:T(8,128)} custom-call(f32[256,256]{1,0:T(8,128)S(1)} %collective-permute-done.13.above, f32[256,256]{1,0:T(8,128)S(1)} %collective-permute-done.14.below, f32[4,64,3072]{2,1,0:T(8,128)} %arrived0.1.window_in), custom_call_target="tpu_custom_call", output_to_operand_aliasing={{}: (2, {})} | custom-call | flops 1024 | bytes 1024 | tf_op jit(solution)/shard_map/arrived1/pallas_call | solution.py:401
  57.0 7.8 %collective-permute-done.11.above = f32[256,256]{1,0:T(8,128)S(1)} collective-permute-done((f32[256,256]{1,0:T(8,128)S(1)}, f32[256,256]{1,0:T(8,128)S(1)}, u32[]{:S(2)}, u32[]{:S(2)}) %collective-permute-start.11) | collective-permute-done | bytes 262176 | tf_op jit(solution)/shard_map/ppermute | solution.py:24
  64.8 0.8 %arrived2.1.window_in = f32[4,64,3072]{2,1,0:T(8,128)} custom-call(f32[256,256]{1,0:T(8,128)S(1)} %collective-permute-done.11.above, f32[256,256]{1,0:T(8,128)S(1)} %collective-permute-done.12.below, f32[4,64,3072]{2,1,0:T(8,128)} %arrived1.1.window_in), custom_call_target="tpu_custom_call", output_to_operand_aliasing={{}: (2, {})} | custom-call | flops 1024 | bytes 1024 | tf_op jit(solution)/shard_map/arrived2/pallas_call | solution.py:401
  65.7 0.1 collective-permute-done.10.below
  65.8 0.8 %arrived3.1 = f32[4,64,3072]{2,1,0:T(8,128)} custom-call(f32[256,256]{1,0:T(8,128)S(1)} %collective-permute-done.9.above, f32[256,256]{1,0:T(8,128)S(1)} %collective-permute-done.10.below, f32[4,64,3072]{2,1,0:T(8,128)} %arrived2.1.window_in), custom_call_target="tpu_custom_call", output_to_operand_aliasing={{}: (2, {})} | custom-call | flops 1024 | bytes 1024 | tf_op jit(solution)/shard_map/arrived3/pallas_call | solution.py:401
  (7 shorter events, 0.0 us)
Async XLA Ops:
  0.6 20.1 %copy-start = (f32[4,64,768]{2,1,0:T(8,128)S(1)}, f32[4,64,768]{2,1,0:T(8,128)}, u32[]{:S(2)}) copy-start(f32[4,64,768]{2,1,0:T(8,128)} %over.1) | copy-start | bytes 2359300
  1.7 11.2 %collective-permute-start.1 = (f32[2,64,512]{2,1,0:T(8,128)S(1)}, f32[2,64,512]{2,1,0:T(8,128)S(1)}, u32[]{:S(2)}, u32[]{:S(2)}) collective-permute-start(f32[2,64,512]{2,1,0:T(8,128)S(1)} %cut0.1.rest_0_), channel_id=1, source_target_pairs={{0,1},{1,3},{2,0},{3,2},{4,5},{5,7},{6,4},{7,6},{8,9},{9,11},{10,8... | collective-permute-start | bytes 786440 | tf_op jit(solution)/shard_map/ppermute | solution.py:24
  5.7 14.4 %collective-permute-start = (f32[2,64,512]{2,1,0:T(8,128)S(1)}, f32[2,64,512]{2,1,0:T(8,128)S(1)}, u32[]{:S(2)}, u32[]{:S(2)}) collective-permute-start(f32[2,64,512]{2,1,0:T(8,128)S(1)} %cut1.1.rest_1_), channel_id=1, source_target_pairs={{0,1},{1,3},{2,0},{3,2},{4,5},{5,7},{6,4},{7,6},{8,9},{9,11},{10,8... | collective-permute-start | bytes 786440 | tf_op jit(solution)/shard_map/ppermute | solution.py:24
  9.8 7.4 %collective-permute-start.4 = (s32[4,16]{1,0:T(4,128)S(1)}, s32[4,16]{1,0:T(4,128)S(1)}, u32[]{:S(2)}, u32[]{:S(2)}) collective-permute-start(s32[4,16]{1,0:T(4,128)S(1)} %table.1.dens_table), channel_id=1, source_target_pairs={{0,2},{1,0},{2,3},{3,1},{4,6},{5,4},{6,7},{7,5},{8,10},{9,8},{10,1... | collective-permute-start | bytes 776 | tf_op jit(solution)/shard_map/ppermute | solution.py:24
  10.2 9.9 %collective-permute-start.3 = (s32[4,16]{1,0:T(4,128)S(1)}, s32[4,16]{1,0:T(4,128)S(1)}, u32[]{:S(2)}, u32[]{:S(2)}) collective-permute-start(s32[4,16]{1,0:T(4,128)S(1)} %table.1.dens_table), channel_id=1, source_target_pairs={{0,3},{1,2},{2,1},{3,0},{4,7},{5,6},{6,5},{7,4},{8,11},{9,10},{10,... | collective-permute-start | bytes 776 | tf_op jit(solution)/shard_map/ppermute | solution.py:24
  12.6 7.5 %collective-permute-start.2 = (s32[4,16]{1,0:T(4,128)S(1)}, s32[4,16]{1,0:T(4,128)S(1)}, u32[]{:S(2)}, u32[]{:S(2)}) collective-permute-start(s32[4,16]{1,0:T(4,128)S(1)} %table.1.dens_table), channel_id=1, source_target_pairs={{0,1},{1,3},{2,0},{3,2},{4,5},{5,7},{6,4},{7,6},{8,9},{9,11},{10,8... | collective-permute-start | bytes 776 | tf_op jit(solution)/shard_map/ppermute | solution.py:24
  12.9 11.4 %collective-permute-start.6 = (f32[2,64,512]{2,1,0:T(8,128)S(1)}, f32[2,64,512]{2,1,0:T(8,128)S(1)}, u32[]{:S(2)}, u32[]{:S(2)}) collective-permute-start(f32[2,64,512]{2,1,0:T(8,128)S(1)} %collective-permute-done.1.rest_1_), channel_id=1, source_target_pairs={{0,1},{1,3},{2,0},{3,2},{4,5},{5,7},{6,4},{7,6},{8,9},{9,11},{10,8... | collective-permute-start | bytes 786440 | tf_op jit(solution)/shard_map/ppermute | solution.py:24
  20.1 10.1 %collective-permute-start.5 = (f32[2,64,512]{2,1,0:T(8,128)S(1)}, f32[2,64,512]{2,1,0:T(8,128)S(1)}, u32[]{:S(2)}, u32[]{:S(2)}) collective-permute-start(f32[2,64,512]{2,1,0:T(8,128)S(1)} %collective-permute-done.rest_2_), channel_id=1, source_target_pairs={{0,1},{1,3},{2,0},{3,2},{4,5},{5,7},{6,4},{7,6},{8,9},{9,11},{10,8... | collective-permute-start | bytes 786440 | tf_op jit(solution)/shard_map/ppermute | solution.py:24
  24.3 11.6 %collective-permute-start.7 = (f32[2,64,512]{2,1,0:T(8,128)S(1)}, f32[2,64,512]{2,1,0:T(8,128)S(1)}, u32[]{:S(2)}, u32[]{:S(2)}) collective-permute-start(f32[2,64,512]{2,1,0:T(8,128)S(1)} %collective-permute-done.6.rest_1_), channel_id=1, source_target_pairs={{0,1},{1,3},{2,0},{3,2},{4,5},{5,7},{6,4},{7,6},{8,9},{9,11},{10,8... | collective-permute-start | bytes 786440 | tf_op jit(solution)/shard_map/ppermute | solution.py:24
  30.3 10.1 %collective-permute-start.8 = (f32[2,64,512]{2,1,0:T(8,128)S(1)}, f32[2,64,512]{2,1,0:T(8,128)S(1)}, u32[]{:S(2)}, u32[]{:S(2)}) collective-permute-start(f32[2,64,512]{2,1,0:T(8,128)S(1)} %collective-permute-done.5.rest_2_), channel_id=1, source_target_pairs={{0,1},{1,3},{2,0},{3,2},{4,5},{5,7},{6,4},{7,6},{8,9},{9,11},{10,8... | collective-permute-start | bytes 786440 | tf_op jit(solution)/shard_map/ppermute | solution.py:24
  41.2 6.8 %collective-permute-start.15 = (f32[256,256]{1,0:T(8,128)S(1)}, f32[256,256]{1,0:T(8,128)S(1)}, u32[]{:S(2)}, u32[]{:S(2)}) collective-permute-start(f32[256,256]{1,0:T(8,128)S(1)} %get-tuple-element.81), channel_id=1, source_target_pairs={{0,4},{1,5},{2,6},{3,7},{4,8},{5,9},{6,10},{7,11},{8,12},{9,13},{1... | collective-permute-start | bytes 786440 | tf_op jit(solution)/shard_map/ppermute | solution.py:24
  41.3 8.4 %collective-permute-start.16 = (f32[256,256]{1,0:T(8,128)S(1)}, f32[256,256]{1,0:T(8,128)S(1)}, u32[]{:S(2)}, u32[]{:S(2)}) collective-permute-start(f32[256,256]{1,0:T(8,128)S(1)} %get-tuple-element.82), channel_id=1, source_target_pairs={{0,12},{1,13},{2,14},{3,15},{4,0},{5,1},{6,2},{7,3},{8,4},{9,5},{1... | collective-permute-start | bytes 786440 | tf_op jit(solution)/shard_map/ppermute | solution.py:24
  43.9 9.7 %collective-permute-start.13 = (f32[256,256]{1,0:T(8,128)S(1)}, f32[256,256]{1,0:T(8,128)S(1)}, u32[]{:S(2)}, u32[]{:S(2)}) collective-permute-start(f32[256,256]{1,0:T(8,128)S(1)} %get-tuple-element.79), channel_id=1, source_target_pairs={{0,4},{1,5},{2,6},{3,7},{4,8},{5,9},{6,10},{7,11},{8,12},{9,13},{1... | collective-permute-start | bytes 786440 | tf_op jit(solution)/shard_map/ppermute | solution.py:24
  44.0 12.1 %collective-permute-start.14 = (f32[256,256]{1,0:T(8,128)S(1)}, f32[256,256]{1,0:T(8,128)S(1)}, u32[]{:S(2)}, u32[]{:S(2)}) collective-permute-start(f32[256,256]{1,0:T(8,128)S(1)} %get-tuple-element.80), channel_id=1, source_target_pairs={{0,12},{1,13},{2,14},{3,15},{4,0},{5,1},{6,2},{7,3},{8,4},{9,5},{1... | collective-permute-start | bytes 786440 | tf_op jit(solution)/shard_map/ppermute | solution.py:24
  47.5 18.2 %collective-permute-start.9 = (f32[256,256]{1,0:T(8,128)S(1)}, f32[256,256]{1,0:T(8,128)S(1)}, u32[]{:S(2)}, u32[]{:S(2)}) collective-permute-start(f32[256,256]{1,0:T(8,128)S(1)} %get-tuple-element.75), channel_id=1, source_target_pairs={{0,4},{1,5},{2,6},{3,7},{4,8},{5,9},{6,10},{7,11},{8,12},{9,13},{1... | collective-permute-start | bytes 786440 | tf_op jit(solution)/shard_map/ppermute | solution.py:24
  48.0 16.9 %collective-permute-start.11 = (f32[256,256]{1,0:T(8,128)S(1)}, f32[256,256]{1,0:T(8,128)S(1)}, u32[]{:S(2)}, u32[]{:S(2)}) collective-permute-start(f32[256,256]{1,0:T(8,128)S(1)} %get-tuple-element.77), channel_id=1, source_target_pairs={{0,4},{1,5},{2,6},{3,7},{4,8},{5,9},{6,10},{7,11},{8,12},{9,13},{1... | collective-permute-start | bytes 786440 | tf_op jit(solution)/shard_map/ppermute | solution.py:24
  49.7 15.2 %collective-permute-start.12 = (f32[256,256]{1,0:T(8,128)S(1)}, f32[256,256]{1,0:T(8,128)S(1)}, u32[]{:S(2)}, u32[]{:S(2)}) collective-permute-start(f32[256,256]{1,0:T(8,128)S(1)} %get-tuple-element.78), channel_id=1, source_target_pairs={{0,12},{1,13},{2,14},{3,15},{4,0},{5,1},{6,2},{7,3},{8,4},{9,5},{1... | collective-permute-start | bytes 786440 | tf_op jit(solution)/shard_map/ppermute | solution.py:24
  53.6 12.2 %collective-permute-start.10 = (f32[256,256]{1,0:T(8,128)S(1)}, f32[256,256]{1,0:T(8,128)S(1)}, u32[]{:S(2)}, u32[]{:S(2)}) collective-permute-start(f32[256,256]{1,0:T(8,128)S(1)} %get-tuple-element.76), channel_id=1, source_target_pairs={{0,12},{1,13},{2,14},{3,15},{4,0},{5,1},{6,2},{7,3},{8,4},{9,5},{1... | collective-permute-start | bytes 786440 | tf_op jit(solution)/shard_map/ppermute | solution.py:24
